TPU v7x, 32 devices: a whole 2x2x4 slice. The times are simulated.
32 devices in a mesh: docs: 8 (over z, y), anch: 4 (over x, core).
Axes of the slice: x: 2, y: 2, z: 4, core: 2. Of those that a mesh axis runs over, the one named last changes fastest.
Arguments:
- features: bfloat16 [65536, 128], P('docs'), may hold values from -6 to 6
- anchors: bfloat16 [1024, 128], P('anch'), may hold values from -6 to 6
- lab_index: int32 [128], P('docs'), may hold values from 0 to 65535, as said below
- lab_class: int32 [128], P('docs'), may hold values from 0 to 15
Outputs:
- anchor_scores: float32 [1024, 16], P('anch')
- doc_scores: float32 [16, 65536], P('anch', 'docs')
Inputs may be any that keep to these rules, and one draw needn't show every extreme that they name: Entries k * 16 to (k + 1) * 16 - 1 of lab_index name documents k * 8192 to (k + 1) * 8192 - 1; an index may repeat.
All inputs are finite; a program needn't handle non-finite values.
Results may differ from a plain program's by a relative error of at most 0.0003.
Values may be sent and summed in bfloat16 or wider, within the bound.
No kernel may reach another device: no remote copies, remote signals or barrier semaphores. Data moves between devices by JAX's collectives and lax.ppermute only.
A program may use at most 64 MiB of HBM per device.

v0:
```python
import jax
import jax.numpy as jnp
from jax import lax
from jax.sharding import PartitionSpec as P

ANCHORS = 1024
CLASSES = 16
ITERS = 2


width_h = 0.25
ridge = 0.1
highest = lax.Precision.HIGHEST


def kernel_terms(block, points):
    cross = lax.dot_general(
        block, points, (((1,), (1,)), ((), ())), preferred_element_type=jnp.float32
    )
    row_sq = jnp.sum(jnp.square(block.astype(jnp.float32)), axis=1)
    col_sq = jnp.sum(jnp.square(points.astype(jnp.float32)), axis=1)
    dist = (row_sq[:, None] + col_sq[None, :] - 2.0 * cross) / block.shape[1]
    ratio = width_h / (width_h + dist)
    square = ratio * ratio
    fourth = square * square
    return fourth * fourth


def trans_dot(left, right):
    return lax.dot_general(
        left, right, (((0,), (0,)), ((), ())), precision=highest, preferred_element_type=jnp.float32
    )


def plain_dot(left, right):
    return jnp.dot(left, right, precision=highest, preferred_element_type=jnp.float32)


def scores_of(solution, zmat):
    return lax.dot_general(
        solution,
        zmat,
        (((0,), (1,)), ((), ())),
        precision=highest,
        preferred_element_type=jnp.float32,
    )


def per_device(features, anchors, lab_index, lab_class):
    docs_count = features.shape[0]
    n_docs = lax.axis_size("docs")
    lab_scale = ANCHORS / (lab_index.shape[0] * n_docs)
    graph_scale = ANCHORS * ANCHORS / (docs_count * n_docs)
    onehot = (lab_class[:, None] == jnp.arange(CLASSES, dtype=jnp.int32)[None, :]).astype(
        jnp.float32
    )
    local_index = lab_index - lax.axis_index("docs") * docs_count
    kern = kernel_terms(features, anchors)
    totals = lax.psum(jnp.sum(kern, axis=1), "anch")
    zmat = kern / totals[:, None]
    zlab = jnp.take(zmat, local_index, axis=0)
    degree, rhs = lax.psum(
        (jnp.sum(zmat, axis=0), CLASSES * lab_scale * trans_dot(zlab, onehot)), "docs"
    )

    def doc_sum(part):
        return lax.psum(part, "anch")

    solution = jnp.zeros_like(rhs)
    resid = rhs
    direc = rhs
    norm_now = lax.psum(jnp.sum(resid * resid), "anch")
    for step in range(ITERS):
        spread = doc_sum(plain_dot(zmat, direc))
        first, labeled = lax.psum(
            (trans_dot(zmat, spread), trans_dot(zlab, jnp.take(spread, local_index, axis=0))),
            "docs",
        )
        spread_back = doc_sum(plain_dot(zmat, first / degree[:, None]))
        back = lax.psum(trans_dot(zmat, spread_back), "docs")
        image = lab_scale * labeled + graph_scale * (first - back) + ridge * direc
        curv, mixed_term, image_sq = lax.psum(
            (jnp.sum(direc * image), jnp.sum(resid * image), jnp.sum(image * image)), "anch"
        )
        alpha = norm_now / curv
        solution = solution + alpha * direc
        resid = resid - alpha * image
        norm_next = norm_now - 2.0 * alpha * mixed_term + alpha * alpha * image_sq
        direc = resid + norm_next / norm_now * direc
        norm_now = norm_next
    part = solution
    scores = lax.psum_scatter(scores_of(part, zmat), "anch", scatter_dimension=0, tiled=True)
    return (solution, scores)


def solution(mesh):
    in_specs = (P("docs", None), P("anch", None), P("docs"), P("docs"))
    out_specs = (P("anch", None), P("anch", "docs"))
    return jax.shard_map(
        per_device, mesh=mesh, in_specs=in_specs, out_specs=out_specs, check_vma=False
    )
```

profile of v0, /device:TPU:0, one launch (start us, length us, event | category | flops | bytes accessed | tf_op | source)
XLA Modules:
  0.0 489.5 jit_solution(5951919168552184356)
XLA Ops:
  7.2 0.0 all-reduce.11.cloned.1.call-start
  7.2 2.7 multiply_reduce_fusion
  10.0 1.0 multiply_reduce_fusion.1
  10.9 0.0 copy-start.3
  10.9 6.7 %fusion.36 = (f32[8192]{0:T(1024)S(1)}, f32[8192,256]{1,0:T(8,128)}) fusion(bf16[8192,128]{1,0:T(8,128)(2,1)} %param.6, bf16[256,128]{1,0:T(8,128)(2,1)} %param.7, f32[256]{0:T(256)S(1)} %multiply_reduce_fusion.1, f32[8192]{0:T(1024)S(1)} %multiply_reduce_fusion), kind=kOutput, calls=%fused_computation.56 | convolution fusion | flops 557834240 | bytes 10617856 | tf_op jit(solution)/shard_map/dot_general | solution.py:17
  17.6 12.9 %psum.122 = f32[8192]{0:T(1024)S(1)} all-reduce(f32[8192]{0:T(1024)S(1)} %get-tuple-element.20), channel_id=1, replica_groups=mesh['docs'=8,'anch'=4] {'anch'}, use_global_device_ids=true, to_apply=%region_3.0 | all-reduce | flops 8192 | bytes 65536 | tf_op jit(solution)/shard_map/psum | solution.py:59
  30.5 0.0 copy-done.3
  30.6 0.0 copy-start.4
  30.6 6.1 %fusion.35 = (f32[256]{0:T(256)S(1)}, f32[8192,256]{1,0:T(8,128)}) fusion(f32[8192,256]{1,0:T(8,128)} %get-tuple-element.21, f32[8192]{0:T(1024)S(1)} %psum.122), kind=kLoop, calls=%fused_computation.55 | loop fusion | flops 4194048 | bytes 16811008 | tf_op jit(solution)/shard_map/reduce_sum | solution.py:63
  36.6 4.0 gather_fusion
  40.6 0.0 copy-done.4
  40.6 0.3 convolution_multiply_fusion.1
  40.9 37.4 %psum.123 = f32[256,16]{0,1:T(8,128)S(1)} all-reduce(f32[256,16]{0,1:T(8,128)S(1)} %convolution_multiply_fusion.1), channel_id=1, replica_groups=mesh['docs'=8,'anch'=4] {'docs'}, use_global_device_ids=true, to_apply=%region_4.5 | all-reduce | flops 4096 | bytes 32768 | tf_op jit(solution)/shard_map/psum | solution.py:62
  78.3 11.3 %fusion.37 = f32[8192,16]{0,1:T(8,128)} fusion(f32[8192,256]{1,0:T(8,128)} %get-tuple-element.17, f32[256,16]{0,1:T(8,128)S(1)} %psum.123), kind=kOutput, calls=%fused_computation.57 | convolution fusion | flops 402653184 | bytes 8929280 | tf_op jit(solution)/shard_map/dot_general | solution.py:36
  89.5 0.0 all-reduce.11.cloned.1.call-update
  89.6 0.5 all-reduce.13.cloned.1.call-start
  90.1 29.3 %all-reduce.11.cloned.1.call-done = f32[8192,16]{0,1:T(8,128)} async-done(((f32[8192,16]{0,1:T(8,128)}), f32[8192,16]{0,1:T(8,128)}) %all-reduce.11.cloned.1.call-update) | async-done | bytes 524304 | tf_op jit(solution)/shard_map/psum | solution.py:67
  119.4 0.0 copy-start
  119.4 7.5 %fusion.38 = f32[256,16]{0,1:T(8,128)S(1)} fusion(f32[8192,256]{1,0:T(8,128)} %get-tuple-element.17, f32[8192,16]{0,1:T(8,128)} %all-reduce.11.cloned.1.call-done), kind=kOutput, calls=%fused_computation.58 | convolution fusion | flops 402653184 | bytes 8929280 | tf_op jit(solution)/shard_map/dot_general | solution.py:30
  126.9 37.1 %all-reduce.3 = (f32[256,16]{0,1:T(8,128)S(1)}, f32[256]{0:T(256)S(1)}) all-reduce(f32[256,16]{0,1:T(8,128)S(1)} %fusion.38, f32[256]{0:T(256)S(1)} %get-tuple-element.16), channel_id=1, replica_groups=mesh['docs'=8,'anch'=4] {'docs'}, use_global_device_ids=true, to_apply=%region_9.11 | all-reduce | flops 4352 | bytes 34816 | tf_op jit(solution)/shard_map/psum | solution.py:75
  163.9 11.2 %fusion.9 = f32[8192,16]{0,1:T(8,128)} fusion(f32[8192,256]{1,0:T(8,128)} %get-tuple-element.17, f32[256,16]{0,1:T(8,128)S(1)} %get-tuple-element.10, f32[256]{0:T(256)S(1)} %get-tuple-element.11), kind=kOutput, calls=%fused_computation.23 | convolution fusion | flops 402657280 | bytes 8930304 | tf_op jit(solution)/shard_map/dot_general | solution.py:36
  175.2 0.0 all-reduce.13.cloned.1.call-update
  175.2 0.2 all-reduce.15.cloned.1.call-start
  175.4 0.0 copy-done
  175.4 2.7 copy.10
  178.1 2.7 gather_fusion.1
  180.8 0.3 fusion.13
  181.1 24.1 %all-reduce.13.cloned.1.call-done = f32[8192,16]{0,1:T(8,128)} async-done(((f32[8192,16]{0,1:T(8,128)}), f32[8192,16]{0,1:T(8,128)}) %all-reduce.13.cloned.1.call-update) | async-done | bytes 524304 | tf_op jit(solution)/shard_map/psum | solution.py:67
  205.2 7.4 %fusion.39 = f32[256,16]{0,1:T(8,128)S(1)} fusion(f32[8192,256]{1,0:T(8,128)} %get-tuple-element.17, f32[8192,16]{0,1:T(8,128)} %all-reduce.13.cloned.1.call-done), kind=kOutput, calls=%fused_computation.59 | convolution fusion | flops 402653184 | bytes 8929280 | tf_op jit(solution)/shard_map/dot_general | solution.py:30
  212.6 37.1 %all-reduce.2 = (f32[256,16]{0,1:T(8,128)S(1)}, f32[256,16]{0,1:T(8,128)S(1)}) all-reduce(f32[256,16]{0,1:T(8,128)S(1)} %fusion.39, f32[256,16]{0,1:T(8,128)S(1)} %fusion.13), channel_id=1, replica_groups=mesh['docs'=8,'anch'=4] {'docs'}, use_global_device_ids=true, to_apply=%region_13.15 | all-reduce | flops 8192 | bytes 65536 | tf_op jit(solution)/shard_map/psum | solution.py:80
  249.7 0.6 multiply_reduce_fusion.3
  250.3 6.3 %all-reduce.4 = (f32[]{:T(128)}, f32[]{:T(128)}, f32[]{:T(128)}) all-reduce(f32[]{:T(128)} %get-tuple-element.5, f32[]{:T(128)} %get-tuple-element.4, f32[]{:T(128)} %get-tuple-element.3), channel_id=1, replica_groups=mesh['docs'=8,'anch'=4] {'anch'}, use_global_device_ids=true, to_apply=%region_6.7 | all-reduce | flops 3 | bytes 24 | tf_op jit(solution)/shard_map/psum | solution.py:72
  260.5 11.3 %fusion.34 = f32[8192,16]{0,1:T(8,128)} fusion(f32[8192,256]{1,0:T(8,128)} %get-tuple-element.17, f32[256,16]{0,1:T(8,128)S(1)} %psum.123, f32[256,16]{0,1:T(8,128)S(1)} %get-tuple-element.15, f32[]{:T(128)S(6)} %div.48, f32[]{:T(128)S(6)} %div.47), kind=kOutput, calls=%fused_computation.54 | convolution fusion | flops 402669568 | bytes 8945672 | tf_op jit(solution)/shard_map/dot_general | solution.py:36
  271.8 0.0 all-reduce.15.cloned.1.call-update
  271.9 0.3 all-reduce.17.cloned.1.call-start
  272.1 29.8 %all-reduce.15.cloned.1.call-done = f32[8192,16]{0,1:T(8,128)} async-done(((f32[8192,16]{0,1:T(8,128)}), f32[8192,16]{0,1:T(8,128)}) %all-reduce.15.cloned.1.call-update) | async-done | bytes 524304 | tf_op jit(solution)/shard_map/psum | solution.py:67
  301.9 0.0 copy-start.1
  301.9 7.5 %fusion.40 = f32[256,16]{0,1:T(8,128)S(1)} fusion(f32[8192,256]{1,0:T(8,128)} %get-tuple-element.17, f32[8192,16]{0,1:T(8,128)} %all-reduce.15.cloned.1.call-done), kind=kOutput, calls=%fused_computation.60 | convolution fusion | flops 402653184 | bytes 8929280 | tf_op jit(solution)/shard_map/dot_general | solution.py:30
  309.3 37.1 %psum.135 = f32[256,16]{0,1:T(8,128)S(1)} all-reduce(f32[256,16]{0,1:T(8,128)S(1)} %fusion.40), channel_id=1, replica_groups=mesh['docs'=8,'anch'=4] {'docs'}, use_global_device_ids=true, to_apply=%region_20.22 | all-reduce | flops 4096 | bytes 32768 | tf_op jit(solution)/shard_map/psum | solution.py:75
  346.4 11.2 %fusion.7 = f32[8192,16]{0,1:T(8,128)} fusion(f32[8192,256]{1,0:T(8,128)} %get-tuple-element.17, f32[256,16]{0,1:T(8,128)S(1)} %psum.135, f32[256]{0:T(256)S(1)} %get-tuple-element.11), kind=kOutput, calls=%fused_computation.17 | convolution fusion | flops 402657280 | bytes 8930304 | tf_op jit(solution)/shard_map/dot_general | solution.py:36
  357.7 0.0 all-reduce.17.cloned.1.call-update
  357.7 0.3 all-reduce.19.cloned.1.call-start
  358.0 0.0 copy-done.1
  358.0 2.7 copy.11
  360.7 2.7 gather_fusion.2
  363.4 0.3 fusion.11
  363.7 0.0 copy-start.5
  363.7 24.0 %all-reduce.17.cloned.1.call-done = f32[8192,16]{0,1:T(8,128)} async-done(((f32[8192,16]{0,1:T(8,128)}), f32[8192,16]{0,1:T(8,128)}) %all-reduce.17.cloned.1.call-update) | async-done | bytes 524304 | tf_op jit(solution)/shard_map/psum | solution.py:67
  387.7 7.4 %fusion.41 = f32[256,16]{0,1:T(8,128)S(1)} fusion(f32[8192,256]{1,0:T(8,128)} %get-tuple-element.17, f32[8192,16]{0,1:T(8,128)} %all-reduce.17.cloned.1.call-done), kind=kOutput, calls=%fused_computation.61 | convolution fusion | flops 402653184 | bytes 8929280 | tf_op jit(solution)/shard_map/dot_general | solution.py:30
  395.1 37.1 %all-reduce.1 = (f32[256,16]{0,1:T(8,128)S(1)}, f32[256,16]{0,1:T(8,128)S(1)}) all-reduce(f32[256,16]{0,1:T(8,128)S(1)} %fusion.41, f32[256,16]{0,1:T(8,128)S(1)} %fusion.11), channel_id=1, replica_groups=mesh['docs'=8,'anch'=4] {'docs'}, use_global_device_ids=true, to_apply=%region_22.24 | all-reduce | flops 8192 | bytes 65536 | tf_op jit(solution)/shard_map/psum | solution.py:80
  432.2 0.6 multiply_reduce_fusion.2
  432.8 6.3 %psum.138 = f32[]{:T(128)} all-reduce(f32[]{:T(128)} %multiply_reduce_fusion.2), channel_id=1, replica_groups=mesh['docs'=8,'anch'=4] {'anch'}, use_global_device_ids=true, to_apply=%region_24.26 | all-reduce | flops 1 | bytes 8 | tf_op jit(solution)/shard_map/psum | solution.py:82
  439.8 0.0 copy-start.2
  439.8 11.0 %fusion.42 = f32[16,8192]{1,0:T(8,128)} fusion(f32[256,16]{0,1:T(8,128)S(1)} %multiply_add_fusion, f32[8192,256]{1,0:T(8,128)} %get-tuple-element.17), kind=kOutput, calls=%fused_computation.62 | convolution fusion | flops 402653184 | bytes 8929280 | tf_op jit(solution)/shard_map/dot_general | solution.py:40
  450.8 0.0 all-reduce.19.cloned.1.call-update
  450.9 0.0 copy-done.5
  450.9 0.6 dynamic-slice
  452.1 28.8 %all-reduce.19.cloned.1.call-done = f32[16,8192]{1,0:T(8,128)} async-done(((f32[16,8192]{1,0:T(8,128)}), f32[16,8192]{1,0:T(8,128)}) %all-reduce.19.cloned.1.call-update) | async-done | bytes 524304
  480.9 1.6 constant_dynamic-slice_fusion
  482.5 0.0 copy-done.2
  (3 shorter events, 0.0 us)
Async XLA Ops:
  7.2 112.2 %all-reduce.11.cloned.1.call-start = ((), (), s32[]{:S(2)}) async-start(), calls=%async_computation | async-start | bytes 1048576 | tf_op jit(solution)/shard_map/psum | solution.py:67
  10.9 19.6 %copy-start.3 = (s32[16]{0:T(128)S(1)}, s32[16]{0:T(128)}, u32[]{:S(2)}) copy-start(s32[16]{0:T(128)} %param.8) | copy-start | bytes 196
  30.6 10.0 %copy-start.4 = (s32[16]{0:T(128)S(1)}, s32[16]{0:T(128)}, u32[]{:S(2)}) copy-start(s32[16]{0:T(128)} %param.9) | copy-start | bytes 196
  89.6 115.7 %all-reduce.13.cloned.1.call-start = ((), (), s32[]{:S(2)}) async-start(), calls=%async_computation.1 | async-start | bytes 1048576 | tf_op jit(solution)/shard_map/psum | solution.py:67
  119.4 56.1 %copy-start = (f32[8192,16]{0,1:T(8,128)S(1)}, f32[8192,16]{0,1:T(8,128)}, u32[]{:S(2)}) copy-start(f32[8192,16]{0,1:T(8,128)} %all-reduce.11.cloned.1.call-done) | copy-start | bytes 1572868
  175.2 126.7 %all-reduce.15.cloned.1.call-start = ((), (), s32[]{:S(2)}) async-start(), calls=%async_computation.2 | async-start | bytes 1048576 | tf_op jit(solution)/shard_map/psum | solution.py:67
  271.9 115.9 %all-reduce.17.cloned.1.call-start = ((), (), s32[]{:S(2)}) async-start(), calls=%async_computation.3 | async-start | bytes 1048576 | tf_op jit(solution)/shard_map/psum | solution.py:67
  301.9 56.1 %copy-start.1 = (f32[8192,16]{0,1:T(8,128)S(1)}, f32[8192,16]{0,1:T(8,128)}, u32[]{:S(2)}) copy-start(f32[8192,16]{0,1:T(8,128)} %all-reduce.15.cloned.1.call-done) | copy-start | bytes 1572868
  357.7 123.2 %all-reduce.19.cloned.1.call-start = ((), (), s32[]{:S(2)}) async-start(), calls=%async_computation.4 | async-start | bytes 1048576
  363.7 87.2 %copy-start.5 = (u32[32]{0:T(128)S(1)}, u32[32]{0:T(128)}, u32[]{:S(2)}) copy-start(u32[32]{0:T(128)} %constant.53) | copy-start | bytes 388
  439.8 42.7 %copy-start.2 = (f32[256,16]{0,1:T(8,128)}, f32[256,16]{0,1:T(8,128)S(1)}, u32[]{:S(2)}) copy-start(f32[256,16]{0,1:T(8,128)S(1)} %multiply_add_fusion) | copy-start | bytes 49156
Sparse Core Ops, SparseCore 0:
  89.7 29.6 all-reduce.10
  175.3 29.8 all-reduce.12
  272.0 29.8 all-reduce.14
  357.8 29.8 all-reduce.16
  451.0 29.8 all-reduce.18
where the time goes:
time: 497 us; the launch traced here: 489 us
  blocking collectives  211 us (42%)
  waiting for transfers between devices  136 us (27%)
  matrix products  93.3 us (19%)
  between operations  19.6 us (4%)
  local copies, waits for them, and re-layouts  17 us (3%)
  other arithmetic  11 us (2%)
    psum x4, waiting for transfers between devices, doc_sum(): return lax.psum(part, 'anch')  107 us
    psum x2, blocking collectives, per_device(): back = lax.psum(trans_dot(zmat, spread_back), 'docs')  74.2 us
    psum x2, blocking collectives, per_device(): lax.psum((trans_dot(zmat, spread), trans_dot(zlab, jnp.take(spread, local...  74.2 us
    dot_general x4, matrix products, plain_dot(): jnp.dot(left, right, precision=highest, preferred_element_type=jnp.float32)  45.1 us
    psum x1, blocking collectives, per_device(): lax.psum((jnp.sum(zmat, axis=0), CLASSES * lab_scale * trans_dot(zlab, on...  37.4 us
    dot_general x7, matrix products, trans_dot(): lax.dot_general(left, right, (((0,), (0,)), ((), ())), precision=highest,...  30.5 us
    unnamed x6, waiting for transfers between devices  28.8 us
    psum x1, blocking collectives, per_device(): totals = lax.psum(jnp.sum(kern, axis=1), 'anch')  12.9 us
  transfers between devices with their start and end apart: 5, of which 5 were waited for; matrix products, arithmetic and copies ran while one was open for 2% of the time, Pallas kernels for 0%

commit v1 on v0

v1 whole, which is shorter than its diff:
```python
import functools

import jax
import jax.numpy as jnp
from jax import lax
from jax.experimental import pallas as pl
from jax.experimental.pallas import tpu as pltpu
from jax.sharding import PartitionSpec as P

CLASSES = 16
HALF = CLASSES // 2

width_h = 0.25
ridge = 0.1
highest = lax.Precision.HIGHEST
f32 = jnp.float32
bf16 = jnp.bfloat16
EVERY = ("docs", "anch")
LANES = 128

NT = (((1,), (1,)), ((), ()))
NN = (((1,), (0,)), ((), ()))


def mm(left, right, dims=NN, precision=None):
    return lax.dot_general(left, right, dims, precision=precision, preferred_element_type=f32)


def split2(value):
    high = value.astype(bf16)
    return high, (value - high.astype(f32)).astype(bf16)


def swap(value, mask):
    count = lax.axis_size("docs") * lax.axis_size("anch")
    return lax.ppermute(value, EVERY, [(i, i ^ mask) for i in range(count)])


def bit_groups(bits):
    groups = []
    while bits:
        part, bits = bits[:2], bits[2:]
        masks = [1 << part[0]]
        if len(part) == 2:
            masks += [1 << part[1], (1 << part[0]) | (1 << part[1])]
        groups.append(masks)
    return groups


def sum_stage(held, masks):
    got = [swap(held, mask) for mask in masks]
    if len(got) == 1:
        return held + got[0]
    return (held + got[0]) + (got[1] + got[2])


def reduce_all(mine, send, n_bits):
    held = mine + swap(send, 1)
    for masks in bit_groups(list(range(1, n_bits))):
        held = sum_stage(held, masks)
    return held, swap(held, 1)


def aug_columns(first, second, rows):
    lane = lax.broadcasted_iota(jnp.int32, (rows, LANES), 1)
    out = jnp.zeros((rows, LANES), f32)
    for base, column in ((0, first), (3, second)):
        if column is None:
            out = jnp.where((lane >= base) & (lane < base + 3), 1.0, out)
        else:
            rest = column
            for piece in range(3):
                part = rest.astype(bf16).astype(f32)
                out = jnp.where(lane == base + piece, part, out)
                rest = rest - part
    return out.astype(bf16)


def eighth(value):
    square = value * value
    fourth = square * square
    return 1.0 / (fourth * fourth)


def label_kernel(docs_dev, na, me_ref, idx_ref, cls_ref, feat_ref, out_ref, rows, sems):
    base = (me_ref[0] // na) * docs_dev
    count = idx_ref.shape[0]
    copies = []
    for k in range(count):
        local = idx_ref[k] - base
        start = pl.multiple_of((local >> 4) << 4, 16)
        copy = pltpu.make_async_copy(feat_ref.at[pl.ds(start, 16), :], rows.at[k], sems.at[k])
        copy.start()
        copies.append(copy)
    sub = lax.broadcasted_iota(jnp.int32, (16, LANES), 0)
    lane = lax.broadcasted_iota(jnp.int32, (1, LANES), 1)
    for k in range(count):
        out_ref[count + k : count + k + 1, :] = jnp.where(lane == cls_ref[k], 1.0, 0.0)
    for k in range(count):
        copies[k].wait()
        inside = (idx_ref[k] - base) & 15
        chosen = jnp.where(sub == inside, rows[k].astype(f32), 0.0)
        out_ref[k : k + 1, :] = jnp.sum(chosen, axis=0, keepdims=True)


def build_kernel(na, chunk, me_ref, a0, a1, a2, a3, x_ref, khi_ref, klo_ref, tinv_ref, aug_ref, xaug):
    feat = x_ref.shape[1]
    quarter = a0.shape[0]
    scale = 1.0 / (feat * width_h)
    me = me_ref[0] % na

    @pl.when(pl.program_id(0) == 0)
    def _():
        for mask, piece in enumerate((a0, a1, a2, a3)):
            at = pl.ds(pl.multiple_of((me ^ mask) * quarter, quarter), quarter)
            value = piece[...].astype(f32)
            size = jnp.sum(value * value, axis=1, keepdims=True) * scale + 1.0
            aug_ref[at, 0:feat] = (value * (-2.0 * scale)).astype(bf16)
            aug_ref[at, feat : feat + LANES] = aug_columns(size, None, quarter)

    value = x_ref[...].astype(f32)
    size = jnp.sum(value * value, axis=1, keepdims=True) * scale
    xaug[:, 0:feat] = x_ref[...]
    xaug[:, feat : feat + LANES] = aug_columns(None, size, x_ref.shape[0])
    right = xaug[...]
    total = jnp.zeros((8, x_ref.shape[0]), f32)
    for at in range(0, aug_ref.shape[0], chunk):
        kern = eighth(mm(aug_ref[at : at + chunk, :], right, NT))
        high, low = split2(kern)
        khi_ref[at : at + chunk, :] = high
        klo_ref[at : at + chunk, :] = low
        total = total + jnp.sum(kern.reshape(chunk // 8, 8, -1), axis=0)
    tinv_ref[...] = 1.0 / jnp.sum(total, axis=0, keepdims=True)


def apply_block(vec, khi_ref, klo_ref, tinv_ref):
    both = mm(vec[...], khi_ref[...])
    low = mm(vec[0:CLASSES, :], klo_ref[...])
    return (both[0:CLASSES] + (both[CLASSES:] + low)) * tinv_ref[...]


def gather_block(spread, khi_ref, klo_ref, tinv_ref, with_degree):
    tinv = tinv_ref[...]
    high, low = split2(spread * tinv)
    parts, second = [high, low], [high]
    if with_degree:
        row = lax.broadcasted_iota(jnp.int32, (CLASSES, tinv.shape[1]), 0)
        thigh = tinv.astype(bf16).astype(f32)
        ones = jnp.where(row == 0, thigh, jnp.where(row == 1, tinv - thigh, 0.0)).astype(bf16)
        parts.append(ones)
        second.append(ones)
    one = mm(jnp.concatenate(parts, axis=0), khi_ref[...], NT)
    two = mm(jnp.concatenate(second, axis=0), klo_ref[...], NT)
    out = one[0:CLASSES] + (one[CLASSES : 2 * CLASSES] + two[0:CLASSES])
    if not with_degree:
        return out, None
    deg = one[2 * CLASSES :] + two[CLASSES:]
    return out, deg[0:1] + deg[1:2]


def set_vec(vec, value):
    high, low = split2(value)
    vec[0:CLASSES, :] = high
    vec[CLASSES:, :] = low


def put_halves(acc, me, mine_ref, send_ref):
    core = me & 1
    mine_ref[...] = acc[pl.ds(pl.multiple_of(core * HALF, HALF), HALF), :]
    send_ref[...] = acc[pl.ds(pl.multiple_of((1 - core) * HALF, HALF), HALF), :]


def take_halves(acc, me, mine_ref, got_ref):
    core = me & 1
    acc[pl.ds(pl.multiple_of(core * HALF, HALF), HALF), :] = mine_ref[...]
    acc[pl.ds(pl.multiple_of((1 - core) * HALF, HALF), HALF), :] = got_ref[...]


def centred(value):
    return value - jnp.mean(value, axis=1, keepdims=True)


def first_kernel(
    na, labs, slots, gain, me_ref, *refs
):
    lab_refs = refs[: len(slots)]
    (aug_ref, khi_ref, klo_ref, tinv_ref, mine_ref, send_ref, rhs_ref, zlab_ref, spread_ref,
     laug, hot, vec, acc, mean) = refs[len(slots) :]
    step = pl.program_id(0)
    anchors = aug_ref.shape[0]
    feat = laug.shape[1] - LANES

    @pl.when(step == 0)
    def _():
        docs = me_ref[0] // na
        for masks, ref in zip(slots, lab_refs):
            for k, mask in enumerate(masks):
                at = pl.ds(pl.multiple_of((docs ^ mask) * labs, labs), labs)
                laug[at, 0:feat] = ref[2 * labs * k : 2 * labs * k + labs, :].astype(bf16)
                hot[at, :] = ref[2 * labs * k + labs : 2 * labs * (k + 1), :].astype(f32)
        value = laug[:, 0:feat].astype(f32)
        scale = 1.0 / (feat * width_h)
        size = jnp.sum(value * value, axis=1, keepdims=True) * scale
        laug[:, feat:] = aug_columns(None, size, laug.shape[0])
        kern = eighth(mm(aug_ref[...], laug[...], NT))
        zlab = kern / jnp.sum(kern, axis=0, keepdims=True)
        zlab_ref[...] = zlab
        onehot = hot[...].T[0:CLASSES, :]
        rhs = gain * mm(onehot, zlab, NT, highest)
        rhs_ref[...] = rhs
        middle = jnp.mean(rhs, axis=1, keepdims=True)
        mean[...] = jnp.broadcast_to(middle, mean.shape)
        set_vec(vec, rhs - middle)
        acc[...] = jnp.zeros_like(acc)

    spread = apply_block(vec, khi_ref, klo_ref, tinv_ref)
    spread_ref[...] = spread + mean[:, 0:1]
    out, deg = gather_block(spread, khi_ref, klo_ref, tinv_ref, True)
    acc[:, 0:anchors] += out
    for k in range(anchors // LANES):
        acc[k : k + 1, anchors:] += deg[:, k * LANES : (k + 1) * LANES]

    @pl.when(step == pl.num_programs(0) - 1)
    def _():
        put_halves(acc, me_ref[0], mine_ref, send_ref)


def second_kernel(me_ref, held_ref, got_ref, rhs_ref, khi_ref, klo_ref, tinv_ref,
                  mine_ref, send_ref, dinv_ref, vec, whole, acc):
    step = pl.program_id(0)
    anchors = rhs_ref.shape[1]

    @pl.when(step == 0)
    def _():
        take_halves(whole, me_ref[0], held_ref, got_ref)
        for k in range(anchors // LANES):
            dinv_ref[:, k * LANES : (k + 1) * LANES] = 1.0 / whole[k : k + 1, anchors:]
        set_vec(vec, centred(rhs_ref[...]) - whole[:, 0:anchors] * dinv_ref[...])
        acc[...] = jnp.zeros_like(acc)

    spread = apply_block(vec, khi_ref, klo_ref, tinv_ref)
    out, _ = gather_block(spread, khi_ref, klo_ref, tinv_ref, False)
    acc[...] += out

    @pl.when(step == pl.num_programs(0) - 1)
    def _():
        put_halves(acc, me_ref[0], mine_ref, send_ref)


def total_of(value):
    return jnp.sum(jnp.sum(value, axis=1, keepdims=True), axis=0, keepdims=True)


def third_kernel(na, lab_scale, graph_scale, me_ref, held_ref, got_ref, rhs_ref, lab_ref, spread0_ref,
                 khi_ref, klo_ref, tinv_ref, *refs):
    (mine_ref, send_ref, direc_ref, part_ref, next_ref), outs, (vec, acc, stats, slots) = (
        refs[0:5], refs[5 : 5 + na], refs[5 + na :]
    )
    step = pl.program_id(0)
    quarter = CLASSES // na
    me = me_ref[0]

    @pl.when(step == 0)
    def _():
        take_halves(acc, me, held_ref, got_ref)
        rhs = rhs_ref[...]
        image = lab_scale * lab_ref[...] + graph_scale * acc[...] + ridge * rhs
        norm = total_of(rhs * rhs)
        alpha = norm / total_of(rhs * image)
        resid = rhs - alpha * image
        after = total_of(resid * resid)
        direc = resid + (after / norm) * rhs
        direc_ref[...] = direc
        part_ref[...] = alpha * rhs
        next_ref[...] = jnp.broadcast_to(after, next_ref.shape)
        middle = jnp.mean(direc, axis=1, keepdims=True)
        stats[0:CLASSES, :] = jnp.broadcast_to(middle, (CLASSES, LANES))
        stats[CLASSES:, :] = jnp.broadcast_to(alpha, (8, LANES))
        set_vec(vec, direc - middle)
        acc[...] = jnp.zeros_like(acc)

    spread = apply_block(vec, khi_ref, klo_ref, tinv_ref)
    out, _ = gather_block(spread, khi_ref, klo_ref, tinv_ref, False)
    acc[...] += out
    full = spread + stats[0:CLASSES, 0:1]
    part = stats[CLASSES : CLASSES + 1, 0:1] * spread0_ref[...]
    for k in range(na):
        slots[k, 0:quarter, :] = part[k * quarter : (k + 1) * quarter]
        slots[k, quarter : 2 * quarter, :] = full[k * quarter : (k + 1) * quarter]
    for mask in range(na):
        outs[mask][...] = slots[(me % na) ^ mask]

    @pl.when(step == pl.num_programs(0) - 1)
    def _():
        put_halves(acc, me, mine_ref, send_ref)


def label_image_kernel(vec_ref, zlab_ref, out_ref):
    seen = mm(vec_ref[...], zlab_ref[...], NN, highest)
    out_ref[...] = mm(seen, zlab_ref[...], NT, highest)


def label_norm_kernel(lab_scale, vec_ref, zlab_ref, out_ref):
    vec = vec_ref[...]
    seen = mm(vec, zlab_ref[...], NN, highest)
    out_ref[...] = jnp.broadcast_to(lab_scale * total_of(seen * seen) + ridge * total_of(vec * vec), out_ref.shape)


def last_kernel(na, graph_scale, me_ref, held_ref, got_ref, direc_ref, part_ref, next_ref, base_ref, dinv_ref, *refs):
    pieces, (anchor_ref, doc_ref, whole) = refs[0:na], refs[na:]
    me = me_ref[0]
    mine = me % na
    take_halves(whole, me, held_ref, got_ref)
    prod = whole[...]
    direc = direc_ref[...]
    quad = total_of(prod * (centred(direc) - prod * dinv_ref[...]))
    alpha = next_ref[0:1, 0:1] / (base_ref[0:1, 0:1] + graph_scale * quad)
    whole[...] = part_ref[...] + alpha * direc
    rows = anchor_ref.shape[1]
    anchor_ref[...] = whole[:, pl.ds(pl.multiple_of(mine * rows, rows), rows)]
    quarter, docs = doc_ref.shape[0], pieces[0].shape[1]
    for mask in range(na):
        at = pl.ds(pl.multiple_of((mine ^ mask) * docs, docs), docs)
        doc_ref[:, at] = pieces[mask][0:quarter, :] + alpha * pieces[mask][quarter:, :]


def call(kernel, grid, in_specs, out_specs, out_shape, scratch, name, flops=0, moved=0):
    return pl.pallas_call(
        kernel,
        grid_spec=pltpu.PrefetchScalarGridSpec(
            num_scalar_prefetch=1, grid=grid, in_specs=in_specs, out_specs=out_specs, scratch_shapes=scratch
        ),
        out_shape=out_shape,
        name=name,
        compiler_params=pltpu.CompilerParams(dimension_semantics=("arbitrary",) * len(grid)),
        cost_estimate=pl.CostEstimate(flops=flops, bytes_accessed=moved, transcendentals=0),
    )


def whole_spec(shape):
    return pl.BlockSpec(shape, lambda i, me: (0,) * len(shape))


def per_device(features, anchors, lab_index, lab_class):
    docs_dev, feat = features.shape
    nd, na = lax.axis_size("docs"), lax.axis_size("anch")
    n_bits = (nd * na).bit_length() - 1
    a_bits = na.bit_length() - 1
    labs = lab_index.shape[0]
    labeled = labs * nd
    quarter = anchors.shape[0]
    total = quarter * na
    docs = docs_dev // na
    lab_scale = total / labeled
    graph_scale = total * total / (docs_dev * nd)
    assert na == 4 and nd * na == 1 << n_bits and total // LANES <= CLASSES
    sds = jax.ShapeDtypeStruct

    me = lax.axis_index(EVERY).astype(jnp.int32).reshape(1)

    own = pl.pallas_call(
        functools.partial(label_kernel, docs_dev, na),
        grid_spec=pltpu.PrefetchScalarGridSpec(
            num_scalar_prefetch=3,
            grid=(1,),
            in_specs=[pl.BlockSpec(memory_space=pl.ANY)],
            out_specs=pl.BlockSpec((2 * labs, LANES), lambda i, *_: (0, 0)),
            scratch_shapes=[pltpu.VMEM((labs, 16, LANES), bf16), pltpu.SemaphoreType.DMA((labs,))],
        ),
        out_shape=sds((2 * labs, feat), f32),
        name="label_rows",
    )(me, lab_index, lab_class, features).astype(bf16)

    piece = [anchors, swap(anchors, 1), swap(anchors, 2), None]
    piece[3] = swap(piece[2], 1)

    held, masks, stages = own, [0], []
    bits = list(range(a_bits, n_bits))
    stages = bit_groups(bits[:1]) + bit_groups(bits[1:])
    for at, stage in enumerate(stages):
        got = [swap(held, mask) for mask in stage]
        if at < len(stages) - 1:
            masks = masks + [m ^ mask for mask in stage for m in masks]
            held = jnp.concatenate([held] + got, axis=0)
    lab_arrays = [held] + got
    slots = [[m >> a_bits for m in masks]] + [[(m ^ mask) >> a_bits for m in masks] for mask in stages[-1]]

    block = min(256, docs)
    steps = docs // block
    khi, klo, tinv, aug = call(
        functools.partial(build_kernel, na, 128),
        (steps,),
        [whole_spec((quarter, feat))] * 4
        + [pl.BlockSpec((block, feat), lambda i, me: ((me[0] % na) * steps + i, 0))],
        [
            pl.BlockSpec((total, block), lambda i, me: (0, i)),
            pl.BlockSpec((total, block), lambda i, me: (0, i)),
            pl.BlockSpec((1, block), lambda i, me: (0, i)),
            whole_spec((total, feat + LANES)),
        ],
        [sds((total, docs), bf16), sds((total, docs), bf16), sds((1, docs), f32), sds((total, feat + LANES), bf16)],
        [pltpu.VMEM((block, feat + LANES), bf16)],
        "kernel_matrix",
        flops=2 * total * docs * 256,
        moved=4 * total * docs,
    )(me, *piece, features)

    wide = min(512, docs)
    grid = (docs // wide,)
    k_specs = [
        pl.BlockSpec((total, wide), lambda i, me: (0, i)),
        pl.BlockSpec((total, wide), lambda i, me: (0, i)),
        pl.BlockSpec((1, wide), lambda i, me: (0, i)),
    ]
    doc_spec = pl.BlockSpec((CLASSES, wide), lambda i, me: (0, i))
    flat = whole_spec((CLASSES, total))
    half = whole_spec((HALF, total))
    half_sds = sds((HALF, total), f32)
    long = total + LANES
    vec = pltpu.VMEM((2 * CLASSES, total), bf16)
    acc = pltpu.VMEM((CLASSES, total), f32)
    work = dict(flops=8 * total * docs * 64, moved=4 * total * docs)

    mine, send, rhs, zlab, spread = call(
        functools.partial(first_kernel, na, labs, slots, CLASSES * lab_scale),
        grid,
        [whole_spec(arr.shape) for arr in lab_arrays] + [whole_spec((total, feat + LANES))] + k_specs,
        [whole_spec((HALF, long))] * 2 + [flat, whole_spec((total, labeled)), doc_spec],
        [sds((HALF, long), f32)] * 2 + [sds((CLASSES, total), f32), sds((total, labeled), f32), sds((CLASSES, docs), f32)],
        [
            pltpu.VMEM((labeled, feat + LANES), bf16),
            pltpu.VMEM((labeled, LANES), f32),
            vec,
            pltpu.VMEM((CLASSES, long), f32),
            pltpu.VMEM((CLASSES, LANES), f32),
        ],
        "first_gram",
        **work,
    )(me, *lab_arrays, aug, khi, klo, tinv)

    image_lab = pl.pallas_call(
        label_image_kernel, out_shape=sds((CLASSES, total), f32), name="label_image",
        cost_estimate=pl.CostEstimate(flops=1 << 26, bytes_accessed=1 << 20, transcendentals=0),
    )(rhs, zlab)

    held, got = reduce_all(mine, send, n_bits)
    mine, send, dinv = call(
        second_kernel,
        grid,
        [whole_spec((HALF, long))] * 2 + [flat] + k_specs,
        [half, half, whole_spec((1, total))],
        [half_sds, half_sds, sds((1, total), f32)],
        [vec, pltpu.VMEM((CLASSES, long), f32), acc],
        "second_gram",
        **work,
    )(me, held, got, rhs, khi, klo, tinv)

    held, got = reduce_all(mine, send, n_bits)
    part_rows = 2 * CLASSES // na
    mine, send, direc, part, norm, *docs_out = call(
        functools.partial(third_kernel, na, lab_scale, graph_scale),
        grid,
        [half, half, flat, flat, doc_spec] + k_specs,
        [half, half, flat, flat, whole_spec((1, LANES))] + [pl.BlockSpec((part_rows, wide), lambda i, me: (0, i))] * na,
        [half_sds, half_sds, sds((CLASSES, total), f32), sds((CLASSES, total), f32), sds((1, LANES), f32)]
        + [sds((part_rows, docs), f32)] * na,
        [vec, acc, pltpu.VMEM((CLASSES + 8, LANES), f32), pltpu.VMEM((na, part_rows, wide), f32)],
        "third_gram",
        **work,
    )(me, held, got, rhs, image_lab, spread, khi, klo, tinv)

    base = pl.pallas_call(
        functools.partial(label_norm_kernel, lab_scale), out_shape=sds((1, LANES), f32), name="label_norm",
        cost_estimate=pl.CostEstimate(flops=1 << 26, bytes_accessed=1 << 20, transcendentals=0),
    )(direc, zlab)

    held, got = reduce_all(mine, send, n_bits)
    pieces = [docs_out[0]] + [swap(docs_out[mask], mask) for mask in range(1, na)]
    anchor_scores, doc_scores = call(
        functools.partial(last_kernel, na, graph_scale),
        (1,),
        [half, half, flat, flat, whole_spec((1, LANES)), whole_spec((1, LANES)), whole_spec((1, total))]
        + [whole_spec((part_rows, docs))] * na,
        [whole_spec((CLASSES, quarter)), whole_spec((CLASSES // na, docs_dev))],
        [sds((CLASSES, quarter), f32), sds((CLASSES // na, docs_dev), f32)],
        [acc],
        "scores",
    )(me, held, got, direc, part, norm, base, dinv, *pieces)
    return anchor_scores.T, doc_scores


def solution(mesh):
    in_specs = (P("docs", None), P("anch", None), P("docs"), P("docs"))
    out_specs = (P("anch", None), P("anch", "docs"))
    return jax.shard_map(per_device, mesh=mesh, in_specs=in_specs, out_specs=out_specs, check_vma=False)
```

time: 497 us -> 110 us (0.22); the launches traced: 489 us -> 109 us
  blocking collectives: 211 us -> 0 us
  waiting for transfers between devices: 136 us -> 22.6 us
  matrix products: 93.3 us -> 0 us
  Pallas kernels: 0 us -> 42.3 us
  starting transfers between devices: 1.31 us -> 36.4 us
  between operations: 19.6 us -> 0.84 us
  local copies, waits for them, and re-layouts: 17 us -> 3.7 us
  other arithmetic: 11 us -> 3.09 us
    psum x8 -> x0, blocking collectives: 211 us -> none  [the longest x2 74.2 us: per_device(): back = lax.psum(trans_dot(zmat, spread_back), 'docs')]
    psum x4 -> x0, waiting for transfers between devices: 107 us -> none  [doc_sum(): return lax.psum(part, 'anch')]
    dot_general x13 -> x0, matrix products: 93.3 us -> none  [the longest x4 45.1 us: plain_dot(): jnp.dot(left, right, precision=highest, preferred_element_type=jnp.float32)]
    pallas_call x0 -> x8, Pallas kernels: none -> 42.3 us  [the longest x1 9.18 us: per_device(): call(functools.partial(first_kernel, na, labs, slots, CLASSES * lab_scale...]
    ppermute x0 -> x34, starting transfers between devices: none -> 36.4 us  [swap(): return lax.ppermute(value, EVERY, [(i, i ^ mask) for i in range(count)])]
    unnamed x6 -> x0, waiting for transfers between devices: 28.8 us -> none
    ppermute x0 -> x34, waiting for transfers between devices: none -> 22.6 us  [swap(): return lax.ppermute(value, EVERY, [(i, i ^ mask) for i in range(count)])]
    reduce_sum x5 -> x0, other arithmetic: 11 us -> none  [the longest x1 6.06 us: per_device(): jnp.sum(zmat, axis=0)]
  transfers between devices with their start and end apart: 5 -> 34, of which waited for: 5 -> 22; matrix products, arithmetic and copies ran while one was open for 2% -> 1% of each run, Pallas kernels for 0% -> 15%
where the time goes in v1:
time: 110 us; the launch traced here: 109 us
  Pallas kernels  42.3 us (38%)
  starting transfers between devices  36.4 us (33%)
  waiting for transfers between devices  22.6 us (21%)
  local copies, waits for them, and re-layouts  3.7 us (3%)
  other arithmetic  3.09 us (3%)
    ppermute x34, starting transfers between devices, swap(): return lax.ppermute(value, EVERY, [(i, i ^ mask) for i in range(count)])  36.4 us
    ppermute x34, waiting for transfers between devices, swap(): return lax.ppermute(value, EVERY, [(i, i ^ mask) for i in range(count)])  22.6 us
    pallas_call x1, Pallas kernels, per_device(): call(functools.partial(first_kernel, na, labs, slots, CLASSES * lab_scale...  9.18 us
    pallas_call x1, Pallas kernels, per_device(): call(functools.partial(build_kernel, na, 128), (steps,), [whole_spec((qua...  9.04 us
    pallas_call x1, Pallas kernels, per_device(): call(functools.partial(third_kernel, na, lab_scale, graph_scale), grid, [...  7.84 us
    pallas_call x1, Pallas kernels, per_device(): call(second_kernel, grid, [whole_spec((HALF, long))] * 2 + [flat] + k_spe...  7.37 us
    unnamed x32, local copies, waits for them, and re-layouts  3.7 us
    pallas_call x1, Pallas kernels, per_device(): pl.pallas_call(label_image_kernel, out_shape=sds((CLASSES, total), f32),...  2.55 us
  transfers between devices with their start and end apart: 34, of which 22 were waited for; matrix products, arithmetic and copies ran while one was open for 1% of the time, Pallas kernels for 15%

profile of v1, /device:TPU:0, one launch (start us, length us, event | category | flops | bytes accessed | tf_op | source)
XLA Modules:
  0.0 108.9 jit_solution(10460015195080810214)
XLA Ops:
  0.6 3.0 %collective-permute-start.5 = (bf16[256,128]{1,0:T(8,128)(2,1)}, bf16[256,128]{1,0:T(8,128)(2,1)S(1)}, u32[]{:S(2)}, u32[]{:S(2)}) collective-permute-start(bf16[256,128]{1,0:T(8,128)(2,1)} %a0.1), channel_id=1, source_target_pairs={{0,2},{1,3},{2,0},{3,1},{4,6},{5,7},{6,4},{7,5},{8,10},{9,11},{10,... | collective-permute-start | bytes 196616 | tf_op jit(solution)/shard_map/ppermute | solution.py:36
  3.7 2.3 %label_rows.1 = f32[32,128]{1,0:T(8,128)} custom-call(s32[1]{0:T(128)} %bitcast.me_ref, s32[16]{0:T(128)} %idx_ref.1, s32[16]{0:T(128)} %cls_ref.1, bf16[8192,128]{1,0:T(8,128)(2,1)} %x_ref.1), custom_call_target="tpu_custom_call" | custom-call | tf_op jit(solution)/shard_map/label_rows/pallas_call | solution.py:361
  6.0 0.7 convert_element_type.3
  6.7 1.5 %collective-permute-start = (bf16[32,128]{1,0:T(8,128)(2,1)S(1)}, bf16[32,128]{1,0:T(8,128)(2,1)S(1)}, u32[]{:S(2)}, u32[]{:S(2)}) collective-permute-start(bf16[32,128]{1,0:T(8,128)(2,1)S(1)} %convert_element_type.3), channel_id=1, source_target_pairs={{0,4},{1,5},{2,6},{3,7},{4,0},{5,1},{6,2},{7,3},{8,12},{9,13},{10,... | collective-permute-start | bytes 24584 | tf_op jit(solution)/shard_map/ppermute | solution.py:36
  8.3 0.5 collective-permute-start.6
  8.8 1.6 %collective-permute-done = bf16[32,128]{1,0:T(8,128)(2,1)S(1)} collective-permute-done((bf16[32,128]{1,0:T(8,128)(2,1)S(1)}, bf16[32,128]{1,0:T(8,128)(2,1)S(1)}, u32[]{:S(2)}, u32[]{:S(2)}) %collective-permute-start) | collective-permute-done | bytes 8224 | tf_op jit(solution)/shard_map/ppermute | solution.py:36
  10.4 3.6 %collective-permute-start.3 = (bf16[64,128]{1,0:T(8,128)(2,1)S(1)}, bf16[64,128]{1,0:T(8,128)(2,1)S(1)}, u32[]{:S(2)}, u32[]{:S(2)}) collective-permute-start(bf16[64,128]{1,0:T(8,128)(2,1)S(1)} %pad_maximum_fusion.refs_0_), channel_id=1, source_target_pairs={{0,24},{1,25},{2,26},{3,27},{4,28},{5,29},{6,30},{7,31},{8,16},{9,... | collective-permute-start | bytes 49160 | tf_op jit(solution)/shard_map/ppermute | solution.py:36
  14.0 0.8 collective-permute-start.1
  14.8 0.6 copy-done.14
  15.4 0.6 copy-done.15
  16.0 9.0 %kernel_matrix.1 = (bf16[1024,2048]{1,0:T(8,128)(2,1)}, bf16[1024,2048]{1,0:T(8,128)(2,1)}, f32[1,2048]{1,0:T(1,128)}, bf16[1024,256]{1,0:T(8,128)(2,1)}) custom-call(s32[1]{0:T(128)} %bitcast.me_ref, bf16[256,128]{1,0:T(8,128)(2,1)} %a0.1, bf16[256,128]{1,0:T(8,128)(2,1)} %copy-done.14, bf16[256,128]{1,0:T(8,128)(2,1)} %copy-done.13, ...), custom_call_target="tpu_custom_call" | custom-call | flops 1073741824 | bytes 8388608 | tf_op jit(solution)/shard_map/kernel_matrix/pallas_call | solution.py:390
  25.1 0.5 copy-done.10
  25.7 9.2 %first_gram.1 = (f32[8,1152]{1,0:T(8,128)}, f32[8,1152]{1,0:T(8,128)}, f32[16,1024]{1,0:T(8,128)}, f32[1024,128]{1,0:T(8,128)}, f32[16,2048]{1,0:T(8,128)}) custom-call(s32[1]{0:T(128)} %bitcast.me_ref, bf16[64,128]{1,0:T(8,128)(2,1)} %copy-done.3, bf16[64,128]{1,0:T(8,128)(2,1)} %copy-done.12, bf16[64,128]{1,0:T(8,128)(2,1)} %copy-done.11, ...), custom_call_target="tpu_custom_call" | custom-call | flops 1073741824 | bytes 8388608 | tf_op jit(solution)/shard_map/first_gram/pallas_call | solution.py:424
  35.0 1.4 %collective-permute-done.7 = f32[8,1152]{1,0:T(8,128)S(1)} collective-permute-done((f32[8,1152]{1,0:T(8,128)}, f32[8,1152]{1,0:T(8,128)S(1)}, u32[]{:S(2)}, u32[]{:S(2)}) %collective-permute-start.7) | collective-permute-done | bytes 36896 | tf_op jit(solution)/shard_map/ppermute | solution.py:36
  36.4 0.8 add.67
  37.2 1.5 %collective-permute-start.10 = (f32[8,1152]{1,0:T(8,128)S(1)}, f32[8,1152]{1,0:T(8,128)S(1)}, u32[]{:S(2)}, u32[]{:S(2)}) collective-permute-start(f32[8,1152]{1,0:T(8,128)S(1)} %add.67), channel_id=1, source_target_pairs={{0,6},{1,7},{2,4},{3,5},{4,2},{5,3},{6,0},{7,1},{8,14},{9,15},{10,... | collective-permute-start | bytes 110600 | tf_op jit(solution)/shard_map/ppermute | solution.py:36
  38.7 0.3 collective-permute-start.9
  39.0 1.7 %collective-permute-start.8 = (f32[8,1152]{1,0:T(8,128)S(1)}, f32[8,1152]{1,0:T(8,128)S(1)}, u32[]{:S(2)}, u32[]{:S(2)}) collective-permute-start(f32[8,1152]{1,0:T(8,128)S(1)} %add.67), channel_id=1, source_target_pairs={{0,2},{1,3},{2,0},{3,1},{4,6},{5,7},{6,4},{7,5},{8,10},{9,11},{10,... | collective-permute-start | bytes 110600 | tf_op jit(solution)/shard_map/ppermute | solution.py:36
  40.7 1.4 %collective-permute-done.10 = f32[8,1152]{1,0:T(8,128)S(1)} collective-permute-done((f32[8,1152]{1,0:T(8,128)S(1)}, f32[8,1152]{1,0:T(8,128)S(1)}, u32[]{:S(2)}, u32[]{:S(2)}) %collective-permute-start.10) | collective-permute-done | bytes 36896 | tf_op jit(solution)/shard_map/ppermute | solution.py:36
  42.0 0.6 collective-permute-done.9
  42.6 0.3 collective-permute-done.8
  43.0 3.8 %collective-permute-start.13 = (f32[8,1152]{1,0:T(8,128)S(1)}, f32[8,1152]{1,0:T(8,128)S(1)}, u32[]{:S(2)}, u32[]{:S(2)}) collective-permute-start(f32[8,1152]{1,0:T(8,128)S(1)} %add_add_fusion.1), channel_id=1, source_target_pairs={{0,24},{1,25},{2,26},{3,27},{4,28},{5,29},{6,30},{7,31},{8,16},{9,... | collective-permute-start | bytes 110600 | tf_op jit(solution)/shard_map/ppermute | solution.py:36
  46.8 0.6 collective-permute-start.11
  47.4 1.4 %collective-permute-done.13 = f32[8,1152]{1,0:T(8,128)S(1)} collective-permute-done((f32[8,1152]{1,0:T(8,128)S(1)}, f32[8,1152]{1,0:T(8,128)S(1)}, u32[]{:S(2)}, u32[]{:S(2)}) %collective-permute-start.13) | collective-permute-done | bytes 36896 | tf_op jit(solution)/shard_map/ppermute | solution.py:36
  48.8 2.8 %collective-permute-done.12 = f32[8,1152]{1,0:T(8,128)S(1)} collective-permute-done((f32[8,1152]{1,0:T(8,128)S(1)}, f32[8,1152]{1,0:T(8,128)S(1)}, u32[]{:S(2)}, u32[]{:S(2)}) %collective-permute-start.12) | collective-permute-done | bytes 36896 | tf_op jit(solution)/shard_map/ppermute | solution.py:36
  51.7 1.2 %collective-permute-done.14.got_ref = f32[8,1152]{1,0:T(8,128)S(1)} collective-permute-done((f32[8,1152]{1,0:T(8,128)S(1)}, f32[8,1152]{1,0:T(8,128)S(1)}, u32[]{:S(2)}, u32[]{:S(2)}) %collective-permute-start.14) | collective-permute-done | bytes 36896 | tf_op jit(solution)/shard_map/ppermute | solution.py:36
  52.9 0.6 copy-done.7
  53.6 7.4 %second_gram.1 = (f32[8,1024]{1,0:T(8,128)}, f32[8,1024]{1,0:T(8,128)}, f32[1,1024]{1,0:T(1,128)}) custom-call(s32[1]{0:T(128)} %bitcast.me_ref, f32[8,1152]{1,0:T(8,128)} %copy-done, f32[8,1152]{1,0:T(8,128)} %copy-done.7, f32[16,1024]{1,0:T(8,128)} %get-tuple-element.31.rhs_ref.vec_ref, bf16[1024,2048]{1,0:T(8,128)(2,1)} %get-tuple-element.26.refs_5_.khi_ref, ...), custom_call_target="tpu_custom_call" | custom-call | flops 1073741824 | bytes 8388608 | tf_op jit(solution)/shard_map/second_gram/pallas_call | solution.py:447
  61.1 1.3 %collective-permute-done.15 = f32[8,1024]{1,0:T(8,128)S(1)} collective-permute-done((f32[8,1024]{1,0:T(8,128)}, f32[8,1024]{1,0:T(8,128)S(1)}, u32[]{:S(2)}, u32[]{:S(2)}) %collective-permute-start.15) | collective-permute-done | bytes 32800 | tf_op jit(solution)/shard_map/ppermute | solution.py:36
  62.3 0.8 add.74
  63.1 2.5 %collective-permute-start.18 = (f32[8,1024]{1,0:T(8,128)S(1)}, f32[8,1024]{1,0:T(8,128)S(1)}, u32[]{:S(2)}, u32[]{:S(2)}) collective-permute-start(f32[8,1024]{1,0:T(8,128)S(1)} %add.74), channel_id=1, source_target_pairs={{0,6},{1,7},{2,4},{3,5},{4,2},{5,3},{6,0},{7,1},{8,14},{9,15},{10,... | collective-permute-start | bytes 98312 | tf_op jit(solution)/shard_map/ppermute | solution.py:36
  65.6 0.5 collective-permute-start.17
  66.1 0.5 collective-permute-start.16
  66.6 1.3 %collective-permute-done.18 = f32[8,1024]{1,0:T(8,128)S(1)} collective-permute-done((f32[8,1024]{1,0:T(8,128)S(1)}, f32[8,1024]{1,0:T(8,128)S(1)}, u32[]{:S(2)}, u32[]{:S(2)}) %collective-permute-start.18) | collective-permute-done | bytes 32800 | tf_op jit(solution)/shard_map/ppermute | solution.py:36
  67.9 1.6 %collective-permute-done.17 = f32[8,1024]{1,0:T(8,128)S(1)} collective-permute-done((f32[8,1024]{1,0:T(8,128)S(1)}, f32[8,1024]{1,0:T(8,128)S(1)}, u32[]{:S(2)}, u32[]{:S(2)}) %collective-permute-start.17) | collective-permute-done | bytes 32800 | tf_op jit(solution)/shard_map/ppermute | solution.py:36
  69.5 0.5 collective-permute-done.16
  70.0 1.5 %collective-permute-start.21 = (f32[8,1024]{1,0:T(8,128)S(1)}, f32[8,1024]{1,0:T(8,128)S(1)}, u32[]{:S(2)}, u32[]{:S(2)}) collective-permute-start(f32[8,1024]{1,0:T(8,128)S(1)} %add_add_fusion.5), channel_id=1, source_target_pairs={{0,24},{1,25},{2,26},{3,27},{4,28},{5,29},{6,30},{7,31},{8,16},{9,... | collective-permute-start | bytes 98312 | tf_op jit(solution)/shard_map/ppermute | solution.py:36
  71.5 0.6 collective-permute-start.20
  72.2 2.3 %collective-permute-start.19 = (f32[8,1024]{1,0:T(8,128)S(1)}, f32[8,1024]{1,0:T(8,128)S(1)}, u32[]{:S(2)}, u32[]{:S(2)}) collective-permute-start(f32[8,1024]{1,0:T(8,128)S(1)} %add_add_fusion.5), channel_id=1, source_target_pairs={{0,8},{1,9},{2,10},{3,11},{4,12},{5,13},{6,14},{7,15},{8,0},{9,1},... | collective-permute-start | bytes 98312 | tf_op jit(solution)/shard_map/ppermute | solution.py:36
  74.5 1.3 %collective-permute-done.21 = f32[8,1024]{1,0:T(8,128)S(1)} collective-permute-done((f32[8,1024]{1,0:T(8,128)S(1)}, f32[8,1024]{1,0:T(8,128)S(1)}, u32[]{:S(2)}, u32[]{:S(2)}) %collective-permute-start.21) | collective-permute-done | bytes 32800 | tf_op jit(solution)/shard_map/ppermute | solution.py:36
  75.8 0.6 collective-permute-done.20
  76.4 0.3 collective-permute-done.19
  76.8 2.5 %label_image.1.lab_ref = f32[16,1024]{1,0:T(8,128)} custom-call(f32[16,1024]{1,0:T(8,128)} %get-tuple-element.31.rhs_ref.vec_ref, f32[1024,128]{1,0:T(8,128)} %get-tuple-element.34.zlab_ref), custom_call_target="tpu_custom_call" | custom-call | flops 67108864 | bytes 1048576 | tf_op jit(solution)/shard_map/label_image/pallas_call | solution.py:441
  79.4 0.6 copy-done.8
  80.0 7.8 %third_gram.1 = (f32[8,1024]{1,0:T(8,128)}, f32[8,1024]{1,0:T(8,128)}, f32[16,1024]{1,0:T(8,128)}, f32[16,1024]{1,0:T(8,128)}, f32[1,128]{1,0:T(1,128)}, /*index...) custom-call(s32[1]{0:T(128)} %bitcast.me_ref, f32[8,1024]{1,0:T(8,128)} %copy-done.1, ...), custom_call_target="tpu_custom_call" | custom-call | flops 1073741824 | bytes 8388608 | tf_op jit(solution)/shard_map/third_gram/pallas_call | solution.py:460
  87.8 0.6 collective-permute-start.23
  88.4 1.1 collective-permute-done.23
  89.5 0.8 add.81
  90.2 1.5 %collective-permute-start.26 = (f32[8,1024]{1,0:T(8,128)S(1)}, f32[8,1024]{1,0:T(8,128)S(1)}, u32[]{:S(2)}, u32[]{:S(2)}) collective-permute-start(f32[8,1024]{1,0:T(8,128)S(1)} %add.81), channel_id=1, source_target_pairs={{0,6},{1,7},{2,4},{3,5},{4,2},{5,3},{6,0},{7,1},{8,14},{9,15},{10,... | collective-permute-start | bytes 98312 | tf_op jit(solution)/shard_map/ppermute | solution.py:36
  91.7 0.5 collective-permute-start.25
  92.2 1.5 %collective-permute-start.24 = (f32[8,1024]{1,0:T(8,128)S(1)}, f32[8,1024]{1,0:T(8,128)S(1)}, u32[]{:S(2)}, u32[]{:S(2)}) collective-permute-start(f32[8,1024]{1,0:T(8,128)S(1)} %add.81), channel_id=1, source_target_pairs={{0,2},{1,3},{2,0},{3,1},{4,6},{5,7},{6,4},{7,5},{8,10},{9,11},{10,... | collective-permute-start | bytes 98312 | tf_op jit(solution)/shard_map/ppermute | solution.py:36
  93.7 1.3 %collective-permute-done.26 = f32[8,1024]{1,0:T(8,128)S(1)} collective-permute-done((f32[8,1024]{1,0:T(8,128)S(1)}, f32[8,1024]{1,0:T(8,128)S(1)}, u32[]{:S(2)}, u32[]{:S(2)}) %collective-permute-start.26) | collective-permute-done | bytes 32800 | tf_op jit(solution)/shard_map/ppermute | solution.py:36
  95.0 0.6 collective-permute-done.25
  95.6 0.5 collective-permute-done.24
  96.1 2.4 %collective-permute-start.29 = (f32[8,1024]{1,0:T(8,128)S(1)}, f32[8,1024]{1,0:T(8,128)S(1)}, u32[]{:S(2)}, u32[]{:S(2)}) collective-permute-start(f32[8,1024]{1,0:T(8,128)S(1)} %add_add_fusion.3), channel_id=1, source_target_pairs={{0,24},{1,25},{2,26},{3,27},{4,28},{5,29},{6,30},{7,31},{8,16},{9,... | collective-permute-start | bytes 98312 | tf_op jit(solution)/shard_map/ppermute | solution.py:36
  98.6 0.8 collective-permute-start.28
  99.3 1.2 %collective-permute-start.27 = (f32[8,1024]{1,0:T(8,128)S(1)}, f32[8,1024]{1,0:T(8,128)S(1)}, u32[]{:S(2)}, u32[]{:S(2)}) collective-permute-start(f32[8,1024]{1,0:T(8,128)S(1)} %add_add_fusion.3), channel_id=1, source_target_pairs={{0,8},{1,9},{2,10},{3,11},{4,12},{5,13},{6,14},{7,15},{8,0},{9,1},... | collective-permute-start | bytes 98312 | tf_op jit(solution)/shard_map/ppermute | solution.py:36
  100.6 1.5 %collective-permute-start.32 = (f32[8,2048]{1,0:T(8,128)}, f32[8,2048]{1,0:T(8,128)S(1)}, u32[]{:S(2)}, u32[]{:S(2)}) collective-permute-start(f32[8,2048]{1,0:T(8,128)} %get-tuple-element.44), channel_id=1, source_target_pairs={{0,2},{1,3},{2,0},{3,1},{4,6},{5,7},{6,4},{7,5},{8,10},{9,11},{10,... | collective-permute-start | bytes 196616 | tf_op jit(solution)/shard_map/ppermute | solution.py:36
  102.1 0.4 collective-permute-start.33
  102.5 1.0 collective-permute-done.28
  103.9 2.0 %label_norm.1.base_ref = f32[1,128]{1,0:T(1,128)} custom-call(f32[16,1024]{1,0:T(8,128)} %get-tuple-element.38.vec_ref.direc_ref, f32[1024,128]{1,0:T(8,128)} %get-tuple-element.34.zlab_ref), custom_call_target="tpu_custom_call" | custom-call | flops 67108864 | bytes 1048576 | tf_op jit(solution)/shard_map/label_norm/pallas_call | solution.py:472
  105.9 0.4 collective-permute-done.33.refs_3_
  106.6 0.3 copy-done.6
  107.0 2.0 %scores.1 = (f32[16,256]{1,0:T(8,128)}, f32[4,8192]{1,0:T(4,128)}) custom-call(s32[1]{0:T(128)} %bitcast.me_ref, f32[8,1024]{1,0:T(8,128)} %copy-done.2, f32[8,1024]{1,0:T(8,128)} %copy-done.9, f32[16,1024]{1,0:T(8,128)} %get-tuple-element.38.vec_ref.direc_ref, f32[16,1024]{1,0:T(8,128)} %get-tuple-element.39.part_ref, f32[1,128]{1,0:T(1,128)} %get-tuple-element.40.next_ref, ...), custom_call_target="tpu_custom_call" | custom-call | tf_op jit(solution)/shard_map/scores/pallas_call | solution.py:479
  (55 shorter events, 1.3 us)
Async XLA Ops:
  0.6 7.6 %collective-permute-start.5 = (bf16[256,128]{1,0:T(8,128)(2,1)}, bf16[256,128]{1,0:T(8,128)(2,1)S(1)}, u32[]{:S(2)}, u32[]{:S(2)}) collective-permute-start(bf16[256,128]{1,0:T(8,128)(2,1)} %a0.1), channel_id=1, source_target_pairs={{0,2},{1,3},{2,0},{3,1},{4,6},{5,7},{6,4},{7,5},{8,10},{9,11},{10,... | collective-permute-start | bytes 196616 | tf_op jit(solution)/shard_map/ppermute | solution.py:36
  6.7 3.7 %collective-permute-start = (bf16[32,128]{1,0:T(8,128)(2,1)S(1)}, bf16[32,128]{1,0:T(8,128)(2,1)S(1)}, u32[]{:S(2)}, u32[]{:S(2)}) collective-permute-start(bf16[32,128]{1,0:T(8,128)(2,1)S(1)} %convert_element_type.3), channel_id=1, source_target_pairs={{0,4},{1,5},{2,6},{3,7},{4,0},{5,1},{6,2},{7,3},{8,12},{9,13},{10,... | collective-permute-start | bytes 24584 | tf_op jit(solution)/shard_map/ppermute | solution.py:36
  8.2 6.5 %collective-permute-start.4 = (bf16[256,128]{1,0:T(8,128)(2,1)}, bf16[256,128]{1,0:T(8,128)(2,1)S(1)}, u32[]{:S(2)}, u32[]{:S(2)}) collective-permute-start(bf16[256,128]{1,0:T(8,128)(2,1)} %a0.1), channel_id=1, source_target_pairs={{0,1},{1,0},{2,3},{3,2},{4,5},{5,4},{6,7},{7,6},{8,9},{9,8},{10,11... | collective-permute-start | bytes 196616 | tf_op jit(solution)/shard_map/ppermute | solution.py:36
  8.3 6.5 %copy-start.13 = (bf16[256,128]{1,0:T(8,128)(2,1)}, bf16[256,128]{1,0:T(8,128)(2,1)S(1)}, u32[]{:S(2)}) copy-start(bf16[256,128]{1,0:T(8,128)(2,1)S(1)} %collective-permute-done.5.a2) | copy-start | bytes 196612
  8.3 6.5 %collective-permute-start.6 = (bf16[256,128]{1,0:T(8,128)(2,1)S(1)}, bf16[256,128]{1,0:T(8,128)(2,1)S(1)}, u32[]{:S(2)}, u32[]{:S(2)}) collective-permute-start(bf16[256,128]{1,0:T(8,128)(2,1)S(1)} %collective-permute-done.5.a2), channel_id=1, source_target_pairs={{0,1},{1,0},{2,3},{3,2},{4,5},{5,4},{6,7},{7,6},{8,9},{9,8},{10,11... | collective-permute-start | bytes 196616 | tf_op jit(solution)/shard_map/ppermute | solution.py:36
  10.4 14.8 %copy-start.3 = (bf16[64,128]{1,0:T(8,128)(2,1)}, bf16[64,128]{1,0:T(8,128)(2,1)S(1)}, u32[]{:S(2)}) copy-start(bf16[64,128]{1,0:T(8,128)(2,1)S(1)} %pad_maximum_fusion.refs_0_) | copy-start | bytes 49156
  10.4 14.7 %collective-permute-start.3 = (bf16[64,128]{1,0:T(8,128)(2,1)S(1)}, bf16[64,128]{1,0:T(8,128)(2,1)S(1)}, u32[]{:S(2)}, u32[]{:S(2)}) collective-permute-start(bf16[64,128]{1,0:T(8,128)(2,1)S(1)} %pad_maximum_fusion.refs_0_), channel_id=1, source_target_pairs={{0,24},{1,25},{2,26},{3,27},{4,28},{5,29},{6,30},{7,31},{8,16},{9,... | collective-permute-start | bytes 49160 | tf_op jit(solution)/shard_map/ppermute | solution.py:36
  14.0 11.1 %collective-permute-start.2 = (bf16[64,128]{1,0:T(8,128)(2,1)S(1)}, bf16[64,128]{1,0:T(8,128)(2,1)S(1)}, u32[]{:S(2)}, u32[]{:S(2)}) collective-permute-start(bf16[64,128]{1,0:T(8,128)(2,1)S(1)} %pad_maximum_fusion.refs_0_), channel_id=1, source_target_pairs={{0,16},{1,17},{2,18},{3,19},{4,20},{5,21},{6,22},{7,23},{8,24},{9,... | collective-permute-start | bytes 49160 | tf_op jit(solution)/shard_map/ppermute | solution.py:36
  14.0 11.1 %collective-permute-start.1 = (bf16[64,128]{1,0:T(8,128)(2,1)S(1)}, bf16[64,128]{1,0:T(8,128)(2,1)S(1)}, u32[]{:S(2)}, u32[]{:S(2)}) collective-permute-start(bf16[64,128]{1,0:T(8,128)(2,1)S(1)} %pad_maximum_fusion.refs_0_), channel_id=1, source_target_pairs={{0,8},{1,9},{2,10},{3,11},{4,12},{5,13},{6,14},{7,15},{8,0},{9,1},... | collective-permute-start | bytes 49160 | tf_op jit(solution)/shard_map/ppermute | solution.py:36
  14.8 0.6 copy-start.14
  15.4 0.6 copy-start.15
  25.1 0.6 copy-start.10
  25.1 0.6 copy-start.11
  25.1 0.6 copy-start.12
  34.9 1.5 %collective-permute-start.7 = (f32[8,1152]{1,0:T(8,128)}, f32[8,1152]{1,0:T(8,128)S(1)}, u32[]{:S(2)}, u32[]{:S(2)}) collective-permute-start(f32[8,1152]{1,0:T(8,128)} %get-tuple-element.30), channel_id=1, source_target_pairs={{0,1},{1,0},{2,3},{3,2},{4,5},{5,4},{6,7},{7,6},{8,9},{9,8},{10,11... | collective-permute-start | bytes 110600 | tf_op jit(solution)/shard_map/ppermute | solution.py:36
  37.2 4.9 %collective-permute-start.10 = (f32[8,1152]{1,0:T(8,128)S(1)}, f32[8,1152]{1,0:T(8,128)S(1)}, u32[]{:S(2)}, u32[]{:S(2)}) collective-permute-start(f32[8,1152]{1,0:T(8,128)S(1)} %add.67), channel_id=1, source_target_pairs={{0,6},{1,7},{2,4},{3,5},{4,2},{5,3},{6,0},{7,1},{8,14},{9,15},{10,... | collective-permute-start | bytes 110600 | tf_op jit(solution)/shard_map/ppermute | solution.py:36
  38.7 4.0 %collective-permute-start.9 = (f32[8,1152]{1,0:T(8,128)S(1)}, f32[8,1152]{1,0:T(8,128)S(1)}, u32[]{:S(2)}, u32[]{:S(2)}) collective-permute-start(f32[8,1152]{1,0:T(8,128)S(1)} %add.67), channel_id=1, source_target_pairs={{0,4},{1,5},{2,6},{3,7},{4,0},{5,1},{6,2},{7,3},{8,12},{9,13},{10,... | collective-permute-start | bytes 110600 | tf_op jit(solution)/shard_map/ppermute | solution.py:36
  39.0 4.0 %collective-permute-start.8 = (f32[8,1152]{1,0:T(8,128)S(1)}, f32[8,1152]{1,0:T(8,128)S(1)}, u32[]{:S(2)}, u32[]{:S(2)}) collective-permute-start(f32[8,1152]{1,0:T(8,128)S(1)} %add.67), channel_id=1, source_target_pairs={{0,2},{1,3},{2,0},{3,1},{4,6},{5,7},{6,4},{7,5},{8,10},{9,11},{10,... | collective-permute-start | bytes 110600 | tf_op jit(solution)/shard_map/ppermute | solution.py:36
  43.0 5.8 %collective-permute-start.13 = (f32[8,1152]{1,0:T(8,128)S(1)}, f32[8,1152]{1,0:T(8,128)S(1)}, u32[]{:S(2)}, u32[]{:S(2)}) collective-permute-start(f32[8,1152]{1,0:T(8,128)S(1)} %add_add_fusion.1), channel_id=1, source_target_pairs={{0,24},{1,25},{2,26},{3,27},{4,28},{5,29},{6,30},{7,31},{8,16},{9,... | collective-permute-start | bytes 110600 | tf_op jit(solution)/shard_map/ppermute | solution.py:36
  46.8 4.9 %collective-permute-start.12 = (f32[8,1152]{1,0:T(8,128)S(1)}, f32[8,1152]{1,0:T(8,128)S(1)}, u32[]{:S(2)}, u32[]{:S(2)}) collective-permute-start(f32[8,1152]{1,0:T(8,128)S(1)} %add_add_fusion.1), channel_id=1, source_target_pairs={{0,16},{1,17},{2,18},{3,19},{4,20},{5,21},{6,22},{7,23},{8,24},{9,... | collective-permute-start | bytes 110600 | tf_op jit(solution)/shard_map/ppermute | solution.py:36
  46.8 4.9 %collective-permute-start.11 = (f32[8,1152]{1,0:T(8,128)S(1)}, f32[8,1152]{1,0:T(8,128)S(1)}, u32[]{:S(2)}, u32[]{:S(2)}) collective-permute-start(f32[8,1152]{1,0:T(8,128)S(1)} %add_add_fusion.1), channel_id=1, source_target_pairs={{0,8},{1,9},{2,10},{3,11},{4,12},{5,13},{6,14},{7,15},{8,0},{9,1},... | collective-permute-start | bytes 110600 | tf_op jit(solution)/shard_map/ppermute | solution.py:36
  51.7 1.3 %copy-start = (f32[8,1152]{1,0:T(8,128)}, f32[8,1152]{1,0:T(8,128)S(1)}, u32[]{:S(2)}) copy-start(f32[8,1152]{1,0:T(8,128)S(1)} %add_add_fusion.held_ref) | copy-start | bytes 110596
  51.7 1.3 %collective-permute-start.14 = (f32[8,1152]{1,0:T(8,128)S(1)}, f32[8,1152]{1,0:T(8,128)S(1)}, u32[]{:S(2)}, u32[]{:S(2)}) collective-permute-start(f32[8,1152]{1,0:T(8,128)S(1)} %add_add_fusion.held_ref), channel_id=1, source_target_pairs={{0,1},{1,0},{2,3},{3,2},{4,5},{5,4},{6,7},{7,6},{8,9},{9,8},{10,11... | collective-permute-start | bytes 110600 | tf_op jit(solution)/shard_map/ppermute | solution.py:36
  52.9 0.6 copy-start.7
  60.9 1.4 %collective-permute-start.15 = (f32[8,1024]{1,0:T(8,128)}, f32[8,1024]{1,0:T(8,128)S(1)}, u32[]{:S(2)}, u32[]{:S(2)}) collective-permute-start(f32[8,1024]{1,0:T(8,128)} %get-tuple-element.33), channel_id=1, source_target_pairs={{0,1},{1,0},{2,3},{3,2},{4,5},{5,4},{6,7},{7,6},{8,9},{9,8},{10,11... | collective-permute-start | bytes 98312 | tf_op jit(solution)/shard_map/ppermute | solution.py:36
  63.1 4.8 %collective-permute-start.18 = (f32[8,1024]{1,0:T(8,128)S(1)}, f32[8,1024]{1,0:T(8,128)S(1)}, u32[]{:S(2)}, u32[]{:S(2)}) collective-permute-start(f32[8,1024]{1,0:T(8,128)S(1)} %add.74), channel_id=1, source_target_pairs={{0,6},{1,7},{2,4},{3,5},{4,2},{5,3},{6,0},{7,1},{8,14},{9,15},{10,... | collective-permute-start | bytes 98312 | tf_op jit(solution)/shard_map/ppermute | solution.py:36
  65.6 3.9 %collective-permute-start.17 = (f32[8,1024]{1,0:T(8,128)S(1)}, f32[8,1024]{1,0:T(8,128)S(1)}, u32[]{:S(2)}, u32[]{:S(2)}) collective-permute-start(f32[8,1024]{1,0:T(8,128)S(1)} %add.74), channel_id=1, source_target_pairs={{0,4},{1,5},{2,6},{3,7},{4,0},{5,1},{6,2},{7,3},{8,12},{9,13},{10,... | collective-permute-start | bytes 98312 | tf_op jit(solution)/shard_map/ppermute | solution.py:36
  66.1 3.9 %collective-permute-start.16 = (f32[8,1024]{1,0:T(8,128)S(1)}, f32[8,1024]{1,0:T(8,128)S(1)}, u32[]{:S(2)}, u32[]{:S(2)}) collective-permute-start(f32[8,1024]{1,0:T(8,128)S(1)} %add.74), channel_id=1, source_target_pairs={{0,2},{1,3},{2,0},{3,1},{4,6},{5,7},{6,4},{7,5},{8,10},{9,11},{10,... | collective-permute-start | bytes 98312 | tf_op jit(solution)/shard_map/ppermute | solution.py:36
  70.0 5.8 %collective-permute-start.21 = (f32[8,1024]{1,0:T(8,128)S(1)}, f32[8,1024]{1,0:T(8,128)S(1)}, u32[]{:S(2)}, u32[]{:S(2)}) collective-permute-start(f32[8,1024]{1,0:T(8,128)S(1)} %add_add_fusion.5), channel_id=1, source_target_pairs={{0,24},{1,25},{2,26},{3,27},{4,28},{5,29},{6,30},{7,31},{8,16},{9,... | collective-permute-start | bytes 98312 | tf_op jit(solution)/shard_map/ppermute | solution.py:36
  71.5 4.8 %collective-permute-start.20 = (f32[8,1024]{1,0:T(8,128)S(1)}, f32[8,1024]{1,0:T(8,128)S(1)}, u32[]{:S(2)}, u32[]{:S(2)}) collective-permute-start(f32[8,1024]{1,0:T(8,128)S(1)} %add_add_fusion.5), channel_id=1, source_target_pairs={{0,16},{1,17},{2,18},{3,19},{4,20},{5,21},{6,22},{7,23},{8,24},{9,... | collective-permute-start | bytes 98312 | tf_op jit(solution)/shard_map/ppermute | solution.py:36
  72.2 4.5 %collective-permute-start.19 = (f32[8,1024]{1,0:T(8,128)S(1)}, f32[8,1024]{1,0:T(8,128)S(1)}, u32[]{:S(2)}, u32[]{:S(2)}) collective-permute-start(f32[8,1024]{1,0:T(8,128)S(1)} %add_add_fusion.5), channel_id=1, source_target_pairs={{0,8},{1,9},{2,10},{3,11},{4,12},{5,13},{6,14},{7,15},{8,0},{9,1},... | collective-permute-start | bytes 98312 | tf_op jit(solution)/shard_map/ppermute | solution.py:36
  76.7 2.6 %copy-start.1 = (f32[8,1024]{1,0:T(8,128)}, f32[8,1024]{1,0:T(8,128)S(1)}, u32[]{:S(2)}) copy-start(f32[8,1024]{1,0:T(8,128)S(1)} %add_add_fusion.4.held_ref) | copy-start | bytes 98308
  76.7 2.6 %collective-permute-start.22 = (f32[8,1024]{1,0:T(8,128)S(1)}, f32[8,1024]{1,0:T(8,128)S(1)}, u32[]{:S(2)}, u32[]{:S(2)}) collective-permute-start(f32[8,1024]{1,0:T(8,128)S(1)} %add_add_fusion.4.held_ref), channel_id=1, source_target_pairs={{0,1},{1,0},{2,3},{3,2},{4,5},{5,4},{6,7},{7,6},{8,9},{9,8},{10,11... | collective-permute-start | bytes 98312 | tf_op jit(solution)/shard_map/ppermute | solution.py:36
  79.4 0.6 copy-start.8
  87.8 1.6 %collective-permute-start.23 = (f32[8,1024]{1,0:T(8,128)}, f32[8,1024]{1,0:T(8,128)S(1)}, u32[]{:S(2)}, u32[]{:S(2)}) collective-permute-start(f32[8,1024]{1,0:T(8,128)} %get-tuple-element.37), channel_id=1, source_target_pairs={{0,1},{1,0},{2,3},{3,2},{4,5},{5,4},{6,7},{7,6},{8,9},{9,8},{10,11... | collective-permute-start | bytes 98312 | tf_op jit(solution)/shard_map/ppermute | solution.py:36
  90.2 4.8 %collective-permute-start.26 = (f32[8,1024]{1,0:T(8,128)S(1)}, f32[8,1024]{1,0:T(8,128)S(1)}, u32[]{:S(2)}, u32[]{:S(2)}) collective-permute-start(f32[8,1024]{1,0:T(8,128)S(1)} %add.81), channel_id=1, source_target_pairs={{0,6},{1,7},{2,4},{3,5},{4,2},{5,3},{6,0},{7,1},{8,14},{9,15},{10,... | collective-permute-start | bytes 98312 | tf_op jit(solution)/shard_map/ppermute | solution.py:36
  91.7 3.9 %collective-permute-start.25 = (f32[8,1024]{1,0:T(8,128)S(1)}, f32[8,1024]{1,0:T(8,128)S(1)}, u32[]{:S(2)}, u32[]{:S(2)}) collective-permute-start(f32[8,1024]{1,0:T(8,128)S(1)} %add.81), channel_id=1, source_target_pairs={{0,4},{1,5},{2,6},{3,7},{4,0},{5,1},{6,2},{7,3},{8,12},{9,13},{10,... | collective-permute-start | bytes 98312 | tf_op jit(solution)/shard_map/ppermute | solution.py:36
  92.2 3.9 %collective-permute-start.24 = (f32[8,1024]{1,0:T(8,128)S(1)}, f32[8,1024]{1,0:T(8,128)S(1)}, u32[]{:S(2)}, u32[]{:S(2)}) collective-permute-start(f32[8,1024]{1,0:T(8,128)S(1)} %add.81), channel_id=1, source_target_pairs={{0,2},{1,3},{2,0},{3,1},{4,6},{5,7},{6,4},{7,5},{8,10},{9,11},{10,... | collective-permute-start | bytes 98312 | tf_op jit(solution)/shard_map/ppermute | solution.py:36
  96.1 6.0 %collective-permute-start.29 = (f32[8,1024]{1,0:T(8,128)S(1)}, f32[8,1024]{1,0:T(8,128)S(1)}, u32[]{:S(2)}, u32[]{:S(2)}) collective-permute-start(f32[8,1024]{1,0:T(8,128)S(1)} %add_add_fusion.3), channel_id=1, source_target_pairs={{0,24},{1,25},{2,26},{3,27},{4,28},{5,29},{6,30},{7,31},{8,16},{9,... | collective-permute-start | bytes 98312 | tf_op jit(solution)/shard_map/ppermute | solution.py:36
  98.6 4.9 %collective-permute-start.28 = (f32[8,1024]{1,0:T(8,128)S(1)}, f32[8,1024]{1,0:T(8,128)S(1)}, u32[]{:S(2)}, u32[]{:S(2)}) collective-permute-start(f32[8,1024]{1,0:T(8,128)S(1)} %add_add_fusion.3), channel_id=1, source_target_pairs={{0,16},{1,17},{2,18},{3,19},{4,20},{5,21},{6,22},{7,23},{8,24},{9,... | collective-permute-start | bytes 98312 | tf_op jit(solution)/shard_map/ppermute | solution.py:36
  99.3 4.3 %collective-permute-start.27 = (f32[8,1024]{1,0:T(8,128)S(1)}, f32[8,1024]{1,0:T(8,128)S(1)}, u32[]{:S(2)}, u32[]{:S(2)}) collective-permute-start(f32[8,1024]{1,0:T(8,128)S(1)} %add_add_fusion.3), channel_id=1, source_target_pairs={{0,8},{1,9},{2,10},{3,11},{4,12},{5,13},{6,14},{7,15},{8,0},{9,1},... | collective-permute-start | bytes 98312 | tf_op jit(solution)/shard_map/ppermute | solution.py:36
  100.6 5.3 %collective-permute-start.31 = (f32[8,2048]{1,0:T(8,128)}, f32[8,2048]{1,0:T(8,128)S(1)}, u32[]{:S(2)}, u32[]{:S(2)}) collective-permute-start(f32[8,2048]{1,0:T(8,128)} %get-tuple-element.43), channel_id=1, source_target_pairs={{0,1},{1,0},{2,3},{3,2},{4,5},{5,4},{6,7},{7,6},{8,9},{9,8},{10,11... | collective-permute-start | bytes 196616 | tf_op jit(solution)/shard_map/ppermute | solution.py:36
  100.6 5.3 %collective-permute-start.32 = (f32[8,2048]{1,0:T(8,128)}, f32[8,2048]{1,0:T(8,128)S(1)}, u32[]{:S(2)}, u32[]{:S(2)}) collective-permute-start(f32[8,2048]{1,0:T(8,128)} %get-tuple-element.44), channel_id=1, source_target_pairs={{0,2},{1,3},{2,0},{3,1},{4,6},{5,7},{6,4},{7,5},{8,10},{9,11},{10,... | collective-permute-start | bytes 196616 | tf_op jit(solution)/shard_map/ppermute | solution.py:36
  102.1 4.2 %collective-permute-start.33 = (f32[8,2048]{1,0:T(8,128)}, f32[8,2048]{1,0:T(8,128)S(1)}, u32[]{:S(2)}, u32[]{:S(2)}) collective-permute-start(f32[8,2048]{1,0:T(8,128)} %get-tuple-element.45), channel_id=1, source_target_pairs={{0,3},{1,2},{2,1},{3,0},{4,7},{5,6},{6,5},{7,4},{8,11},{9,10},{10,... | collective-permute-start | bytes 196616 | tf_op jit(solution)/shard_map/ppermute | solution.py:36
  103.6 2.7 %copy-start.2 = (f32[8,1024]{1,0:T(8,128)}, f32[8,1024]{1,0:T(8,128)S(1)}, u32[]{:S(2)}) copy-start(f32[8,1024]{1,0:T(8,128)S(1)} %add_add_fusion.2.held_ref) | copy-start | bytes 98308
  103.6 2.7 %collective-permute-start.30 = (f32[8,1024]{1,0:T(8,128)S(1)}, f32[8,1024]{1,0:T(8,128)S(1)}, u32[]{:S(2)}, u32[]{:S(2)}) collective-permute-start(f32[8,1024]{1,0:T(8,128)S(1)} %add_add_fusion.2.held_ref), channel_id=1, source_target_pairs={{0,1},{1,0},{2,3},{3,2},{4,5},{5,4},{6,7},{7,6},{8,9},{9,8},{10,11... | collective-permute-start | bytes 98312 | tf_op jit(solution)/shard_map/ppermute | solution.py:36
  105.9 0.6 copy-start.4
  105.9 0.6 copy-start.5
  106.3 0.6 copy-start.6
  106.3 0.6 copy-start.9

commit v2 on v1

v2 whole, which is shorter than its diff:
```python
import functools

import jax
import jax.numpy as jnp
from jax import lax
from jax.experimental import pallas as pl
from jax.experimental.pallas import tpu as pltpu
from jax.sharding import PartitionSpec as P

CLASSES = 16
HALF = CLASSES // 2

width_h = 0.25
ridge = 0.1
highest = lax.Precision.HIGHEST
f32 = jnp.float32
bf16 = jnp.bfloat16
EVERY = ("docs", "anch")
LANES = 128

NT = (((1,), (1,)), ((), ()))
NN = (((1,), (0,)), ((), ()))


def mm(left, right, dims=NN, precision=None):
    return lax.dot_general(left, right, dims, precision=precision, preferred_element_type=f32)


def split2(value):
    high = value.astype(bf16)
    return high, (value - high.astype(f32)).astype(bf16)


def swap(value, mask):
    count = lax.axis_size("docs") * lax.axis_size("anch")
    return lax.ppermute(value, EVERY, [(i, i ^ mask) for i in range(count)])


def bit_groups(bits):
    groups = []
    while bits:
        part, bits = bits[:2], bits[2:]
        masks = [1 << part[0]]
        if len(part) == 2:
            masks += [1 << part[1], (1 << part[0]) | (1 << part[1])]
        groups.append(masks)
    return groups


def sum_stage(held, masks):
    got = [swap(held, mask) for mask in masks]
    if len(got) == 1:
        return held + got[0]
    return (held + got[0]) + (got[1] + got[2])


def reduce_all(mine, send, n_bits):
    held = mine + swap(send, 1)
    for masks in bit_groups(list(range(1, n_bits))):
        held = sum_stage(held, masks)
    return held, swap(held, 1)


def aug_columns(first, second, rows):
    lane = lax.broadcasted_iota(jnp.int32, (rows, LANES), 1)
    out = jnp.zeros((rows, LANES), f32)
    for base, column in ((0, first), (3, second)):
        if column is None:
            out = jnp.where((lane >= base) & (lane < base + 3), 1.0, out)
        else:
            rest = column
            for piece in range(3):
                part = rest.astype(bf16).astype(f32)
                out = jnp.where(lane == base + piece, part, out)
                rest = rest - part
    return out.astype(bf16)


def row_sizes(value):
    return jnp.sum(value * value, axis=1, keepdims=True)


def eighth(value):
    square = value * value
    fourth = square * square
    return 1.0 / (fourth * fourth)


def label_kernel(na, me_ref, idx_ref, cls_ref, feat_ref, out_ref, x_ref, rows, picked, sems, xsem):
    docs_dev = feat_ref.shape[0]
    docs = x_ref.shape[0]
    base = (me_ref[0] // na) * docs_dev
    count = idx_ref.shape[0]
    copies = []
    for k in range(count):
        start = pl.multiple_of(((idx_ref[k] - base) >> 4) << 4, 16)
        copy = pltpu.make_async_copy(feat_ref.at[pl.ds(start, 16), :], rows.at[k], sems.at[k])
        copy.start()
        copies.append(copy)
    own = pl.ds(pl.multiple_of((me_ref[0] % na) * docs, docs), docs)
    bulk = pltpu.make_async_copy(feat_ref.at[own, :], x_ref, xsem)
    bulk.start()
    sub = lax.broadcasted_iota(jnp.int32, (16, LANES), 0)
    lane = lax.broadcasted_iota(jnp.int32, (1, LANES), 1)
    for k in range(count):
        picked[count + k : count + k + 1, :] = jnp.where(lane == cls_ref[k], 1.0, 0.0)
    for k in range(count):
        copies[k].wait()
        chosen = jnp.where(sub == ((idx_ref[k] - base) & 15), rows[k].astype(f32), 0.0)
        picked[k : k + 1, :] = jnp.sum(chosen, axis=0, keepdims=True)
    out_ref[...] = picked[...].astype(bf16)
    bulk.wait()


def build_kernel(na, me_ref, a0, a1, a2, a3, x_ref, khi_ref, klo_ref, tinv_ref, aug_ref):
    docs, feat = x_ref.shape
    quarter = a0.shape[0]
    scale = 1.0 / (feat * width_h)
    me = me_ref[0] % na
    for mask, piece in enumerate((a0, a1, a2, a3)):
        at = pl.ds(pl.multiple_of((me ^ mask) * quarter, quarter), quarter)
        value = piece[...].astype(f32)
        aug_ref[at, 0:feat] = (value * (-2.0 * scale)).astype(bf16)
        aug_ref[at, feat:] = aug_columns(row_sizes(value) * scale + 1.0, None, quarter)
    tile = min(256, docs)
    for col in range(0, docs, tile):
        raw = x_ref[col : col + tile, :]
        right = jnp.concatenate([raw, aug_columns(None, row_sizes(raw.astype(f32)) * scale, tile)], axis=1)
        total = jnp.zeros((8, tile), f32)
        for at in range(0, aug_ref.shape[0], 256):
            kern = eighth(mm(aug_ref[at : at + 256, :], right, NT))
            high, low = split2(kern)
            khi_ref[at : at + 256, col : col + tile] = high
            klo_ref[at : at + 256, col : col + tile] = low
            total = total + jnp.sum(kern.reshape(32, 8, tile), axis=0)
        tinv_ref[:, col : col + tile] = 1.0 / jnp.sum(total, axis=0, keepdims=True)


def times(vec, khi, klo):
    both = mm(vec, khi)
    return both[0:CLASSES] + (both[CLASSES:] + mm(vec[0:CLASSES], klo))


def times_back(value, khi, klo):
    high, low = split2(value)
    both = mm(jnp.concatenate([high, low], axis=0), khi, NT)
    return both[0:CLASSES] + (both[CLASSES:] + mm(high, klo, NT))


def pieces(value):
    return jnp.concatenate(split2(value), axis=0)


def gram(vec, khi_ref, klo_ref, tinv_ref, with_degree=False):
    khi, klo, tinv = khi_ref[...], klo_ref[...], tinv_ref[...]
    spread = times(vec, khi, klo) * tinv
    high, low = split2(spread * tinv)
    parts, second = [high, low], [high]
    if with_degree:
        row = lax.broadcasted_iota(jnp.int32, (CLASSES, tinv.shape[1]), 0)
        thigh = tinv.astype(bf16).astype(f32)
        ones = jnp.where(row == 0, thigh, jnp.where(row == 1, tinv - thigh, 0.0)).astype(bf16)
        parts.append(ones)
        second.append(ones)
    one = mm(jnp.concatenate(parts, axis=0), khi, NT)
    two = mm(jnp.concatenate(second, axis=0), klo, NT)
    out = one[0:CLASSES] + (one[CLASSES : 2 * CLASSES] + two[0:CLASSES])
    if not with_degree:
        return spread, out
    deg = one[2 * CLASSES :] + two[CLASSES:]
    return spread, out, deg[0:1] + deg[1:2]


def put_halves(acc, me, mine_ref, send_ref):
    core = me & 1
    mine_ref[...] = acc[pl.ds(pl.multiple_of(core * HALF, HALF), HALF), :]
    send_ref[...] = acc[pl.ds(pl.multiple_of((1 - core) * HALF, HALF), HALF), :]


def take_halves(acc, me, mine_ref, got_ref):
    core = me & 1
    acc[pl.ds(pl.multiple_of(core * HALF, HALF), HALF), :] = mine_ref[...]
    acc[pl.ds(pl.multiple_of((1 - core) * HALF, HALF), HALF), :] = got_ref[...]


def mean_of(value):
    return jnp.mean(value, axis=1, keepdims=True)


def total_of(value):
    return jnp.sum(jnp.sum(value, axis=1, keepdims=True), axis=0, keepdims=True)


def first_kernel(na, labs, slots, gain, me_ref, *refs):
    lab_refs = refs[: len(slots)]
    (aug_ref, khi_ref, klo_ref, tinv_ref, mine_ref, send_ref, rhs_ref, zhi_ref, zlo_ref, spread_ref,
     laug, hot, acc) = refs[len(slots) :]
    anchors = aug_ref.shape[0]
    feat = laug.shape[1] - LANES
    docs = me_ref[0] // na
    for masks, ref in zip(slots, lab_refs):
        for k, mask in enumerate(masks):
            at = pl.ds(pl.multiple_of((docs ^ mask) * labs, labs), labs)
            laug[at, 0:feat] = ref[2 * labs * k : 2 * labs * k + labs, :]
            hot[at, :] = ref[2 * labs * k + labs : 2 * labs * (k + 1), :].astype(f32)
    size = row_sizes(laug[:, 0:feat].astype(f32)) * (1.0 / (feat * width_h))
    laug[:, feat:] = aug_columns(None, size, laug.shape[0])
    kern = eighth(mm(aug_ref[...], laug[...], NT))
    zlab = kern / jnp.sum(kern, axis=0, keepdims=True)
    zhi_ref[...], zlo_ref[...] = split2(zlab)
    onehot = hot[...].T[0:CLASSES, :]
    rhs = gain * mm(onehot, zlab, NT, highest)
    rhs_ref[...] = rhs
    middle = mean_of(rhs)
    spread, out, deg = gram(pieces(rhs - middle), khi_ref, klo_ref, tinv_ref, True)
    spread_ref[...] = spread + middle
    acc[:, 0:anchors] = out
    acc[:, anchors:] = jnp.zeros((CLASSES, LANES), f32)
    for k in range(anchors // LANES):
        acc[k : k + 1, anchors:] = deg[:, k * LANES : (k + 1) * LANES]
    put_halves(acc, me_ref[0], mine_ref, send_ref)


def second_kernel(me_ref, held_ref, got_ref, rhs_ref, zhi_ref, zlo_ref, khi_ref, klo_ref, tinv_ref,
                  mine_ref, send_ref, dinv_ref, lab_ref, whole, acc):
    anchors = rhs_ref.shape[1]
    take_halves(whole, me_ref[0], held_ref, got_ref)
    for k in range(anchors // LANES):
        dinv_ref[:, k * LANES : (k + 1) * LANES] = 1.0 / whole[k : k + 1, anchors:]
    rhs = rhs_ref[...]
    vec = rhs - mean_of(rhs) - whole[:, 0:anchors] * dinv_ref[...]
    acc[...] = gram(pieces(vec), khi_ref, klo_ref, tinv_ref)[1]
    put_halves(acc, me_ref[0], mine_ref, send_ref)
    zhi, zlo = zhi_ref[...], zlo_ref[...]
    lab_ref[...] = times_back(times(pieces(rhs), zhi, zlo), zhi, zlo)


def third_kernel(na, lab_scale, graph_scale, me_ref, held_ref, got_ref, rhs_ref, lab_ref, spread0_ref,
                 zhi_ref, zlo_ref, khi_ref, klo_ref, tinv_ref, *refs):
    (mine_ref, send_ref, direc_ref, part_ref, next_ref), outs, (acc, slots) = refs[0:5], refs[5 : 5 + na], refs[5 + na :]
    quarter = CLASSES // na
    me = me_ref[0]
    take_halves(acc, me, held_ref, got_ref)
    rhs = rhs_ref[...]
    image = lab_scale * lab_ref[...] + graph_scale * acc[...] + ridge * rhs
    norm = total_of(rhs * rhs)
    alpha = norm / total_of(rhs * image)
    resid = rhs - alpha * image
    after = total_of(resid * resid)
    direc = resid + (after / norm) * rhs
    direc_ref[...] = direc
    part_ref[...] = alpha * rhs
    middle = mean_of(direc)
    spread, out = gram(pieces(direc - middle), khi_ref, klo_ref, tinv_ref)
    acc[...] = out
    put_halves(acc, me, mine_ref, send_ref)
    full = spread + middle
    part = alpha * spread0_ref[...]
    for k in range(na):
        slots[k, 0:quarter, :] = part[k * quarter : (k + 1) * quarter]
        slots[k, quarter : 2 * quarter, :] = full[k * quarter : (k + 1) * quarter]
    for mask in range(na):
        outs[mask][...] = slots[(me % na) ^ mask]
    seen = times(pieces(direc), zhi_ref[...], zlo_ref[...])
    base = lab_scale * total_of(seen * seen) + ridge * total_of(direc * direc)
    next_ref[0:8, :] = jnp.broadcast_to(after, (8, LANES))
    next_ref[8:, :] = jnp.broadcast_to(base, (8, LANES))


def last_kernel(na, graph_scale, me_ref, held_ref, got_ref, direc_ref, part_ref, next_ref, dinv_ref, *refs):
    parts, (anchor_ref, doc_ref, whole) = refs[0:na], refs[na:]
    me = me_ref[0]
    mine = me % na
    take_halves(whole, me, held_ref, got_ref)
    prod = whole[...]
    direc = direc_ref[...]
    quad = total_of(prod * (direc - mean_of(direc) - prod * dinv_ref[...]))
    alpha = next_ref[0:1, 0:1] / (next_ref[8:9, 0:1] + graph_scale * quad)
    whole[...] = part_ref[...] + alpha * direc
    rows = anchor_ref.shape[1]
    anchor_ref[...] = whole[:, pl.ds(pl.multiple_of(mine * rows, rows), rows)]
    quarter, docs = doc_ref.shape[0], parts[0].shape[1]
    for mask in range(na):
        at = pl.ds(pl.multiple_of((mine ^ mask) * docs, docs), docs)
        doc_ref[:, at] = parts[mask][0:quarter, :] + alpha * parts[mask][quarter:, :]


VMEM = pl.BlockSpec(memory_space=pltpu.MemorySpace.VMEM)
SMEM = pl.BlockSpec(memory_space=pltpu.MemorySpace.SMEM)


def call(kernel, in_specs, out_shape, scratch, name, flops=1 << 20, moved=1 << 18):
    return pl.pallas_call(
        kernel,
        in_specs=in_specs,
        out_specs=[VMEM] * len(out_shape),
        out_shape=out_shape,
        scratch_shapes=scratch,
        name=name,
        compiler_params=pltpu.CompilerParams(vmem_limit_bytes=24 << 20),
        cost_estimate=pl.CostEstimate(flops=flops, bytes_accessed=moved, transcendentals=0),
    )


def per_device(features, anchors, lab_index, lab_class):
    docs_dev, feat = features.shape
    nd, na = lax.axis_size("docs"), lax.axis_size("anch")
    n_bits = (nd * na).bit_length() - 1
    a_bits = na.bit_length() - 1
    labs = lab_index.shape[0]
    labeled = labs * nd
    quarter = anchors.shape[0]
    total = quarter * na
    docs = docs_dev // na
    lab_scale = total / labeled
    graph_scale = total * total / (docs_dev * nd)
    assert na == 4 and nd * na == 1 << n_bits and total // LANES <= CLASSES and feat == LANES
    sds = jax.ShapeDtypeStruct

    me = lax.axis_index(EVERY).astype(jnp.int32).reshape(1)

    own, mine_x = call(
        functools.partial(label_kernel, na),
        [SMEM, SMEM, SMEM, pl.BlockSpec(memory_space=pl.ANY)],
        [sds((2 * labs, feat), bf16), sds((docs, feat), bf16)],
        [
            pltpu.VMEM((labs, 16, LANES), bf16),
            pltpu.VMEM((2 * labs, LANES), f32),
            pltpu.SemaphoreType.DMA((labs,)),
            pltpu.SemaphoreType.DMA,
        ],
        "label_rows",
    )(me, lab_index, lab_class, features)

    piece = [anchors, swap(anchors, 1), swap(anchors, 2), None]
    piece[3] = swap(piece[2], 1)

    held, masks = own, [0]
    bits = list(range(a_bits, n_bits))
    stages = bit_groups(bits[:1]) + bit_groups(bits[1:])
    for at, stage in enumerate(stages):
        got = [swap(held, mask) for mask in stage]
        if at < len(stages) - 1:
            masks = masks + [m ^ mask for mask in stage for m in masks]
            held = jnp.concatenate([held] + got, axis=0)
    lab_arrays = [held] + got
    slots = [[m >> a_bits for m in masks]] + [[(m ^ mask) >> a_bits for m in masks] for mask in stages[-1]]

    k_sds = sds((total, docs), bf16)
    khi, klo, tinv, aug = call(
        functools.partial(build_kernel, na),
        [SMEM] + [VMEM] * 5,
        [k_sds, k_sds, sds((1, docs), f32), sds((total, feat + LANES), bf16)],
        [],
        "kernel_matrix",
        flops=2 * total * docs * 256,
        moved=4 * total * docs,
    )(me, *piece, mine_x)

    long = total + LANES
    flat_sds = sds((CLASSES, total), f32)
    half_sds = sds((HALF, total), f32)
    z_sds = sds((total, labeled), bf16)
    acc = pltpu.VMEM((CLASSES, total), f32)
    work = dict(flops=8 * total * docs * 64, moved=4 * total * docs)

    mine, send, rhs, zhi, zlo, spread = call(
        functools.partial(first_kernel, na, labs, slots, CLASSES * lab_scale),
        [SMEM] + [VMEM] * (len(lab_arrays) + 4),
        [sds((HALF, long), f32)] * 2 + [flat_sds, z_sds, z_sds, sds((CLASSES, docs), f32)],
        [
            pltpu.VMEM((labeled, feat + LANES), bf16),
            pltpu.VMEM((labeled, LANES), f32),
            pltpu.VMEM((CLASSES, long), f32),
        ],
        "first_gram",
        **work,
    )(me, *lab_arrays, aug, khi, klo, tinv)

    held, got = reduce_all(mine, send, n_bits)
    mine, send, dinv, lab = call(
        second_kernel,
        [SMEM] + [VMEM] * 8,
        [half_sds, half_sds, sds((1, total), f32), flat_sds],
        [pltpu.VMEM((CLASSES, long), f32), acc],
        "second_gram",
        **work,
    )(me, held, got, rhs, zhi, zlo, khi, klo, tinv)

    held, got = reduce_all(mine, send, n_bits)
    part_rows = 2 * CLASSES // na
    mine, send, direc, part, stats, *docs_out = call(
        functools.partial(third_kernel, na, lab_scale, graph_scale),
        [SMEM] + [VMEM] * 10,
        [half_sds, half_sds, flat_sds, flat_sds, sds((16, LANES), f32)] + [sds((part_rows, docs), f32)] * na,
        [acc, pltpu.VMEM((na, part_rows, docs), f32)],
        "third_gram",
        **work,
    )(me, held, got, rhs, lab, spread, zhi, zlo, khi, klo, tinv)

    held, got = reduce_all(mine, send, n_bits)
    parts = [docs_out[0]] + [swap(docs_out[mask], mask) for mask in range(1, na)]
    anchor_scores, doc_scores = call(
        functools.partial(last_kernel, na, graph_scale),
        [SMEM] + [VMEM] * (6 + na),
        [sds((CLASSES, quarter), f32), sds((CLASSES // na, docs_dev), f32)],
        [acc],
        "scores",
    )(me, held, got, direc, part, stats, dinv, *parts)
    return anchor_scores.T, doc_scores


def solution(mesh):
    in_specs = (P("docs", None), P("anch", None), P("docs"), P("docs"))
    out_specs = (P("anch", None), P("anch", "docs"))
    return jax.shard_map(per_device, mesh=mesh, in_specs=in_specs, out_specs=out_specs, check_vma=False)
```

time: 110 us -> 84.9 us (0.77)
  Pallas kernels: 42.3 us -> 18.7 us
  waiting for transfers between devices: 22.6 us -> 25.8 us
  other arithmetic: 3.09 us -> 0.08 us
    pallas_call x7 -> x5, Pallas kernels: 33.1 us -> 13.5 us  [the longest x1 4.08 us: per_device(): call(functools.partial(third_kernel, na, lab_scale, graph_scale), [SMEM]...]
    pallas_call x1, Pallas kernels: 9.18 us -> 5.17 us  [per_device(): call(functools.partial(first_kernel, na, labs, slots, CLASSES * lab_scale...]
    ppermute x34, waiting for transfers between devices: 22.6 us -> 25.8 us  [swap(): return lax.ppermute(value, EVERY, [(i, i ^ mask) for i in range(count)])]
    add x3, other arithmetic: 2.31 us -> 0.02 us  [reduce_all(): held = mine + swap(send, 1)]
    unnamed x32 -> x9, local copies, waits for them, and re-layouts: 3.7 us -> 3.74 us
  transfers between devices with their start and end apart: 34 -> 34, of which waited for: 22 -> 24; matrix products, arithmetic and copies ran while one was open for 1% -> 0% of each run, Pallas kernels for 15% -> 5%
where the time goes in v2:
time: 84.9 us; the launch traced here: 84.7 us
  starting transfers between devices  35.6 us (42%)
  waiting for transfers between devices  25.8 us (30%)
  Pallas kernels  18.7 us (22%)
  local copies, waits for them, and re-layouts  3.75 us (4%)
    ppermute x34, starting transfers between devices, swap(): return lax.ppermute(value, EVERY, [(i, i ^ mask) for i in range(count)])  35.6 us
    ppermute x34, waiting for transfers between devices, swap(): return lax.ppermute(value, EVERY, [(i, i ^ mask) for i in range(count)])  25.8 us
    pallas_call x1, Pallas kernels, per_device(): call(functools.partial(first_kernel, na, labs, slots, CLASSES * lab_scale...  5.17 us
    pallas_call x1, Pallas kernels, per_device(): call(functools.partial(third_kernel, na, lab_scale, graph_scale), [SMEM]...  4.08 us
    pallas_call x1, Pallas kernels, per_device(): call(second_kernel, [SMEM] + [VMEM] * 8, [half_sds, half_sds, sds((1, tot...  3.97 us
    unnamed x9, local copies, waits for them, and re-layouts  3.74 us
    pallas_call x1, Pallas kernels, per_device(): call(functools.partial(build_kernel, na), [SMEM] + [VMEM] * 5, [k_sds, k_...  3.44 us
  transfers between devices with their start and end apart: 34, of which 24 were waited for; matrix products, arithmetic and copies ran while one was open for 0% of the time, Pallas kernels for 5%

profile of v2, /device:TPU:0, one launch (start us, length us, event | category | flops | bytes accessed | tf_op | source)
XLA Modules:
  0.0 84.7 jit_solution(11919281765397788965)
XLA Ops:
  0.6 0.6 collective-permute-start.4
  1.2 2.6 %collective-permute-start.5 = (bf16[256,128]{1,0:T(8,128)(2,1)}, bf16[256,128]{1,0:T(8,128)(2,1)S(1)}, u32[]{:S(2)}, u32[]{:S(2)}) collective-permute-start(bf16[256,128]{1,0:T(8,128)(2,1)} %a0.1), channel_id=1, source_target_pairs={{0,2},{1,3},{2,0},{3,1},{4,6},{5,7},{6,4},{7,5},{8,10},{9,11},{10,... | collective-permute-start | bytes 196616 | tf_op jit(solution)/shard_map/ppermute | solution.py:36
  3.7 1.6 %copy-done = bf16[8192,128]{1,0:T(8,128)(2,1)S(1)} copy-done((bf16[8192,128]{1,0:T(8,128)(2,1)S(1)}, bf16[8192,128]{1,0:T(8,128)(2,1)}, u32[]{:S(2)}) %copy-start) | copy-done | bytes 2097176
  5.3 0.7 copy-done.1
  6.0 0.7 copy-done.2
  6.6 1.1 %label_rows.1 = (bf16[32,128]{1,0:T(8,128)(2,1)S(1)}, bf16[2048,128]{1,0:T(8,128)(2,1)S(1)}) custom-call(s32[1]{0:T(128)} %bitcast.me_ref, s32[16]{0:T(128)S(1)} %copy-done.1, s32[16]{0:T(128)S(1)} %copy-done.2, bf16[8192,128]{1,0:T(8,128)(2,1)S(1)} %copy-done), custom_call_target="tpu_custom_call" | custom-call | flops 1048576 | bytes 262144 | tf_op jit(solution)/shard_map/label_rows/pallas_call | solution.py:322
  7.8 1.6 %collective-permute-start = (bf16[32,128]{1,0:T(8,128)(2,1)S(1)}, bf16[32,128]{1,0:T(8,128)(2,1)S(1)}, u32[]{:S(2)}, u32[]{:S(2)}) collective-permute-start(bf16[32,128]{1,0:T(8,128)(2,1)S(1)} %get-tuple-element.29), channel_id=1, source_target_pairs={{0,4},{1,5},{2,6},{3,7},{4,0},{5,1},{6,2},{7,3},{8,12},{9,13},{10,... | collective-permute-start | bytes 24584 | tf_op jit(solution)/shard_map/ppermute | solution.py:36
  9.4 2.1 %collective-permute-done = bf16[32,128]{1,0:T(8,128)(2,1)S(1)} collective-permute-done((bf16[32,128]{1,0:T(8,128)(2,1)S(1)}, bf16[32,128]{1,0:T(8,128)(2,1)S(1)}, u32[]{:S(2)}, u32[]{:S(2)}) %collective-permute-start) | collective-permute-done | bytes 8224 | tf_op jit(solution)/shard_map/ppermute | solution.py:36
  11.5 3.6 %collective-permute-start.3 = (bf16[64,128]{1,0:T(8,128)(2,1)S(1)}, bf16[64,128]{1,0:T(8,128)(2,1)S(1)}, u32[]{:S(2)}, u32[]{:S(2)}) collective-permute-start(bf16[64,128]{1,0:T(8,128)(2,1)S(1)} %constant_dynamic-update-slice_fusion.refs_0_), channel_id=1, source_target_pairs={{0,24},{1,25},{2,26},{3,27},{4,28},{5,29},{6,30},{7,31},{8,16},{9,... | collective-permute-start | bytes 49160 | tf_op jit(solution)/shard_map/ppermute | solution.py:36
  15.1 0.8 collective-permute-start.1
  15.9 0.8 copy-done.3
  16.7 3.4 %kernel_matrix.1 = (bf16[1024,2048]{1,0:T(8,128)(2,1)S(1)}, bf16[1024,2048]{1,0:T(8,128)(2,1)S(1)}, f32[1,2048]{1,0:T(1,128)S(1)}, bf16[1024,256]{1,0:T(8,128)(2,1)S(1)}) custom-call(s32[1]{0:T(128)} %bitcast.me_ref, bf16[256,128]{1,0:T(8,128)(2,1)S(1)} %copy-done.3, bf16[256,128]{1,0:T(8,128)(2,1)S(1)} %collective-permute-done.4.a1, ...), custom_call_target="tpu_custom_call" | custom-call | flops 1073741824 | bytes 8388608 | tf_op jit(solution)/shard_map/kernel_matrix/pallas_call | solution.py:350
  20.2 5.2 %first_gram.1 = (f32[8,1152]{1,0:T(8,128)S(1)}, f32[8,1152]{1,0:T(8,128)S(1)}, f32[16,1024]{1,0:T(8,128)S(1)}, bf16[1024,128]{1,0:T(8,128)(2,1)S(1)}, bf16[1024,...) custom-call(s32[1]{0:T(128)} %bitcast.me_ref, bf16[64,128]{1,0:T(8,128)(2,1)S(1)} %constant_dynamic-update-slice_fusion.refs_0_, ...), custom_call_target="tpu_custom_call" | custom-call | flops 1073741824 | bytes 8388608 | tf_op jit(solution)/shard_map/first_gram/pallas_call | solution.py:367
  25.4 0.0 collective-permute-start.7
  25.4 1.2 %collective-permute-done.7 = f32[8,1152]{1,0:T(8,128)S(1)} collective-permute-done((f32[8,1152]{1,0:T(8,128)S(1)}, f32[8,1152]{1,0:T(8,128)S(1)}, u32[]{:S(2)}, u32[]{:S(2)}) %collective-permute-start.7) | collective-permute-done | bytes 36896 | tf_op jit(solution)/shard_map/ppermute | solution.py:36
  26.7 1.5 %collective-permute-start.10 = (f32[8,1152]{1,0:T(8,128)S(1)}, f32[8,1152]{1,0:T(8,128)S(1)}, u32[]{:S(2)}, u32[]{:S(2)}) collective-permute-start(f32[8,1152]{1,0:T(8,128)S(1)} %add.67), channel_id=1, source_target_pairs={{0,6},{1,7},{2,4},{3,5},{4,2},{5,3},{6,0},{7,1},{8,14},{9,15},{10,... | collective-permute-start | bytes 110600 | tf_op jit(solution)/shard_map/ppermute | solution.py:36
  28.1 0.3 collective-permute-start.9
  28.4 1.7 %collective-permute-start.8 = (f32[8,1152]{1,0:T(8,128)S(1)}, f32[8,1152]{1,0:T(8,128)S(1)}, u32[]{:S(2)}, u32[]{:S(2)}) collective-permute-start(f32[8,1152]{1,0:T(8,128)S(1)} %add.67), channel_id=1, source_target_pairs={{0,2},{1,3},{2,0},{3,1},{4,6},{5,7},{6,4},{7,5},{8,10},{9,11},{10,... | collective-permute-start | bytes 110600 | tf_op jit(solution)/shard_map/ppermute | solution.py:36
  30.1 1.4 %collective-permute-done.10 = f32[8,1152]{1,0:T(8,128)S(1)} collective-permute-done((f32[8,1152]{1,0:T(8,128)S(1)}, f32[8,1152]{1,0:T(8,128)S(1)}, u32[]{:S(2)}, u32[]{:S(2)}) %collective-permute-start.10) | collective-permute-done | bytes 36896 | tf_op jit(solution)/shard_map/ppermute | solution.py:36
  31.5 0.6 collective-permute-done.9
  32.1 0.3 collective-permute-done.8
  32.4 3.9 %collective-permute-start.13 = (f32[8,1152]{1,0:T(8,128)S(1)}, f32[8,1152]{1,0:T(8,128)S(1)}, u32[]{:S(2)}, u32[]{:S(2)}) collective-permute-start(f32[8,1152]{1,0:T(8,128)S(1)} %add_add_fusion.1), channel_id=1, source_target_pairs={{0,24},{1,25},{2,26},{3,27},{4,28},{5,29},{6,30},{7,31},{8,16},{9,... | collective-permute-start | bytes 110600 | tf_op jit(solution)/shard_map/ppermute | solution.py:36
  36.3 0.6 collective-permute-start.11
  36.9 1.3 %collective-permute-done.13 = f32[8,1152]{1,0:T(8,128)S(1)} collective-permute-done((f32[8,1152]{1,0:T(8,128)S(1)}, f32[8,1152]{1,0:T(8,128)S(1)}, u32[]{:S(2)}, u32[]{:S(2)}) %collective-permute-start.13) | collective-permute-done | bytes 36896 | tf_op jit(solution)/shard_map/ppermute | solution.py:36
  38.2 2.9 %collective-permute-done.12 = f32[8,1152]{1,0:T(8,128)S(1)} collective-permute-done((f32[8,1152]{1,0:T(8,128)S(1)}, f32[8,1152]{1,0:T(8,128)S(1)}, u32[]{:S(2)}, u32[]{:S(2)}) %collective-permute-start.12) | collective-permute-done | bytes 36896 | tf_op jit(solution)/shard_map/ppermute | solution.py:36
  41.2 0.1 collective-permute-start.14
  41.2 1.2 %collective-permute-done.14.got_ref = f32[8,1152]{1,0:T(8,128)S(1)} collective-permute-done((f32[8,1152]{1,0:T(8,128)S(1)}, f32[8,1152]{1,0:T(8,128)S(1)}, u32[]{:S(2)}, u32[]{:S(2)}) %collective-permute-start.14) | collective-permute-done | bytes 36896 | tf_op jit(solution)/shard_map/ppermute | solution.py:36
  42.4 4.0 %second_gram.1 = (f32[8,1024]{1,0:T(8,128)S(1)}, f32[8,1024]{1,0:T(8,128)S(1)}, f32[1,1024]{1,0:T(1,128)S(1)}, f32[16,1024]{1,0:T(8,128)S(1)}) custom-call(s32[1]{0:T(128)} %bitcast.me_ref, f32[8,1152]{1,0:T(8,128)S(1)} %add_add_fusion.held_ref, f32[8,1152]{1,0:T(8,128)S(1)} %collective-permute-done.14.got_ref, f32[16,1024]{1,0:T(8,128)S(1)} %get-tuple-element.37.rhs_ref, ...), custom_call_target="tpu_custom_call" | custom-call | flops 1073741824 | bytes 8388608 | tf_op jit(solution)/shard_map/second_gram/pallas_call | solution.py:381
  46.4 0.2 collective-permute-start.15
  46.6 1.0 %collective-permute-done.15 = f32[8,1024]{1,0:T(8,128)S(1)} collective-permute-done((f32[8,1024]{1,0:T(8,128)S(1)}, f32[8,1024]{1,0:T(8,128)S(1)}, u32[]{:S(2)}, u32[]{:S(2)}) %collective-permute-start.15) | collective-permute-done | bytes 32800 | tf_op jit(solution)/shard_map/ppermute | solution.py:36
  47.7 2.4 %collective-permute-start.18 = (f32[8,1024]{1,0:T(8,128)S(1)}, f32[8,1024]{1,0:T(8,128)S(1)}, u32[]{:S(2)}, u32[]{:S(2)}) collective-permute-start(f32[8,1024]{1,0:T(8,128)S(1)} %add.74), channel_id=1, source_target_pairs={{0,6},{1,7},{2,4},{3,5},{4,2},{5,3},{6,0},{7,1},{8,14},{9,15},{10,... | collective-permute-start | bytes 98312 | tf_op jit(solution)/shard_map/ppermute | solution.py:36
  50.1 0.5 collective-permute-start.17
  50.6 0.5 collective-permute-start.16
  51.1 1.3 %collective-permute-done.18 = f32[8,1024]{1,0:T(8,128)S(1)} collective-permute-done((f32[8,1024]{1,0:T(8,128)S(1)}, f32[8,1024]{1,0:T(8,128)S(1)}, u32[]{:S(2)}, u32[]{:S(2)}) %collective-permute-start.18) | collective-permute-done | bytes 32800 | tf_op jit(solution)/shard_map/ppermute | solution.py:36
  52.5 1.5 %collective-permute-done.17 = f32[8,1024]{1,0:T(8,128)S(1)} collective-permute-done((f32[8,1024]{1,0:T(8,128)S(1)}, f32[8,1024]{1,0:T(8,128)S(1)}, u32[]{:S(2)}, u32[]{:S(2)}) %collective-permute-start.17) | collective-permute-done | bytes 32800 | tf_op jit(solution)/shard_map/ppermute | solution.py:36
  54.0 0.5 collective-permute-done.16
  54.5 1.5 %collective-permute-start.21 = (f32[8,1024]{1,0:T(8,128)S(1)}, f32[8,1024]{1,0:T(8,128)S(1)}, u32[]{:S(2)}, u32[]{:S(2)}) collective-permute-start(f32[8,1024]{1,0:T(8,128)S(1)} %add_add_fusion.5), channel_id=1, source_target_pairs={{0,24},{1,25},{2,26},{3,27},{4,28},{5,29},{6,30},{7,31},{8,16},{9,... | collective-permute-start | bytes 98312 | tf_op jit(solution)/shard_map/ppermute | solution.py:36
  56.1 0.6 collective-permute-start.20
  56.7 2.3 %collective-permute-start.19 = (f32[8,1024]{1,0:T(8,128)S(1)}, f32[8,1024]{1,0:T(8,128)S(1)}, u32[]{:S(2)}, u32[]{:S(2)}) collective-permute-start(f32[8,1024]{1,0:T(8,128)S(1)} %add_add_fusion.5), channel_id=1, source_target_pairs={{0,8},{1,9},{2,10},{3,11},{4,12},{5,13},{6,14},{7,15},{8,0},{9,1},... | collective-permute-start | bytes 98312 | tf_op jit(solution)/shard_map/ppermute | solution.py:36
  59.0 1.3 %collective-permute-done.21 = f32[8,1024]{1,0:T(8,128)S(1)} collective-permute-done((f32[8,1024]{1,0:T(8,128)S(1)}, f32[8,1024]{1,0:T(8,128)S(1)}, u32[]{:S(2)}, u32[]{:S(2)}) %collective-permute-start.21) | collective-permute-done | bytes 32800 | tf_op jit(solution)/shard_map/ppermute | solution.py:36
  60.3 0.6 collective-permute-done.20
  60.9 0.3 collective-permute-done.19
  61.2 0.1 collective-permute-start.22
  61.3 1.2 %collective-permute-done.22.got_ref = f32[8,1024]{1,0:T(8,128)S(1)} collective-permute-done((f32[8,1024]{1,0:T(8,128)S(1)}, f32[8,1024]{1,0:T(8,128)S(1)}, u32[]{:S(2)}, u32[]{:S(2)}) %collective-permute-start.22) | collective-permute-done | bytes 32800 | tf_op jit(solution)/shard_map/ppermute | solution.py:36
  62.5 4.1 %third_gram.1 = (f32[8,1024]{1,0:T(8,128)S(1)}, f32[8,1024]{1,0:T(8,128)S(1)}, f32[16,1024]{1,0:T(8,128)S(1)}, f32[16,1024]{1,0:T(8,128)S(1)}, f32[16,128]{1,0:T...) custom-call(s32[1]{0:T(128)} %bitcast.me_ref, ...), custom_call_target="tpu_custom_call" | custom-call | flops 1073741824 | bytes 8388608 | tf_op jit(solution)/shard_map/third_gram/pallas_call | solution.py:392
  66.6 0.2 collective-permute-start.23
  66.8 1.0 %collective-permute-done.23 = f32[8,1024]{1,0:T(8,128)S(1)} collective-permute-done((f32[8,1024]{1,0:T(8,128)S(1)}, f32[8,1024]{1,0:T(8,128)S(1)}, u32[]{:S(2)}, u32[]{:S(2)}) %collective-permute-start.23) | collective-permute-done | bytes 32800 | tf_op jit(solution)/shard_map/ppermute | solution.py:36
  67.8 1.5 %collective-permute-start.26 = (f32[8,1024]{1,0:T(8,128)S(1)}, f32[8,1024]{1,0:T(8,128)S(1)}, u32[]{:S(2)}, u32[]{:S(2)}) collective-permute-start(f32[8,1024]{1,0:T(8,128)S(1)} %add.81), channel_id=1, source_target_pairs={{0,6},{1,7},{2,4},{3,5},{4,2},{5,3},{6,0},{7,1},{8,14},{9,15},{10,... | collective-permute-start | bytes 98312 | tf_op jit(solution)/shard_map/ppermute | solution.py:36
  69.3 0.5 collective-permute-start.25
  69.8 1.5 %collective-permute-start.24 = (f32[8,1024]{1,0:T(8,128)S(1)}, f32[8,1024]{1,0:T(8,128)S(1)}, u32[]{:S(2)}, u32[]{:S(2)}) collective-permute-start(f32[8,1024]{1,0:T(8,128)S(1)} %add.81), channel_id=1, source_target_pairs={{0,2},{1,3},{2,0},{3,1},{4,6},{5,7},{6,4},{7,5},{8,10},{9,11},{10,... | collective-permute-start | bytes 98312 | tf_op jit(solution)/shard_map/ppermute | solution.py:36
  71.3 1.3 %collective-permute-done.26 = f32[8,1024]{1,0:T(8,128)S(1)} collective-permute-done((f32[8,1024]{1,0:T(8,128)S(1)}, f32[8,1024]{1,0:T(8,128)S(1)}, u32[]{:S(2)}, u32[]{:S(2)}) %collective-permute-start.26) | collective-permute-done | bytes 32800 | tf_op jit(solution)/shard_map/ppermute | solution.py:36
  72.6 0.6 collective-permute-done.25
  73.2 0.5 collective-permute-done.24
  73.8 2.4 %collective-permute-start.29 = (f32[8,1024]{1,0:T(8,128)S(1)}, f32[8,1024]{1,0:T(8,128)S(1)}, u32[]{:S(2)}, u32[]{:S(2)}) collective-permute-start(f32[8,1024]{1,0:T(8,128)S(1)} %add_add_fusion.3), channel_id=1, source_target_pairs={{0,24},{1,25},{2,26},{3,27},{4,28},{5,29},{6,30},{7,31},{8,16},{9,... | collective-permute-start | bytes 98312 | tf_op jit(solution)/shard_map/ppermute | solution.py:36
  76.2 0.8 collective-permute-start.28
  77.0 1.2 %collective-permute-start.27 = (f32[8,1024]{1,0:T(8,128)S(1)}, f32[8,1024]{1,0:T(8,128)S(1)}, u32[]{:S(2)}, u32[]{:S(2)}) collective-permute-start(f32[8,1024]{1,0:T(8,128)S(1)} %add_add_fusion.3), channel_id=1, source_target_pairs={{0,8},{1,9},{2,10},{3,11},{4,12},{5,13},{6,14},{7,15},{8,0},{9,1},... | collective-permute-start | bytes 98312 | tf_op jit(solution)/shard_map/ppermute | solution.py:36
  78.2 1.5 %collective-permute-start.32 = (f32[8,2048]{1,0:T(8,128)S(1)}, f32[8,2048]{1,0:T(8,128)S(1)}, u32[]{:S(2)}, u32[]{:S(2)}) collective-permute-start(f32[8,2048]{1,0:T(8,128)S(1)} %get-tuple-element.52), channel_id=1, source_target_pairs={{0,2},{1,3},{2,0},{3,1},{4,6},{5,7},{6,4},{7,5},{8,10},{9,11},{10,... | collective-permute-start | bytes 196616 | tf_op jit(solution)/shard_map/ppermute | solution.py:36
  79.7 0.4 collective-permute-start.33
  80.1 1.0 %collective-permute-done.28 = f32[8,1024]{1,0:T(8,128)S(1)} collective-permute-done((f32[8,1024]{1,0:T(8,128)S(1)}, f32[8,1024]{1,0:T(8,128)S(1)}, u32[]{:S(2)}, u32[]{:S(2)}) %collective-permute-start.28) | collective-permute-done | bytes 32800 | tf_op jit(solution)/shard_map/ppermute | solution.py:36
  81.1 0.1 collective-permute-done.27
  81.3 0.2 collective-permute-start.30
  81.4 1.3 %collective-permute-done.32.refs_2_ = f32[8,2048]{1,0:T(8,128)S(1)} collective-permute-done((f32[8,2048]{1,0:T(8,128)S(1)}, f32[8,2048]{1,0:T(8,128)S(1)}, u32[]{:S(2)}, u32[]{:S(2)}) %collective-permute-start.32) | collective-permute-done | bytes 65568 | tf_op jit(solution)/shard_map/ppermute | solution.py:36
  82.7 1.0 %collective-permute-done.33.refs_3_ = f32[8,2048]{1,0:T(8,128)S(1)} collective-permute-done((f32[8,2048]{1,0:T(8,128)S(1)}, f32[8,2048]{1,0:T(8,128)S(1)}, u32[]{:S(2)}, u32[]{:S(2)}) %collective-permute-start.33) | collective-permute-done | bytes 65568 | tf_op jit(solution)/shard_map/ppermute | solution.py:36
  83.8 0.9 %scores.1 = (f32[16,256]{1,0:T(8,128)}, f32[4,8192]{1,0:T(4,128)}) custom-call(s32[1]{0:T(128)} %bitcast.me_ref, f32[8,1024]{1,0:T(8,128)S(1)} %add_add_fusion.2.held_ref, f32[8,1024]{1,0:T(8,128)S(1)} %collective-permute-done.30.got_ref, f32[16,1024]{1,0:T(8,128)S(1)} %get-tuple-element.46.direc_ref, f32[16,1024]{1,0:T(8,128)S(1)} %get-tuple-element.47.part_ref, ...), custom_call_target="tpu_custom_call" | custom-call | flops 1048576 | bytes 262144 | tf_op jit(solution)/shard_map/scores/pallas_call | solution.py:403
  (29 shorter events, 0.1 us)
Async XLA Ops:
  0.6 15.3 %collective-permute-start.4 = (bf16[256,128]{1,0:T(8,128)(2,1)}, bf16[256,128]{1,0:T(8,128)(2,1)S(1)}, u32[]{:S(2)}, u32[]{:S(2)}) collective-permute-start(bf16[256,128]{1,0:T(8,128)(2,1)} %a0.1), channel_id=1, source_target_pairs={{0,1},{1,0},{2,3},{3,2},{4,5},{5,4},{6,7},{7,6},{8,9},{9,8},{10,11... | collective-permute-start | bytes 196616 | tf_op jit(solution)/shard_map/ppermute | solution.py:36
  1.2 8.2 %collective-permute-start.5 = (bf16[256,128]{1,0:T(8,128)(2,1)}, bf16[256,128]{1,0:T(8,128)(2,1)S(1)}, u32[]{:S(2)}, u32[]{:S(2)}) collective-permute-start(bf16[256,128]{1,0:T(8,128)(2,1)} %a0.1), channel_id=1, source_target_pairs={{0,2},{1,3},{2,0},{3,1},{4,6},{5,7},{6,4},{7,5},{8,10},{9,11},{10,... | collective-permute-start | bytes 196616 | tf_op jit(solution)/shard_map/ppermute | solution.py:36
  3.7 1.6 %copy-start = (bf16[8192,128]{1,0:T(8,128)(2,1)S(1)}, bf16[8192,128]{1,0:T(8,128)(2,1)}, u32[]{:S(2)}) copy-start(bf16[8192,128]{1,0:T(8,128)(2,1)} %feat_ref.1) | copy-start | bytes 6291460
  5.3 0.7 copy-start.1
  6.0 0.7 copy-start.2
  7.8 3.7 %collective-permute-start = (bf16[32,128]{1,0:T(8,128)(2,1)S(1)}, bf16[32,128]{1,0:T(8,128)(2,1)S(1)}, u32[]{:S(2)}, u32[]{:S(2)}) collective-permute-start(bf16[32,128]{1,0:T(8,128)(2,1)S(1)} %get-tuple-element.29), channel_id=1, source_target_pairs={{0,4},{1,5},{2,6},{3,7},{4,0},{5,1},{6,2},{7,3},{8,12},{9,13},{10,... | collective-permute-start | bytes 24584 | tf_op jit(solution)/shard_map/ppermute | solution.py:36
  9.4 6.5 %collective-permute-start.6 = (bf16[256,128]{1,0:T(8,128)(2,1)S(1)}, bf16[256,128]{1,0:T(8,128)(2,1)S(1)}, u32[]{:S(2)}, u32[]{:S(2)}) collective-permute-start(bf16[256,128]{1,0:T(8,128)(2,1)S(1)} %collective-permute-done.5.a2), channel_id=1, source_target_pairs={{0,1},{1,0},{2,3},{3,2},{4,5},{5,4},{6,7},{7,6},{8,9},{9,8},{10,11... | collective-permute-start | bytes 196616 | tf_op jit(solution)/shard_map/ppermute | solution.py:36
  11.5 8.7 %collective-permute-start.3 = (bf16[64,128]{1,0:T(8,128)(2,1)S(1)}, bf16[64,128]{1,0:T(8,128)(2,1)S(1)}, u32[]{:S(2)}, u32[]{:S(2)}) collective-permute-start(bf16[64,128]{1,0:T(8,128)(2,1)S(1)} %constant_dynamic-update-slice_fusion.refs_0_), channel_id=1, source_target_pairs={{0,24},{1,25},{2,26},{3,27},{4,28},{5,29},{6,30},{7,31},{8,16},{9,... | collective-permute-start | bytes 49160 | tf_op jit(solution)/shard_map/ppermute | solution.py:36
  15.1 5.1 %collective-permute-start.2 = (bf16[64,128]{1,0:T(8,128)(2,1)S(1)}, bf16[64,128]{1,0:T(8,128)(2,1)S(1)}, u32[]{:S(2)}, u32[]{:S(2)}) collective-permute-start(bf16[64,128]{1,0:T(8,128)(2,1)S(1)} %constant_dynamic-update-slice_fusion.refs_0_), channel_id=1, source_target_pairs={{0,16},{1,17},{2,18},{3,19},{4,20},{5,21},{6,22},{7,23},{8,24},{9,... | collective-permute-start | bytes 49160 | tf_op jit(solution)/shard_map/ppermute | solution.py:36
  15.1 5.1 %collective-permute-start.1 = (bf16[64,128]{1,0:T(8,128)(2,1)S(1)}, bf16[64,128]{1,0:T(8,128)(2,1)S(1)}, u32[]{:S(2)}, u32[]{:S(2)}) collective-permute-start(bf16[64,128]{1,0:T(8,128)(2,1)S(1)} %constant_dynamic-update-slice_fusion.refs_0_), channel_id=1, source_target_pairs={{0,8},{1,9},{2,10},{3,11},{4,12},{5,13},{6,14},{7,15},{8,0},{9,1},... | collective-permute-start | bytes 49160 | tf_op jit(solution)/shard_map/ppermute | solution.py:36
  15.9 0.8 copy-start.3
  25.4 1.2 %collective-permute-start.7 = (f32[8,1152]{1,0:T(8,128)S(1)}, f32[8,1152]{1,0:T(8,128)S(1)}, u32[]{:S(2)}, u32[]{:S(2)}) collective-permute-start(f32[8,1152]{1,0:T(8,128)S(1)} %get-tuple-element.36), channel_id=1, source_target_pairs={{0,1},{1,0},{2,3},{3,2},{4,5},{5,4},{6,7},{7,6},{8,9},{9,8},{10,11... | collective-permute-start | bytes 110600 | tf_op jit(solution)/shard_map/ppermute | solution.py:36
  26.7 4.9 %collective-permute-start.10 = (f32[8,1152]{1,0:T(8,128)S(1)}, f32[8,1152]{1,0:T(8,128)S(1)}, u32[]{:S(2)}, u32[]{:S(2)}) collective-permute-start(f32[8,1152]{1,0:T(8,128)S(1)} %add.67), channel_id=1, source_target_pairs={{0,6},{1,7},{2,4},{3,5},{4,2},{5,3},{6,0},{7,1},{8,14},{9,15},{10,... | collective-permute-start | bytes 110600 | tf_op jit(solution)/shard_map/ppermute | solution.py:36
  28.1 4.0 %collective-permute-start.9 = (f32[8,1152]{1,0:T(8,128)S(1)}, f32[8,1152]{1,0:T(8,128)S(1)}, u32[]{:S(2)}, u32[]{:S(2)}) collective-permute-start(f32[8,1152]{1,0:T(8,128)S(1)} %add.67), channel_id=1, source_target_pairs={{0,4},{1,5},{2,6},{3,7},{4,0},{5,1},{6,2},{7,3},{8,12},{9,13},{10,... | collective-permute-start | bytes 110600 | tf_op jit(solution)/shard_map/ppermute | solution.py:36
  28.4 4.0 %collective-permute-start.8 = (f32[8,1152]{1,0:T(8,128)S(1)}, f32[8,1152]{1,0:T(8,128)S(1)}, u32[]{:S(2)}, u32[]{:S(2)}) collective-permute-start(f32[8,1152]{1,0:T(8,128)S(1)} %add.67), channel_id=1, source_target_pairs={{0,2},{1,3},{2,0},{3,1},{4,6},{5,7},{6,4},{7,5},{8,10},{9,11},{10,... | collective-permute-start | bytes 110600 | tf_op jit(solution)/shard_map/ppermute | solution.py:36
  32.4 5.8 %collective-permute-start.13 = (f32[8,1152]{1,0:T(8,128)S(1)}, f32[8,1152]{1,0:T(8,128)S(1)}, u32[]{:S(2)}, u32[]{:S(2)}) collective-permute-start(f32[8,1152]{1,0:T(8,128)S(1)} %add_add_fusion.1), channel_id=1, source_target_pairs={{0,24},{1,25},{2,26},{3,27},{4,28},{5,29},{6,30},{7,31},{8,16},{9,... | collective-permute-start | bytes 110600 | tf_op jit(solution)/shard_map/ppermute | solution.py:36
  36.3 4.9 %collective-permute-start.12 = (f32[8,1152]{1,0:T(8,128)S(1)}, f32[8,1152]{1,0:T(8,128)S(1)}, u32[]{:S(2)}, u32[]{:S(2)}) collective-permute-start(f32[8,1152]{1,0:T(8,128)S(1)} %add_add_fusion.1), channel_id=1, source_target_pairs={{0,16},{1,17},{2,18},{3,19},{4,20},{5,21},{6,22},{7,23},{8,24},{9,... | collective-permute-start | bytes 110600 | tf_op jit(solution)/shard_map/ppermute | solution.py:36
  36.3 4.9 %collective-permute-start.11 = (f32[8,1152]{1,0:T(8,128)S(1)}, f32[8,1152]{1,0:T(8,128)S(1)}, u32[]{:S(2)}, u32[]{:S(2)}) collective-permute-start(f32[8,1152]{1,0:T(8,128)S(1)} %add_add_fusion.1), channel_id=1, source_target_pairs={{0,8},{1,9},{2,10},{3,11},{4,12},{5,13},{6,14},{7,15},{8,0},{9,1},... | collective-permute-start | bytes 110600 | tf_op jit(solution)/shard_map/ppermute | solution.py:36
  41.2 1.3 %collective-permute-start.14 = (f32[8,1152]{1,0:T(8,128)S(1)}, f32[8,1152]{1,0:T(8,128)S(1)}, u32[]{:S(2)}, u32[]{:S(2)}) collective-permute-start(f32[8,1152]{1,0:T(8,128)S(1)} %add_add_fusion.held_ref), channel_id=1, source_target_pairs={{0,1},{1,0},{2,3},{3,2},{4,5},{5,4},{6,7},{7,6},{8,9},{9,8},{10,11... | collective-permute-start | bytes 110600 | tf_op jit(solution)/shard_map/ppermute | solution.py:36
  46.4 1.2 %collective-permute-start.15 = (f32[8,1024]{1,0:T(8,128)S(1)}, f32[8,1024]{1,0:T(8,128)S(1)}, u32[]{:S(2)}, u32[]{:S(2)}) collective-permute-start(f32[8,1024]{1,0:T(8,128)S(1)} %get-tuple-element.41), channel_id=1, source_target_pairs={{0,1},{1,0},{2,3},{3,2},{4,5},{5,4},{6,7},{7,6},{8,9},{9,8},{10,11... | collective-permute-start | bytes 98312 | tf_op jit(solution)/shard_map/ppermute | solution.py:36
  47.7 4.8 %collective-permute-start.18 = (f32[8,1024]{1,0:T(8,128)S(1)}, f32[8,1024]{1,0:T(8,128)S(1)}, u32[]{:S(2)}, u32[]{:S(2)}) collective-permute-start(f32[8,1024]{1,0:T(8,128)S(1)} %add.74), channel_id=1, source_target_pairs={{0,6},{1,7},{2,4},{3,5},{4,2},{5,3},{6,0},{7,1},{8,14},{9,15},{10,... | collective-permute-start | bytes 98312 | tf_op jit(solution)/shard_map/ppermute | solution.py:36
  50.1 3.9 %collective-permute-start.17 = (f32[8,1024]{1,0:T(8,128)S(1)}, f32[8,1024]{1,0:T(8,128)S(1)}, u32[]{:S(2)}, u32[]{:S(2)}) collective-permute-start(f32[8,1024]{1,0:T(8,128)S(1)} %add.74), channel_id=1, source_target_pairs={{0,4},{1,5},{2,6},{3,7},{4,0},{5,1},{6,2},{7,3},{8,12},{9,13},{10,... | collective-permute-start | bytes 98312 | tf_op jit(solution)/shard_map/ppermute | solution.py:36
  50.6 3.9 %collective-permute-start.16 = (f32[8,1024]{1,0:T(8,128)S(1)}, f32[8,1024]{1,0:T(8,128)S(1)}, u32[]{:S(2)}, u32[]{:S(2)}) collective-permute-start(f32[8,1024]{1,0:T(8,128)S(1)} %add.74), channel_id=1, source_target_pairs={{0,2},{1,3},{2,0},{3,1},{4,6},{5,7},{6,4},{7,5},{8,10},{9,11},{10,... | collective-permute-start | bytes 98312 | tf_op jit(solution)/shard_map/ppermute | solution.py:36
  54.5 5.8 %collective-permute-start.21 = (f32[8,1024]{1,0:T(8,128)S(1)}, f32[8,1024]{1,0:T(8,128)S(1)}, u32[]{:S(2)}, u32[]{:S(2)}) collective-permute-start(f32[8,1024]{1,0:T(8,128)S(1)} %add_add_fusion.5), channel_id=1, source_target_pairs={{0,24},{1,25},{2,26},{3,27},{4,28},{5,29},{6,30},{7,31},{8,16},{9,... | collective-permute-start | bytes 98312 | tf_op jit(solution)/shard_map/ppermute | solution.py:36
  56.1 4.8 %collective-permute-start.20 = (f32[8,1024]{1,0:T(8,128)S(1)}, f32[8,1024]{1,0:T(8,128)S(1)}, u32[]{:S(2)}, u32[]{:S(2)}) collective-permute-start(f32[8,1024]{1,0:T(8,128)S(1)} %add_add_fusion.5), channel_id=1, source_target_pairs={{0,16},{1,17},{2,18},{3,19},{4,20},{5,21},{6,22},{7,23},{8,24},{9,... | collective-permute-start | bytes 98312 | tf_op jit(solution)/shard_map/ppermute | solution.py:36
  56.7 4.5 %collective-permute-start.19 = (f32[8,1024]{1,0:T(8,128)S(1)}, f32[8,1024]{1,0:T(8,128)S(1)}, u32[]{:S(2)}, u32[]{:S(2)}) collective-permute-start(f32[8,1024]{1,0:T(8,128)S(1)} %add_add_fusion.5), channel_id=1, source_target_pairs={{0,8},{1,9},{2,10},{3,11},{4,12},{5,13},{6,14},{7,15},{8,0},{9,1},... | collective-permute-start | bytes 98312 | tf_op jit(solution)/shard_map/ppermute | solution.py:36
  61.2 1.3 %collective-permute-start.22 = (f32[8,1024]{1,0:T(8,128)S(1)}, f32[8,1024]{1,0:T(8,128)S(1)}, u32[]{:S(2)}, u32[]{:S(2)}) collective-permute-start(f32[8,1024]{1,0:T(8,128)S(1)} %add_add_fusion.4.held_ref), channel_id=1, source_target_pairs={{0,1},{1,0},{2,3},{3,2},{4,5},{5,4},{6,7},{7,6},{8,9},{9,8},{10,11... | collective-permute-start | bytes 98312 | tf_op jit(solution)/shard_map/ppermute | solution.py:36
  66.6 1.2 %collective-permute-start.23 = (f32[8,1024]{1,0:T(8,128)S(1)}, f32[8,1024]{1,0:T(8,128)S(1)}, u32[]{:S(2)}, u32[]{:S(2)}) collective-permute-start(f32[8,1024]{1,0:T(8,128)S(1)} %get-tuple-element.45), channel_id=1, source_target_pairs={{0,1},{1,0},{2,3},{3,2},{4,5},{5,4},{6,7},{7,6},{8,9},{9,8},{10,11... | collective-permute-start | bytes 98312 | tf_op jit(solution)/shard_map/ppermute | solution.py:36
  67.8 4.8 %collective-permute-start.26 = (f32[8,1024]{1,0:T(8,128)S(1)}, f32[8,1024]{1,0:T(8,128)S(1)}, u32[]{:S(2)}, u32[]{:S(2)}) collective-permute-start(f32[8,1024]{1,0:T(8,128)S(1)} %add.81), channel_id=1, source_target_pairs={{0,6},{1,7},{2,4},{3,5},{4,2},{5,3},{6,0},{7,1},{8,14},{9,15},{10,... | collective-permute-start | bytes 98312 | tf_op jit(solution)/shard_map/ppermute | solution.py:36
  69.3 3.9 %collective-permute-start.25 = (f32[8,1024]{1,0:T(8,128)S(1)}, f32[8,1024]{1,0:T(8,128)S(1)}, u32[]{:S(2)}, u32[]{:S(2)}) collective-permute-start(f32[8,1024]{1,0:T(8,128)S(1)} %add.81), channel_id=1, source_target_pairs={{0,4},{1,5},{2,6},{3,7},{4,0},{5,1},{6,2},{7,3},{8,12},{9,13},{10,... | collective-permute-start | bytes 98312 | tf_op jit(solution)/shard_map/ppermute | solution.py:36
  69.8 3.9 %collective-permute-start.24 = (f32[8,1024]{1,0:T(8,128)S(1)}, f32[8,1024]{1,0:T(8,128)S(1)}, u32[]{:S(2)}, u32[]{:S(2)}) collective-permute-start(f32[8,1024]{1,0:T(8,128)S(1)} %add.81), channel_id=1, source_target_pairs={{0,2},{1,3},{2,0},{3,1},{4,6},{5,7},{6,4},{7,5},{8,10},{9,11},{10,... | collective-permute-start | bytes 98312 | tf_op jit(solution)/shard_map/ppermute | solution.py:36
  73.8 5.9 %collective-permute-start.29 = (f32[8,1024]{1,0:T(8,128)S(1)}, f32[8,1024]{1,0:T(8,128)S(1)}, u32[]{:S(2)}, u32[]{:S(2)}) collective-permute-start(f32[8,1024]{1,0:T(8,128)S(1)} %add_add_fusion.3), channel_id=1, source_target_pairs={{0,24},{1,25},{2,26},{3,27},{4,28},{5,29},{6,30},{7,31},{8,16},{9,... | collective-permute-start | bytes 98312 | tf_op jit(solution)/shard_map/ppermute | solution.py:36
  76.2 4.9 %collective-permute-start.28 = (f32[8,1024]{1,0:T(8,128)S(1)}, f32[8,1024]{1,0:T(8,128)S(1)}, u32[]{:S(2)}, u32[]{:S(2)}) collective-permute-start(f32[8,1024]{1,0:T(8,128)S(1)} %add_add_fusion.3), channel_id=1, source_target_pairs={{0,16},{1,17},{2,18},{3,19},{4,20},{5,21},{6,22},{7,23},{8,24},{9,... | collective-permute-start | bytes 98312 | tf_op jit(solution)/shard_map/ppermute | solution.py:36
  77.0 4.3 %collective-permute-start.27 = (f32[8,1024]{1,0:T(8,128)S(1)}, f32[8,1024]{1,0:T(8,128)S(1)}, u32[]{:S(2)}, u32[]{:S(2)}) collective-permute-start(f32[8,1024]{1,0:T(8,128)S(1)} %add_add_fusion.3), channel_id=1, source_target_pairs={{0,8},{1,9},{2,10},{3,11},{4,12},{5,13},{6,14},{7,15},{8,0},{9,1},... | collective-permute-start | bytes 98312 | tf_op jit(solution)/shard_map/ppermute | solution.py:36
  78.2 3.2 %collective-permute-start.31 = (f32[8,2048]{1,0:T(8,128)S(1)}, f32[8,2048]{1,0:T(8,128)S(1)}, u32[]{:S(2)}, u32[]{:S(2)}) collective-permute-start(f32[8,2048]{1,0:T(8,128)S(1)} %get-tuple-element.51), channel_id=1, source_target_pairs={{0,1},{1,0},{2,3},{3,2},{4,5},{5,4},{6,7},{7,6},{8,9},{9,8},{10,11... | collective-permute-start | bytes 196616 | tf_op jit(solution)/shard_map/ppermute | solution.py:36
  78.2 4.5 %collective-permute-start.32 = (f32[8,2048]{1,0:T(8,128)S(1)}, f32[8,2048]{1,0:T(8,128)S(1)}, u32[]{:S(2)}, u32[]{:S(2)}) collective-permute-start(f32[8,2048]{1,0:T(8,128)S(1)} %get-tuple-element.52), channel_id=1, source_target_pairs={{0,2},{1,3},{2,0},{3,1},{4,6},{5,7},{6,4},{7,5},{8,10},{9,11},{10,... | collective-permute-start | bytes 196616 | tf_op jit(solution)/shard_map/ppermute | solution.py:36
  79.7 4.0 %collective-permute-start.33 = (f32[8,2048]{1,0:T(8,128)S(1)}, f32[8,2048]{1,0:T(8,128)S(1)}, u32[]{:S(2)}, u32[]{:S(2)}) collective-permute-start(f32[8,2048]{1,0:T(8,128)S(1)} %get-tuple-element.53), channel_id=1, source_target_pairs={{0,3},{1,2},{2,1},{3,0},{4,7},{5,6},{6,5},{7,4},{8,11},{9,10},{10,... | collective-permute-start | bytes 196616 | tf_op jit(solution)/shard_map/ppermute | solution.py:36
  81.3 2.5 %collective-permute-start.30 = (f32[8,1024]{1,0:T(8,128)S(1)}, f32[8,1024]{1,0:T(8,128)S(1)}, u32[]{:S(2)}, u32[]{:S(2)}) collective-permute-start(f32[8,1024]{1,0:T(8,128)S(1)} %add_add_fusion.2.held_ref), channel_id=1, source_target_pairs={{0,1},{1,0},{2,3},{3,2},{4,5},{5,4},{6,7},{7,6},{8,9},{9,8},{10,11... | collective-permute-start | bytes 98312 | tf_op jit(solution)/shard_map/ppermute | solution.py:36

commit v3 on v2

--- a/solution.py
+++ b/solution.py
@@ -6,6 +6,7 @@
 from jax.experimental import pallas as pl
 from jax.experimental.pallas import tpu as pltpu
 from jax.sharding import PartitionSpec as P
+
 
 CLASSES = 16
 HALF = CLASSES // 2
@@ -86,7 +87,7 @@
     return 1.0 / (fourth * fourth)
 
 
-def label_kernel(na, me_ref, idx_ref, cls_ref, feat_ref, out_ref, x_ref, rows, picked, sems, xsem):
+def label_kernel(na, me_ref, idx_ref, cls_ref, feat_ref, anch_ref, out_ref, x_ref, a_ref, rows, picked, sems, xsem, asem):
     docs_dev = feat_ref.shape[0]
     docs = x_ref.shape[0]
     base = (me_ref[0] // na) * docs_dev
@@ -100,6 +101,8 @@
     own = pl.ds(pl.multiple_of((me_ref[0] % na) * docs, docs), docs)
     bulk = pltpu.make_async_copy(feat_ref.at[own, :], x_ref, xsem)
     bulk.start()
+    points = pltpu.make_async_copy(anch_ref, a_ref, asem)
+    points.start()
     sub = lax.broadcasted_iota(jnp.int32, (16, LANES), 0)
     lane = lax.broadcasted_iota(jnp.int32, (1, LANES), 1)
     for k in range(count):
@@ -110,30 +113,53 @@
         picked[k : k + 1, :] = jnp.sum(chosen, axis=0, keepdims=True)
     out_ref[...] = picked[...].astype(bf16)
     bulk.wait()
-
-
-def build_kernel(na, me_ref, a0, a1, a2, a3, x_ref, khi_ref, klo_ref, tinv_ref, aug_ref):
+    points.wait()
+
+
+def build_rows(at_rows, value, x_ref, khi_ref, klo_ref, aug_ref, sums):
     docs, feat = x_ref.shape
-    quarter = a0.shape[0]
     scale = 1.0 / (feat * width_h)
-    me = me_ref[0] % na
-    for mask, piece in enumerate((a0, a1, a2, a3)):
-        at = pl.ds(pl.multiple_of((me ^ mask) * quarter, quarter), quarter)
-        value = piece[...].astype(f32)
-        aug_ref[at, 0:feat] = (value * (-2.0 * scale)).astype(bf16)
-        aug_ref[at, feat:] = aug_columns(row_sizes(value) * scale + 1.0, None, quarter)
     tile = min(256, docs)
-    for col in range(0, docs, tile):
+    lefts = []
+    for at, piece in zip(at_rows, value):
+        wide = piece[...].astype(f32)
+        left = jnp.concatenate(
+            [(wide * (-2.0 * scale)).astype(bf16), aug_columns(row_sizes(wide) * scale + 1.0, None, wide.shape[0])], axis=1
+        )
+        aug_ref[at, :] = left
+        lefts.append(left)
+    for k, col in enumerate(range(0, docs, tile)):
         raw = x_ref[col : col + tile, :]
         right = jnp.concatenate([raw, aug_columns(None, row_sizes(raw.astype(f32)) * scale, tile)], axis=1)
-        total = jnp.zeros((8, tile), f32)
-        for at in range(0, aug_ref.shape[0], 256):
-            kern = eighth(mm(aug_ref[at : at + 256, :], right, NT))
+        for at, left in zip(at_rows, lefts):
+            kern = eighth(mm(left, right, NT))
             high, low = split2(kern)
-            khi_ref[at : at + 256, col : col + tile] = high
-            klo_ref[at : at + 256, col : col + tile] = low
-            total = total + jnp.sum(kern.reshape(32, 8, tile), axis=0)
-        tinv_ref[:, col : col + tile] = 1.0 / jnp.sum(total, axis=0, keepdims=True)
+            khi_ref[at, col : col + tile] = high
+            klo_ref[at, col : col + tile] = low
+            part = jnp.sum(kern.reshape(-1, 8, tile), axis=0)
+            sums[k] = part if sums[k] is None else sums[k] + part
+    return sums
+
+
+def rows_of(me_ref, na, quarter, masks):
+    mine = me_ref[0] % na
+    return [pl.ds(pl.multiple_of((mine ^ mask) * quarter, quarter), quarter) for mask in masks]
+
+
+def build_near(na, me_ref, a0, a1, x_ref, khi_ref, klo_ref, aug_ref, sum_ref):
+    tile = min(256, x_ref.shape[0])
+    sums = [None] * (x_ref.shape[0] // tile)
+    build_rows(rows_of(me_ref, na, a0.shape[0], (0, 1)), (a0, a1), x_ref, khi_ref, klo_ref, aug_ref, sums)
+    for k, part in enumerate(sums):
+        sum_ref[:, k * tile : (k + 1) * tile] = part
+
+
+def build_far(na, me_ref, a2, a3, x_ref, sum_ref, kh0, kl0, aug0, khi_ref, klo_ref, aug_ref, tinv_ref):
+    tile = min(256, x_ref.shape[0])
+    sums = [sum_ref[:, k * tile : (k + 1) * tile] for k in range(x_ref.shape[0] // tile)]
+    build_rows(rows_of(me_ref, na, a2.shape[0], (2, 3)), (a2, a3), x_ref, khi_ref, klo_ref, aug_ref, sums)
+    for k, part in enumerate(sums):
+        tinv_ref[:, k * tile : (k + 1) * tile] = 1.0 / jnp.sum(part, axis=0, keepdims=True)
 
 
 def times(vec, khi, klo):
@@ -289,20 +315,24 @@
 SMEM = pl.BlockSpec(memory_space=pltpu.MemorySpace.SMEM)
 
 
-def call(kernel, in_specs, out_shape, scratch, name, flops=1 << 20, moved=1 << 18):
+def in_hbm(value):
+    return pltpu.with_memory_space_constraint(value, pltpu.MemorySpace.HBM)
+
+
+def call(kernel, in_specs, out_shape, scratch, flops=1 << 20, moved=1 << 18, aliases={}):
     return pl.pallas_call(
         kernel,
         in_specs=in_specs,
         out_specs=[VMEM] * len(out_shape),
         out_shape=out_shape,
         scratch_shapes=scratch,
-        name=name,
+        input_output_aliases=aliases,
         compiler_params=pltpu.CompilerParams(vmem_limit_bytes=24 << 20),
         cost_estimate=pl.CostEstimate(flops=flops, bytes_accessed=moved, transcendentals=0),
     )
 
 
-def per_device(features, anchors, lab_index, lab_class):
+def run(features, anchors, lab_index, lab_class):
     docs_dev, feat = features.shape
     nd, na = lax.axis_size("docs"), lax.axis_size("anch")
     n_bits = (nd * na).bit_length() - 1
@@ -319,20 +349,27 @@
 
     me = lax.axis_index(EVERY).astype(jnp.int32).reshape(1)
 
-    own, mine_x = call(
+    own, mine_x, near = pl.pallas_call(
         functools.partial(label_kernel, na),
-        [SMEM, SMEM, SMEM, pl.BlockSpec(memory_space=pl.ANY)],
-        [sds((2 * labs, feat), bf16), sds((docs, feat), bf16)],
-        [
-            pltpu.VMEM((labs, 16, LANES), bf16),
-            pltpu.VMEM((2 * labs, LANES), f32),
-            pltpu.SemaphoreType.DMA((labs,)),
-            pltpu.SemaphoreType.DMA,
-        ],
-        "label_rows",
-    )(me, lab_index, lab_class, features)
-
-    piece = [anchors, swap(anchors, 1), swap(anchors, 2), None]
+        grid_spec=pltpu.PrefetchScalarGridSpec(
+            num_scalar_prefetch=3,
+            grid=(1,),
+            in_specs=[pl.BlockSpec(memory_space=pltpu.MemorySpace.HBM)] * 2,
+            out_specs=[VMEM] * 3,
+            scratch_shapes=[
+                pltpu.VMEM((labs, 16, LANES), bf16),
+                pltpu.VMEM((2 * labs, LANES), f32),
+                pltpu.SemaphoreType.DMA((labs,)),
+                pltpu.SemaphoreType.DMA,
+                pltpu.SemaphoreType.DMA,
+            ],
+        ),
+        out_shape=[sds((2 * labs, feat), bf16), sds((docs, feat), bf16), sds((quarter, feat), bf16)],
+        name="label_rows",
+        compiler_params=pltpu.CompilerParams(vmem_limit_bytes=4 << 20),
+    )(me, in_hbm(lab_index), in_hbm(lab_class), in_hbm(features), in_hbm(anchors))
+
+    piece = [near, swap(anchors, 1), swap(anchors, 2), None]
     piece[3] = swap(piece[2], 1)
 
     held, masks = own, [0]
@@ -347,15 +384,19 @@
     slots = [[m >> a_bits for m in masks]] + [[(m ^ mask) >> a_bits for m in masks] for mask in stages[-1]]
 
     k_sds = sds((total, docs), bf16)
-    khi, klo, tinv, aug = call(
-        functools.partial(build_kernel, na),
-        [SMEM] + [VMEM] * 5,
-        [k_sds, k_sds, sds((1, docs), f32), sds((total, feat + LANES), bf16)],
+    a_sds = sds((total, feat + LANES), bf16)
+    build = dict(flops=total * docs * 256, moved=2 * total * docs)
+    khi, klo, aug, sums = call(
+        functools.partial(build_near, na), [SMEM] + [VMEM] * 3, [k_sds, k_sds, a_sds, sds((8, docs), f32)], [], **build
+    )(me, piece[0], piece[1], mine_x)
+    khi, klo, aug, tinv = call(
+        functools.partial(build_far, na),
+        [SMEM] + [VMEM] * 7,
+        [k_sds, k_sds, a_sds, sds((1, docs), f32)],
         [],
-        "kernel_matrix",
-        flops=2 * total * docs * 256,
-        moved=4 * total * docs,
-    )(me, *piece, mine_x)
+        aliases={5: 0, 6: 1, 7: 2},
+        **build,
+    )(me, piece[2], piece[3], mine_x, sums, khi, klo, aug)
 
     long = total + LANES
     flat_sds = sds((CLASSES, total), f32)
@@ -373,7 +414,6 @@
             pltpu.VMEM((labeled, LANES), f32),
             pltpu.VMEM((CLASSES, long), f32),
         ],
-        "first_gram",
         **work,
     )(me, *lab_arrays, aug, khi, klo, tinv)
 
@@ -383,7 +423,6 @@
         [SMEM] + [VMEM] * 8,
         [half_sds, half_sds, sds((1, total), f32), flat_sds],
         [pltpu.VMEM((CLASSES, long), f32), acc],
-        "second_gram",
         **work,
     )(me, held, got, rhs, zhi, zlo, khi, klo, tinv)
 
@@ -394,7 +433,6 @@
         [SMEM] + [VMEM] * 10,
         [half_sds, half_sds, flat_sds, flat_sds, sds((16, LANES), f32)] + [sds((part_rows, docs), f32)] * na,
         [acc, pltpu.VMEM((na, part_rows, docs), f32)],
-        "third_gram",
         **work,
     )(me, held, got, rhs, lab, spread, zhi, zlo, khi, klo, tinv)
 
@@ -405,7 +443,6 @@
         [SMEM] + [VMEM] * (6 + na),
         [sds((CLASSES, quarter), f32), sds((CLASSES // na, docs_dev), f32)],
         [acc],
-        "scores",
     )(me, held, got, direc, part, stats, dinv, *parts)
     return anchor_scores.T, doc_scores
 
@@ -413,4 +450,4 @@
 def solution(mesh):
     in_specs = (P("docs", None), P("anch", None), P("docs"), P("docs"))
     out_specs = (P("anch", None), P("anch", "docs"))
-    return jax.shard_map(per_device, mesh=mesh, in_specs=in_specs, out_specs=out_specs, check_vma=False)
+    return jax.shard_map(run, mesh=mesh, in_specs=in_specs, out_specs=out_specs, check_vma=False)

time: 84.9 us -> 87.7 us (1.033)
  waiting for transfers between devices: 25.8 us -> 30.5 us
  local copies, waits for them, and re-layouts: 3.75 us -> 0.01 us
  Pallas kernels: 18.7 us -> 20.8 us
    ppermute x34, waiting for transfers between devices: 25.8 us -> 30.5 us  [swap(): return lax.ppermute(value, EVERY, [(i, i ^ mask) for i in range(count)])]
    unnamed x9 -> x1, local copies, waits for them, and re-layouts: 3.74 us -> 0.01 us
    pallas_call x6 -> x7, Pallas kernels: 18.7 us -> 20.8 us  [the longest x1 5.16 us: run(): call(functools.partial(first_kernel, na, labs, slots, CLASSES * lab_scale...]
  transfers between devices with their start and end apart: 34 -> 34, of which waited for: 24 -> 24; matrix products, arithmetic and copies ran while one was open for 0% -> 0% of each run, Pallas kernels for 5% -> 7%
where the time goes in v3:
time: 87.7 us; the launch traced here: 87.5 us
  starting transfers between devices  35.4 us (40%)
  waiting for transfers between devices  30.5 us (35%)
  Pallas kernels  20.8 us (24%)
    ppermute x34, starting transfers between devices, swap(): return lax.ppermute(value, EVERY, [(i, i ^ mask) for i in range(count)])  35.4 us
    ppermute x34, waiting for transfers between devices, swap(): return lax.ppermute(value, EVERY, [(i, i ^ mask) for i in range(count)])  30.5 us
    pallas_call x1, Pallas kernels, run(): call(functools.partial(first_kernel, na, labs, slots, CLASSES * lab_scale...  5.16 us
    pallas_call x1, Pallas kernels, run(): call(functools.partial(third_kernel, na, lab_scale, graph_scale), [SMEM]...  4.25 us
    pallas_call x1, Pallas kernels, run(): call(second_kernel, [SMEM] + [VMEM] * 8, [half_sds, half_sds, sds((1, tot...  3.98 us
    pallas_call x1, Pallas kernels, run(): call(functools.partial(build_far, na), [SMEM] + [VMEM] * 7, [k_sds, k_sds...  2.25 us
    pallas_call x1, Pallas kernels, run(): call(functools.partial(build_near, na), [SMEM] + [VMEM] * 3, [k_sds, k_sd...  2.22 us
    pallas_call x1, Pallas kernels, run(): pl.pallas_call(functools.partial(label_kernel, na), grid_spec=pltpu.Prefe...  2.06 us
  transfers between devices with their start and end apart: 34, of which 24 were waited for; matrix products, arithmetic and copies ran while one was open for 0% of the time, Pallas kernels for 7%

profile of v3, /device:TPU:0, one launch (start us, length us, event | category | flops | bytes accessed | tf_op | source)
XLA Modules:
  0.0 87.5 jit_solution(5408005353987665781)
XLA Ops:
  0.6 0.6 collective-permute-start.6
  1.2 2.6 %collective-permute-start.4 = (bf16[256,128]{1,0:T(8,128)(2,1)}, bf16[256,128]{1,0:T(8,128)(2,1)S(1)}, u32[]{:S(2)}, u32[]{:S(2)}) collective-permute-start(bf16[256,128]{1,0:T(8,128)(2,1)} %anch_ref.1), channel_id=1, source_target_pairs={{0,2},{1,3},{2,0},{3,1},{4,6},{5,7},{6,4},{7,5},{8,10},{9,11},{10,... | collective-permute-start | bytes 196616 | tf_op jit(solution)/shard_map/ppermute | solution.py:37
  3.7 2.1 %label_rows.1 = (bf16[32,128]{1,0:T(8,128)(2,1)S(1)}, bf16[2048,128]{1,0:T(8,128)(2,1)S(1)}, bf16[256,128]{1,0:T(8,128)(2,1)S(1)}) custom-call(s32[1]{0:T(128)} %bitcast.me_ref, s32[16]{0:T(128)} %idx_ref.1, s32[16]{0:T(128)} %cls_ref.1, bf16[8192,128]{1,0:T(8,128)(2,1)} %feat_ref.1, bf16[256,128]{1,0:T(8,128)(2,1)} %anch_ref.1), custom_call_target="tpu_custom_call" | custom-call | tf_op jit(solution)/shard_map/label_rows/pallas_call | solution.py:352
  5.8 1.6 %collective-permute-start = (bf16[32,128]{1,0:T(8,128)(2,1)S(1)}, bf16[32,128]{1,0:T(8,128)(2,1)S(1)}, u32[]{:S(2)}, u32[]{:S(2)}) collective-permute-start(bf16[32,128]{1,0:T(8,128)(2,1)S(1)} %get-tuple-element.34), channel_id=1, source_target_pairs={{0,4},{1,5},{2,6},{3,7},{4,0},{5,1},{6,2},{7,3},{8,12},{9,13},{10,... | collective-permute-start | bytes 24584 | tf_op jit(solution)/shard_map/ppermute | solution.py:37
  7.4 0.0 collective-permute-done.4.a2
  7.4 2.1 %collective-permute-done = bf16[32,128]{1,0:T(8,128)(2,1)S(1)} collective-permute-done((bf16[32,128]{1,0:T(8,128)(2,1)S(1)}, bf16[32,128]{1,0:T(8,128)(2,1)S(1)}, u32[]{:S(2)}, u32[]{:S(2)}) %collective-permute-start) | collective-permute-done | bytes 8224 | tf_op jit(solution)/shard_map/ppermute | solution.py:37
  9.5 1.6 %collective-permute-start.1 = (bf16[64,128]{1,0:T(8,128)(2,1)S(1)}, bf16[64,128]{1,0:T(8,128)(2,1)S(1)}, u32[]{:S(2)}, u32[]{:S(2)}) collective-permute-start(bf16[64,128]{1,0:T(8,128)(2,1)S(1)} %constant_dynamic-update-slice_fusion.refs_0_), channel_id=1, source_target_pairs={{0,8},{1,9},{2,10},{3,11},{4,12},{5,13},{6,14},{7,15},{8,0},{9,1},... | collective-permute-start | bytes 49160 | tf_op jit(solution)/shard_map/ppermute | solution.py:37
  11.1 2.6 %collective-permute-start.2 = (bf16[64,128]{1,0:T(8,128)(2,1)S(1)}, bf16[64,128]{1,0:T(8,128)(2,1)S(1)}, u32[]{:S(2)}, u32[]{:S(2)}) collective-permute-start(bf16[64,128]{1,0:T(8,128)(2,1)S(1)} %constant_dynamic-update-slice_fusion.refs_0_), channel_id=1, source_target_pairs={{0,16},{1,17},{2,18},{3,19},{4,20},{5,21},{6,22},{7,23},{8,24},{9,... | collective-permute-start | bytes 49160 | tf_op jit(solution)/shard_map/ppermute | solution.py:37
  13.7 0.2 collective-permute-start.3
  13.9 2.2 %shard_map.59 = (bf16[1024,2048]{1,0:T(8,128)(2,1)S(1)}, bf16[1024,2048]{1,0:T(8,128)(2,1)S(1)}, bf16[1024,256]{1,0:T(8,128)(2,1)S(1)}, f32[8,2048]{1,0:T(8,128)S(1)}) custom-call(s32[1]{0:T(128)} %bitcast.me_ref, bf16[256,128]{1,0:T(8,128)(2,1)S(1)} %get-tuple-element.36.a0, bf16[256,128]{1,0:T(8,128)(2,1)S(1)} %collective-permute-done.6.a1, ...), custom_call_target="tpu_custom_call" | custom-call | flops 536870912 | bytes 4194304 | tf_op jit(solution)/shard_map/pallas_call | solution.py:389
  16.2 2.2 %shard_map.60 = (bf16[1024,2048]{1,0:T(8,128)(2,1)S(1)}, bf16[1024,2048]{1,0:T(8,128)(2,1)S(1)}, bf16[1024,256]{1,0:T(8,128)(2,1)S(1)}, f32[1,2048]{1,0:T(1,128)S(1)}) custom-call(s32[1]{0:T(128)} %bitcast.me_ref, bf16[256,128]{1,0:T(8,128)(2,1)S(1)} %collective-permute-done.4.a2, ...), custom_call_target="tpu_custom_call", output_to_operand_aliasing={{0}: (5, {}), {1}: (6, {}), {2}: (7, {})} | custom-call | flops 536870912 | bytes 4194304 | tf_op jit(solution)/shard_map/pallas_call | solution.py:392
  18.4 0.8 collective-permute-done.3.refs_3_
  19.2 5.2 %shard_map.61 = (f32[8,1152]{1,0:T(8,128)S(1)}, f32[8,1152]{1,0:T(8,128)S(1)}, f32[16,1024]{1,0:T(8,128)S(1)}, bf16[1024,128]{1,0:T(8,128)(2,1)S(1)}, bf16[1024,...) custom-call(s32[1]{0:T(128)} %bitcast.me_ref, bf16[64,128]{1,0:T(8,128)(2,1)S(1)} %constant_dynamic-update-slice_fusion.refs_0_, ...), custom_call_target="tpu_custom_call" | custom-call | flops 1073741824 | bytes 8388608 | tf_op jit(solution)/shard_map/pallas_call | solution.py:408
  24.4 0.0 collective-permute-start.7
  24.4 1.2 %collective-permute-done.7 = f32[8,1152]{1,0:T(8,128)S(1)} collective-permute-done((f32[8,1152]{1,0:T(8,128)S(1)}, f32[8,1152]{1,0:T(8,128)S(1)}, u32[]{:S(2)}, u32[]{:S(2)}) %collective-permute-start.7) | collective-permute-done | bytes 36896 | tf_op jit(solution)/shard_map/ppermute | solution.py:37
  25.6 1.5 %collective-permute-start.10 = (f32[8,1152]{1,0:T(8,128)S(1)}, f32[8,1152]{1,0:T(8,128)S(1)}, u32[]{:S(2)}, u32[]{:S(2)}) collective-permute-start(f32[8,1152]{1,0:T(8,128)S(1)} %add.67), channel_id=1, source_target_pairs={{0,6},{1,7},{2,4},{3,5},{4,2},{5,3},{6,0},{7,1},{8,14},{9,15},{10,... | collective-permute-start | bytes 110600 | tf_op jit(solution)/shard_map/ppermute | solution.py:37
  27.1 1.5 %collective-permute-start.8 = (f32[8,1152]{1,0:T(8,128)S(1)}, f32[8,1152]{1,0:T(8,128)S(1)}, u32[]{:S(2)}, u32[]{:S(2)}) collective-permute-start(f32[8,1152]{1,0:T(8,128)S(1)} %add.67), channel_id=1, source_target_pairs={{0,2},{1,3},{2,0},{3,1},{4,6},{5,7},{6,4},{7,5},{8,10},{9,11},{10,... | collective-permute-start | bytes 110600 | tf_op jit(solution)/shard_map/ppermute | solution.py:37
  28.6 0.5 collective-permute-start.9
  29.1 1.4 %collective-permute-done.10 = f32[8,1152]{1,0:T(8,128)S(1)} collective-permute-done((f32[8,1152]{1,0:T(8,128)S(1)}, f32[8,1152]{1,0:T(8,128)S(1)}, u32[]{:S(2)}, u32[]{:S(2)}) %collective-permute-start.10) | collective-permute-done | bytes 36896 | tf_op jit(solution)/shard_map/ppermute | solution.py:37
  30.5 0.6 collective-permute-done.8
  31.1 1.5 %collective-permute-done.9 = f32[8,1152]{1,0:T(8,128)S(1)} collective-permute-done((f32[8,1152]{1,0:T(8,128)S(1)}, f32[8,1152]{1,0:T(8,128)S(1)}, u32[]{:S(2)}, u32[]{:S(2)}) %collective-permute-start.9) | collective-permute-done | bytes 36896 | tf_op jit(solution)/shard_map/ppermute | solution.py:37
  32.6 0.1 collective-permute-start.11
  32.7 3.4 %collective-permute-start.12 = (f32[8,1152]{1,0:T(8,128)S(1)}, f32[8,1152]{1,0:T(8,128)S(1)}, u32[]{:S(2)}, u32[]{:S(2)}) collective-permute-start(f32[8,1152]{1,0:T(8,128)S(1)} %add_add_fusion.1), channel_id=1, source_target_pairs={{0,16},{1,17},{2,18},{3,19},{4,20},{5,21},{6,22},{7,23},{8,24},{9,... | collective-permute-start | bytes 110600 | tf_op jit(solution)/shard_map/ppermute | solution.py:37
  36.1 1.0 %collective-permute-start.13 = (f32[8,1152]{1,0:T(8,128)S(1)}, f32[8,1152]{1,0:T(8,128)S(1)}, u32[]{:S(2)}, u32[]{:S(2)}) collective-permute-start(f32[8,1152]{1,0:T(8,128)S(1)} %add_add_fusion.1), channel_id=1, source_target_pairs={{0,24},{1,25},{2,26},{3,27},{4,28},{5,29},{6,30},{7,31},{8,16},{9,... | collective-permute-start | bytes 110600 | tf_op jit(solution)/shard_map/ppermute | solution.py:37
  37.1 0.9 %collective-permute-done.12 = f32[8,1152]{1,0:T(8,128)S(1)} collective-permute-done((f32[8,1152]{1,0:T(8,128)S(1)}, f32[8,1152]{1,0:T(8,128)S(1)}, u32[]{:S(2)}, u32[]{:S(2)}) %collective-permute-start.12) | collective-permute-done | bytes 36896 | tf_op jit(solution)/shard_map/ppermute | solution.py:37
  38.0 3.8 %collective-permute-done.13 = f32[8,1152]{1,0:T(8,128)S(1)} collective-permute-done((f32[8,1152]{1,0:T(8,128)S(1)}, f32[8,1152]{1,0:T(8,128)S(1)}, u32[]{:S(2)}, u32[]{:S(2)}) %collective-permute-start.13) | collective-permute-done | bytes 36896 | tf_op jit(solution)/shard_map/ppermute | solution.py:37
  41.8 0.1 collective-permute-start.14
  41.9 1.2 %collective-permute-done.14.got_ref = f32[8,1152]{1,0:T(8,128)S(1)} collective-permute-done((f32[8,1152]{1,0:T(8,128)S(1)}, f32[8,1152]{1,0:T(8,128)S(1)}, u32[]{:S(2)}, u32[]{:S(2)}) %collective-permute-start.14) | collective-permute-done | bytes 36896 | tf_op jit(solution)/shard_map/ppermute | solution.py:37
  43.1 4.0 %shard_map.62 = (f32[8,1024]{1,0:T(8,128)S(1)}, f32[8,1024]{1,0:T(8,128)S(1)}, f32[1,1024]{1,0:T(1,128)S(1)}, f32[16,1024]{1,0:T(8,128)S(1)}) custom-call(s32[1]{0:T(128)} %bitcast.me_ref, f32[8,1152]{1,0:T(8,128)S(1)} %add_add_fusion.held_ref, f32[8,1152]{1,0:T(8,128)S(1)} %collective-permute-done.14.got_ref, f32[16,1024]{1,0:T(8,128)S(1)} %get-tuple-element.47.rhs_ref, ...), custom_call_target="tpu_custom_call" | custom-call | flops 1073741824 | bytes 8388608 | tf_op jit(solution)/shard_map/pallas_call | solution.py:421
  47.1 0.2 collective-permute-start.15
  47.3 1.1 %collective-permute-done.15 = f32[8,1024]{1,0:T(8,128)S(1)} collective-permute-done((f32[8,1024]{1,0:T(8,128)S(1)}, f32[8,1024]{1,0:T(8,128)S(1)}, u32[]{:S(2)}, u32[]{:S(2)}) %collective-permute-start.15) | collective-permute-done | bytes 32800 | tf_op jit(solution)/shard_map/ppermute | solution.py:37
  48.3 0.5 collective-permute-start.16
  48.9 0.5 collective-permute-start.17
  49.4 2.5 %collective-permute-start.18 = (f32[8,1024]{1,0:T(8,128)S(1)}, f32[8,1024]{1,0:T(8,128)S(1)}, u32[]{:S(2)}, u32[]{:S(2)}) collective-permute-start(f32[8,1024]{1,0:T(8,128)S(1)} %add.74), channel_id=1, source_target_pairs={{0,6},{1,7},{2,4},{3,5},{4,2},{5,3},{6,0},{7,1},{8,14},{9,15},{10,... | collective-permute-start | bytes 98312 | tf_op jit(solution)/shard_map/ppermute | solution.py:37
  51.8 0.4 collective-permute-done.16
  52.2 0.9 %collective-permute-done.17 = f32[8,1024]{1,0:T(8,128)S(1)} collective-permute-done((f32[8,1024]{1,0:T(8,128)S(1)}, f32[8,1024]{1,0:T(8,128)S(1)}, u32[]{:S(2)}, u32[]{:S(2)}) %collective-permute-start.17) | collective-permute-done | bytes 32800 | tf_op jit(solution)/shard_map/ppermute | solution.py:37
  53.1 1.1 %collective-permute-done.18 = f32[8,1024]{1,0:T(8,128)S(1)} collective-permute-done((f32[8,1024]{1,0:T(8,128)S(1)}, f32[8,1024]{1,0:T(8,128)S(1)}, u32[]{:S(2)}, u32[]{:S(2)}) %collective-permute-start.18) | collective-permute-done | bytes 32800 | tf_op jit(solution)/shard_map/ppermute | solution.py:37
  54.2 0.1 collective-permute-start.19
  54.3 1.6 %collective-permute-start.20 = (f32[8,1024]{1,0:T(8,128)S(1)}, f32[8,1024]{1,0:T(8,128)S(1)}, u32[]{:S(2)}, u32[]{:S(2)}) collective-permute-start(f32[8,1024]{1,0:T(8,128)S(1)} %add_add_fusion.5), channel_id=1, source_target_pairs={{0,16},{1,17},{2,18},{3,19},{4,20},{5,21},{6,22},{7,23},{8,24},{9,... | collective-permute-start | bytes 98312 | tf_op jit(solution)/shard_map/ppermute | solution.py:37
  55.8 2.8 %collective-permute-start.21 = (f32[8,1024]{1,0:T(8,128)S(1)}, f32[8,1024]{1,0:T(8,128)S(1)}, u32[]{:S(2)}, u32[]{:S(2)}) collective-permute-start(f32[8,1024]{1,0:T(8,128)S(1)} %add_add_fusion.5), channel_id=1, source_target_pairs={{0,24},{1,25},{2,26},{3,27},{4,28},{5,29},{6,30},{7,31},{8,16},{9,... | collective-permute-start | bytes 98312 | tf_op jit(solution)/shard_map/ppermute | solution.py:37
  58.6 0.5 collective-permute-done.20
  59.1 2.4 %collective-permute-done.21 = f32[8,1024]{1,0:T(8,128)S(1)} collective-permute-done((f32[8,1024]{1,0:T(8,128)S(1)}, f32[8,1024]{1,0:T(8,128)S(1)}, u32[]{:S(2)}, u32[]{:S(2)}) %collective-permute-start.21) | collective-permute-done | bytes 32800 | tf_op jit(solution)/shard_map/ppermute | solution.py:37
  61.5 0.1 collective-permute-start.22
  61.6 1.2 %collective-permute-done.22.got_ref = f32[8,1024]{1,0:T(8,128)S(1)} collective-permute-done((f32[8,1024]{1,0:T(8,128)S(1)}, f32[8,1024]{1,0:T(8,128)S(1)}, u32[]{:S(2)}, u32[]{:S(2)}) %collective-permute-start.22) | collective-permute-done | bytes 32800 | tf_op jit(solution)/shard_map/ppermute | solution.py:37
  62.8 4.2 %shard_map.63 = (f32[8,1024]{1,0:T(8,128)S(1)}, f32[8,1024]{1,0:T(8,128)S(1)}, f32[16,1024]{1,0:T(8,128)S(1)}, f32[16,1024]{1,0:T(8,128)S(1)}, f32[16,128]{1,0:T...) custom-call(s32[1]{0:T(128)} %bitcast.me_ref, ...), custom_call_target="tpu_custom_call" | custom-call | flops 1073741824 | bytes 8388608 | tf_op jit(solution)/shard_map/pallas_call | solution.py:431
  67.1 0.2 collective-permute-start.23
  67.3 1.0 %collective-permute-done.23 = f32[8,1024]{1,0:T(8,128)S(1)} collective-permute-done((f32[8,1024]{1,0:T(8,128)S(1)}, f32[8,1024]{1,0:T(8,128)S(1)}, u32[]{:S(2)}, u32[]{:S(2)}) %collective-permute-start.23) | collective-permute-done | bytes 32800 | tf_op jit(solution)/shard_map/ppermute | solution.py:37
  68.3 1.5 %collective-permute-start.24 = (f32[8,1024]{1,0:T(8,128)S(1)}, f32[8,1024]{1,0:T(8,128)S(1)}, u32[]{:S(2)}, u32[]{:S(2)}) collective-permute-start(f32[8,1024]{1,0:T(8,128)S(1)} %add.81), channel_id=1, source_target_pairs={{0,2},{1,3},{2,0},{3,1},{4,6},{5,7},{6,4},{7,5},{8,10},{9,11},{10,... | collective-permute-start | bytes 98312 | tf_op jit(solution)/shard_map/ppermute | solution.py:37
  69.8 1.5 %collective-permute-start.25 = (f32[8,1024]{1,0:T(8,128)S(1)}, f32[8,1024]{1,0:T(8,128)S(1)}, u32[]{:S(2)}, u32[]{:S(2)}) collective-permute-start(f32[8,1024]{1,0:T(8,128)S(1)} %add.81), channel_id=1, source_target_pairs={{0,4},{1,5},{2,6},{3,7},{4,0},{5,1},{6,2},{7,3},{8,12},{9,13},{10,... | collective-permute-start | bytes 98312 | tf_op jit(solution)/shard_map/ppermute | solution.py:37
  71.3 0.5 collective-permute-start.26
  71.8 0.4 collective-permute-done.24
  72.2 1.5 %collective-permute-done.25 = f32[8,1024]{1,0:T(8,128)S(1)} collective-permute-done((f32[8,1024]{1,0:T(8,128)S(1)}, f32[8,1024]{1,0:T(8,128)S(1)}, u32[]{:S(2)}, u32[]{:S(2)}) %collective-permute-start.25) | collective-permute-done | bytes 32800 | tf_op jit(solution)/shard_map/ppermute | solution.py:37
  73.7 2.4 %collective-permute-done.26 = f32[8,1024]{1,0:T(8,128)S(1)} collective-permute-done((f32[8,1024]{1,0:T(8,128)S(1)}, f32[8,1024]{1,0:T(8,128)S(1)}, u32[]{:S(2)}, u32[]{:S(2)}) %collective-permute-start.26) | collective-permute-done | bytes 32800 | tf_op jit(solution)/shard_map/ppermute | solution.py:37
  76.1 0.1 collective-permute-start.27
  76.2 3.4 %collective-permute-start.28 = (f32[8,1024]{1,0:T(8,128)S(1)}, f32[8,1024]{1,0:T(8,128)S(1)}, u32[]{:S(2)}, u32[]{:S(2)}) collective-permute-start(f32[8,1024]{1,0:T(8,128)S(1)} %add_add_fusion.3), channel_id=1, source_target_pairs={{0,16},{1,17},{2,18},{3,19},{4,20},{5,21},{6,22},{7,23},{8,24},{9,... | collective-permute-start | bytes 98312 | tf_op jit(solution)/shard_map/ppermute | solution.py:37
  79.6 1.0 %collective-permute-start.29 = (f32[8,1024]{1,0:T(8,128)S(1)}, f32[8,1024]{1,0:T(8,128)S(1)}, u32[]{:S(2)}, u32[]{:S(2)}) collective-permute-start(f32[8,1024]{1,0:T(8,128)S(1)} %add_add_fusion.3), channel_id=1, source_target_pairs={{0,24},{1,25},{2,26},{3,27},{4,28},{5,29},{6,30},{7,31},{8,16},{9,... | collective-permute-start | bytes 98312 | tf_op jit(solution)/shard_map/ppermute | solution.py:37
  80.6 0.5 collective-permute-start.32
  81.1 1.3 %collective-permute-start.33 = (f32[8,2048]{1,0:T(8,128)S(1)}, f32[8,2048]{1,0:T(8,128)S(1)}, u32[]{:S(2)}, u32[]{:S(2)}) collective-permute-start(f32[8,2048]{1,0:T(8,128)S(1)} %get-tuple-element.63), channel_id=1, source_target_pairs={{0,3},{1,2},{2,1},{3,0},{4,7},{5,6},{6,5},{7,4},{8,11},{9,10},{10,... | collective-permute-start | bytes 196616 | tf_op jit(solution)/shard_map/ppermute | solution.py:37
  82.5 2.8 %collective-permute-done.29 = f32[8,1024]{1,0:T(8,128)S(1)} collective-permute-done((f32[8,1024]{1,0:T(8,128)S(1)}, f32[8,1024]{1,0:T(8,128)S(1)}, u32[]{:S(2)}, u32[]{:S(2)}) %collective-permute-start.29) | collective-permute-done | bytes 32800 | tf_op jit(solution)/shard_map/ppermute | solution.py:37
  85.3 0.1 collective-permute-start.30
  85.4 0.1 collective-permute-done.32.refs_2_
  85.6 0.5 collective-permute-done.33.refs_3_
  86.0 0.6 collective-permute-done.30.got_ref
  86.6 0.9 %shard_map.64 = (f32[16,256]{1,0:T(8,128)}, f32[4,8192]{1,0:T(4,128)}) custom-call(s32[1]{0:T(128)} %bitcast.me_ref, f32[8,1024]{1,0:T(8,128)S(1)} %add_add_fusion.2.held_ref, f32[8,1024]{1,0:T(8,128)S(1)} %collective-permute-done.30.got_ref, f32[16,1024]{1,0:T(8,128)S(1)} %get-tuple-element.56.direc_ref, f32[16,1024]{1,0:T(8,128)S(1)} %get-tuple-element.57.part_ref, ...), custom_call_target="tpu_custom_call" | custom-call | flops 1048576 | bytes 262144 | tf_op jit(solution)/shard_map/pallas_call | solution.py:441
  (22 shorter events, 0.1 us)
Async XLA Ops:
  0.6 13.3 %collective-permute-start.6 = (bf16[256,128]{1,0:T(8,128)(2,1)}, bf16[256,128]{1,0:T(8,128)(2,1)S(1)}, u32[]{:S(2)}, u32[]{:S(2)}) collective-permute-start(bf16[256,128]{1,0:T(8,128)(2,1)} %anch_ref.1), channel_id=1, source_target_pairs={{0,1},{1,0},{2,3},{3,2},{4,5},{5,4},{6,7},{7,6},{8,9},{9,8},{10,11... | collective-permute-start | bytes 196616 | tf_op jit(solution)/shard_map/ppermute | solution.py:37
  1.2 6.2 %collective-permute-start.4 = (bf16[256,128]{1,0:T(8,128)(2,1)}, bf16[256,128]{1,0:T(8,128)(2,1)S(1)}, u32[]{:S(2)}, u32[]{:S(2)}) collective-permute-start(bf16[256,128]{1,0:T(8,128)(2,1)} %anch_ref.1), channel_id=1, source_target_pairs={{0,2},{1,3},{2,0},{3,1},{4,6},{5,7},{6,4},{7,5},{8,10},{9,11},{10,... | collective-permute-start | bytes 196616 | tf_op jit(solution)/shard_map/ppermute | solution.py:37
  5.8 3.7 %collective-permute-start = (bf16[32,128]{1,0:T(8,128)(2,1)S(1)}, bf16[32,128]{1,0:T(8,128)(2,1)S(1)}, u32[]{:S(2)}, u32[]{:S(2)}) collective-permute-start(bf16[32,128]{1,0:T(8,128)(2,1)S(1)} %get-tuple-element.34), channel_id=1, source_target_pairs={{0,4},{1,5},{2,6},{3,7},{4,0},{5,1},{6,2},{7,3},{8,12},{9,13},{10,... | collective-permute-start | bytes 24584 | tf_op jit(solution)/shard_map/ppermute | solution.py:37
  7.4 8.8 %collective-permute-start.5 = (bf16[256,128]{1,0:T(8,128)(2,1)S(1)}, bf16[256,128]{1,0:T(8,128)(2,1)S(1)}, u32[]{:S(2)}, u32[]{:S(2)}) collective-permute-start(bf16[256,128]{1,0:T(8,128)(2,1)S(1)} %collective-permute-done.4.a2), channel_id=1, source_target_pairs={{0,1},{1,0},{2,3},{3,2},{4,5},{5,4},{6,7},{7,6},{8,9},{9,8},{10,11... | collective-permute-start | bytes 196616 | tf_op jit(solution)/shard_map/ppermute | solution.py:37
  9.5 8.9 %collective-permute-start.1 = (bf16[64,128]{1,0:T(8,128)(2,1)S(1)}, bf16[64,128]{1,0:T(8,128)(2,1)S(1)}, u32[]{:S(2)}, u32[]{:S(2)}) collective-permute-start(bf16[64,128]{1,0:T(8,128)(2,1)S(1)} %constant_dynamic-update-slice_fusion.refs_0_), channel_id=1, source_target_pairs={{0,8},{1,9},{2,10},{3,11},{4,12},{5,13},{6,14},{7,15},{8,0},{9,1},... | collective-permute-start | bytes 49160 | tf_op jit(solution)/shard_map/ppermute | solution.py:37
  11.1 7.3 %collective-permute-start.2 = (bf16[64,128]{1,0:T(8,128)(2,1)S(1)}, bf16[64,128]{1,0:T(8,128)(2,1)S(1)}, u32[]{:S(2)}, u32[]{:S(2)}) collective-permute-start(bf16[64,128]{1,0:T(8,128)(2,1)S(1)} %constant_dynamic-update-slice_fusion.refs_0_), channel_id=1, source_target_pairs={{0,16},{1,17},{2,18},{3,19},{4,20},{5,21},{6,22},{7,23},{8,24},{9,... | collective-permute-start | bytes 49160 | tf_op jit(solution)/shard_map/ppermute | solution.py:37
  13.7 5.5 %collective-permute-start.3 = (bf16[64,128]{1,0:T(8,128)(2,1)S(1)}, bf16[64,128]{1,0:T(8,128)(2,1)S(1)}, u32[]{:S(2)}, u32[]{:S(2)}) collective-permute-start(bf16[64,128]{1,0:T(8,128)(2,1)S(1)} %constant_dynamic-update-slice_fusion.refs_0_), channel_id=1, source_target_pairs={{0,24},{1,25},{2,26},{3,27},{4,28},{5,29},{6,30},{7,31},{8,16},{9,... | collective-permute-start | bytes 49160 | tf_op jit(solution)/shard_map/ppermute | solution.py:37
  24.4 1.2 %collective-permute-start.7 = (f32[8,1152]{1,0:T(8,128)S(1)}, f32[8,1152]{1,0:T(8,128)S(1)}, u32[]{:S(2)}, u32[]{:S(2)}) collective-permute-start(f32[8,1152]{1,0:T(8,128)S(1)} %get-tuple-element.46), channel_id=1, source_target_pairs={{0,1},{1,0},{2,3},{3,2},{4,5},{5,4},{6,7},{7,6},{8,9},{9,8},{10,11... | collective-permute-start | bytes 110600 | tf_op jit(solution)/shard_map/ppermute | solution.py:37
  25.6 4.9 %collective-permute-start.10 = (f32[8,1152]{1,0:T(8,128)S(1)}, f32[8,1152]{1,0:T(8,128)S(1)}, u32[]{:S(2)}, u32[]{:S(2)}) collective-permute-start(f32[8,1152]{1,0:T(8,128)S(1)} %add.67), channel_id=1, source_target_pairs={{0,6},{1,7},{2,4},{3,5},{4,2},{5,3},{6,0},{7,1},{8,14},{9,15},{10,... | collective-permute-start | bytes 110600 | tf_op jit(solution)/shard_map/ppermute | solution.py:37
  27.1 4.0 %collective-permute-start.8 = (f32[8,1152]{1,0:T(8,128)S(1)}, f32[8,1152]{1,0:T(8,128)S(1)}, u32[]{:S(2)}, u32[]{:S(2)}) collective-permute-start(f32[8,1152]{1,0:T(8,128)S(1)} %add.67), channel_id=1, source_target_pairs={{0,2},{1,3},{2,0},{3,1},{4,6},{5,7},{6,4},{7,5},{8,10},{9,11},{10,... | collective-permute-start | bytes 110600 | tf_op jit(solution)/shard_map/ppermute | solution.py:37
  28.6 4.0 %collective-permute-start.9 = (f32[8,1152]{1,0:T(8,128)S(1)}, f32[8,1152]{1,0:T(8,128)S(1)}, u32[]{:S(2)}, u32[]{:S(2)}) collective-permute-start(f32[8,1152]{1,0:T(8,128)S(1)} %add.67), channel_id=1, source_target_pairs={{0,4},{1,5},{2,6},{3,7},{4,0},{5,1},{6,2},{7,3},{8,12},{9,13},{10,... | collective-permute-start | bytes 110600 | tf_op jit(solution)/shard_map/ppermute | solution.py:37
  32.6 4.5 %collective-permute-start.11 = (f32[8,1152]{1,0:T(8,128)S(1)}, f32[8,1152]{1,0:T(8,128)S(1)}, u32[]{:S(2)}, u32[]{:S(2)}) collective-permute-start(f32[8,1152]{1,0:T(8,128)S(1)} %add_add_fusion.1), channel_id=1, source_target_pairs={{0,8},{1,9},{2,10},{3,11},{4,12},{5,13},{6,14},{7,15},{8,0},{9,1},... | collective-permute-start | bytes 110600 | tf_op jit(solution)/shard_map/ppermute | solution.py:37
  32.7 5.3 %collective-permute-start.12 = (f32[8,1152]{1,0:T(8,128)S(1)}, f32[8,1152]{1,0:T(8,128)S(1)}, u32[]{:S(2)}, u32[]{:S(2)}) collective-permute-start(f32[8,1152]{1,0:T(8,128)S(1)} %add_add_fusion.1), channel_id=1, source_target_pairs={{0,16},{1,17},{2,18},{3,19},{4,20},{5,21},{6,22},{7,23},{8,24},{9,... | collective-permute-start | bytes 110600 | tf_op jit(solution)/shard_map/ppermute | solution.py:37
  36.1 5.8 %collective-permute-start.13 = (f32[8,1152]{1,0:T(8,128)S(1)}, f32[8,1152]{1,0:T(8,128)S(1)}, u32[]{:S(2)}, u32[]{:S(2)}) collective-permute-start(f32[8,1152]{1,0:T(8,128)S(1)} %add_add_fusion.1), channel_id=1, source_target_pairs={{0,24},{1,25},{2,26},{3,27},{4,28},{5,29},{6,30},{7,31},{8,16},{9,... | collective-permute-start | bytes 110600 | tf_op jit(solution)/shard_map/ppermute | solution.py:37
  41.8 1.3 %collective-permute-start.14 = (f32[8,1152]{1,0:T(8,128)S(1)}, f32[8,1152]{1,0:T(8,128)S(1)}, u32[]{:S(2)}, u32[]{:S(2)}) collective-permute-start(f32[8,1152]{1,0:T(8,128)S(1)} %add_add_fusion.held_ref), channel_id=1, source_target_pairs={{0,1},{1,0},{2,3},{3,2},{4,5},{5,4},{6,7},{7,6},{8,9},{9,8},{10,11... | collective-permute-start | bytes 110600 | tf_op jit(solution)/shard_map/ppermute | solution.py:37
  47.1 1.2 %collective-permute-start.15 = (f32[8,1024]{1,0:T(8,128)S(1)}, f32[8,1024]{1,0:T(8,128)S(1)}, u32[]{:S(2)}, u32[]{:S(2)}) collective-permute-start(f32[8,1024]{1,0:T(8,128)S(1)} %get-tuple-element.51), channel_id=1, source_target_pairs={{0,1},{1,0},{2,3},{3,2},{4,5},{5,4},{6,7},{7,6},{8,9},{9,8},{10,11... | collective-permute-start | bytes 98312 | tf_op jit(solution)/shard_map/ppermute | solution.py:37
  48.3 3.9 %collective-permute-start.16 = (f32[8,1024]{1,0:T(8,128)S(1)}, f32[8,1024]{1,0:T(8,128)S(1)}, u32[]{:S(2)}, u32[]{:S(2)}) collective-permute-start(f32[8,1024]{1,0:T(8,128)S(1)} %add.74), channel_id=1, source_target_pairs={{0,2},{1,3},{2,0},{3,1},{4,6},{5,7},{6,4},{7,5},{8,10},{9,11},{10,... | collective-permute-start | bytes 98312 | tf_op jit(solution)/shard_map/ppermute | solution.py:37
  48.9 4.3 %collective-permute-start.17 = (f32[8,1024]{1,0:T(8,128)S(1)}, f32[8,1024]{1,0:T(8,128)S(1)}, u32[]{:S(2)}, u32[]{:S(2)}) collective-permute-start(f32[8,1024]{1,0:T(8,128)S(1)} %add.74), channel_id=1, source_target_pairs={{0,4},{1,5},{2,6},{3,7},{4,0},{5,1},{6,2},{7,3},{8,12},{9,13},{10,... | collective-permute-start | bytes 98312 | tf_op jit(solution)/shard_map/ppermute | solution.py:37
  49.4 4.8 %collective-permute-start.18 = (f32[8,1024]{1,0:T(8,128)S(1)}, f32[8,1024]{1,0:T(8,128)S(1)}, u32[]{:S(2)}, u32[]{:S(2)}) collective-permute-start(f32[8,1024]{1,0:T(8,128)S(1)} %add.74), channel_id=1, source_target_pairs={{0,6},{1,7},{2,4},{3,5},{4,2},{5,3},{6,0},{7,1},{8,14},{9,15},{10,... | collective-permute-start | bytes 98312 | tf_op jit(solution)/shard_map/ppermute | solution.py:37
  54.2 4.5 %collective-permute-start.19 = (f32[8,1024]{1,0:T(8,128)S(1)}, f32[8,1024]{1,0:T(8,128)S(1)}, u32[]{:S(2)}, u32[]{:S(2)}) collective-permute-start(f32[8,1024]{1,0:T(8,128)S(1)} %add_add_fusion.5), channel_id=1, source_target_pairs={{0,8},{1,9},{2,10},{3,11},{4,12},{5,13},{6,14},{7,15},{8,0},{9,1},... | collective-permute-start | bytes 98312 | tf_op jit(solution)/shard_map/ppermute | solution.py:37
  54.3 4.9 %collective-permute-start.20 = (f32[8,1024]{1,0:T(8,128)S(1)}, f32[8,1024]{1,0:T(8,128)S(1)}, u32[]{:S(2)}, u32[]{:S(2)}) collective-permute-start(f32[8,1024]{1,0:T(8,128)S(1)} %add_add_fusion.5), channel_id=1, source_target_pairs={{0,16},{1,17},{2,18},{3,19},{4,20},{5,21},{6,22},{7,23},{8,24},{9,... | collective-permute-start | bytes 98312 | tf_op jit(solution)/shard_map/ppermute | solution.py:37
  55.8 5.7 %collective-permute-start.21 = (f32[8,1024]{1,0:T(8,128)S(1)}, f32[8,1024]{1,0:T(8,128)S(1)}, u32[]{:S(2)}, u32[]{:S(2)}) collective-permute-start(f32[8,1024]{1,0:T(8,128)S(1)} %add_add_fusion.5), channel_id=1, source_target_pairs={{0,24},{1,25},{2,26},{3,27},{4,28},{5,29},{6,30},{7,31},{8,16},{9,... | collective-permute-start | bytes 98312 | tf_op jit(solution)/shard_map/ppermute | solution.py:37
  61.5 1.3 %collective-permute-start.22 = (f32[8,1024]{1,0:T(8,128)S(1)}, f32[8,1024]{1,0:T(8,128)S(1)}, u32[]{:S(2)}, u32[]{:S(2)}) collective-permute-start(f32[8,1024]{1,0:T(8,128)S(1)} %add_add_fusion.4.held_ref), channel_id=1, source_target_pairs={{0,1},{1,0},{2,3},{3,2},{4,5},{5,4},{6,7},{7,6},{8,9},{9,8},{10,11... | collective-permute-start | bytes 98312 | tf_op jit(solution)/shard_map/ppermute | solution.py:37
  67.1 1.2 %collective-permute-start.23 = (f32[8,1024]{1,0:T(8,128)S(1)}, f32[8,1024]{1,0:T(8,128)S(1)}, u32[]{:S(2)}, u32[]{:S(2)}) collective-permute-start(f32[8,1024]{1,0:T(8,128)S(1)} %get-tuple-element.55), channel_id=1, source_target_pairs={{0,1},{1,0},{2,3},{3,2},{4,5},{5,4},{6,7},{7,6},{8,9},{9,8},{10,11... | collective-permute-start | bytes 98312 | tf_op jit(solution)/shard_map/ppermute | solution.py:37
  68.3 3.9 %collective-permute-start.24 = (f32[8,1024]{1,0:T(8,128)S(1)}, f32[8,1024]{1,0:T(8,128)S(1)}, u32[]{:S(2)}, u32[]{:S(2)}) collective-permute-start(f32[8,1024]{1,0:T(8,128)S(1)} %add.81), channel_id=1, source_target_pairs={{0,2},{1,3},{2,0},{3,1},{4,6},{5,7},{6,4},{7,5},{8,10},{9,11},{10,... | collective-permute-start | bytes 98312 | tf_op jit(solution)/shard_map/ppermute | solution.py:37
  69.8 3.9 %collective-permute-start.25 = (f32[8,1024]{1,0:T(8,128)S(1)}, f32[8,1024]{1,0:T(8,128)S(1)}, u32[]{:S(2)}, u32[]{:S(2)}) collective-permute-start(f32[8,1024]{1,0:T(8,128)S(1)} %add.81), channel_id=1, source_target_pairs={{0,4},{1,5},{2,6},{3,7},{4,0},{5,1},{6,2},{7,3},{8,12},{9,13},{10,... | collective-permute-start | bytes 98312 | tf_op jit(solution)/shard_map/ppermute | solution.py:37
  71.3 4.8 %collective-permute-start.26 = (f32[8,1024]{1,0:T(8,128)S(1)}, f32[8,1024]{1,0:T(8,128)S(1)}, u32[]{:S(2)}, u32[]{:S(2)}) collective-permute-start(f32[8,1024]{1,0:T(8,128)S(1)} %add.81), channel_id=1, source_target_pairs={{0,6},{1,7},{2,4},{3,5},{4,2},{5,3},{6,0},{7,1},{8,14},{9,15},{10,... | collective-permute-start | bytes 98312 | tf_op jit(solution)/shard_map/ppermute | solution.py:37
  76.1 5.0 %collective-permute-start.27 = (f32[8,1024]{1,0:T(8,128)S(1)}, f32[8,1024]{1,0:T(8,128)S(1)}, u32[]{:S(2)}, u32[]{:S(2)}) collective-permute-start(f32[8,1024]{1,0:T(8,128)S(1)} %add_add_fusion.3), channel_id=1, source_target_pairs={{0,8},{1,9},{2,10},{3,11},{4,12},{5,13},{6,14},{7,15},{8,0},{9,1},... | collective-permute-start | bytes 98312 | tf_op jit(solution)/shard_map/ppermute | solution.py:37
  76.2 6.2 %collective-permute-start.28 = (f32[8,1024]{1,0:T(8,128)S(1)}, f32[8,1024]{1,0:T(8,128)S(1)}, u32[]{:S(2)}, u32[]{:S(2)}) collective-permute-start(f32[8,1024]{1,0:T(8,128)S(1)} %add_add_fusion.3), channel_id=1, source_target_pairs={{0,16},{1,17},{2,18},{3,19},{4,20},{5,21},{6,22},{7,23},{8,24},{9,... | collective-permute-start | bytes 98312 | tf_op jit(solution)/shard_map/ppermute | solution.py:37
  79.6 5.7 %collective-permute-start.29 = (f32[8,1024]{1,0:T(8,128)S(1)}, f32[8,1024]{1,0:T(8,128)S(1)}, u32[]{:S(2)}, u32[]{:S(2)}) collective-permute-start(f32[8,1024]{1,0:T(8,128)S(1)} %add_add_fusion.3), channel_id=1, source_target_pairs={{0,24},{1,25},{2,26},{3,27},{4,28},{5,29},{6,30},{7,31},{8,16},{9,... | collective-permute-start | bytes 98312 | tf_op jit(solution)/shard_map/ppermute | solution.py:37
  80.6 4.8 %collective-permute-start.31 = (f32[8,2048]{1,0:T(8,128)S(1)}, f32[8,2048]{1,0:T(8,128)S(1)}, u32[]{:S(2)}, u32[]{:S(2)}) collective-permute-start(f32[8,2048]{1,0:T(8,128)S(1)} %get-tuple-element.61), channel_id=1, source_target_pairs={{0,1},{1,0},{2,3},{3,2},{4,5},{5,4},{6,7},{7,6},{8,9},{9,8},{10,11... | collective-permute-start | bytes 196616 | tf_op jit(solution)/shard_map/ppermute | solution.py:37
  80.6 5.0 %collective-permute-start.32 = (f32[8,2048]{1,0:T(8,128)S(1)}, f32[8,2048]{1,0:T(8,128)S(1)}, u32[]{:S(2)}, u32[]{:S(2)}) collective-permute-start(f32[8,2048]{1,0:T(8,128)S(1)} %get-tuple-element.62), channel_id=1, source_target_pairs={{0,2},{1,3},{2,0},{3,1},{4,6},{5,7},{6,4},{7,5},{8,10},{9,11},{10,... | collective-permute-start | bytes 196616 | tf_op jit(solution)/shard_map/ppermute | solution.py:37
  81.1 4.9 %collective-permute-start.33 = (f32[8,2048]{1,0:T(8,128)S(1)}, f32[8,2048]{1,0:T(8,128)S(1)}, u32[]{:S(2)}, u32[]{:S(2)}) collective-permute-start(f32[8,2048]{1,0:T(8,128)S(1)} %get-tuple-element.63), channel_id=1, source_target_pairs={{0,3},{1,2},{2,1},{3,0},{4,7},{5,6},{6,5},{7,4},{8,11},{9,10},{10,... | collective-permute-start | bytes 196616 | tf_op jit(solution)/shard_map/ppermute | solution.py:37
  85.3 1.3 %collective-permute-start.30 = (f32[8,1024]{1,0:T(8,128)S(1)}, f32[8,1024]{1,0:T(8,128)S(1)}, u32[]{:S(2)}, u32[]{:S(2)}) collective-permute-start(f32[8,1024]{1,0:T(8,128)S(1)} %add_add_fusion.2.held_ref), channel_id=1, source_target_pairs={{0,1},{1,0},{2,3},{3,2},{4,5},{5,4},{6,7},{7,6},{8,9},{9,8},{10,11... | collective-permute-start | bytes 98312 | tf_op jit(solution)/shard_map/ppermute | solution.py:37

commit v4 on v3

--- a/solution.py
+++ b/solution.py
@@ -48,8 +48,15 @@
     return groups
 
 
+def exchange(value, masks):
+    got = []
+    for mask in masks:
+        got.append(swap(value, mask))
+    return got
+
+
 def sum_stage(held, masks):
-    got = [swap(held, mask) for mask in masks]
+    got = exchange(held, masks)
     if len(got) == 1:
         return held + got[0]
     return (held + got[0]) + (got[1] + got[2])
@@ -376,7 +383,7 @@
     bits = list(range(a_bits, n_bits))
     stages = bit_groups(bits[:1]) + bit_groups(bits[1:])
     for at, stage in enumerate(stages):
-        got = [swap(held, mask) for mask in stage]
+        got = exchange(held, stage)
         if at < len(stages) - 1:
             masks = masks + [m ^ mask for mask in stage for m in masks]
             held = jnp.concatenate([held] + got, axis=0)
@@ -437,7 +444,9 @@
     )(me, held, got, rhs, lab, spread, zhi, zlo, khi, klo, tinv)
 
     held, got = reduce_all(mine, send, n_bits)
-    parts = [docs_out[0]] + [swap(docs_out[mask], mask) for mask in range(1, na)]
+    parts = [docs_out[0]]
+    for mask in range(1, na):
+        parts.append(swap(docs_out[mask], mask))
     anchor_scores, doc_scores = call(
         functools.partial(last_kernel, na, graph_scale),
         [SMEM] + [VMEM] * (6 + na),

time: 87.7 us -> 87.7 us (level)
  no operation moved by 1% of the time
where the time goes in v4:
time: 87.7 us; the launch traced here: 87.5 us
  starting transfers between devices  35.4 us (40%)
  waiting for transfers between devices  30.5 us (35%)
  Pallas kernels  20.8 us (24%)
    ppermute x34, starting transfers between devices, swap(): return lax.ppermute(value, EVERY, [(i, i ^ mask) for i in range(count)])  35.4 us
    ppermute x34, waiting for transfers between devices, swap(): return lax.ppermute(value, EVERY, [(i, i ^ mask) for i in range(count)])  30.5 us
    pallas_call x1, Pallas kernels, run(): call(functools.partial(first_kernel, na, labs, slots, CLASSES * lab_scale...  5.16 us
    pallas_call x1, Pallas kernels, run(): call(functools.partial(third_kernel, na, lab_scale, graph_scale), [SMEM]...  4.25 us
    pallas_call x1, Pallas kernels, run(): call(second_kernel, [SMEM] + [VMEM] * 8, [half_sds, half_sds, sds((1, tot...  3.98 us
    pallas_call x1, Pallas kernels, run(): call(functools.partial(build_far, na), [SMEM] + [VMEM] * 7, [k_sds, k_sds...  2.25 us
    pallas_call x1, Pallas kernels, run(): call(functools.partial(build_near, na), [SMEM] + [VMEM] * 3, [k_sds, k_sd...  2.22 us
    pallas_call x1, Pallas kernels, run(): pl.pallas_call(functools.partial(label_kernel, na), grid_spec=pltpu.Prefe...  2.06 us
  transfers between devices with their start and end apart: 34, of which 24 were waited for; matrix products, arithmetic and copies ran while one was open for 0% of the time, Pallas kernels for 7%

profile of v4, /device:TPU:0, one launch (start us, length us, event | category | flops | bytes accessed | tf_op | source)
XLA Modules:
  0.0 87.5 jit_solution(5408005353987665781)
XLA Ops:
  0.6 0.6 collective-permute-start.6
  1.2 2.6 %collective-permute-start.4 = (bf16[256,128]{1,0:T(8,128)(2,1)}, bf16[256,128]{1,0:T(8,128)(2,1)S(1)}, u32[]{:S(2)}, u32[]{:S(2)}) collective-permute-start(bf16[256,128]{1,0:T(8,128)(2,1)} %anch_ref.1), channel_id=1, source_target_pairs={{0,2},{1,3},{2,0},{3,1},{4,6},{5,7},{6,4},{7,5},{8,10},{9,11},{10,... | collective-permute-start | bytes 196616 | tf_op jit(solution)/shard_map/ppermute | solution.py:37
  3.7 2.1 %label_rows.1 = (bf16[32,128]{1,0:T(8,128)(2,1)S(1)}, bf16[2048,128]{1,0:T(8,128)(2,1)S(1)}, bf16[256,128]{1,0:T(8,128)(2,1)S(1)}) custom-call(s32[1]{0:T(128)} %bitcast.me_ref, s32[16]{0:T(128)} %idx_ref.1, s32[16]{0:T(128)} %cls_ref.1, bf16[8192,128]{1,0:T(8,128)(2,1)} %feat_ref.1, bf16[256,128]{1,0:T(8,128)(2,1)} %anch_ref.1), custom_call_target="tpu_custom_call" | custom-call | tf_op jit(solution)/shard_map/label_rows/pallas_call | solution.py:359
  5.8 1.6 %collective-permute-start = (bf16[32,128]{1,0:T(8,128)(2,1)S(1)}, bf16[32,128]{1,0:T(8,128)(2,1)S(1)}, u32[]{:S(2)}, u32[]{:S(2)}) collective-permute-start(bf16[32,128]{1,0:T(8,128)(2,1)S(1)} %get-tuple-element.34), channel_id=1, source_target_pairs={{0,4},{1,5},{2,6},{3,7},{4,0},{5,1},{6,2},{7,3},{8,12},{9,13},{10,... | collective-permute-start | bytes 24584 | tf_op jit(solution)/shard_map/ppermute | solution.py:37
  7.4 0.0 collective-permute-done.4.a2
  7.4 2.1 %collective-permute-done = bf16[32,128]{1,0:T(8,128)(2,1)S(1)} collective-permute-done((bf16[32,128]{1,0:T(8,128)(2,1)S(1)}, bf16[32,128]{1,0:T(8,128)(2,1)S(1)}, u32[]{:S(2)}, u32[]{:S(2)}) %collective-permute-start) | collective-permute-done | bytes 8224 | tf_op jit(solution)/shard_map/ppermute | solution.py:37
  9.5 1.6 %collective-permute-start.1 = (bf16[64,128]{1,0:T(8,128)(2,1)S(1)}, bf16[64,128]{1,0:T(8,128)(2,1)S(1)}, u32[]{:S(2)}, u32[]{:S(2)}) collective-permute-start(bf16[64,128]{1,0:T(8,128)(2,1)S(1)} %constant_dynamic-update-slice_fusion.refs_0_), channel_id=1, source_target_pairs={{0,8},{1,9},{2,10},{3,11},{4,12},{5,13},{6,14},{7,15},{8,0},{9,1},... | collective-permute-start | bytes 49160 | tf_op jit(solution)/shard_map/ppermute | solution.py:37
  11.1 2.6 %collective-permute-start.2 = (bf16[64,128]{1,0:T(8,128)(2,1)S(1)}, bf16[64,128]{1,0:T(8,128)(2,1)S(1)}, u32[]{:S(2)}, u32[]{:S(2)}) collective-permute-start(bf16[64,128]{1,0:T(8,128)(2,1)S(1)} %constant_dynamic-update-slice_fusion.refs_0_), channel_id=1, source_target_pairs={{0,16},{1,17},{2,18},{3,19},{4,20},{5,21},{6,22},{7,23},{8,24},{9,... | collective-permute-start | bytes 49160 | tf_op jit(solution)/shard_map/ppermute | solution.py:37
  13.7 0.2 collective-permute-start.3
  13.9 2.2 %shard_map.59 = (bf16[1024,2048]{1,0:T(8,128)(2,1)S(1)}, bf16[1024,2048]{1,0:T(8,128)(2,1)S(1)}, bf16[1024,256]{1,0:T(8,128)(2,1)S(1)}, f32[8,2048]{1,0:T(8,128)S(1)}) custom-call(s32[1]{0:T(128)} %bitcast.me_ref, bf16[256,128]{1,0:T(8,128)(2,1)S(1)} %get-tuple-element.36.a0, bf16[256,128]{1,0:T(8,128)(2,1)S(1)} %collective-permute-done.6.a1, ...), custom_call_target="tpu_custom_call" | custom-call | flops 536870912 | bytes 4194304 | tf_op jit(solution)/shard_map/pallas_call | solution.py:396
  16.2 2.2 %shard_map.60 = (bf16[1024,2048]{1,0:T(8,128)(2,1)S(1)}, bf16[1024,2048]{1,0:T(8,128)(2,1)S(1)}, bf16[1024,256]{1,0:T(8,128)(2,1)S(1)}, f32[1,2048]{1,0:T(1,128)S(1)}) custom-call(s32[1]{0:T(128)} %bitcast.me_ref, bf16[256,128]{1,0:T(8,128)(2,1)S(1)} %collective-permute-done.4.a2, ...), custom_call_target="tpu_custom_call", output_to_operand_aliasing={{0}: (5, {}), {1}: (6, {}), {2}: (7, {})} | custom-call | flops 536870912 | bytes 4194304 | tf_op jit(solution)/shard_map/pallas_call | solution.py:399
  18.4 0.8 collective-permute-done.3.refs_3_
  19.2 5.2 %shard_map.61 = (f32[8,1152]{1,0:T(8,128)S(1)}, f32[8,1152]{1,0:T(8,128)S(1)}, f32[16,1024]{1,0:T(8,128)S(1)}, bf16[1024,128]{1,0:T(8,128)(2,1)S(1)}, bf16[1024,...) custom-call(s32[1]{0:T(128)} %bitcast.me_ref, bf16[64,128]{1,0:T(8,128)(2,1)S(1)} %constant_dynamic-update-slice_fusion.refs_0_, ...), custom_call_target="tpu_custom_call" | custom-call | flops 1073741824 | bytes 8388608 | tf_op jit(solution)/shard_map/pallas_call | solution.py:415
  24.4 0.0 collective-permute-start.7
  24.4 1.2 %collective-permute-done.7 = f32[8,1152]{1,0:T(8,128)S(1)} collective-permute-done((f32[8,1152]{1,0:T(8,128)S(1)}, f32[8,1152]{1,0:T(8,128)S(1)}, u32[]{:S(2)}, u32[]{:S(2)}) %collective-permute-start.7) | collective-permute-done | bytes 36896 | tf_op jit(solution)/shard_map/ppermute | solution.py:37
  25.6 1.5 %collective-permute-start.10 = (f32[8,1152]{1,0:T(8,128)S(1)}, f32[8,1152]{1,0:T(8,128)S(1)}, u32[]{:S(2)}, u32[]{:S(2)}) collective-permute-start(f32[8,1152]{1,0:T(8,128)S(1)} %add.67), channel_id=1, source_target_pairs={{0,6},{1,7},{2,4},{3,5},{4,2},{5,3},{6,0},{7,1},{8,14},{9,15},{10,... | collective-permute-start | bytes 110600 | tf_op jit(solution)/shard_map/ppermute | solution.py:37
  27.1 1.5 %collective-permute-start.8 = (f32[8,1152]{1,0:T(8,128)S(1)}, f32[8,1152]{1,0:T(8,128)S(1)}, u32[]{:S(2)}, u32[]{:S(2)}) collective-permute-start(f32[8,1152]{1,0:T(8,128)S(1)} %add.67), channel_id=1, source_target_pairs={{0,2},{1,3},{2,0},{3,1},{4,6},{5,7},{6,4},{7,5},{8,10},{9,11},{10,... | collective-permute-start | bytes 110600 | tf_op jit(solution)/shard_map/ppermute | solution.py:37
  28.6 0.5 collective-permute-start.9
  29.1 1.4 %collective-permute-done.10 = f32[8,1152]{1,0:T(8,128)S(1)} collective-permute-done((f32[8,1152]{1,0:T(8,128)S(1)}, f32[8,1152]{1,0:T(8,128)S(1)}, u32[]{:S(2)}, u32[]{:S(2)}) %collective-permute-start.10) | collective-permute-done | bytes 36896 | tf_op jit(solution)/shard_map/ppermute | solution.py:37
  30.5 0.6 collective-permute-done.8
  31.1 1.5 %collective-permute-done.9 = f32[8,1152]{1,0:T(8,128)S(1)} collective-permute-done((f32[8,1152]{1,0:T(8,128)S(1)}, f32[8,1152]{1,0:T(8,128)S(1)}, u32[]{:S(2)}, u32[]{:S(2)}) %collective-permute-start.9) | collective-permute-done | bytes 36896 | tf_op jit(solution)/shard_map/ppermute | solution.py:37
  32.6 0.1 collective-permute-start.11
  32.7 3.4 %collective-permute-start.12 = (f32[8,1152]{1,0:T(8,128)S(1)}, f32[8,1152]{1,0:T(8,128)S(1)}, u32[]{:S(2)}, u32[]{:S(2)}) collective-permute-start(f32[8,1152]{1,0:T(8,128)S(1)} %add_add_fusion.1), channel_id=1, source_target_pairs={{0,16},{1,17},{2,18},{3,19},{4,20},{5,21},{6,22},{7,23},{8,24},{9,... | collective-permute-start | bytes 110600 | tf_op jit(solution)/shard_map/ppermute | solution.py:37
  36.1 1.0 %collective-permute-start.13 = (f32[8,1152]{1,0:T(8,128)S(1)}, f32[8,1152]{1,0:T(8,128)S(1)}, u32[]{:S(2)}, u32[]{:S(2)}) collective-permute-start(f32[8,1152]{1,0:T(8,128)S(1)} %add_add_fusion.1), channel_id=1, source_target_pairs={{0,24},{1,25},{2,26},{3,27},{4,28},{5,29},{6,30},{7,31},{8,16},{9,... | collective-permute-start | bytes 110600 | tf_op jit(solution)/shard_map/ppermute | solution.py:37
  37.1 0.9 %collective-permute-done.12 = f32[8,1152]{1,0:T(8,128)S(1)} collective-permute-done((f32[8,1152]{1,0:T(8,128)S(1)}, f32[8,1152]{1,0:T(8,128)S(1)}, u32[]{:S(2)}, u32[]{:S(2)}) %collective-permute-start.12) | collective-permute-done | bytes 36896 | tf_op jit(solution)/shard_map/ppermute | solution.py:37
  38.0 3.8 %collective-permute-done.13 = f32[8,1152]{1,0:T(8,128)S(1)} collective-permute-done((f32[8,1152]{1,0:T(8,128)S(1)}, f32[8,1152]{1,0:T(8,128)S(1)}, u32[]{:S(2)}, u32[]{:S(2)}) %collective-permute-start.13) | collective-permute-done | bytes 36896 | tf_op jit(solution)/shard_map/ppermute | solution.py:37
  41.8 0.1 collective-permute-start.14
  41.9 1.2 %collective-permute-done.14.got_ref = f32[8,1152]{1,0:T(8,128)S(1)} collective-permute-done((f32[8,1152]{1,0:T(8,128)S(1)}, f32[8,1152]{1,0:T(8,128)S(1)}, u32[]{:S(2)}, u32[]{:S(2)}) %collective-permute-start.14) | collective-permute-done | bytes 36896 | tf_op jit(solution)/shard_map/ppermute | solution.py:37
  43.1 4.0 %shard_map.62 = (f32[8,1024]{1,0:T(8,128)S(1)}, f32[8,1024]{1,0:T(8,128)S(1)}, f32[1,1024]{1,0:T(1,128)S(1)}, f32[16,1024]{1,0:T(8,128)S(1)}) custom-call(s32[1]{0:T(128)} %bitcast.me_ref, f32[8,1152]{1,0:T(8,128)S(1)} %add_add_fusion.held_ref, f32[8,1152]{1,0:T(8,128)S(1)} %collective-permute-done.14.got_ref, f32[16,1024]{1,0:T(8,128)S(1)} %get-tuple-element.47.rhs_ref, ...), custom_call_target="tpu_custom_call" | custom-call | flops 1073741824 | bytes 8388608 | tf_op jit(solution)/shard_map/pallas_call | solution.py:428
  47.1 0.2 collective-permute-start.15
  47.3 1.1 %collective-permute-done.15 = f32[8,1024]{1,0:T(8,128)S(1)} collective-permute-done((f32[8,1024]{1,0:T(8,128)S(1)}, f32[8,1024]{1,0:T(8,128)S(1)}, u32[]{:S(2)}, u32[]{:S(2)}) %collective-permute-start.15) | collective-permute-done | bytes 32800 | tf_op jit(solution)/shard_map/ppermute | solution.py:37
  48.3 0.5 collective-permute-start.16
  48.9 0.5 collective-permute-start.17
  49.4 2.5 %collective-permute-start.18 = (f32[8,1024]{1,0:T(8,128)S(1)}, f32[8,1024]{1,0:T(8,128)S(1)}, u32[]{:S(2)}, u32[]{:S(2)}) collective-permute-start(f32[8,1024]{1,0:T(8,128)S(1)} %add.74), channel_id=1, source_target_pairs={{0,6},{1,7},{2,4},{3,5},{4,2},{5,3},{6,0},{7,1},{8,14},{9,15},{10,... | collective-permute-start | bytes 98312 | tf_op jit(solution)/shard_map/ppermute | solution.py:37
  51.8 0.4 collective-permute-done.16
  52.2 0.9 %collective-permute-done.17 = f32[8,1024]{1,0:T(8,128)S(1)} collective-permute-done((f32[8,1024]{1,0:T(8,128)S(1)}, f32[8,1024]{1,0:T(8,128)S(1)}, u32[]{:S(2)}, u32[]{:S(2)}) %collective-permute-start.17) | collective-permute-done | bytes 32800 | tf_op jit(solution)/shard_map/ppermute | solution.py:37
  53.1 1.1 %collective-permute-done.18 = f32[8,1024]{1,0:T(8,128)S(1)} collective-permute-done((f32[8,1024]{1,0:T(8,128)S(1)}, f32[8,1024]{1,0:T(8,128)S(1)}, u32[]{:S(2)}, u32[]{:S(2)}) %collective-permute-start.18) | collective-permute-done | bytes 32800 | tf_op jit(solution)/shard_map/ppermute | solution.py:37
  54.2 0.1 collective-permute-start.19
  54.3 1.6 %collective-permute-start.20 = (f32[8,1024]{1,0:T(8,128)S(1)}, f32[8,1024]{1,0:T(8,128)S(1)}, u32[]{:S(2)}, u32[]{:S(2)}) collective-permute-start(f32[8,1024]{1,0:T(8,128)S(1)} %add_add_fusion.5), channel_id=1, source_target_pairs={{0,16},{1,17},{2,18},{3,19},{4,20},{5,21},{6,22},{7,23},{8,24},{9,... | collective-permute-start | bytes 98312 | tf_op jit(solution)/shard_map/ppermute | solution.py:37
  55.8 2.8 %collective-permute-start.21 = (f32[8,1024]{1,0:T(8,128)S(1)}, f32[8,1024]{1,0:T(8,128)S(1)}, u32[]{:S(2)}, u32[]{:S(2)}) collective-permute-start(f32[8,1024]{1,0:T(8,128)S(1)} %add_add_fusion.5), channel_id=1, source_target_pairs={{0,24},{1,25},{2,26},{3,27},{4,28},{5,29},{6,30},{7,31},{8,16},{9,... | collective-permute-start | bytes 98312 | tf_op jit(solution)/shard_map/ppermute | solution.py:37
  58.6 0.5 collective-permute-done.20
  59.1 2.4 %collective-permute-done.21 = f32[8,1024]{1,0:T(8,128)S(1)} collective-permute-done((f32[8,1024]{1,0:T(8,128)S(1)}, f32[8,1024]{1,0:T(8,128)S(1)}, u32[]{:S(2)}, u32[]{:S(2)}) %collective-permute-start.21) | collective-permute-done | bytes 32800 | tf_op jit(solution)/shard_map/ppermute | solution.py:37
  61.5 0.1 collective-permute-start.22
  61.6 1.2 %collective-permute-done.22.got_ref = f32[8,1024]{1,0:T(8,128)S(1)} collective-permute-done((f32[8,1024]{1,0:T(8,128)S(1)}, f32[8,1024]{1,0:T(8,128)S(1)}, u32[]{:S(2)}, u32[]{:S(2)}) %collective-permute-start.22) | collective-permute-done | bytes 32800 | tf_op jit(solution)/shard_map/ppermute | solution.py:37
  62.8 4.2 %shard_map.63 = (f32[8,1024]{1,0:T(8,128)S(1)}, f32[8,1024]{1,0:T(8,128)S(1)}, f32[16,1024]{1,0:T(8,128)S(1)}, f32[16,1024]{1,0:T(8,128)S(1)}, f32[16,128]{1,0:T...) custom-call(s32[1]{0:T(128)} %bitcast.me_ref, ...), custom_call_target="tpu_custom_call" | custom-call | flops 1073741824 | bytes 8388608 | tf_op jit(solution)/shard_map/pallas_call | solution.py:438
  67.1 0.2 collective-permute-start.23
  67.3 1.0 %collective-permute-done.23 = f32[8,1024]{1,0:T(8,128)S(1)} collective-permute-done((f32[8,1024]{1,0:T(8,128)S(1)}, f32[8,1024]{1,0:T(8,128)S(1)}, u32[]{:S(2)}, u32[]{:S(2)}) %collective-permute-start.23) | collective-permute-done | bytes 32800 | tf_op jit(solution)/shard_map/ppermute | solution.py:37
  68.3 1.5 %collective-permute-start.24 = (f32[8,1024]{1,0:T(8,128)S(1)}, f32[8,1024]{1,0:T(8,128)S(1)}, u32[]{:S(2)}, u32[]{:S(2)}) collective-permute-start(f32[8,1024]{1,0:T(8,128)S(1)} %add.81), channel_id=1, source_target_pairs={{0,2},{1,3},{2,0},{3,1},{4,6},{5,7},{6,4},{7,5},{8,10},{9,11},{10,... | collective-permute-start | bytes 98312 | tf_op jit(solution)/shard_map/ppermute | solution.py:37
  69.8 1.5 %collective-permute-start.25 = (f32[8,1024]{1,0:T(8,128)S(1)}, f32[8,1024]{1,0:T(8,128)S(1)}, u32[]{:S(2)}, u32[]{:S(2)}) collective-permute-start(f32[8,1024]{1,0:T(8,128)S(1)} %add.81), channel_id=1, source_target_pairs={{0,4},{1,5},{2,6},{3,7},{4,0},{5,1},{6,2},{7,3},{8,12},{9,13},{10,... | collective-permute-start | bytes 98312 | tf_op jit(solution)/shard_map/ppermute | solution.py:37
  71.3 0.5 collective-permute-start.26
  71.8 0.4 collective-permute-done.24
  72.2 1.5 %collective-permute-done.25 = f32[8,1024]{1,0:T(8,128)S(1)} collective-permute-done((f32[8,1024]{1,0:T(8,128)S(1)}, f32[8,1024]{1,0:T(8,128)S(1)}, u32[]{:S(2)}, u32[]{:S(2)}) %collective-permute-start.25) | collective-permute-done | bytes 32800 | tf_op jit(solution)/shard_map/ppermute | solution.py:37
  73.7 2.4 %collective-permute-done.26 = f32[8,1024]{1,0:T(8,128)S(1)} collective-permute-done((f32[8,1024]{1,0:T(8,128)S(1)}, f32[8,1024]{1,0:T(8,128)S(1)}, u32[]{:S(2)}, u32[]{:S(2)}) %collective-permute-start.26) | collective-permute-done | bytes 32800 | tf_op jit(solution)/shard_map/ppermute | solution.py:37
  76.1 0.1 collective-permute-start.27
  76.2 3.4 %collective-permute-start.28 = (f32[8,1024]{1,0:T(8,128)S(1)}, f32[8,1024]{1,0:T(8,128)S(1)}, u32[]{:S(2)}, u32[]{:S(2)}) collective-permute-start(f32[8,1024]{1,0:T(8,128)S(1)} %add_add_fusion.3), channel_id=1, source_target_pairs={{0,16},{1,17},{2,18},{3,19},{4,20},{5,21},{6,22},{7,23},{8,24},{9,... | collective-permute-start | bytes 98312 | tf_op jit(solution)/shard_map/ppermute | solution.py:37
  79.6 1.0 %collective-permute-start.29 = (f32[8,1024]{1,0:T(8,128)S(1)}, f32[8,1024]{1,0:T(8,128)S(1)}, u32[]{:S(2)}, u32[]{:S(2)}) collective-permute-start(f32[8,1024]{1,0:T(8,128)S(1)} %add_add_fusion.3), channel_id=1, source_target_pairs={{0,24},{1,25},{2,26},{3,27},{4,28},{5,29},{6,30},{7,31},{8,16},{9,... | collective-permute-start | bytes 98312 | tf_op jit(solution)/shard_map/ppermute | solution.py:37
  80.6 0.5 collective-permute-start.32
  81.1 1.3 %collective-permute-start.33 = (f32[8,2048]{1,0:T(8,128)S(1)}, f32[8,2048]{1,0:T(8,128)S(1)}, u32[]{:S(2)}, u32[]{:S(2)}) collective-permute-start(f32[8,2048]{1,0:T(8,128)S(1)} %get-tuple-element.63), channel_id=1, source_target_pairs={{0,3},{1,2},{2,1},{3,0},{4,7},{5,6},{6,5},{7,4},{8,11},{9,10},{10,... | collective-permute-start | bytes 196616 | tf_op jit(solution)/shard_map/ppermute | solution.py:37
  82.5 2.8 %collective-permute-done.29 = f32[8,1024]{1,0:T(8,128)S(1)} collective-permute-done((f32[8,1024]{1,0:T(8,128)S(1)}, f32[8,1024]{1,0:T(8,128)S(1)}, u32[]{:S(2)}, u32[]{:S(2)}) %collective-permute-start.29) | collective-permute-done | bytes 32800 | tf_op jit(solution)/shard_map/ppermute | solution.py:37
  85.3 0.1 collective-permute-start.30
  85.4 0.1 collective-permute-done.32.refs_2_
  85.6 0.5 collective-permute-done.33.refs_3_
  86.0 0.6 collective-permute-done.30.got_ref
  86.6 0.9 %shard_map.64 = (f32[16,256]{1,0:T(8,128)}, f32[4,8192]{1,0:T(4,128)}) custom-call(s32[1]{0:T(128)} %bitcast.me_ref, f32[8,1024]{1,0:T(8,128)S(1)} %add_add_fusion.2.held_ref, f32[8,1024]{1,0:T(8,128)S(1)} %collective-permute-done.30.got_ref, f32[16,1024]{1,0:T(8,128)S(1)} %get-tuple-element.56.direc_ref, f32[16,1024]{1,0:T(8,128)S(1)} %get-tuple-element.57.part_ref, ...), custom_call_target="tpu_custom_call" | custom-call | flops 1048576 | bytes 262144 | tf_op jit(solution)/shard_map/pallas_call | solution.py:450
  (22 shorter events, 0.1 us)
Async XLA Ops:
  0.6 13.3 %collective-permute-start.6 = (bf16[256,128]{1,0:T(8,128)(2,1)}, bf16[256,128]{1,0:T(8,128)(2,1)S(1)}, u32[]{:S(2)}, u32[]{:S(2)}) collective-permute-start(bf16[256,128]{1,0:T(8,128)(2,1)} %anch_ref.1), channel_id=1, source_target_pairs={{0,1},{1,0},{2,3},{3,2},{4,5},{5,4},{6,7},{7,6},{8,9},{9,8},{10,11... | collective-permute-start | bytes 196616 | tf_op jit(solution)/shard_map/ppermute | solution.py:37
  1.2 6.2 %collective-permute-start.4 = (bf16[256,128]{1,0:T(8,128)(2,1)}, bf16[256,128]{1,0:T(8,128)(2,1)S(1)}, u32[]{:S(2)}, u32[]{:S(2)}) collective-permute-start(bf16[256,128]{1,0:T(8,128)(2,1)} %anch_ref.1), channel_id=1, source_target_pairs={{0,2},{1,3},{2,0},{3,1},{4,6},{5,7},{6,4},{7,5},{8,10},{9,11},{10,... | collective-permute-start | bytes 196616 | tf_op jit(solution)/shard_map/ppermute | solution.py:37
  5.8 3.7 %collective-permute-start = (bf16[32,128]{1,0:T(8,128)(2,1)S(1)}, bf16[32,128]{1,0:T(8,128)(2,1)S(1)}, u32[]{:S(2)}, u32[]{:S(2)}) collective-permute-start(bf16[32,128]{1,0:T(8,128)(2,1)S(1)} %get-tuple-element.34), channel_id=1, source_target_pairs={{0,4},{1,5},{2,6},{3,7},{4,0},{5,1},{6,2},{7,3},{8,12},{9,13},{10,... | collective-permute-start | bytes 24584 | tf_op jit(solution)/shard_map/ppermute | solution.py:37
  7.4 8.8 %collective-permute-start.5 = (bf16[256,128]{1,0:T(8,128)(2,1)S(1)}, bf16[256,128]{1,0:T(8,128)(2,1)S(1)}, u32[]{:S(2)}, u32[]{:S(2)}) collective-permute-start(bf16[256,128]{1,0:T(8,128)(2,1)S(1)} %collective-permute-done.4.a2), channel_id=1, source_target_pairs={{0,1},{1,0},{2,3},{3,2},{4,5},{5,4},{6,7},{7,6},{8,9},{9,8},{10,11... | collective-permute-start | bytes 196616 | tf_op jit(solution)/shard_map/ppermute | solution.py:37
  9.5 8.9 %collective-permute-start.1 = (bf16[64,128]{1,0:T(8,128)(2,1)S(1)}, bf16[64,128]{1,0:T(8,128)(2,1)S(1)}, u32[]{:S(2)}, u32[]{:S(2)}) collective-permute-start(bf16[64,128]{1,0:T(8,128)(2,1)S(1)} %constant_dynamic-update-slice_fusion.refs_0_), channel_id=1, source_target_pairs={{0,8},{1,9},{2,10},{3,11},{4,12},{5,13},{6,14},{7,15},{8,0},{9,1},... | collective-permute-start | bytes 49160 | tf_op jit(solution)/shard_map/ppermute | solution.py:37
  11.1 7.3 %collective-permute-start.2 = (bf16[64,128]{1,0:T(8,128)(2,1)S(1)}, bf16[64,128]{1,0:T(8,128)(2,1)S(1)}, u32[]{:S(2)}, u32[]{:S(2)}) collective-permute-start(bf16[64,128]{1,0:T(8,128)(2,1)S(1)} %constant_dynamic-update-slice_fusion.refs_0_), channel_id=1, source_target_pairs={{0,16},{1,17},{2,18},{3,19},{4,20},{5,21},{6,22},{7,23},{8,24},{9,... | collective-permute-start | bytes 49160 | tf_op jit(solution)/shard_map/ppermute | solution.py:37
  13.7 5.5 %collective-permute-start.3 = (bf16[64,128]{1,0:T(8,128)(2,1)S(1)}, bf16[64,128]{1,0:T(8,128)(2,1)S(1)}, u32[]{:S(2)}, u32[]{:S(2)}) collective-permute-start(bf16[64,128]{1,0:T(8,128)(2,1)S(1)} %constant_dynamic-update-slice_fusion.refs_0_), channel_id=1, source_target_pairs={{0,24},{1,25},{2,26},{3,27},{4,28},{5,29},{6,30},{7,31},{8,16},{9,... | collective-permute-start | bytes 49160 | tf_op jit(solution)/shard_map/ppermute | solution.py:37
  24.4 1.2 %collective-permute-start.7 = (f32[8,1152]{1,0:T(8,128)S(1)}, f32[8,1152]{1,0:T(8,128)S(1)}, u32[]{:S(2)}, u32[]{:S(2)}) collective-permute-start(f32[8,1152]{1,0:T(8,128)S(1)} %get-tuple-element.46), channel_id=1, source_target_pairs={{0,1},{1,0},{2,3},{3,2},{4,5},{5,4},{6,7},{7,6},{8,9},{9,8},{10,11... | collective-permute-start | bytes 110600 | tf_op jit(solution)/shard_map/ppermute | solution.py:37
  25.6 4.9 %collective-permute-start.10 = (f32[8,1152]{1,0:T(8,128)S(1)}, f32[8,1152]{1,0:T(8,128)S(1)}, u32[]{:S(2)}, u32[]{:S(2)}) collective-permute-start(f32[8,1152]{1,0:T(8,128)S(1)} %add.67), channel_id=1, source_target_pairs={{0,6},{1,7},{2,4},{3,5},{4,2},{5,3},{6,0},{7,1},{8,14},{9,15},{10,... | collective-permute-start | bytes 110600 | tf_op jit(solution)/shard_map/ppermute | solution.py:37
  27.1 4.0 %collective-permute-start.8 = (f32[8,1152]{1,0:T(8,128)S(1)}, f32[8,1152]{1,0:T(8,128)S(1)}, u32[]{:S(2)}, u32[]{:S(2)}) collective-permute-start(f32[8,1152]{1,0:T(8,128)S(1)} %add.67), channel_id=1, source_target_pairs={{0,2},{1,3},{2,0},{3,1},{4,6},{5,7},{6,4},{7,5},{8,10},{9,11},{10,... | collective-permute-start | bytes 110600 | tf_op jit(solution)/shard_map/ppermute | solution.py:37
  28.6 4.0 %collective-permute-start.9 = (f32[8,1152]{1,0:T(8,128)S(1)}, f32[8,1152]{1,0:T(8,128)S(1)}, u32[]{:S(2)}, u32[]{:S(2)}) collective-permute-start(f32[8,1152]{1,0:T(8,128)S(1)} %add.67), channel_id=1, source_target_pairs={{0,4},{1,5},{2,6},{3,7},{4,0},{5,1},{6,2},{7,3},{8,12},{9,13},{10,... | collective-permute-start | bytes 110600 | tf_op jit(solution)/shard_map/ppermute | solution.py:37
  32.6 4.5 %collective-permute-start.11 = (f32[8,1152]{1,0:T(8,128)S(1)}, f32[8,1152]{1,0:T(8,128)S(1)}, u32[]{:S(2)}, u32[]{:S(2)}) collective-permute-start(f32[8,1152]{1,0:T(8,128)S(1)} %add_add_fusion.1), channel_id=1, source_target_pairs={{0,8},{1,9},{2,10},{3,11},{4,12},{5,13},{6,14},{7,15},{8,0},{9,1},... | collective-permute-start | bytes 110600 | tf_op jit(solution)/shard_map/ppermute | solution.py:37
  32.7 5.3 %collective-permute-start.12 = (f32[8,1152]{1,0:T(8,128)S(1)}, f32[8,1152]{1,0:T(8,128)S(1)}, u32[]{:S(2)}, u32[]{:S(2)}) collective-permute-start(f32[8,1152]{1,0:T(8,128)S(1)} %add_add_fusion.1), channel_id=1, source_target_pairs={{0,16},{1,17},{2,18},{3,19},{4,20},{5,21},{6,22},{7,23},{8,24},{9,... | collective-permute-start | bytes 110600 | tf_op jit(solution)/shard_map/ppermute | solution.py:37
  36.1 5.8 %collective-permute-start.13 = (f32[8,1152]{1,0:T(8,128)S(1)}, f32[8,1152]{1,0:T(8,128)S(1)}, u32[]{:S(2)}, u32[]{:S(2)}) collective-permute-start(f32[8,1152]{1,0:T(8,128)S(1)} %add_add_fusion.1), channel_id=1, source_target_pairs={{0,24},{1,25},{2,26},{3,27},{4,28},{5,29},{6,30},{7,31},{8,16},{9,... | collective-permute-start | bytes 110600 | tf_op jit(solution)/shard_map/ppermute | solution.py:37
  41.8 1.3 %collective-permute-start.14 = (f32[8,1152]{1,0:T(8,128)S(1)}, f32[8,1152]{1,0:T(8,128)S(1)}, u32[]{:S(2)}, u32[]{:S(2)}) collective-permute-start(f32[8,1152]{1,0:T(8,128)S(1)} %add_add_fusion.held_ref), channel_id=1, source_target_pairs={{0,1},{1,0},{2,3},{3,2},{4,5},{5,4},{6,7},{7,6},{8,9},{9,8},{10,11... | collective-permute-start | bytes 110600 | tf_op jit(solution)/shard_map/ppermute | solution.py:37
  47.1 1.2 %collective-permute-start.15 = (f32[8,1024]{1,0:T(8,128)S(1)}, f32[8,1024]{1,0:T(8,128)S(1)}, u32[]{:S(2)}, u32[]{:S(2)}) collective-permute-start(f32[8,1024]{1,0:T(8,128)S(1)} %get-tuple-element.51), channel_id=1, source_target_pairs={{0,1},{1,0},{2,3},{3,2},{4,5},{5,4},{6,7},{7,6},{8,9},{9,8},{10,11... | collective-permute-start | bytes 98312 | tf_op jit(solution)/shard_map/ppermute | solution.py:37
  48.3 3.9 %collective-permute-start.16 = (f32[8,1024]{1,0:T(8,128)S(1)}, f32[8,1024]{1,0:T(8,128)S(1)}, u32[]{:S(2)}, u32[]{:S(2)}) collective-permute-start(f32[8,1024]{1,0:T(8,128)S(1)} %add.74), channel_id=1, source_target_pairs={{0,2},{1,3},{2,0},{3,1},{4,6},{5,7},{6,4},{7,5},{8,10},{9,11},{10,... | collective-permute-start | bytes 98312 | tf_op jit(solution)/shard_map/ppermute | solution.py:37
  48.9 4.3 %collective-permute-start.17 = (f32[8,1024]{1,0:T(8,128)S(1)}, f32[8,1024]{1,0:T(8,128)S(1)}, u32[]{:S(2)}, u32[]{:S(2)}) collective-permute-start(f32[8,1024]{1,0:T(8,128)S(1)} %add.74), channel_id=1, source_target_pairs={{0,4},{1,5},{2,6},{3,7},{4,0},{5,1},{6,2},{7,3},{8,12},{9,13},{10,... | collective-permute-start | bytes 98312 | tf_op jit(solution)/shard_map/ppermute | solution.py:37
  49.4 4.8 %collective-permute-start.18 = (f32[8,1024]{1,0:T(8,128)S(1)}, f32[8,1024]{1,0:T(8,128)S(1)}, u32[]{:S(2)}, u32[]{:S(2)}) collective-permute-start(f32[8,1024]{1,0:T(8,128)S(1)} %add.74), channel_id=1, source_target_pairs={{0,6},{1,7},{2,4},{3,5},{4,2},{5,3},{6,0},{7,1},{8,14},{9,15},{10,... | collective-permute-start | bytes 98312 | tf_op jit(solution)/shard_map/ppermute | solution.py:37
  54.2 4.5 %collective-permute-start.19 = (f32[8,1024]{1,0:T(8,128)S(1)}, f32[8,1024]{1,0:T(8,128)S(1)}, u32[]{:S(2)}, u32[]{:S(2)}) collective-permute-start(f32[8,1024]{1,0:T(8,128)S(1)} %add_add_fusion.5), channel_id=1, source_target_pairs={{0,8},{1,9},{2,10},{3,11},{4,12},{5,13},{6,14},{7,15},{8,0},{9,1},... | collective-permute-start | bytes 98312 | tf_op jit(solution)/shard_map/ppermute | solution.py:37
  54.3 4.9 %collective-permute-start.20 = (f32[8,1024]{1,0:T(8,128)S(1)}, f32[8,1024]{1,0:T(8,128)S(1)}, u32[]{:S(2)}, u32[]{:S(2)}) collective-permute-start(f32[8,1024]{1,0:T(8,128)S(1)} %add_add_fusion.5), channel_id=1, source_target_pairs={{0,16},{1,17},{2,18},{3,19},{4,20},{5,21},{6,22},{7,23},{8,24},{9,... | collective-permute-start | bytes 98312 | tf_op jit(solution)/shard_map/ppermute | solution.py:37
  55.8 5.7 %collective-permute-start.21 = (f32[8,1024]{1,0:T(8,128)S(1)}, f32[8,1024]{1,0:T(8,128)S(1)}, u32[]{:S(2)}, u32[]{:S(2)}) collective-permute-start(f32[8,1024]{1,0:T(8,128)S(1)} %add_add_fusion.5), channel_id=1, source_target_pairs={{0,24},{1,25},{2,26},{3,27},{4,28},{5,29},{6,30},{7,31},{8,16},{9,... | collective-permute-start | bytes 98312 | tf_op jit(solution)/shard_map/ppermute | solution.py:37
  61.5 1.3 %collective-permute-start.22 = (f32[8,1024]{1,0:T(8,128)S(1)}, f32[8,1024]{1,0:T(8,128)S(1)}, u32[]{:S(2)}, u32[]{:S(2)}) collective-permute-start(f32[8,1024]{1,0:T(8,128)S(1)} %add_add_fusion.4.held_ref), channel_id=1, source_target_pairs={{0,1},{1,0},{2,3},{3,2},{4,5},{5,4},{6,7},{7,6},{8,9},{9,8},{10,11... | collective-permute-start | bytes 98312 | tf_op jit(solution)/shard_map/ppermute | solution.py:37
  67.1 1.2 %collective-permute-start.23 = (f32[8,1024]{1,0:T(8,128)S(1)}, f32[8,1024]{1,0:T(8,128)S(1)}, u32[]{:S(2)}, u32[]{:S(2)}) collective-permute-start(f32[8,1024]{1,0:T(8,128)S(1)} %get-tuple-element.55), channel_id=1, source_target_pairs={{0,1},{1,0},{2,3},{3,2},{4,5},{5,4},{6,7},{7,6},{8,9},{9,8},{10,11... | collective-permute-start | bytes 98312 | tf_op jit(solution)/shard_map/ppermute | solution.py:37
  68.3 3.9 %collective-permute-start.24 = (f32[8,1024]{1,0:T(8,128)S(1)}, f32[8,1024]{1,0:T(8,128)S(1)}, u32[]{:S(2)}, u32[]{:S(2)}) collective-permute-start(f32[8,1024]{1,0:T(8,128)S(1)} %add.81), channel_id=1, source_target_pairs={{0,2},{1,3},{2,0},{3,1},{4,6},{5,7},{6,4},{7,5},{8,10},{9,11},{10,... | collective-permute-start | bytes 98312 | tf_op jit(solution)/shard_map/ppermute | solution.py:37
  69.8 3.9 %collective-permute-start.25 = (f32[8,1024]{1,0:T(8,128)S(1)}, f32[8,1024]{1,0:T(8,128)S(1)}, u32[]{:S(2)}, u32[]{:S(2)}) collective-permute-start(f32[8,1024]{1,0:T(8,128)S(1)} %add.81), channel_id=1, source_target_pairs={{0,4},{1,5},{2,6},{3,7},{4,0},{5,1},{6,2},{7,3},{8,12},{9,13},{10,... | collective-permute-start | bytes 98312 | tf_op jit(solution)/shard_map/ppermute | solution.py:37
  71.3 4.8 %collective-permute-start.26 = (f32[8,1024]{1,0:T(8,128)S(1)}, f32[8,1024]{1,0:T(8,128)S(1)}, u32[]{:S(2)}, u32[]{:S(2)}) collective-permute-start(f32[8,1024]{1,0:T(8,128)S(1)} %add.81), channel_id=1, source_target_pairs={{0,6},{1,7},{2,4},{3,5},{4,2},{5,3},{6,0},{7,1},{8,14},{9,15},{10,... | collective-permute-start | bytes 98312 | tf_op jit(solution)/shard_map/ppermute | solution.py:37
  76.1 5.0 %collective-permute-start.27 = (f32[8,1024]{1,0:T(8,128)S(1)}, f32[8,1024]{1,0:T(8,128)S(1)}, u32[]{:S(2)}, u32[]{:S(2)}) collective-permute-start(f32[8,1024]{1,0:T(8,128)S(1)} %add_add_fusion.3), channel_id=1, source_target_pairs={{0,8},{1,9},{2,10},{3,11},{4,12},{5,13},{6,14},{7,15},{8,0},{9,1},... | collective-permute-start | bytes 98312 | tf_op jit(solution)/shard_map/ppermute | solution.py:37
  76.2 6.2 %collective-permute-start.28 = (f32[8,1024]{1,0:T(8,128)S(1)}, f32[8,1024]{1,0:T(8,128)S(1)}, u32[]{:S(2)}, u32[]{:S(2)}) collective-permute-start(f32[8,1024]{1,0:T(8,128)S(1)} %add_add_fusion.3), channel_id=1, source_target_pairs={{0,16},{1,17},{2,18},{3,19},{4,20},{5,21},{6,22},{7,23},{8,24},{9,... | collective-permute-start | bytes 98312 | tf_op jit(solution)/shard_map/ppermute | solution.py:37
  79.6 5.7 %collective-permute-start.29 = (f32[8,1024]{1,0:T(8,128)S(1)}, f32[8,1024]{1,0:T(8,128)S(1)}, u32[]{:S(2)}, u32[]{:S(2)}) collective-permute-start(f32[8,1024]{1,0:T(8,128)S(1)} %add_add_fusion.3), channel_id=1, source_target_pairs={{0,24},{1,25},{2,26},{3,27},{4,28},{5,29},{6,30},{7,31},{8,16},{9,... | collective-permute-start | bytes 98312 | tf_op jit(solution)/shard_map/ppermute | solution.py:37
  80.6 4.8 %collective-permute-start.31 = (f32[8,2048]{1,0:T(8,128)S(1)}, f32[8,2048]{1,0:T(8,128)S(1)}, u32[]{:S(2)}, u32[]{:S(2)}) collective-permute-start(f32[8,2048]{1,0:T(8,128)S(1)} %get-tuple-element.61), channel_id=1, source_target_pairs={{0,1},{1,0},{2,3},{3,2},{4,5},{5,4},{6,7},{7,6},{8,9},{9,8},{10,11... | collective-permute-start | bytes 196616 | tf_op jit(solution)/shard_map/ppermute | solution.py:37
  80.6 5.0 %collective-permute-start.32 = (f32[8,2048]{1,0:T(8,128)S(1)}, f32[8,2048]{1,0:T(8,128)S(1)}, u32[]{:S(2)}, u32[]{:S(2)}) collective-permute-start(f32[8,2048]{1,0:T(8,128)S(1)} %get-tuple-element.62), channel_id=1, source_target_pairs={{0,2},{1,3},{2,0},{3,1},{4,6},{5,7},{6,4},{7,5},{8,10},{9,11},{10,... | collective-permute-start | bytes 196616 | tf_op jit(solution)/shard_map/ppermute | solution.py:37
  81.1 4.9 %collective-permute-start.33 = (f32[8,2048]{1,0:T(8,128)S(1)}, f32[8,2048]{1,0:T(8,128)S(1)}, u32[]{:S(2)}, u32[]{:S(2)}) collective-permute-start(f32[8,2048]{1,0:T(8,128)S(1)} %get-tuple-element.63), channel_id=1, source_target_pairs={{0,3},{1,2},{2,1},{3,0},{4,7},{5,6},{6,5},{7,4},{8,11},{9,10},{10,... | collective-permute-start | bytes 196616 | tf_op jit(solution)/shard_map/ppermute | solution.py:37
  85.3 1.3 %collective-permute-start.30 = (f32[8,1024]{1,0:T(8,128)S(1)}, f32[8,1024]{1,0:T(8,128)S(1)}, u32[]{:S(2)}, u32[]{:S(2)}) collective-permute-start(f32[8,1024]{1,0:T(8,128)S(1)} %add_add_fusion.2.held_ref), channel_id=1, source_target_pairs={{0,1},{1,0},{2,3},{3,2},{4,5},{5,4},{6,7},{7,6},{8,9},{9,8},{10,11... | collective-permute-start | bytes 98312 | tf_op jit(solution)/shard_map/ppermute | solution.py:37

commit v5 on v4

--- a/solution.py
+++ b/solution.py
@@ -9,11 +9,9 @@
 
 
 CLASSES = 16
-HALF = CLASSES // 2
 
 width_h = 0.25
 ridge = 0.1
-highest = lax.Precision.HIGHEST
 f32 = jnp.float32
 bf16 = jnp.bfloat16
 EVERY = ("docs", "anch")
@@ -62,11 +60,14 @@
     return (held + got[0]) + (got[1] + got[2])
 
 
-def reduce_all(mine, send, n_bits):
-    held = mine + swap(send, 1)
+def reduce_chips(held, n_bits):
     for masks in bit_groups(list(range(1, n_bits))):
         held = sum_stage(held, masks)
-    return held, swap(held, 1)
+    return held
+
+
+def swap_core(value):
+    return swap(value, 1)
 
 
 def aug_columns(first, second, rows):
@@ -184,36 +185,32 @@
     return jnp.concatenate(split2(value), axis=0)
 
 
-def gram(vec, khi_ref, klo_ref, tinv_ref, with_degree=False):
-    khi, klo, tinv = khi_ref[...], klo_ref[...], tinv_ref[...]
-    spread = times(vec, khi, klo) * tinv
+def halves(me_ref, size):
+    core = me_ref[0] & 1
+    return [pl.ds(pl.multiple_of(part * size, size), size) for part in (core, 1 - core)]
+
+
+def put_weights(w_ref, spread, tinv):
     high, low = split2(spread * tinv)
-    parts, second = [high, low], [high]
-    if with_degree:
-        row = lax.broadcasted_iota(jnp.int32, (CLASSES, tinv.shape[1]), 0)
-        thigh = tinv.astype(bf16).astype(f32)
-        ones = jnp.where(row == 0, thigh, jnp.where(row == 1, tinv - thigh, 0.0)).astype(bf16)
-        parts.append(ones)
-        second.append(ones)
-    one = mm(jnp.concatenate(parts, axis=0), khi, NT)
-    two = mm(jnp.concatenate(second, axis=0), klo, NT)
-    out = one[0:CLASSES] + (one[CLASSES : 2 * CLASSES] + two[0:CLASSES])
-    if not with_degree:
-        return spread, out
-    deg = one[2 * CLASSES :] + two[CLASSES:]
-    return spread, out, deg[0:1] + deg[1:2]
-
-
-def put_halves(acc, me, mine_ref, send_ref):
-    core = me & 1
-    mine_ref[...] = acc[pl.ds(pl.multiple_of(core * HALF, HALF), HALF), :]
-    send_ref[...] = acc[pl.ds(pl.multiple_of((1 - core) * HALF, HALF), HALF), :]
-
-
-def take_halves(acc, me, mine_ref, got_ref):
-    core = me & 1
-    acc[pl.ds(pl.multiple_of(core * HALF, HALF), HALF), :] = mine_ref[...]
-    acc[pl.ds(pl.multiple_of((1 - core) * HALF, HALF), HALF), :] = got_ref[...]
+    w_ref[0:CLASSES, :] = high
+    w_ref[CLASSES:, :] = low
+
+
+def back_rows(w_ref, khi, klo):
+    one = mm(w_ref[...], khi, NT)
+    return one[0:CLASSES] + (one[CLASSES:] + mm(w_ref[0:CLASSES, :], klo, NT))
+
+
+def back_degree(w_ref, khi, klo, out_ref):
+    one = mm(w_ref[...], khi, NT)
+    two = mm(w_ref[0 : 2 * CLASSES, :], klo, NT)
+    size = one.shape[1]
+    out_ref[:, 0:size] = one[0:CLASSES] + (one[2 * CLASSES :] + two[0:CLASSES])
+    deg = one[CLASSES : 2 * CLASSES] + two[CLASSES:]
+    deg = deg[0:1] + deg[1:2]
+    out_ref[:, size:] = jnp.zeros((CLASSES, LANES), f32)
+    for k in range(size // LANES):
+        out_ref[k : k + 1, size:] = deg[:, k * LANES : (k + 1) * LANES]
 
 
 def mean_of(value):
@@ -224,11 +221,10 @@
     return jnp.sum(jnp.sum(value, axis=1, keepdims=True), axis=0, keepdims=True)
 
 
-def first_kernel(na, labs, slots, gain, me_ref, *refs):
+def first_send(na, labs, slots, gain, me_ref, *refs):
     lab_refs = refs[: len(slots)]
-    (aug_ref, khi_ref, klo_ref, tinv_ref, mine_ref, send_ref, rhs_ref, zhi_ref, zlo_ref, spread_ref,
-     laug, hot, acc) = refs[len(slots) :]
-    anchors = aug_ref.shape[0]
+    (aug_ref, khi_ref, klo_ref, tinv_ref, send_ref, w_ref, rhs_ref, mid_ref, zhi_ref, zlo_ref, spread_ref,
+     laug, hot) = refs[len(slots) :]
     feat = laug.shape[1] - LANES
     docs = me_ref[0] // na
     for masks, ref in zip(slots, lab_refs):
@@ -239,77 +235,131 @@
     size = row_sizes(laug[:, 0:feat].astype(f32)) * (1.0 / (feat * width_h))
     laug[:, feat:] = aug_columns(None, size, laug.shape[0])
     kern = eighth(mm(aug_ref[...], laug[...], NT))
-    zlab = kern / jnp.sum(kern, axis=0, keepdims=True)
-    zhi_ref[...], zlo_ref[...] = split2(zlab)
-    onehot = hot[...].T[0:CLASSES, :]
-    rhs = gain * mm(onehot, zlab, NT, highest)
+    zhi, zlo = split2(kern / jnp.sum(kern, axis=0, keepdims=True))
+    zhi_ref[...], zlo_ref[...] = zhi, zlo
+    onehot = hot[...].T[0:CLASSES, :].astype(bf16)
+    rhs = gain * (mm(onehot, zhi, NT) + mm(onehot, zlo, NT))
     rhs_ref[...] = rhs
-    middle = mean_of(rhs)
-    spread, out, deg = gram(pieces(rhs - middle), khi_ref, klo_ref, tinv_ref, True)
-    spread_ref[...] = spread + middle
-    acc[:, 0:anchors] = out
-    acc[:, anchors:] = jnp.zeros((CLASSES, LANES), f32)
-    for k in range(anchors // LANES):
-        acc[k : k + 1, anchors:] = deg[:, k * LANES : (k + 1) * LANES]
-    put_halves(acc, me_ref[0], mine_ref, send_ref)
-
-
-def second_kernel(me_ref, held_ref, got_ref, rhs_ref, zhi_ref, zlo_ref, khi_ref, klo_ref, tinv_ref,
-                  mine_ref, send_ref, dinv_ref, lab_ref, whole, acc):
-    anchors = rhs_ref.shape[1]
-    take_halves(whole, me_ref[0], held_ref, got_ref)
-    for k in range(anchors // LANES):
-        dinv_ref[:, k * LANES : (k + 1) * LANES] = 1.0 / whole[k : k + 1, anchors:]
-    rhs = rhs_ref[...]
-    vec = rhs - mean_of(rhs) - whole[:, 0:anchors] * dinv_ref[...]
-    acc[...] = gram(pieces(vec), khi_ref, klo_ref, tinv_ref)[1]
-    put_halves(acc, me_ref[0], mine_ref, send_ref)
+    middle = rhs - mean_of(rhs)
+    mid_ref[...] = middle
+    tinv = tinv_ref[...]
+    spread = times(pieces(middle), khi_ref[...], klo_ref[...]) * tinv
+    spread_ref[...] = spread
+    high, low = split2(spread * tinv)
+    row = lax.broadcasted_iota(jnp.int32, (CLASSES, tinv.shape[1]), 0)
+    thigh = tinv.astype(bf16).astype(f32)
+    w_ref[0:CLASSES, :] = high
+    w_ref[CLASSES : 2 * CLASSES, :] = jnp.where(row == 0, thigh, jnp.where(row == 1, tinv - thigh, 0.0)).astype(bf16)
+    w_ref[2 * CLASSES :, :] = low
+    _, other = halves(me_ref, khi_ref.shape[0] // 2)
+    back_degree(w_ref, khi_ref[other, :], klo_ref[other, :], send_ref)
+
+
+def first_own(me_ref, w_ref, khi_ref, klo_ref, mine_ref):
+    own, _ = halves(me_ref, khi_ref.shape[0] // 2)
+    back_degree(w_ref, khi_ref[own, :], klo_ref[own, :], mine_ref)
+
+
+def product_own(me_ref, w_ref, khi_ref, klo_ref, mine_ref):
+    own, _ = halves(me_ref, khi_ref.shape[0] // 2)
+    mine_ref[...] = back_rows(w_ref, khi_ref[own, :], klo_ref[own, :])
+
+
+def residual_part(sums_ref, mid_ref, at, dinv_ref):
+    size = sums_ref.shape[1] - LANES
+    for k in range(size // LANES):
+        dinv_ref[:, k * LANES : (k + 1) * LANES] = 1.0 / sums_ref[k : k + 1, size:]
+    return mid_ref[:, at] - sums_ref[:, 0:size] * dinv_ref[...]
+
+
+def second_own(me_ref, held_ref, mid_ref, khi_ref, klo_ref, part_ref, dinv_ref):
+    own, _ = halves(me_ref, khi_ref.shape[0] // 2)
+    part_ref[...] = times(pieces(residual_part(held_ref, mid_ref, own, dinv_ref)), khi_ref[own, :], klo_ref[own, :])
+
+
+def second_send(me_ref, got_ref, mid_ref, khi_ref, klo_ref, tinv_ref, part_ref, dinv_own, send_ref, w_ref, dinv_ref, dinv_other):
+    own, other = halves(me_ref, khi_ref.shape[0] // 2)
+    rest = times(pieces(residual_part(got_ref, mid_ref, other, dinv_other)), khi_ref[other, :], klo_ref[other, :])
+    dinv_ref[:, own] = dinv_own[...]
+    dinv_ref[:, other] = dinv_other[...]
+    tinv = tinv_ref[...]
+    put_weights(w_ref, (part_ref[...] + rest) * tinv, tinv)
+    send_ref[...] = back_rows(w_ref, khi_ref[other, :], klo_ref[other, :])
+
+
+def label_image(rhs_ref, zhi_ref, zlo_ref, lab_ref):
     zhi, zlo = zhi_ref[...], zlo_ref[...]
-    lab_ref[...] = times_back(times(pieces(rhs), zhi, zlo), zhi, zlo)
-
-
-def third_kernel(na, lab_scale, graph_scale, me_ref, held_ref, got_ref, rhs_ref, lab_ref, spread0_ref,
-                 zhi_ref, zlo_ref, khi_ref, klo_ref, tinv_ref, *refs):
-    (mine_ref, send_ref, direc_ref, part_ref, next_ref), outs, (acc, slots) = refs[0:5], refs[5 : 5 + na], refs[5 + na :]
-    quarter = CLASSES // na
-    me = me_ref[0]
-    take_halves(acc, me, held_ref, got_ref)
-    rhs = rhs_ref[...]
-    image = lab_scale * lab_ref[...] + graph_scale * acc[...] + ridge * rhs
+    lab_ref[...] = times_back(times(pieces(rhs_ref[...]), zhi, zlo), zhi, zlo)
+
+
+def image_shift(lab_scale, lab, rhs):
+    return lab_scale * mean_of(lab) + ridge * mean_of(rhs)
+
+
+def third_own(lab_scale, graph_scale, me_ref, held_ref, rhs_ref, lab_ref, khi_ref, klo_ref, part_ref):
+    own, _ = halves(me_ref, khi_ref.shape[0] // 2)
+    shift = image_shift(lab_scale, lab_ref[...], rhs_ref[...])
+    image = lab_scale * lab_ref[:, own] + graph_scale * held_ref[...] + ridge * rhs_ref[:, own]
+    part_ref[...] = times(pieces(image - shift), khi_ref[own, :], klo_ref[own, :])
+
+
+def third_send(lab_scale, graph_scale, me_ref, held_ref, got_ref, rhs_ref, lab_ref, part_ref, spread0_ref, khi_ref, klo_ref, tinv_ref,
+               send_ref, w_ref, spread_ref, direc_ref, mid_ref, first_ref, stats_ref, whole):
+    own, other = halves(me_ref, khi_ref.shape[0] // 2)
+    rhs, lab = rhs_ref[...], lab_ref[...]
+    whole[:, own] = held_ref[...]
+    whole[:, other] = got_ref[...]
+    image = lab_scale * lab + graph_scale * whole[...] + ridge * rhs
+    shift = image_shift(lab_scale, lab, rhs)
+    whole[...] = image - shift
+    rest = times(pieces(whole[:, other]), khi_ref[other, :], klo_ref[other, :])
     norm = total_of(rhs * rhs)
     alpha = norm / total_of(rhs * image)
     resid = rhs - alpha * image
     after = total_of(resid * resid)
-    direc = resid + (after / norm) * rhs
+    beta = after / norm
+    direc = resid + beta * rhs
+    base = mean_of(rhs)
+    level = (1.0 + beta) * base - alpha * shift
     direc_ref[...] = direc
-    part_ref[...] = alpha * rhs
-    middle = mean_of(direc)
-    spread, out = gram(pieces(direc - middle), khi_ref, klo_ref, tinv_ref)
-    acc[...] = out
-    put_halves(acc, me, mine_ref, send_ref)
-    full = spread + middle
-    part = alpha * spread0_ref[...]
+    mid_ref[...] = direc - level
+    first_ref[...] = alpha * rhs
+    tinv = tinv_ref[...]
+    spread = (1.0 + beta) * spread0_ref[...] - alpha * ((part_ref[...] + rest) * tinv)
+    put_weights(w_ref, spread, tinv)
+    send_ref[...] = back_rows(w_ref, khi_ref[other, :], klo_ref[other, :])
+    spread_ref[...] = spread
+    stats_ref[0:CLASSES, :] = jnp.broadcast_to(level, (CLASSES, LANES))
+    stats_ref[CLASSES : 2 * CLASSES, :] = jnp.broadcast_to(alpha * base, (CLASSES, LANES))
+    stats_ref[2 * CLASSES : 2 * CLASSES + 8, :] = jnp.broadcast_to(alpha, (8, LANES))
+    stats_ref[2 * CLASSES + 8 :, :] = jnp.broadcast_to(after, (8, LANES))
+
+
+def doc_parts(na, lab_scale, me_ref, spread0_ref, spread_ref, stats_ref, direc_ref, zhi_ref, zlo_ref, *refs):
+    outs, (base_ref, slots) = refs[0:na], refs[na:]
+    quarter = CLASSES // na
+    part = stats_ref[2 * CLASSES : 2 * CLASSES + 1, 0:1] * spread0_ref[...] + stats_ref[CLASSES : 2 * CLASSES, 0:1]
+    full = spread_ref[...] + stats_ref[0:CLASSES, 0:1]
     for k in range(na):
         slots[k, 0:quarter, :] = part[k * quarter : (k + 1) * quarter]
         slots[k, quarter : 2 * quarter, :] = full[k * quarter : (k + 1) * quarter]
     for mask in range(na):
-        outs[mask][...] = slots[(me % na) ^ mask]
+        outs[mask][...] = slots[(me_ref[0] % na) ^ mask]
+    direc = direc_ref[...]
     seen = times(pieces(direc), zhi_ref[...], zlo_ref[...])
-    base = lab_scale * total_of(seen * seen) + ridge * total_of(direc * direc)
-    next_ref[0:8, :] = jnp.broadcast_to(after, (8, LANES))
-    next_ref[8:, :] = jnp.broadcast_to(base, (8, LANES))
-
-
-def last_kernel(na, graph_scale, me_ref, held_ref, got_ref, direc_ref, part_ref, next_ref, dinv_ref, *refs):
+    base_ref[...] = jnp.broadcast_to(lab_scale * total_of(seen * seen) + ridge * total_of(direc * direc), base_ref.shape)
+
+
+def last_kernel(na, graph_scale, me_ref, held_ref, got_ref, direc_ref, mid_ref, first_ref, stats_ref, base_ref, dinv_ref, *refs):
     parts, (anchor_ref, doc_ref, whole) = refs[0:na], refs[na:]
-    me = me_ref[0]
-    mine = me % na
-    take_halves(whole, me, held_ref, got_ref)
+    mine = me_ref[0] % na
+    own, other = halves(me_ref, whole.shape[1] // 2)
+    whole[:, own] = held_ref[...]
+    whole[:, other] = got_ref[...]
     prod = whole[...]
-    direc = direc_ref[...]
-    quad = total_of(prod * (direc - mean_of(direc) - prod * dinv_ref[...]))
-    alpha = next_ref[0:1, 0:1] / (next_ref[8:9, 0:1] + graph_scale * quad)
-    whole[...] = part_ref[...] + alpha * direc
+    quad = total_of(prod * (mid_ref[...] - prod * dinv_ref[...]))
+    alpha = stats_ref[2 * CLASSES + 8 : 2 * CLASSES + 9, 0:1] / (base_ref[0:1, 0:1] + graph_scale * quad)
+    whole[...] = first_ref[...] + alpha * direc_ref[...]
     rows = anchor_ref.shape[1]
     anchor_ref[...] = whole[:, pl.ds(pl.multiple_of(mine * rows, rows), rows)]
     quarter, docs = doc_ref.shape[0], parts[0].shape[1]
@@ -405,54 +455,70 @@
         **build,
     )(me, piece[2], piece[3], mine_x, sums, khi, klo, aug)
 
-    long = total + LANES
+    half = total // 2
     flat_sds = sds((CLASSES, total), f32)
-    half_sds = sds((HALF, total), f32)
+    half_sds = sds((CLASSES, half), f32)
+    long_sds = sds((CLASSES, half + LANES), f32)
+    docs_sds = sds((CLASSES, docs), f32)
     z_sds = sds((total, labeled), bf16)
-    acc = pltpu.VMEM((CLASSES, total), f32)
-    work = dict(flops=8 * total * docs * 64, moved=4 * total * docs)
-
-    mine, send, rhs, zhi, zlo, spread = call(
-        functools.partial(first_kernel, na, labs, slots, CLASSES * lab_scale),
+    w_sds = sds((2 * CLASSES, docs), bf16)
+    work = dict(flops=4 * total * docs * 64, moved=2 * total * docs)
+
+    send, w, rhs, middle, zhi, zlo, spread0 = call(
+        functools.partial(first_send, na, labs, slots, CLASSES * lab_scale),
         [SMEM] + [VMEM] * (len(lab_arrays) + 4),
-        [sds((HALF, long), f32)] * 2 + [flat_sds, z_sds, z_sds, sds((CLASSES, docs), f32)],
-        [
-            pltpu.VMEM((labeled, feat + LANES), bf16),
-            pltpu.VMEM((labeled, LANES), f32),
-            pltpu.VMEM((CLASSES, long), f32),
-        ],
+        [long_sds, sds((3 * CLASSES, docs), bf16), flat_sds, flat_sds, z_sds, z_sds, docs_sds],
+        [pltpu.VMEM((labeled, feat + LANES), bf16), pltpu.VMEM((labeled, LANES), f32)],
         **work,
     )(me, *lab_arrays, aug, khi, klo, tinv)
-
-    held, got = reduce_all(mine, send, n_bits)
-    mine, send, dinv, lab = call(
-        second_kernel,
-        [SMEM] + [VMEM] * 8,
-        [half_sds, half_sds, sds((1, total), f32), flat_sds],
-        [pltpu.VMEM((CLASSES, long), f32), acc],
+    got = swap_core(send)
+    mine = call(first_own, [SMEM] + [VMEM] * 3, [long_sds], [], **work)(me, w, khi, klo)[0]
+    held = reduce_chips(mine + got, n_bits)
+    lab = call(label_image, [VMEM] * 3, [flat_sds], [])(rhs, zhi, zlo)[0]
+
+    got = swap_core(held)
+    part, dinv_own = call(
+        second_own, [SMEM] + [VMEM] * 4, [docs_sds, sds((1, half), f32)], [], **work
+    )(me, held, middle, khi, klo)
+    send, w, dinv = call(
+        second_send, [SMEM] + [VMEM] * 7, [half_sds, w_sds, sds((1, total), f32)], [pltpu.VMEM((1, half), f32)], **work
+    )(me, got, middle, khi, klo, tinv, part, dinv_own)
+    got = swap_core(send)
+    mine = call(product_own, [SMEM] + [VMEM] * 3, [half_sds], [], **work)(me, w, khi, klo)[0]
+    held = reduce_chips(mine + got, n_bits)
+
+    got = swap_core(held)
+    part = call(
+        functools.partial(third_own, lab_scale, graph_scale), [SMEM] + [VMEM] * 5, [docs_sds], [], **work
+    )(me, held, rhs, lab, khi, klo)[0]
+    send, w, spread, direc, middle, first, stats = call(
+        functools.partial(third_send, lab_scale, graph_scale),
+        [SMEM] + [VMEM] * 9,
+        [half_sds, w_sds, docs_sds, flat_sds, flat_sds, flat_sds, sds((2 * CLASSES + 16, LANES), f32)],
+        [pltpu.VMEM((CLASSES, total), f32)],
         **work,
-    )(me, held, got, rhs, zhi, zlo, khi, klo, tinv)
-
-    held, got = reduce_all(mine, send, n_bits)
+    )(me, held, got, rhs, lab, part, spread0, khi, klo, tinv)
+    got = swap_core(send)
+    mine = call(product_own, [SMEM] + [VMEM] * 3, [half_sds], [], **work)(me, w, khi, klo)[0]
     part_rows = 2 * CLASSES // na
-    mine, send, direc, part, stats, *docs_out = call(
-        functools.partial(third_kernel, na, lab_scale, graph_scale),
-        [SMEM] + [VMEM] * 10,
-        [half_sds, half_sds, flat_sds, flat_sds, sds((16, LANES), f32)] + [sds((part_rows, docs), f32)] * na,
-        [acc, pltpu.VMEM((na, part_rows, docs), f32)],
-        **work,
-    )(me, held, got, rhs, lab, spread, zhi, zlo, khi, klo, tinv)
-
-    held, got = reduce_all(mine, send, n_bits)
+    *docs_out, base = call(
+        functools.partial(doc_parts, na, lab_scale),
+        [SMEM] + [VMEM] * 6,
+        [sds((part_rows, docs), f32)] * na + [sds((8, LANES), f32)],
+        [pltpu.VMEM((na, part_rows, docs), f32)],
+    )(me, spread0, spread, stats, direc, zhi, zlo)
+    held = reduce_chips(mine + got, n_bits)
+    got = swap_core(held)
+
     parts = [docs_out[0]]
     for mask in range(1, na):
         parts.append(swap(docs_out[mask], mask))
     anchor_scores, doc_scores = call(
         functools.partial(last_kernel, na, graph_scale),
-        [SMEM] + [VMEM] * (6 + na),
+        [SMEM] + [VMEM] * (8 + na),
         [sds((CLASSES, quarter), f32), sds((CLASSES // na, docs_dev), f32)],
-        [acc],
-    )(me, held, got, direc, part, stats, dinv, *parts)
+        [pltpu.VMEM((CLASSES, total), f32)],
+    )(me, held, got, direc, middle, first, stats, base, dinv, *parts)
     return anchor_scores.T, doc_scores
 
 

time: 87.7 us -> 82.6 us (0.942)
  waiting for transfers between devices: 30.5 us -> 24.8 us
    ppermute x34, waiting for transfers between devices: 30.5 us -> 24.8 us  [swap(): return lax.ppermute(value, EVERY, [(i, i ^ mask) for i in range(count)])]
    pallas_call x3 -> x10, Pallas kernels: 13.4 us -> 13.6 us  [the longest x1 3.58 us: run(): call(functools.partial(first_send, na, labs, slots, CLASSES * lab_scale),...]
  transfers between devices with their start and end apart: 34 -> 34, of which waited for: 24 -> 21; matrix products, arithmetic and copies ran while one was open for 0% -> 0% of each run, Pallas kernels for 7% -> 15%
where the time goes in v5:
time: 82.6 us; the launch traced here: 82.4 us
  starting transfers between devices  35.7 us (43%)
  waiting for transfers between devices  24.8 us (30%)
  Pallas kernels  21 us (25%)
  between operations  0.84 us (1%)
    ppermute x34, starting transfers between devices, swap(): return lax.ppermute(value, EVERY, [(i, i ^ mask) for i in range(count)])  35.7 us
    ppermute x34, waiting for transfers between devices, swap(): return lax.ppermute(value, EVERY, [(i, i ^ mask) for i in range(count)])  24.8 us
    pallas_call x1, Pallas kernels, run(): call(functools.partial(first_send, na, labs, slots, CLASSES * lab_scale),...  3.58 us
    pallas_call x2, Pallas kernels, run(): call(product_own, [SMEM] + [VMEM] * 3, [half_sds], [], **work)  2.47 us
    pallas_call x1, Pallas kernels, run(): call(functools.partial(build_far, na), [SMEM] + [VMEM] * 7, [k_sds, k_sds...  2.25 us
    pallas_call x1, Pallas kernels, run(): call(functools.partial(build_near, na), [SMEM] + [VMEM] * 3, [k_sds, k_sd...  2.22 us
    pallas_call x1, Pallas kernels, run(): pl.pallas_call(functools.partial(label_kernel, na), grid_spec=pltpu.Prefe...  2.06 us
    pallas_call x1, Pallas kernels, run(): call(functools.partial(third_send, lab_scale, graph_scale), [SMEM] + [VME...  1.96 us
  transfers between devices with their start and end apart: 34, of which 21 were waited for; matrix products, arithmetic and copies ran while one was open for 0% of the time, Pallas kernels for 15%

profile of v5, /device:TPU:0, one launch (start us, length us, event | category | flops | bytes accessed | tf_op | source)
XLA Modules:
  0.0 82.4 jit_solution(16226633138634946936)
XLA Ops:
  0.6 0.6 collective-permute-start.6
  1.2 2.6 %collective-permute-start.4 = (bf16[256,128]{1,0:T(8,128)(2,1)}, bf16[256,128]{1,0:T(8,128)(2,1)S(1)}, u32[]{:S(2)}, u32[]{:S(2)}) collective-permute-start(bf16[256,128]{1,0:T(8,128)(2,1)} %anch_ref.1), channel_id=1, source_target_pairs={{0,2},{1,3},{2,0},{3,1},{4,6},{5,7},{6,4},{7,5},{8,10},{9,11},{10,... | collective-permute-start | bytes 196616 | tf_op jit(solution)/shard_map/ppermute | solution.py:35
  3.7 2.1 %label_rows.1 = (bf16[32,128]{1,0:T(8,128)(2,1)S(1)}, bf16[2048,128]{1,0:T(8,128)(2,1)S(1)}, bf16[256,128]{1,0:T(8,128)(2,1)S(1)}) custom-call(s32[1]{0:T(128)} %bitcast.me_ref, s32[16]{0:T(128)} %idx_ref.1, s32[16]{0:T(128)} %cls_ref.1, bf16[8192,128]{1,0:T(8,128)(2,1)} %feat_ref.1, bf16[256,128]{1,0:T(8,128)(2,1)} %anch_ref.1), custom_call_target="tpu_custom_call" | custom-call | tf_op jit(solution)/shard_map/label_rows/pallas_call | solution.py:409
  5.8 1.6 %collective-permute-start = (bf16[32,128]{1,0:T(8,128)(2,1)S(1)}, bf16[32,128]{1,0:T(8,128)(2,1)S(1)}, u32[]{:S(2)}, u32[]{:S(2)}) collective-permute-start(bf16[32,128]{1,0:T(8,128)(2,1)S(1)} %get-tuple-element.39), channel_id=1, source_target_pairs={{0,4},{1,5},{2,6},{3,7},{4,0},{5,1},{6,2},{7,3},{8,12},{9,13},{10,... | collective-permute-start | bytes 24584 | tf_op jit(solution)/shard_map/ppermute | solution.py:35
  7.4 2.1 %collective-permute-done = bf16[32,128]{1,0:T(8,128)(2,1)S(1)} collective-permute-done((bf16[32,128]{1,0:T(8,128)(2,1)S(1)}, bf16[32,128]{1,0:T(8,128)(2,1)S(1)}, u32[]{:S(2)}, u32[]{:S(2)}) %collective-permute-start) | collective-permute-done | bytes 8224 | tf_op jit(solution)/shard_map/ppermute | solution.py:35
  9.5 1.6 %collective-permute-start.1 = (bf16[64,128]{1,0:T(8,128)(2,1)S(1)}, bf16[64,128]{1,0:T(8,128)(2,1)S(1)}, u32[]{:S(2)}, u32[]{:S(2)}) collective-permute-start(bf16[64,128]{1,0:T(8,128)(2,1)S(1)} %constant_dynamic-update-slice_fusion.refs_0_), channel_id=1, source_target_pairs={{0,8},{1,9},{2,10},{3,11},{4,12},{5,13},{6,14},{7,15},{8,0},{9,1},... | collective-permute-start | bytes 49160 | tf_op jit(solution)/shard_map/ppermute | solution.py:35
  11.1 2.6 %collective-permute-start.2 = (bf16[64,128]{1,0:T(8,128)(2,1)S(1)}, bf16[64,128]{1,0:T(8,128)(2,1)S(1)}, u32[]{:S(2)}, u32[]{:S(2)}) collective-permute-start(bf16[64,128]{1,0:T(8,128)(2,1)S(1)} %constant_dynamic-update-slice_fusion.refs_0_), channel_id=1, source_target_pairs={{0,16},{1,17},{2,18},{3,19},{4,20},{5,21},{6,22},{7,23},{8,24},{9,... | collective-permute-start | bytes 49160 | tf_op jit(solution)/shard_map/ppermute | solution.py:35
  13.7 0.2 collective-permute-start.3
  13.9 2.2 %shard_map.59 = (bf16[1024,2048]{1,0:T(8,128)(2,1)S(1)}, bf16[1024,2048]{1,0:T(8,128)(2,1)S(1)}, bf16[1024,256]{1,0:T(8,128)(2,1)S(1)}, f32[8,2048]{1,0:T(8,128)S(1)}) custom-call(s32[1]{0:T(128)} %bitcast.me_ref, bf16[256,128]{1,0:T(8,128)(2,1)S(1)} %get-tuple-element.41.a0, bf16[256,128]{1,0:T(8,128)(2,1)S(1)} %collective-permute-done.6.a1, ...), custom_call_target="tpu_custom_call" | custom-call | flops 536870912 | bytes 4194304 | tf_op jit(solution)/shard_map/pallas_call | solution.py:446
  16.2 2.2 %shard_map.60 = (bf16[1024,2048]{1,0:T(8,128)(2,1)S(1)}, bf16[1024,2048]{1,0:T(8,128)(2,1)S(1)}, bf16[1024,256]{1,0:T(8,128)(2,1)S(1)}, f32[1,2048]{1,0:T(1,128)S(1)}) custom-call(s32[1]{0:T(128)} %bitcast.me_ref, bf16[256,128]{1,0:T(8,128)(2,1)S(1)} %collective-permute-done.4.a2, ...), custom_call_target="tpu_custom_call", output_to_operand_aliasing={{0}: (5, {}), {1}: (6, {}), {2}: (7, {})} | custom-call | flops 536870912 | bytes 4194304 | tf_op jit(solution)/shard_map/pallas_call | solution.py:449
  18.4 0.8 collective-permute-done.3.refs_3_
  19.2 3.6 %shard_map.61 = (f32[16,640]{1,0:T(8,128)S(1)}, bf16[48,2048]{1,0:T(8,128)(2,1)S(1)}, f32[16,1024]{1,0:T(8,128)S(1)}, f32[16,1024]{1,0:T(8,128)S(1)}, bf16[1024,...) custom-call(s32[1]{0:T(128)} %bitcast.me_ref, ...), custom_call_target="tpu_custom_call" | custom-call | flops 536870912 | bytes 4194304 | tf_op jit(solution)/shard_map/pallas_call | solution.py:467
  22.8 1.3 %shard_map.62 = f32[16,640]{1,0:T(8,128)S(1)} custom-call(s32[1]{0:T(128)} %bitcast.me_ref, bf16[48,2048]{1,0:T(8,128)(2,1)S(1)} %get-tuple-element.50.w_ref, bf16[1024,2048]{1,0:T(8,128)(2,1)S(1)} %get-tuple-element.47.refs_5_.khi_ref, bf16[1024,2048]{1,0:T(8,128)(2,1)S(1)} %get-tuple-element.48.refs_6_.klo_ref), custom_call_target="tpu_custom_call" | custom-call | flops 536870912 | bytes 4194304 | tf_op jit(solution)/shard_map/pallas_call | solution.py:475
  24.2 1.6 %collective-permute-start.10 = (f32[16,640]{1,0:T(8,128)S(1)}, f32[16,640]{1,0:T(8,128)S(1)}, u32[]{:S(2)}, u32[]{:S(2)}) collective-permute-start(f32[16,640]{1,0:T(8,128)S(1)} %add.67), channel_id=1, source_target_pairs={{0,6},{1,7},{2,4},{3,5},{4,2},{5,3},{6,0},{7,1},{8,14},{9,15},{10,... | collective-permute-start | bytes 122888 | tf_op jit(solution)/shard_map/ppermute | solution.py:35
  25.8 1.5 %collective-permute-start.8 = (f32[16,640]{1,0:T(8,128)S(1)}, f32[16,640]{1,0:T(8,128)S(1)}, u32[]{:S(2)}, u32[]{:S(2)}) collective-permute-start(f32[16,640]{1,0:T(8,128)S(1)} %add.67), channel_id=1, source_target_pairs={{0,2},{1,3},{2,0},{3,1},{4,6},{5,7},{6,4},{7,5},{8,10},{9,11},{10,... | collective-permute-start | bytes 122888 | tf_op jit(solution)/shard_map/ppermute | solution.py:35
  27.3 0.5 collective-permute-start.9
  27.8 1.8 %collective-permute-done.10 = f32[16,640]{1,0:T(8,128)S(1)} collective-permute-done((f32[16,640]{1,0:T(8,128)S(1)}, f32[16,640]{1,0:T(8,128)S(1)}, u32[]{:S(2)}, u32[]{:S(2)}) %collective-permute-start.10) | collective-permute-done | bytes 40992 | tf_op jit(solution)/shard_map/ppermute | solution.py:35
  29.6 0.5 collective-permute-done.8
  30.1 1.2 %collective-permute-done.9 = f32[16,640]{1,0:T(8,128)S(1)} collective-permute-done((f32[16,640]{1,0:T(8,128)S(1)}, f32[16,640]{1,0:T(8,128)S(1)}, u32[]{:S(2)}, u32[]{:S(2)}) %collective-permute-start.9) | collective-permute-done | bytes 40992 | tf_op jit(solution)/shard_map/ppermute | solution.py:35
  31.3 0.1 collective-permute-start.11
  31.4 3.4 %collective-permute-start.12 = (f32[16,640]{1,0:T(8,128)S(1)}, f32[16,640]{1,0:T(8,128)S(1)}, u32[]{:S(2)}, u32[]{:S(2)}) collective-permute-start(f32[16,640]{1,0:T(8,128)S(1)} %add_add_fusion.1), channel_id=1, source_target_pairs={{0,16},{1,17},{2,18},{3,19},{4,20},{5,21},{6,22},{7,23},{8,24},{9,... | collective-permute-start | bytes 122888 | tf_op jit(solution)/shard_map/ppermute | solution.py:35
  34.7 1.0 %collective-permute-start.13 = (f32[16,640]{1,0:T(8,128)S(1)}, f32[16,640]{1,0:T(8,128)S(1)}, u32[]{:S(2)}, u32[]{:S(2)}) collective-permute-start(f32[16,640]{1,0:T(8,128)S(1)} %add_add_fusion.1), channel_id=1, source_target_pairs={{0,24},{1,25},{2,26},{3,27},{4,28},{5,29},{6,30},{7,31},{8,16},{9,... | collective-permute-start | bytes 122888 | tf_op jit(solution)/shard_map/ppermute | solution.py:35
  35.7 1.0 %collective-permute-done.12 = f32[16,640]{1,0:T(8,128)S(1)} collective-permute-done((f32[16,640]{1,0:T(8,128)S(1)}, f32[16,640]{1,0:T(8,128)S(1)}, u32[]{:S(2)}, u32[]{:S(2)}) %collective-permute-start.12) | collective-permute-done | bytes 40992 | tf_op jit(solution)/shard_map/ppermute | solution.py:35
  36.7 3.8 %collective-permute-done.13 = f32[16,640]{1,0:T(8,128)S(1)} collective-permute-done((f32[16,640]{1,0:T(8,128)S(1)}, f32[16,640]{1,0:T(8,128)S(1)}, u32[]{:S(2)}, u32[]{:S(2)}) %collective-permute-start.13) | collective-permute-done | bytes 40992 | tf_op jit(solution)/shard_map/ppermute | solution.py:35
  40.6 0.1 collective-permute-start.14
  40.6 0.7 shard_map.63
  41.3 0.5 collective-permute-done.14.got_ref
  41.8 1.9 %shard_map.64 = (f32[16,512]{1,0:T(8,128)S(1)}, bf16[32,2048]{1,0:T(8,128)(2,1)S(1)}, f32[1,1024]{1,0:T(1,128)S(1)}) custom-call(s32[1]{0:T(128)} %bitcast.me_ref, f32[16,640]{1,0:T(8,128)S(1)} %collective-permute-done.14.got_ref, f32[16,1024]{1,0:T(8,128)S(1)} %get-tuple-element.52.mid_ref, bf16[1024,2048]{1,0:T(8,128)(2,1)S(1)} %get-tuple-element.47.refs_5_.khi_ref, ...), custom_call_target="tpu_custom_call" | custom-call | flops 536870912 | bytes 4194304 | tf_op jit(solution)/shard_map/pallas_call | solution.py:483
  43.7 0.2 collective-permute-start.15
  43.9 1.2 %shard_map.65 = f32[16,512]{1,0:T(8,128)S(1)} custom-call(s32[1]{0:T(128)} %bitcast.me_ref, bf16[32,2048]{1,0:T(8,128)(2,1)S(1)} %get-tuple-element.55.w_ref, bf16[1024,2048]{1,0:T(8,128)(2,1)S(1)} %get-tuple-element.47.refs_5_.khi_ref, bf16[1024,2048]{1,0:T(8,128)(2,1)S(1)} %get-tuple-element.48.refs_6_.klo_ref), custom_call_target="tpu_custom_call" | custom-call | flops 536870912 | bytes 4194304 | tf_op jit(solution)/shard_map/pallas_call | solution.py:487
  45.1 0.6 collective-permute-start.16
  45.7 0.5 collective-permute-start.17
  46.3 2.4 %collective-permute-start.18 = (f32[16,512]{1,0:T(8,128)S(1)}, f32[16,512]{1,0:T(8,128)S(1)}, u32[]{:S(2)}, u32[]{:S(2)}) collective-permute-start(f32[16,512]{1,0:T(8,128)S(1)} %add.74), channel_id=1, source_target_pairs={{0,6},{1,7},{2,4},{3,5},{4,2},{5,3},{6,0},{7,1},{8,14},{9,15},{10,... | collective-permute-start | bytes 98312 | tf_op jit(solution)/shard_map/ppermute | solution.py:35
  48.7 0.4 collective-permute-done.16
  49.1 0.9 %collective-permute-done.17 = f32[16,512]{1,0:T(8,128)S(1)} collective-permute-done((f32[16,512]{1,0:T(8,128)S(1)}, f32[16,512]{1,0:T(8,128)S(1)}, u32[]{:S(2)}, u32[]{:S(2)}) %collective-permute-start.17) | collective-permute-done | bytes 32800 | tf_op jit(solution)/shard_map/ppermute | solution.py:35
  50.0 1.1 %collective-permute-done.18 = f32[16,512]{1,0:T(8,128)S(1)} collective-permute-done((f32[16,512]{1,0:T(8,128)S(1)}, f32[16,512]{1,0:T(8,128)S(1)}, u32[]{:S(2)}, u32[]{:S(2)}) %collective-permute-start.18) | collective-permute-done | bytes 32800 | tf_op jit(solution)/shard_map/ppermute | solution.py:35
  51.1 0.1 collective-permute-start.19
  51.2 1.5 %collective-permute-start.20 = (f32[16,512]{1,0:T(8,128)S(1)}, f32[16,512]{1,0:T(8,128)S(1)}, u32[]{:S(2)}, u32[]{:S(2)}) collective-permute-start(f32[16,512]{1,0:T(8,128)S(1)} %add_add_fusion.5), channel_id=1, source_target_pairs={{0,16},{1,17},{2,18},{3,19},{4,20},{5,21},{6,22},{7,23},{8,24},{9,... | collective-permute-start | bytes 98312 | tf_op jit(solution)/shard_map/ppermute | solution.py:35
  52.7 2.8 %collective-permute-start.21 = (f32[16,512]{1,0:T(8,128)S(1)}, f32[16,512]{1,0:T(8,128)S(1)}, u32[]{:S(2)}, u32[]{:S(2)}) collective-permute-start(f32[16,512]{1,0:T(8,128)S(1)} %add_add_fusion.5), channel_id=1, source_target_pairs={{0,24},{1,25},{2,26},{3,27},{4,28},{5,29},{6,30},{7,31},{8,16},{9,... | collective-permute-start | bytes 98312 | tf_op jit(solution)/shard_map/ppermute | solution.py:35
  55.5 0.4 shard_map.66.lab_ref
  56.0 0.1 collective-permute-done.20
  56.0 2.4 %collective-permute-done.21 = f32[16,512]{1,0:T(8,128)S(1)} collective-permute-done((f32[16,512]{1,0:T(8,128)S(1)}, f32[16,512]{1,0:T(8,128)S(1)}, u32[]{:S(2)}, u32[]{:S(2)}) %collective-permute-start.21) | collective-permute-done | bytes 32800 | tf_op jit(solution)/shard_map/ppermute | solution.py:35
  58.4 0.1 collective-permute-start.22
  58.5 1.0 %shard_map.67.part_ref = f32[16,2048]{1,0:T(8,128)S(1)} custom-call(s32[1]{0:T(128)} %bitcast.me_ref, f32[16,512]{1,0:T(8,128)S(1)} %add_add_fusion.4.held_ref, f32[16,1024]{1,0:T(8,128)S(1)} %get-tuple-element.57.rhs_ref, f32[16,1024]{1,0:T(8,128)S(1)} %shard_map.66.lab_ref, bf16[1024,2048]{1,0:T(8,128)(2,1)S(1)} %get-tuple-element.47.refs_5_.khi_ref, ...), custom_call_target="tpu_custom_call" | custom-call | flops 536870912 | bytes 4194304 | tf_op jit(solution)/shard_map/pallas_call | solution.py:491
  59.5 0.2 collective-permute-done.22.got_ref
  59.7 2.0 %shard_map.68 = (f32[16,512]{1,0:T(8,128)S(1)}, bf16[32,2048]{1,0:T(8,128)(2,1)S(1)}, f32[16,2048]{1,0:T(8,128)S(1)}, f32[16,1024]{1,0:T(8,128)S(1)}, f32[16,102...) custom-call(s32[1]{0:T(128)} %bitcast.me_ref, f32[16,512]{1,0:T(8,128)S(1)} %add_add_fusion.4.held_ref, ...), custom_call_target="tpu_custom_call" | custom-call | flops 536870912 | bytes 4194304 | tf_op jit(solution)/shard_map/pallas_call | solution.py:494
  61.7 0.3 collective-permute-start.23
  62.0 1.2 %shard_map.69 = f32[16,512]{1,0:T(8,128)S(1)} custom-call(s32[1]{0:T(128)} %bitcast.me_ref, bf16[32,2048]{1,0:T(8,128)(2,1)S(1)} %get-tuple-element.61.w_ref, bf16[1024,2048]{1,0:T(8,128)(2,1)S(1)} %get-tuple-element.47.refs_5_.khi_ref, bf16[1024,2048]{1,0:T(8,128)(2,1)S(1)} %get-tuple-element.48.refs_6_.klo_ref), custom_call_target="tpu_custom_call" | custom-call | flops 536870912 | bytes 4194304 | tf_op jit(solution)/shard_map/pallas_call | solution.py:502
  63.2 1.6 %collective-permute-start.24 = (f32[16,512]{1,0:T(8,128)S(1)}, f32[16,512]{1,0:T(8,128)S(1)}, u32[]{:S(2)}, u32[]{:S(2)}) collective-permute-start(f32[16,512]{1,0:T(8,128)S(1)} %add.81), channel_id=1, source_target_pairs={{0,2},{1,3},{2,0},{3,1},{4,6},{5,7},{6,4},{7,5},{8,10},{9,11},{10,... | collective-permute-start | bytes 98312 | tf_op jit(solution)/shard_map/ppermute | solution.py:35
  64.8 1.5 %collective-permute-start.25 = (f32[16,512]{1,0:T(8,128)S(1)}, f32[16,512]{1,0:T(8,128)S(1)}, u32[]{:S(2)}, u32[]{:S(2)}) collective-permute-start(f32[16,512]{1,0:T(8,128)S(1)} %add.81), channel_id=1, source_target_pairs={{0,4},{1,5},{2,6},{3,7},{4,0},{5,1},{6,2},{7,3},{8,12},{9,13},{10,... | collective-permute-start | bytes 98312 | tf_op jit(solution)/shard_map/ppermute | solution.py:35
  66.3 0.5 collective-permute-start.26
  66.8 0.4 collective-permute-done.24
  67.2 1.5 %collective-permute-done.25 = f32[16,512]{1,0:T(8,128)S(1)} collective-permute-done((f32[16,512]{1,0:T(8,128)S(1)}, f32[16,512]{1,0:T(8,128)S(1)}, u32[]{:S(2)}, u32[]{:S(2)}) %collective-permute-start.25) | collective-permute-done | bytes 32800 | tf_op jit(solution)/shard_map/ppermute | solution.py:35
  68.7 2.4 %collective-permute-done.26 = f32[16,512]{1,0:T(8,128)S(1)} collective-permute-done((f32[16,512]{1,0:T(8,128)S(1)}, f32[16,512]{1,0:T(8,128)S(1)}, u32[]{:S(2)}, u32[]{:S(2)}) %collective-permute-start.26) | collective-permute-done | bytes 32800 | tf_op jit(solution)/shard_map/ppermute | solution.py:35
  71.2 3.4 %collective-permute-start.28 = (f32[16,512]{1,0:T(8,128)S(1)}, f32[16,512]{1,0:T(8,128)S(1)}, u32[]{:S(2)}, u32[]{:S(2)}) collective-permute-start(f32[16,512]{1,0:T(8,128)S(1)} %add_add_fusion.3), channel_id=1, source_target_pairs={{0,16},{1,17},{2,18},{3,19},{4,20},{5,21},{6,22},{7,23},{8,24},{9,... | collective-permute-start | bytes 98312 | tf_op jit(solution)/shard_map/ppermute | solution.py:35
  74.6 1.0 %collective-permute-start.29 = (f32[16,512]{1,0:T(8,128)S(1)}, f32[16,512]{1,0:T(8,128)S(1)}, u32[]{:S(2)}, u32[]{:S(2)}) collective-permute-start(f32[16,512]{1,0:T(8,128)S(1)} %add_add_fusion.3), channel_id=1, source_target_pairs={{0,24},{1,25},{2,26},{3,27},{4,28},{5,29},{6,30},{7,31},{8,16},{9,... | collective-permute-start | bytes 98312 | tf_op jit(solution)/shard_map/ppermute | solution.py:35
  75.6 0.3 shard_map.70
  76.0 0.6 collective-permute-start.32
  76.6 1.2 %collective-permute-start.33 = (f32[8,2048]{1,0:T(8,128)S(1)}, f32[8,2048]{1,0:T(8,128)S(1)}, u32[]{:S(2)}, u32[]{:S(2)}) collective-permute-start(f32[8,2048]{1,0:T(8,128)S(1)} %get-tuple-element.73), channel_id=1, source_target_pairs={{0,3},{1,2},{2,1},{3,0},{4,7},{5,6},{6,5},{7,4},{8,11},{9,10},{10,... | collective-permute-start | bytes 196616 | tf_op jit(solution)/shard_map/ppermute | solution.py:35
  77.8 2.5 %collective-permute-done.29 = f32[16,512]{1,0:T(8,128)S(1)} collective-permute-done((f32[16,512]{1,0:T(8,128)S(1)}, f32[16,512]{1,0:T(8,128)S(1)}, u32[]{:S(2)}, u32[]{:S(2)}) %collective-permute-start.29) | collective-permute-done | bytes 32800 | tf_op jit(solution)/shard_map/ppermute | solution.py:35
  80.4 0.6 collective-permute-done.32.refs_2_
  81.0 0.3 collective-permute-done.33.refs_3_
  81.3 0.2 collective-permute-done.30.got_ref
  81.6 0.8 %shard_map.71 = (f32[16,256]{1,0:T(8,128)}, f32[4,8192]{1,0:T(4,128)}) custom-call(s32[1]{0:T(128)} %bitcast.me_ref, f32[16,512]{1,0:T(8,128)S(1)} %add_add_fusion.2.held_ref, f32[16,512]{1,0:T(8,128)S(1)} %collective-permute-done.30.got_ref, f32[16,1024]{1,0:T(8,128)S(1)} %get-tuple-element.63.direc_ref, f32[16,1024]{1,0:T(8,128)S(1)} %get-tuple-element.64.mid_ref, ...), custom_call_target="tpu_custom_call" | custom-call | flops 1048576 | bytes 262144 | tf_op jit(solution)/shard_map/pallas_call | solution.py:516
  (29 shorter events, 0.4 us)
Async XLA Ops:
  0.6 13.3 %collective-permute-start.6 = (bf16[256,128]{1,0:T(8,128)(2,1)}, bf16[256,128]{1,0:T(8,128)(2,1)S(1)}, u32[]{:S(2)}, u32[]{:S(2)}) collective-permute-start(bf16[256,128]{1,0:T(8,128)(2,1)} %anch_ref.1), channel_id=1, source_target_pairs={{0,1},{1,0},{2,3},{3,2},{4,5},{5,4},{6,7},{7,6},{8,9},{9,8},{10,11... | collective-permute-start | bytes 196616 | tf_op jit(solution)/shard_map/ppermute | solution.py:35
  1.2 6.2 %collective-permute-start.4 = (bf16[256,128]{1,0:T(8,128)(2,1)}, bf16[256,128]{1,0:T(8,128)(2,1)S(1)}, u32[]{:S(2)}, u32[]{:S(2)}) collective-permute-start(bf16[256,128]{1,0:T(8,128)(2,1)} %anch_ref.1), channel_id=1, source_target_pairs={{0,2},{1,3},{2,0},{3,1},{4,6},{5,7},{6,4},{7,5},{8,10},{9,11},{10,... | collective-permute-start | bytes 196616 | tf_op jit(solution)/shard_map/ppermute | solution.py:35
  5.8 3.7 %collective-permute-start = (bf16[32,128]{1,0:T(8,128)(2,1)S(1)}, bf16[32,128]{1,0:T(8,128)(2,1)S(1)}, u32[]{:S(2)}, u32[]{:S(2)}) collective-permute-start(bf16[32,128]{1,0:T(8,128)(2,1)S(1)} %get-tuple-element.39), channel_id=1, source_target_pairs={{0,4},{1,5},{2,6},{3,7},{4,0},{5,1},{6,2},{7,3},{8,12},{9,13},{10,... | collective-permute-start | bytes 24584 | tf_op jit(solution)/shard_map/ppermute | solution.py:35
  7.4 8.8 %collective-permute-start.5 = (bf16[256,128]{1,0:T(8,128)(2,1)S(1)}, bf16[256,128]{1,0:T(8,128)(2,1)S(1)}, u32[]{:S(2)}, u32[]{:S(2)}) collective-permute-start(bf16[256,128]{1,0:T(8,128)(2,1)S(1)} %collective-permute-done.4.a2), channel_id=1, source_target_pairs={{0,1},{1,0},{2,3},{3,2},{4,5},{5,4},{6,7},{7,6},{8,9},{9,8},{10,11... | collective-permute-start | bytes 196616 | tf_op jit(solution)/shard_map/ppermute | solution.py:35
  9.5 8.9 %collective-permute-start.1 = (bf16[64,128]{1,0:T(8,128)(2,1)S(1)}, bf16[64,128]{1,0:T(8,128)(2,1)S(1)}, u32[]{:S(2)}, u32[]{:S(2)}) collective-permute-start(bf16[64,128]{1,0:T(8,128)(2,1)S(1)} %constant_dynamic-update-slice_fusion.refs_0_), channel_id=1, source_target_pairs={{0,8},{1,9},{2,10},{3,11},{4,12},{5,13},{6,14},{7,15},{8,0},{9,1},... | collective-permute-start | bytes 49160 | tf_op jit(solution)/shard_map/ppermute | solution.py:35
  11.1 7.3 %collective-permute-start.2 = (bf16[64,128]{1,0:T(8,128)(2,1)S(1)}, bf16[64,128]{1,0:T(8,128)(2,1)S(1)}, u32[]{:S(2)}, u32[]{:S(2)}) collective-permute-start(bf16[64,128]{1,0:T(8,128)(2,1)S(1)} %constant_dynamic-update-slice_fusion.refs_0_), channel_id=1, source_target_pairs={{0,16},{1,17},{2,18},{3,19},{4,20},{5,21},{6,22},{7,23},{8,24},{9,... | collective-permute-start | bytes 49160 | tf_op jit(solution)/shard_map/ppermute | solution.py:35
  13.7 5.5 %collective-permute-start.3 = (bf16[64,128]{1,0:T(8,128)(2,1)S(1)}, bf16[64,128]{1,0:T(8,128)(2,1)S(1)}, u32[]{:S(2)}, u32[]{:S(2)}) collective-permute-start(bf16[64,128]{1,0:T(8,128)(2,1)S(1)} %constant_dynamic-update-slice_fusion.refs_0_), channel_id=1, source_target_pairs={{0,24},{1,25},{2,26},{3,27},{4,28},{5,29},{6,30},{7,31},{8,16},{9,... | collective-permute-start | bytes 49160 | tf_op jit(solution)/shard_map/ppermute | solution.py:35
  22.8 1.4 %collective-permute-start.7 = (f32[16,640]{1,0:T(8,128)S(1)}, f32[16,640]{1,0:T(8,128)S(1)}, u32[]{:S(2)}, u32[]{:S(2)}) collective-permute-start(f32[16,640]{1,0:T(8,128)S(1)} %get-tuple-element.51), channel_id=1, source_target_pairs={{0,1},{1,0},{2,3},{3,2},{4,5},{5,4},{6,7},{7,6},{8,9},{9,8},{10,11... | collective-permute-start | bytes 122888 | tf_op jit(solution)/shard_map/ppermute | solution.py:35
  24.2 5.4 %collective-permute-start.10 = (f32[16,640]{1,0:T(8,128)S(1)}, f32[16,640]{1,0:T(8,128)S(1)}, u32[]{:S(2)}, u32[]{:S(2)}) collective-permute-start(f32[16,640]{1,0:T(8,128)S(1)} %add.67), channel_id=1, source_target_pairs={{0,6},{1,7},{2,4},{3,5},{4,2},{5,3},{6,0},{7,1},{8,14},{9,15},{10,... | collective-permute-start | bytes 122888 | tf_op jit(solution)/shard_map/ppermute | solution.py:35
  25.8 4.3 %collective-permute-start.8 = (f32[16,640]{1,0:T(8,128)S(1)}, f32[16,640]{1,0:T(8,128)S(1)}, u32[]{:S(2)}, u32[]{:S(2)}) collective-permute-start(f32[16,640]{1,0:T(8,128)S(1)} %add.67), channel_id=1, source_target_pairs={{0,2},{1,3},{2,0},{3,1},{4,6},{5,7},{6,4},{7,5},{8,10},{9,11},{10,... | collective-permute-start | bytes 122888 | tf_op jit(solution)/shard_map/ppermute | solution.py:35
  27.3 4.0 %collective-permute-start.9 = (f32[16,640]{1,0:T(8,128)S(1)}, f32[16,640]{1,0:T(8,128)S(1)}, u32[]{:S(2)}, u32[]{:S(2)}) collective-permute-start(f32[16,640]{1,0:T(8,128)S(1)} %add.67), channel_id=1, source_target_pairs={{0,4},{1,5},{2,6},{3,7},{4,0},{5,1},{6,2},{7,3},{8,12},{9,13},{10,... | collective-permute-start | bytes 122888 | tf_op jit(solution)/shard_map/ppermute | solution.py:35
  31.3 4.5 %collective-permute-start.11 = (f32[16,640]{1,0:T(8,128)S(1)}, f32[16,640]{1,0:T(8,128)S(1)}, u32[]{:S(2)}, u32[]{:S(2)}) collective-permute-start(f32[16,640]{1,0:T(8,128)S(1)} %add_add_fusion.1), channel_id=1, source_target_pairs={{0,8},{1,9},{2,10},{3,11},{4,12},{5,13},{6,14},{7,15},{8,0},{9,1},... | collective-permute-start | bytes 122888 | tf_op jit(solution)/shard_map/ppermute | solution.py:35
  31.4 5.4 %collective-permute-start.12 = (f32[16,640]{1,0:T(8,128)S(1)}, f32[16,640]{1,0:T(8,128)S(1)}, u32[]{:S(2)}, u32[]{:S(2)}) collective-permute-start(f32[16,640]{1,0:T(8,128)S(1)} %add_add_fusion.1), channel_id=1, source_target_pairs={{0,16},{1,17},{2,18},{3,19},{4,20},{5,21},{6,22},{7,23},{8,24},{9,... | collective-permute-start | bytes 122888 | tf_op jit(solution)/shard_map/ppermute | solution.py:35
  34.7 5.8 %collective-permute-start.13 = (f32[16,640]{1,0:T(8,128)S(1)}, f32[16,640]{1,0:T(8,128)S(1)}, u32[]{:S(2)}, u32[]{:S(2)}) collective-permute-start(f32[16,640]{1,0:T(8,128)S(1)} %add_add_fusion.1), channel_id=1, source_target_pairs={{0,24},{1,25},{2,26},{3,27},{4,28},{5,29},{6,30},{7,31},{8,16},{9,... | collective-permute-start | bytes 122888 | tf_op jit(solution)/shard_map/ppermute | solution.py:35
  40.6 1.3 %collective-permute-start.14 = (f32[16,640]{1,0:T(8,128)S(1)}, f32[16,640]{1,0:T(8,128)S(1)}, u32[]{:S(2)}, u32[]{:S(2)}) collective-permute-start(f32[16,640]{1,0:T(8,128)S(1)} %add_add_fusion.held_ref), channel_id=1, source_target_pairs={{0,1},{1,0},{2,3},{3,2},{4,5},{5,4},{6,7},{7,6},{8,9},{9,8},{10,11... | collective-permute-start | bytes 122888 | tf_op jit(solution)/shard_map/ppermute | solution.py:35
  43.7 1.4 %collective-permute-start.15 = (f32[16,512]{1,0:T(8,128)S(1)}, f32[16,512]{1,0:T(8,128)S(1)}, u32[]{:S(2)}, u32[]{:S(2)}) collective-permute-start(f32[16,512]{1,0:T(8,128)S(1)} %get-tuple-element.56), channel_id=1, source_target_pairs={{0,1},{1,0},{2,3},{3,2},{4,5},{5,4},{6,7},{7,6},{8,9},{9,8},{10,11... | collective-permute-start | bytes 98312 | tf_op jit(solution)/shard_map/ppermute | solution.py:35
  45.1 4.0 %collective-permute-start.16 = (f32[16,512]{1,0:T(8,128)S(1)}, f32[16,512]{1,0:T(8,128)S(1)}, u32[]{:S(2)}, u32[]{:S(2)}) collective-permute-start(f32[16,512]{1,0:T(8,128)S(1)} %add.74), channel_id=1, source_target_pairs={{0,2},{1,3},{2,0},{3,1},{4,6},{5,7},{6,4},{7,5},{8,10},{9,11},{10,... | collective-permute-start | bytes 98312 | tf_op jit(solution)/shard_map/ppermute | solution.py:35
  45.7 4.3 %collective-permute-start.17 = (f32[16,512]{1,0:T(8,128)S(1)}, f32[16,512]{1,0:T(8,128)S(1)}, u32[]{:S(2)}, u32[]{:S(2)}) collective-permute-start(f32[16,512]{1,0:T(8,128)S(1)} %add.74), channel_id=1, source_target_pairs={{0,4},{1,5},{2,6},{3,7},{4,0},{5,1},{6,2},{7,3},{8,12},{9,13},{10,... | collective-permute-start | bytes 98312 | tf_op jit(solution)/shard_map/ppermute | solution.py:35
  46.3 4.8 %collective-permute-start.18 = (f32[16,512]{1,0:T(8,128)S(1)}, f32[16,512]{1,0:T(8,128)S(1)}, u32[]{:S(2)}, u32[]{:S(2)}) collective-permute-start(f32[16,512]{1,0:T(8,128)S(1)} %add.74), channel_id=1, source_target_pairs={{0,6},{1,7},{2,4},{3,5},{4,2},{5,3},{6,0},{7,1},{8,14},{9,15},{10,... | collective-permute-start | bytes 98312 | tf_op jit(solution)/shard_map/ppermute | solution.py:35
  51.1 4.9 %collective-permute-start.19 = (f32[16,512]{1,0:T(8,128)S(1)}, f32[16,512]{1,0:T(8,128)S(1)}, u32[]{:S(2)}, u32[]{:S(2)}) collective-permute-start(f32[16,512]{1,0:T(8,128)S(1)} %add_add_fusion.5), channel_id=1, source_target_pairs={{0,8},{1,9},{2,10},{3,11},{4,12},{5,13},{6,14},{7,15},{8,0},{9,1},... | collective-permute-start | bytes 98312 | tf_op jit(solution)/shard_map/ppermute | solution.py:35
  51.2 4.9 %collective-permute-start.20 = (f32[16,512]{1,0:T(8,128)S(1)}, f32[16,512]{1,0:T(8,128)S(1)}, u32[]{:S(2)}, u32[]{:S(2)}) collective-permute-start(f32[16,512]{1,0:T(8,128)S(1)} %add_add_fusion.5), channel_id=1, source_target_pairs={{0,16},{1,17},{2,18},{3,19},{4,20},{5,21},{6,22},{7,23},{8,24},{9,... | collective-permute-start | bytes 98312 | tf_op jit(solution)/shard_map/ppermute | solution.py:35
  52.7 5.7 %collective-permute-start.21 = (f32[16,512]{1,0:T(8,128)S(1)}, f32[16,512]{1,0:T(8,128)S(1)}, u32[]{:S(2)}, u32[]{:S(2)}) collective-permute-start(f32[16,512]{1,0:T(8,128)S(1)} %add_add_fusion.5), channel_id=1, source_target_pairs={{0,24},{1,25},{2,26},{3,27},{4,28},{5,29},{6,30},{7,31},{8,16},{9,... | collective-permute-start | bytes 98312 | tf_op jit(solution)/shard_map/ppermute | solution.py:35
  58.4 1.3 %collective-permute-start.22 = (f32[16,512]{1,0:T(8,128)S(1)}, f32[16,512]{1,0:T(8,128)S(1)}, u32[]{:S(2)}, u32[]{:S(2)}) collective-permute-start(f32[16,512]{1,0:T(8,128)S(1)} %add_add_fusion.4.held_ref), channel_id=1, source_target_pairs={{0,1},{1,0},{2,3},{3,2},{4,5},{5,4},{6,7},{7,6},{8,9},{9,8},{10,11... | collective-permute-start | bytes 98312 | tf_op jit(solution)/shard_map/ppermute | solution.py:35
  61.7 1.5 %collective-permute-start.23 = (f32[16,512]{1,0:T(8,128)S(1)}, f32[16,512]{1,0:T(8,128)S(1)}, u32[]{:S(2)}, u32[]{:S(2)}) collective-permute-start(f32[16,512]{1,0:T(8,128)S(1)} %get-tuple-element.62), channel_id=1, source_target_pairs={{0,1},{1,0},{2,3},{3,2},{4,5},{5,4},{6,7},{7,6},{8,9},{9,8},{10,11... | collective-permute-start | bytes 98312 | tf_op jit(solution)/shard_map/ppermute | solution.py:35
  63.2 4.0 %collective-permute-start.24 = (f32[16,512]{1,0:T(8,128)S(1)}, f32[16,512]{1,0:T(8,128)S(1)}, u32[]{:S(2)}, u32[]{:S(2)}) collective-permute-start(f32[16,512]{1,0:T(8,128)S(1)} %add.81), channel_id=1, source_target_pairs={{0,2},{1,3},{2,0},{3,1},{4,6},{5,7},{6,4},{7,5},{8,10},{9,11},{10,... | collective-permute-start | bytes 98312 | tf_op jit(solution)/shard_map/ppermute | solution.py:35
  64.8 3.9 %collective-permute-start.25 = (f32[16,512]{1,0:T(8,128)S(1)}, f32[16,512]{1,0:T(8,128)S(1)}, u32[]{:S(2)}, u32[]{:S(2)}) collective-permute-start(f32[16,512]{1,0:T(8,128)S(1)} %add.81), channel_id=1, source_target_pairs={{0,4},{1,5},{2,6},{3,7},{4,0},{5,1},{6,2},{7,3},{8,12},{9,13},{10,... | collective-permute-start | bytes 98312 | tf_op jit(solution)/shard_map/ppermute | solution.py:35
  66.3 4.8 %collective-permute-start.26 = (f32[16,512]{1,0:T(8,128)S(1)}, f32[16,512]{1,0:T(8,128)S(1)}, u32[]{:S(2)}, u32[]{:S(2)}) collective-permute-start(f32[16,512]{1,0:T(8,128)S(1)} %add.81), channel_id=1, source_target_pairs={{0,6},{1,7},{2,4},{3,5},{4,2},{5,3},{6,0},{7,1},{8,14},{9,15},{10,... | collective-permute-start | bytes 98312 | tf_op jit(solution)/shard_map/ppermute | solution.py:35
  71.1 5.5 %collective-permute-start.27 = (f32[16,512]{1,0:T(8,128)S(1)}, f32[16,512]{1,0:T(8,128)S(1)}, u32[]{:S(2)}, u32[]{:S(2)}) collective-permute-start(f32[16,512]{1,0:T(8,128)S(1)} %add_add_fusion.3), channel_id=1, source_target_pairs={{0,8},{1,9},{2,10},{3,11},{4,12},{5,13},{6,14},{7,15},{8,0},{9,1},... | collective-permute-start | bytes 98312 | tf_op jit(solution)/shard_map/ppermute | solution.py:35
  71.2 6.6 %collective-permute-start.28 = (f32[16,512]{1,0:T(8,128)S(1)}, f32[16,512]{1,0:T(8,128)S(1)}, u32[]{:S(2)}, u32[]{:S(2)}) collective-permute-start(f32[16,512]{1,0:T(8,128)S(1)} %add_add_fusion.3), channel_id=1, source_target_pairs={{0,16},{1,17},{2,18},{3,19},{4,20},{5,21},{6,22},{7,23},{8,24},{9,... | collective-permute-start | bytes 98312 | tf_op jit(solution)/shard_map/ppermute | solution.py:35
  74.6 5.7 %collective-permute-start.29 = (f32[16,512]{1,0:T(8,128)S(1)}, f32[16,512]{1,0:T(8,128)S(1)}, u32[]{:S(2)}, u32[]{:S(2)}) collective-permute-start(f32[16,512]{1,0:T(8,128)S(1)} %add_add_fusion.3), channel_id=1, source_target_pairs={{0,24},{1,25},{2,26},{3,27},{4,28},{5,29},{6,30},{7,31},{8,16},{9,... | collective-permute-start | bytes 98312 | tf_op jit(solution)/shard_map/ppermute | solution.py:35
  75.9 4.5 %collective-permute-start.31 = (f32[8,2048]{1,0:T(8,128)S(1)}, f32[8,2048]{1,0:T(8,128)S(1)}, u32[]{:S(2)}, u32[]{:S(2)}) collective-permute-start(f32[8,2048]{1,0:T(8,128)S(1)} %get-tuple-element.71), channel_id=1, source_target_pairs={{0,1},{1,0},{2,3},{3,2},{4,5},{5,4},{6,7},{7,6},{8,9},{9,8},{10,11... | collective-permute-start | bytes 196616 | tf_op jit(solution)/shard_map/ppermute | solution.py:35
  76.0 5.0 %collective-permute-start.32 = (f32[8,2048]{1,0:T(8,128)S(1)}, f32[8,2048]{1,0:T(8,128)S(1)}, u32[]{:S(2)}, u32[]{:S(2)}) collective-permute-start(f32[8,2048]{1,0:T(8,128)S(1)} %get-tuple-element.72), channel_id=1, source_target_pairs={{0,2},{1,3},{2,0},{3,1},{4,6},{5,7},{6,4},{7,5},{8,10},{9,11},{10,... | collective-permute-start | bytes 196616 | tf_op jit(solution)/shard_map/ppermute | solution.py:35
  76.6 4.8 %collective-permute-start.33 = (f32[8,2048]{1,0:T(8,128)S(1)}, f32[8,2048]{1,0:T(8,128)S(1)}, u32[]{:S(2)}, u32[]{:S(2)}) collective-permute-start(f32[8,2048]{1,0:T(8,128)S(1)} %get-tuple-element.73), channel_id=1, source_target_pairs={{0,3},{1,2},{2,1},{3,0},{4,7},{5,6},{6,5},{7,4},{8,11},{9,10},{10,... | collective-permute-start | bytes 196616 | tf_op jit(solution)/shard_map/ppermute | solution.py:35
  80.3 1.3 %collective-permute-start.30 = (f32[16,512]{1,0:T(8,128)S(1)}, f32[16,512]{1,0:T(8,128)S(1)}, u32[]{:S(2)}, u32[]{:S(2)}) collective-permute-start(f32[16,512]{1,0:T(8,128)S(1)} %add_add_fusion.2.held_ref), channel_id=1, source_target_pairs={{0,1},{1,0},{2,3},{3,2},{4,5},{5,4},{6,7},{7,6},{8,9},{9,8},{10,11... | collective-permute-start | bytes 98312 | tf_op jit(solution)/shard_map/ppermute | solution.py:35

commit v6 on v5

--- a/solution.py
+++ b/solution.py
@@ -124,50 +124,28 @@
     points.wait()
 
 
-def build_rows(at_rows, value, x_ref, khi_ref, klo_ref, aug_ref, sums):
+def build_kernel(na, me_ref, a0, a1, a2, a3, x_ref, khi_ref, klo_ref, tinv_ref, aug_ref):
     docs, feat = x_ref.shape
+    quarter = a0.shape[0]
     scale = 1.0 / (feat * width_h)
+    me = me_ref[0] % na
+    for mask, piece in enumerate((a0, a1, a2, a3)):
+        at = pl.ds(pl.multiple_of((me ^ mask) * quarter, quarter), quarter)
+        value = piece[...].astype(f32)
+        aug_ref[at, 0:feat] = (value * (-2.0 * scale)).astype(bf16)
+        aug_ref[at, feat:] = aug_columns(row_sizes(value) * scale + 1.0, None, quarter)
     tile = min(256, docs)
-    lefts = []
-    for at, piece in zip(at_rows, value):
-        wide = piece[...].astype(f32)
-        left = jnp.concatenate(
-            [(wide * (-2.0 * scale)).astype(bf16), aug_columns(row_sizes(wide) * scale + 1.0, None, wide.shape[0])], axis=1
-        )
-        aug_ref[at, :] = left
-        lefts.append(left)
-    for k, col in enumerate(range(0, docs, tile)):
+    for col in range(0, docs, tile):
         raw = x_ref[col : col + tile, :]
         right = jnp.concatenate([raw, aug_columns(None, row_sizes(raw.astype(f32)) * scale, tile)], axis=1)
-        for at, left in zip(at_rows, lefts):
-            kern = eighth(mm(left, right, NT))
+        total = jnp.zeros((8, tile), f32)
+        for at in range(0, aug_ref.shape[0], 256):
+            kern = eighth(mm(aug_ref[at : at + 256, :], right, NT))
             high, low = split2(kern)
-            khi_ref[at, col : col + tile] = high
-            klo_ref[at, col : col + tile] = low
-            part = jnp.sum(kern.reshape(-1, 8, tile), axis=0)
-            sums[k] = part if sums[k] is None else sums[k] + part
-    return sums
-
-
-def rows_of(me_ref, na, quarter, masks):
-    mine = me_ref[0] % na
-    return [pl.ds(pl.multiple_of((mine ^ mask) * quarter, quarter), quarter) for mask in masks]
-
-
-def build_near(na, me_ref, a0, a1, x_ref, khi_ref, klo_ref, aug_ref, sum_ref):
-    tile = min(256, x_ref.shape[0])
-    sums = [None] * (x_ref.shape[0] // tile)
-    build_rows(rows_of(me_ref, na, a0.shape[0], (0, 1)), (a0, a1), x_ref, khi_ref, klo_ref, aug_ref, sums)
-    for k, part in enumerate(sums):
-        sum_ref[:, k * tile : (k + 1) * tile] = part
-
-
-def build_far(na, me_ref, a2, a3, x_ref, sum_ref, kh0, kl0, aug0, khi_ref, klo_ref, aug_ref, tinv_ref):
-    tile = min(256, x_ref.shape[0])
-    sums = [sum_ref[:, k * tile : (k + 1) * tile] for k in range(x_ref.shape[0] // tile)]
-    build_rows(rows_of(me_ref, na, a2.shape[0], (2, 3)), (a2, a3), x_ref, khi_ref, klo_ref, aug_ref, sums)
-    for k, part in enumerate(sums):
-        tinv_ref[:, k * tile : (k + 1) * tile] = 1.0 / jnp.sum(part, axis=0, keepdims=True)
+            khi_ref[at : at + 256, col : col + tile] = high
+            klo_ref[at : at + 256, col : col + tile] = low
+            total = total + jnp.sum(kern.reshape(32, 8, tile), axis=0)
+        tinv_ref[:, col : col + tile] = 1.0 / jnp.sum(total, axis=0, keepdims=True)
 
 
 def times(vec, khi, klo):
@@ -376,14 +354,13 @@
     return pltpu.with_memory_space_constraint(value, pltpu.MemorySpace.HBM)
 
 
-def call(kernel, in_specs, out_shape, scratch, flops=1 << 20, moved=1 << 18, aliases={}):
+def call(kernel, in_specs, out_shape, scratch, flops=1 << 20, moved=1 << 18):
     return pl.pallas_call(
         kernel,
         in_specs=in_specs,
         out_specs=[VMEM] * len(out_shape),
         out_shape=out_shape,
         scratch_shapes=scratch,
-        input_output_aliases=aliases,
         compiler_params=pltpu.CompilerParams(vmem_limit_bytes=24 << 20),
         cost_estimate=pl.CostEstimate(flops=flops, bytes_accessed=moved, transcendentals=0),
     )
@@ -426,8 +403,9 @@
         compiler_params=pltpu.CompilerParams(vmem_limit_bytes=4 << 20),
     )(me, in_hbm(lab_index), in_hbm(lab_class), in_hbm(features), in_hbm(anchors))
 
-    piece = [near, swap(anchors, 1), swap(anchors, 2), None]
-    piece[3] = swap(piece[2], 1)
+    piece = [near, swap_core(anchors), None, None]
+    piece[2] = swap(anchors, 2)
+    piece[3] = swap_core(piece[2])
 
     held, masks = own, [0]
     bits = list(range(a_bits, n_bits))
@@ -441,19 +419,14 @@
     slots = [[m >> a_bits for m in masks]] + [[(m ^ mask) >> a_bits for m in masks] for mask in stages[-1]]
 
     k_sds = sds((total, docs), bf16)
-    a_sds = sds((total, feat + LANES), bf16)
-    build = dict(flops=total * docs * 256, moved=2 * total * docs)
-    khi, klo, aug, sums = call(
-        functools.partial(build_near, na), [SMEM] + [VMEM] * 3, [k_sds, k_sds, a_sds, sds((8, docs), f32)], [], **build
-    )(me, piece[0], piece[1], mine_x)
-    khi, klo, aug, tinv = call(
-        functools.partial(build_far, na),
-        [SMEM] + [VMEM] * 7,
-        [k_sds, k_sds, a_sds, sds((1, docs), f32)],
+    khi, klo, tinv, aug = call(
+        functools.partial(build_kernel, na),
+        [SMEM] + [VMEM] * 5,
+        [k_sds, k_sds, sds((1, docs), f32), sds((total, feat + LANES), bf16)],
         [],
-        aliases={5: 0, 6: 1, 7: 2},
-        **build,
-    )(me, piece[2], piece[3], mine_x, sums, khi, klo, aug)
+        flops=2 * total * docs * 256,
+        moved=4 * total * docs,
+    )(me, *piece, mine_x)
 
     half = total // 2
     flat_sds = sds((CLASSES, total), f32)

time: 82.6 us -> 77.6 us (0.939)
  waiting for transfers between devices: 24.8 us -> 20.6 us
  Pallas kernels: 21 us -> 20 us
    ppermute x34, waiting for transfers between devices: 24.8 us -> 20.6 us  [swap(): return lax.ppermute(value, EVERY, [(i, i ^ mask) for i in range(count)])]
    pallas_call x2 -> x1, Pallas kernels: 4.46 us -> 3.45 us  [run(): call(functools.partial(build_kernel, na), [SMEM] + [VMEM] * 5, [k_sds, k_...]
  transfers between devices with their start and end apart: 34 -> 34, of which waited for: 21 -> 22; matrix products, arithmetic and copies ran while one was open for 0% -> 0% of each run, Pallas kernels for 15% -> 15%
where the time goes in v6:
time: 77.6 us; the launch traced here: 77.4 us
  starting transfers between devices  36 us (46%)
  waiting for transfers between devices  20.6 us (27%)
  Pallas kernels  20 us (26%)
  between operations  0.78 us (1%)
    ppermute x34, starting transfers between devices, swap(): return lax.ppermute(value, EVERY, [(i, i ^ mask) for i in range(count)])  36 us
    ppermute x34, waiting for transfers between devices, swap(): return lax.ppermute(value, EVERY, [(i, i ^ mask) for i in range(count)])  20.6 us
    pallas_call x1, Pallas kernels, run(): call(functools.partial(first_send, na, labs, slots, CLASSES * lab_scale),...  3.58 us
    pallas_call x1, Pallas kernels, run(): call(functools.partial(build_kernel, na), [SMEM] + [VMEM] * 5, [k_sds, k_...  3.45 us
    pallas_call x2, Pallas kernels, run(): call(product_own, [SMEM] + [VMEM] * 3, [half_sds], [], **work)  2.47 us
    pallas_call x1, Pallas kernels, run(): call(functools.partial(third_send, lab_scale, graph_scale), [SMEM] + [VME...  2.13 us
    pallas_call x1, Pallas kernels, run(): pl.pallas_call(functools.partial(label_kernel, na), grid_spec=pltpu.Prefe...  2.06 us
    pallas_call x1, Pallas kernels, run(): call(second_send, [SMEM] + [VMEM] * 7, [half_sds, w_sds, sds((1, total),...  1.86 us
  transfers between devices with their start and end apart: 34, of which 22 were waited for; matrix products, arithmetic and copies ran while one was open for 0% of the time, Pallas kernels for 15%

profile of v6, /device:TPU:0, one launch (start us, length us, event | category | flops | bytes accessed | tf_op | source)
XLA Modules:
  0.0 77.4 jit_solution(10097288309866536898)
XLA Ops:
  0.6 3.0 %collective-permute-start.5 = (bf16[256,128]{1,0:T(8,128)(2,1)}, bf16[256,128]{1,0:T(8,128)(2,1)S(1)}, u32[]{:S(2)}, u32[]{:S(2)}) collective-permute-start(bf16[256,128]{1,0:T(8,128)(2,1)} %anch_ref.1), channel_id=1, source_target_pairs={{0,2},{1,3},{2,0},{3,1},{4,6},{5,7},{6,4},{7,5},{8,10},{9,11},{10,... | collective-permute-start | bytes 196616 | tf_op jit(solution)/shard_map/ppermute | solution.py:35
  3.7 2.1 %label_rows.1 = (bf16[32,128]{1,0:T(8,128)(2,1)S(1)}, bf16[2048,128]{1,0:T(8,128)(2,1)S(1)}, bf16[256,128]{1,0:T(8,128)(2,1)S(1)}) custom-call(s32[1]{0:T(128)} %bitcast.me_ref, s32[16]{0:T(128)} %idx_ref.1, s32[16]{0:T(128)} %cls_ref.1, bf16[8192,128]{1,0:T(8,128)(2,1)} %feat_ref.1, bf16[256,128]{1,0:T(8,128)(2,1)} %anch_ref.1), custom_call_target="tpu_custom_call" | custom-call | tf_op jit(solution)/shard_map/label_rows/pallas_call | solution.py:386
  5.7 1.6 %collective-permute-start = (bf16[32,128]{1,0:T(8,128)(2,1)S(1)}, bf16[32,128]{1,0:T(8,128)(2,1)S(1)}, u32[]{:S(2)}, u32[]{:S(2)}) collective-permute-start(bf16[32,128]{1,0:T(8,128)(2,1)S(1)} %get-tuple-element.35), channel_id=1, source_target_pairs={{0,4},{1,5},{2,6},{3,7},{4,0},{5,1},{6,2},{7,3},{8,12},{9,13},{10,... | collective-permute-start | bytes 24584 | tf_op jit(solution)/shard_map/ppermute | solution.py:35
  7.3 0.2 collective-permute-start.6
  7.5 1.9 %collective-permute-done = bf16[32,128]{1,0:T(8,128)(2,1)S(1)} collective-permute-done((bf16[32,128]{1,0:T(8,128)(2,1)S(1)}, bf16[32,128]{1,0:T(8,128)(2,1)S(1)}, u32[]{:S(2)}, u32[]{:S(2)}) %collective-permute-start) | collective-permute-done | bytes 8224 | tf_op jit(solution)/shard_map/ppermute | solution.py:35
  9.5 3.6 %collective-permute-start.3 = (bf16[64,128]{1,0:T(8,128)(2,1)S(1)}, bf16[64,128]{1,0:T(8,128)(2,1)S(1)}, u32[]{:S(2)}, u32[]{:S(2)}) collective-permute-start(bf16[64,128]{1,0:T(8,128)(2,1)S(1)} %constant_dynamic-update-slice_fusion.refs_0_), channel_id=1, source_target_pairs={{0,24},{1,25},{2,26},{3,27},{4,28},{5,29},{6,30},{7,31},{8,16},{9,... | collective-permute-start | bytes 49160 | tf_op jit(solution)/shard_map/ppermute | solution.py:35
  13.1 0.8 %collective-permute-start.1 = (bf16[64,128]{1,0:T(8,128)(2,1)S(1)}, bf16[64,128]{1,0:T(8,128)(2,1)S(1)}, u32[]{:S(2)}, u32[]{:S(2)}) collective-permute-start(bf16[64,128]{1,0:T(8,128)(2,1)S(1)} %constant_dynamic-update-slice_fusion.refs_0_), channel_id=1, source_target_pairs={{0,8},{1,9},{2,10},{3,11},{4,12},{5,13},{6,14},{7,15},{8,0},{9,1},... | collective-permute-start | bytes 49160 | tf_op jit(solution)/shard_map/ppermute | solution.py:35
  13.8 3.5 %shard_map.59 = (bf16[1024,2048]{1,0:T(8,128)(2,1)S(1)}, bf16[1024,2048]{1,0:T(8,128)(2,1)S(1)}, f32[1,2048]{1,0:T(1,128)S(1)}, bf16[1024,256]{1,0:T(8,128)(2,1)S(1)}) custom-call(s32[1]{0:T(128)} %bitcast.me_ref, bf16[256,128]{1,0:T(8,128)(2,1)S(1)} %get-tuple-element.36.a0, bf16[256,128]{1,0:T(8,128)(2,1)S(1)} %collective-permute-done.4.a1, ...), custom_call_target="tpu_custom_call" | custom-call | flops 1073741824 | bytes 8388608 | tf_op jit(solution)/shard_map/pallas_call | solution.py:422
  17.3 0.4 collective-permute-done.2.refs_2_
  17.7 3.6 %shard_map.60 = (f32[16,640]{1,0:T(8,128)S(1)}, bf16[48,2048]{1,0:T(8,128)(2,1)S(1)}, f32[16,1024]{1,0:T(8,128)S(1)}, f32[16,1024]{1,0:T(8,128)S(1)}, bf16[1024,...) custom-call(s32[1]{0:T(128)} %bitcast.me_ref, ...), custom_call_target="tpu_custom_call" | custom-call | flops 536870912 | bytes 4194304 | tf_op jit(solution)/shard_map/pallas_call | solution.py:440
  21.3 1.3 %shard_map.61 = f32[16,640]{1,0:T(8,128)S(1)} custom-call(s32[1]{0:T(128)} %bitcast.me_ref, bf16[48,2048]{1,0:T(8,128)(2,1)S(1)} %get-tuple-element.42.w_ref, bf16[1024,2048]{1,0:T(8,128)(2,1)S(1)} %get-tuple-element.39.refs_5_.khi_ref, bf16[1024,2048]{1,0:T(8,128)(2,1)S(1)} %get-tuple-element.40.refs_6_.klo_ref), custom_call_target="tpu_custom_call" | custom-call | flops 536870912 | bytes 4194304 | tf_op jit(solution)/shard_map/pallas_call | solution.py:448
  22.7 1.5 %collective-permute-start.10 = (f32[16,640]{1,0:T(8,128)S(1)}, f32[16,640]{1,0:T(8,128)S(1)}, u32[]{:S(2)}, u32[]{:S(2)}) collective-permute-start(f32[16,640]{1,0:T(8,128)S(1)} %add.67), channel_id=1, source_target_pairs={{0,6},{1,7},{2,4},{3,5},{4,2},{5,3},{6,0},{7,1},{8,14},{9,15},{10,... | collective-permute-start | bytes 122888 | tf_op jit(solution)/shard_map/ppermute | solution.py:35
  24.2 0.5 collective-permute-start.9
  24.7 1.5 %collective-permute-start.8 = (f32[16,640]{1,0:T(8,128)S(1)}, f32[16,640]{1,0:T(8,128)S(1)}, u32[]{:S(2)}, u32[]{:S(2)}) collective-permute-start(f32[16,640]{1,0:T(8,128)S(1)} %add.67), channel_id=1, source_target_pairs={{0,2},{1,3},{2,0},{3,1},{4,6},{5,7},{6,4},{7,5},{8,10},{9,11},{10,... | collective-permute-start | bytes 122888 | tf_op jit(solution)/shard_map/ppermute | solution.py:35
  26.2 1.5 %collective-permute-done.10 = f32[16,640]{1,0:T(8,128)S(1)} collective-permute-done((f32[16,640]{1,0:T(8,128)S(1)}, f32[16,640]{1,0:T(8,128)S(1)}, u32[]{:S(2)}, u32[]{:S(2)}) %collective-permute-start.10) | collective-permute-done | bytes 40992 | tf_op jit(solution)/shard_map/ppermute | solution.py:35
  27.7 0.8 %collective-permute-done.9 = f32[16,640]{1,0:T(8,128)S(1)} collective-permute-done((f32[16,640]{1,0:T(8,128)S(1)}, f32[16,640]{1,0:T(8,128)S(1)}, u32[]{:S(2)}, u32[]{:S(2)}) %collective-permute-start.9) | collective-permute-done | bytes 40992 | tf_op jit(solution)/shard_map/ppermute | solution.py:35
  28.5 0.2 collective-permute-done.8
  28.8 3.3 %collective-permute-start.13 = (f32[16,640]{1,0:T(8,128)S(1)}, f32[16,640]{1,0:T(8,128)S(1)}, u32[]{:S(2)}, u32[]{:S(2)}) collective-permute-start(f32[16,640]{1,0:T(8,128)S(1)} %add_add_fusion.1), channel_id=1, source_target_pairs={{0,24},{1,25},{2,26},{3,27},{4,28},{5,29},{6,30},{7,31},{8,16},{9,... | collective-permute-start | bytes 122888 | tf_op jit(solution)/shard_map/ppermute | solution.py:35
  32.1 1.1 %collective-permute-start.11 = (f32[16,640]{1,0:T(8,128)S(1)}, f32[16,640]{1,0:T(8,128)S(1)}, u32[]{:S(2)}, u32[]{:S(2)}) collective-permute-start(f32[16,640]{1,0:T(8,128)S(1)} %add_add_fusion.1), channel_id=1, source_target_pairs={{0,8},{1,9},{2,10},{3,11},{4,12},{5,13},{6,14},{7,15},{8,0},{9,1},... | collective-permute-start | bytes 122888 | tf_op jit(solution)/shard_map/ppermute | solution.py:35
  33.2 1.5 %collective-permute-done.13 = f32[16,640]{1,0:T(8,128)S(1)} collective-permute-done((f32[16,640]{1,0:T(8,128)S(1)}, f32[16,640]{1,0:T(8,128)S(1)}, u32[]{:S(2)}, u32[]{:S(2)}) %collective-permute-start.13) | collective-permute-done | bytes 40992 | tf_op jit(solution)/shard_map/ppermute | solution.py:35
  34.7 2.3 %collective-permute-done.12 = f32[16,640]{1,0:T(8,128)S(1)} collective-permute-done((f32[16,640]{1,0:T(8,128)S(1)}, f32[16,640]{1,0:T(8,128)S(1)}, u32[]{:S(2)}, u32[]{:S(2)}) %collective-permute-start.12) | collective-permute-done | bytes 40992 | tf_op jit(solution)/shard_map/ppermute | solution.py:35
  37.0 0.1 collective-permute-start.14
  37.1 0.7 shard_map.62
  37.8 0.5 collective-permute-done.14.got_ref
  38.3 1.9 %shard_map.63 = (f32[16,512]{1,0:T(8,128)S(1)}, bf16[32,2048]{1,0:T(8,128)(2,1)S(1)}, f32[1,1024]{1,0:T(1,128)S(1)}) custom-call(s32[1]{0:T(128)} %bitcast.me_ref, f32[16,640]{1,0:T(8,128)S(1)} %collective-permute-done.14.got_ref, f32[16,1024]{1,0:T(8,128)S(1)} %get-tuple-element.44.mid_ref, bf16[1024,2048]{1,0:T(8,128)(2,1)S(1)} %get-tuple-element.39.refs_5_.khi_ref, ...), custom_call_target="tpu_custom_call" | custom-call | flops 536870912 | bytes 4194304 | tf_op jit(solution)/shard_map/pallas_call | solution.py:456
  40.2 0.2 collective-permute-start.15
  40.3 1.2 %shard_map.64 = f32[16,512]{1,0:T(8,128)S(1)} custom-call(s32[1]{0:T(128)} %bitcast.me_ref, bf16[32,2048]{1,0:T(8,128)(2,1)S(1)} %get-tuple-element.47.w_ref, bf16[1024,2048]{1,0:T(8,128)(2,1)S(1)} %get-tuple-element.39.refs_5_.khi_ref, bf16[1024,2048]{1,0:T(8,128)(2,1)S(1)} %get-tuple-element.40.refs_6_.klo_ref), custom_call_target="tpu_custom_call" | custom-call | flops 536870912 | bytes 4194304 | tf_op jit(solution)/shard_map/pallas_call | solution.py:460
  41.6 2.5 %collective-permute-start.18 = (f32[16,512]{1,0:T(8,128)S(1)}, f32[16,512]{1,0:T(8,128)S(1)}, u32[]{:S(2)}, u32[]{:S(2)}) collective-permute-start(f32[16,512]{1,0:T(8,128)S(1)} %add.74), channel_id=1, source_target_pairs={{0,6},{1,7},{2,4},{3,5},{4,2},{5,3},{6,0},{7,1},{8,14},{9,15},{10,... | collective-permute-start | bytes 98312 | tf_op jit(solution)/shard_map/ppermute | solution.py:35
  44.1 0.5 collective-permute-start.17
  44.6 0.5 collective-permute-start.16
  45.2 1.3 %collective-permute-done.18 = f32[16,512]{1,0:T(8,128)S(1)} collective-permute-done((f32[16,512]{1,0:T(8,128)S(1)}, f32[16,512]{1,0:T(8,128)S(1)}, u32[]{:S(2)}, u32[]{:S(2)}) %collective-permute-start.18) | collective-permute-done | bytes 32800 | tf_op jit(solution)/shard_map/ppermute | solution.py:35
  46.5 1.5 %collective-permute-done.17 = f32[16,512]{1,0:T(8,128)S(1)} collective-permute-done((f32[16,512]{1,0:T(8,128)S(1)}, f32[16,512]{1,0:T(8,128)S(1)}, u32[]{:S(2)}, u32[]{:S(2)}) %collective-permute-start.17) | collective-permute-done | bytes 32800 | tf_op jit(solution)/shard_map/ppermute | solution.py:35
  48.0 0.5 collective-permute-done.16
  48.5 1.5 %collective-permute-start.21 = (f32[16,512]{1,0:T(8,128)S(1)}, f32[16,512]{1,0:T(8,128)S(1)}, u32[]{:S(2)}, u32[]{:S(2)}) collective-permute-start(f32[16,512]{1,0:T(8,128)S(1)} %add_add_fusion.5), channel_id=1, source_target_pairs={{0,24},{1,25},{2,26},{3,27},{4,28},{5,29},{6,30},{7,31},{8,16},{9,... | collective-permute-start | bytes 98312 | tf_op jit(solution)/shard_map/ppermute | solution.py:35
  50.1 0.6 collective-permute-start.20
  50.7 2.3 %collective-permute-start.19 = (f32[16,512]{1,0:T(8,128)S(1)}, f32[16,512]{1,0:T(8,128)S(1)}, u32[]{:S(2)}, u32[]{:S(2)}) collective-permute-start(f32[16,512]{1,0:T(8,128)S(1)} %add_add_fusion.5), channel_id=1, source_target_pairs={{0,8},{1,9},{2,10},{3,11},{4,12},{5,13},{6,14},{7,15},{8,0},{9,1},... | collective-permute-start | bytes 98312 | tf_op jit(solution)/shard_map/ppermute | solution.py:35
  53.0 0.4 shard_map.65.lab_ref
  53.4 0.9 %collective-permute-done.21 = f32[16,512]{1,0:T(8,128)S(1)} collective-permute-done((f32[16,512]{1,0:T(8,128)S(1)}, f32[16,512]{1,0:T(8,128)S(1)}, u32[]{:S(2)}, u32[]{:S(2)}) %collective-permute-start.21) | collective-permute-done | bytes 32800 | tf_op jit(solution)/shard_map/ppermute | solution.py:35
  54.3 0.7 collective-permute-done.20
  55.0 0.2 collective-permute-done.19
  55.3 0.1 collective-permute-start.22
  55.3 0.8 %shard_map.66.part_ref = f32[16,2048]{1,0:T(8,128)S(1)} custom-call(s32[1]{0:T(128)} %bitcast.me_ref, f32[16,512]{1,0:T(8,128)S(1)} %add_add_fusion.4.held_ref, f32[16,1024]{1,0:T(8,128)S(1)} %get-tuple-element.49.rhs_ref, f32[16,1024]{1,0:T(8,128)S(1)} %shard_map.65.lab_ref, bf16[1024,2048]{1,0:T(8,128)(2,1)S(1)} %get-tuple-element.39.refs_5_.khi_ref, ...), custom_call_target="tpu_custom_call" | custom-call | flops 536870912 | bytes 4194304 | tf_op jit(solution)/shard_map/pallas_call | solution.py:464
  56.1 0.4 collective-permute-done.22.got_ref
  56.5 2.1 %shard_map.67 = (f32[16,512]{1,0:T(8,128)S(1)}, bf16[32,2048]{1,0:T(8,128)(2,1)S(1)}, f32[16,2048]{1,0:T(8,128)S(1)}, f32[16,1024]{1,0:T(8,128)S(1)}, f32[16,102...) custom-call(s32[1]{0:T(128)} %bitcast.me_ref, f32[16,512]{1,0:T(8,128)S(1)} %add_add_fusion.4.held_ref, ...), custom_call_target="tpu_custom_call" | custom-call | flops 536870912 | bytes 4194304 | tf_op jit(solution)/shard_map/pallas_call | solution.py:467
  58.7 0.2 collective-permute-start.23
  58.8 1.2 %shard_map.68 = f32[16,512]{1,0:T(8,128)S(1)} custom-call(s32[1]{0:T(128)} %bitcast.me_ref, bf16[32,2048]{1,0:T(8,128)(2,1)S(1)} %get-tuple-element.53.w_ref, bf16[1024,2048]{1,0:T(8,128)(2,1)S(1)} %get-tuple-element.39.refs_5_.khi_ref, bf16[1024,2048]{1,0:T(8,128)(2,1)S(1)} %get-tuple-element.40.refs_6_.klo_ref), custom_call_target="tpu_custom_call" | custom-call | flops 536870912 | bytes 4194304 | tf_op jit(solution)/shard_map/pallas_call | solution.py:475
  60.1 1.6 %collective-permute-start.26 = (f32[16,512]{1,0:T(8,128)S(1)}, f32[16,512]{1,0:T(8,128)S(1)}, u32[]{:S(2)}, u32[]{:S(2)}) collective-permute-start(f32[16,512]{1,0:T(8,128)S(1)} %add.81), channel_id=1, source_target_pairs={{0,6},{1,7},{2,4},{3,5},{4,2},{5,3},{6,0},{7,1},{8,14},{9,15},{10,... | collective-permute-start | bytes 98312 | tf_op jit(solution)/shard_map/ppermute | solution.py:35
  61.7 0.5 collective-permute-start.25
  62.2 1.5 %collective-permute-start.24 = (f32[16,512]{1,0:T(8,128)S(1)}, f32[16,512]{1,0:T(8,128)S(1)}, u32[]{:S(2)}, u32[]{:S(2)}) collective-permute-start(f32[16,512]{1,0:T(8,128)S(1)} %add.81), channel_id=1, source_target_pairs={{0,2},{1,3},{2,0},{3,1},{4,6},{5,7},{6,4},{7,5},{8,10},{9,11},{10,... | collective-permute-start | bytes 98312 | tf_op jit(solution)/shard_map/ppermute | solution.py:35
  63.7 1.3 %collective-permute-done.26 = f32[16,512]{1,0:T(8,128)S(1)} collective-permute-done((f32[16,512]{1,0:T(8,128)S(1)}, f32[16,512]{1,0:T(8,128)S(1)}, u32[]{:S(2)}, u32[]{:S(2)}) %collective-permute-start.26) | collective-permute-done | bytes 32800 | tf_op jit(solution)/shard_map/ppermute | solution.py:35
  65.0 0.6 collective-permute-done.25
  65.6 0.5 collective-permute-done.24
  66.1 2.4 %collective-permute-start.29 = (f32[16,512]{1,0:T(8,128)S(1)}, f32[16,512]{1,0:T(8,128)S(1)}, u32[]{:S(2)}, u32[]{:S(2)}) collective-permute-start(f32[16,512]{1,0:T(8,128)S(1)} %add_add_fusion.3), channel_id=1, source_target_pairs={{0,24},{1,25},{2,26},{3,27},{4,28},{5,29},{6,30},{7,31},{8,16},{9,... | collective-permute-start | bytes 98312 | tf_op jit(solution)/shard_map/ppermute | solution.py:35
  68.5 0.8 collective-permute-start.28
  69.3 1.3 %collective-permute-start.27 = (f32[16,512]{1,0:T(8,128)S(1)}, f32[16,512]{1,0:T(8,128)S(1)}, u32[]{:S(2)}, u32[]{:S(2)}) collective-permute-start(f32[16,512]{1,0:T(8,128)S(1)} %add_add_fusion.3), channel_id=1, source_target_pairs={{0,8},{1,9},{2,10},{3,11},{4,12},{5,13},{6,14},{7,15},{8,0},{9,1},... | collective-permute-start | bytes 98312 | tf_op jit(solution)/shard_map/ppermute | solution.py:35
  70.6 0.3 shard_map.69
  71.0 1.5 %collective-permute-start.32 = (f32[8,2048]{1,0:T(8,128)S(1)}, f32[8,2048]{1,0:T(8,128)S(1)}, u32[]{:S(2)}, u32[]{:S(2)}) collective-permute-start(f32[8,2048]{1,0:T(8,128)S(1)} %get-tuple-element.64), channel_id=1, source_target_pairs={{0,2},{1,3},{2,0},{3,1},{4,6},{5,7},{6,4},{7,5},{8,10},{9,11},{10,... | collective-permute-start | bytes 196616 | tf_op jit(solution)/shard_map/ppermute | solution.py:35
  72.5 0.3 collective-permute-start.33
  72.8 0.6 collective-permute-done.28
  73.4 0.1 collective-permute-done.27
  73.6 0.3 collective-permute-start.30
  73.9 1.6 %collective-permute-done.32.refs_2_ = f32[8,2048]{1,0:T(8,128)S(1)} collective-permute-done((f32[8,2048]{1,0:T(8,128)S(1)}, f32[8,2048]{1,0:T(8,128)S(1)}, u32[]{:S(2)}, u32[]{:S(2)}) %collective-permute-start.32) | collective-permute-done | bytes 65568 | tf_op jit(solution)/shard_map/ppermute | solution.py:35
  75.5 1.1 %collective-permute-done.33.refs_3_ = f32[8,2048]{1,0:T(8,128)S(1)} collective-permute-done((f32[8,2048]{1,0:T(8,128)S(1)}, f32[8,2048]{1,0:T(8,128)S(1)}, u32[]{:S(2)}, u32[]{:S(2)}) %collective-permute-start.33) | collective-permute-done | bytes 65568 | tf_op jit(solution)/shard_map/ppermute | solution.py:35
  76.6 0.8 %shard_map.70 = (f32[16,256]{1,0:T(8,128)}, f32[4,8192]{1,0:T(4,128)}) custom-call(s32[1]{0:T(128)} %bitcast.me_ref, f32[16,512]{1,0:T(8,128)S(1)} %add_add_fusion.2.held_ref, f32[16,512]{1,0:T(8,128)S(1)} %collective-permute-done.30.got_ref, f32[16,1024]{1,0:T(8,128)S(1)} %get-tuple-element.55.direc_ref, f32[16,1024]{1,0:T(8,128)S(1)} %get-tuple-element.56.mid_ref, ...), custom_call_target="tpu_custom_call" | custom-call | flops 1048576 | bytes 262144 | tf_op jit(solution)/shard_map/pallas_call | solution.py:489
  (28 shorter events, 0.3 us)
Async XLA Ops:
  0.6 6.7 %collective-permute-start.5 = (bf16[256,128]{1,0:T(8,128)(2,1)}, bf16[256,128]{1,0:T(8,128)(2,1)S(1)}, u32[]{:S(2)}, u32[]{:S(2)}) collective-permute-start(bf16[256,128]{1,0:T(8,128)(2,1)} %anch_ref.1), channel_id=1, source_target_pairs={{0,2},{1,3},{2,0},{3,1},{4,6},{5,7},{6,4},{7,5},{8,10},{9,11},{10,... | collective-permute-start | bytes 196616 | tf_op jit(solution)/shard_map/ppermute | solution.py:35
  3.7 10.2 %collective-permute-start.4 = (bf16[256,128]{1,0:T(8,128)(2,1)}, bf16[256,128]{1,0:T(8,128)(2,1)S(1)}, u32[]{:S(2)}, u32[]{:S(2)}) collective-permute-start(bf16[256,128]{1,0:T(8,128)(2,1)} %anch_ref.1), channel_id=1, source_target_pairs={{0,1},{1,0},{2,3},{3,2},{4,5},{5,4},{6,7},{7,6},{8,9},{9,8},{10,11... | collective-permute-start | bytes 196616 | tf_op jit(solution)/shard_map/ppermute | solution.py:35
  5.7 3.7 %collective-permute-start = (bf16[32,128]{1,0:T(8,128)(2,1)S(1)}, bf16[32,128]{1,0:T(8,128)(2,1)S(1)}, u32[]{:S(2)}, u32[]{:S(2)}) collective-permute-start(bf16[32,128]{1,0:T(8,128)(2,1)S(1)} %get-tuple-element.35), channel_id=1, source_target_pairs={{0,4},{1,5},{2,6},{3,7},{4,0},{5,1},{6,2},{7,3},{8,12},{9,13},{10,... | collective-permute-start | bytes 24584 | tf_op jit(solution)/shard_map/ppermute | solution.py:35
  7.3 6.5 %collective-permute-start.6 = (bf16[256,128]{1,0:T(8,128)(2,1)S(1)}, bf16[256,128]{1,0:T(8,128)(2,1)S(1)}, u32[]{:S(2)}, u32[]{:S(2)}) collective-permute-start(bf16[256,128]{1,0:T(8,128)(2,1)S(1)} %collective-permute-done.5.a2), channel_id=1, source_target_pairs={{0,1},{1,0},{2,3},{3,2},{4,5},{5,4},{6,7},{7,6},{8,9},{9,8},{10,11... | collective-permute-start | bytes 196616 | tf_op jit(solution)/shard_map/ppermute | solution.py:35
  9.5 7.9 %collective-permute-start.3 = (bf16[64,128]{1,0:T(8,128)(2,1)S(1)}, bf16[64,128]{1,0:T(8,128)(2,1)S(1)}, u32[]{:S(2)}, u32[]{:S(2)}) collective-permute-start(bf16[64,128]{1,0:T(8,128)(2,1)S(1)} %constant_dynamic-update-slice_fusion.refs_0_), channel_id=1, source_target_pairs={{0,24},{1,25},{2,26},{3,27},{4,28},{5,29},{6,30},{7,31},{8,16},{9,... | collective-permute-start | bytes 49160 | tf_op jit(solution)/shard_map/ppermute | solution.py:35
  13.1 4.6 %collective-permute-start.2 = (bf16[64,128]{1,0:T(8,128)(2,1)S(1)}, bf16[64,128]{1,0:T(8,128)(2,1)S(1)}, u32[]{:S(2)}, u32[]{:S(2)}) collective-permute-start(bf16[64,128]{1,0:T(8,128)(2,1)S(1)} %constant_dynamic-update-slice_fusion.refs_0_), channel_id=1, source_target_pairs={{0,16},{1,17},{2,18},{3,19},{4,20},{5,21},{6,22},{7,23},{8,24},{9,... | collective-permute-start | bytes 49160 | tf_op jit(solution)/shard_map/ppermute | solution.py:35
  13.1 4.6 %collective-permute-start.1 = (bf16[64,128]{1,0:T(8,128)(2,1)S(1)}, bf16[64,128]{1,0:T(8,128)(2,1)S(1)}, u32[]{:S(2)}, u32[]{:S(2)}) collective-permute-start(bf16[64,128]{1,0:T(8,128)(2,1)S(1)} %constant_dynamic-update-slice_fusion.refs_0_), channel_id=1, source_target_pairs={{0,8},{1,9},{2,10},{3,11},{4,12},{5,13},{6,14},{7,15},{8,0},{9,1},... | collective-permute-start | bytes 49160 | tf_op jit(solution)/shard_map/ppermute | solution.py:35
  21.3 1.4 %collective-permute-start.7 = (f32[16,640]{1,0:T(8,128)S(1)}, f32[16,640]{1,0:T(8,128)S(1)}, u32[]{:S(2)}, u32[]{:S(2)}) collective-permute-start(f32[16,640]{1,0:T(8,128)S(1)} %get-tuple-element.43), channel_id=1, source_target_pairs={{0,1},{1,0},{2,3},{3,2},{4,5},{5,4},{6,7},{7,6},{8,9},{9,8},{10,11... | collective-permute-start | bytes 122888 | tf_op jit(solution)/shard_map/ppermute | solution.py:35
  22.7 5.0 %collective-permute-start.10 = (f32[16,640]{1,0:T(8,128)S(1)}, f32[16,640]{1,0:T(8,128)S(1)}, u32[]{:S(2)}, u32[]{:S(2)}) collective-permute-start(f32[16,640]{1,0:T(8,128)S(1)} %add.67), channel_id=1, source_target_pairs={{0,6},{1,7},{2,4},{3,5},{4,2},{5,3},{6,0},{7,1},{8,14},{9,15},{10,... | collective-permute-start | bytes 122888 | tf_op jit(solution)/shard_map/ppermute | solution.py:35
  24.2 4.3 %collective-permute-start.9 = (f32[16,640]{1,0:T(8,128)S(1)}, f32[16,640]{1,0:T(8,128)S(1)}, u32[]{:S(2)}, u32[]{:S(2)}) collective-permute-start(f32[16,640]{1,0:T(8,128)S(1)} %add.67), channel_id=1, source_target_pairs={{0,4},{1,5},{2,6},{3,7},{4,0},{5,1},{6,2},{7,3},{8,12},{9,13},{10,... | collective-permute-start | bytes 122888 | tf_op jit(solution)/shard_map/ppermute | solution.py:35
  24.7 4.0 %collective-permute-start.8 = (f32[16,640]{1,0:T(8,128)S(1)}, f32[16,640]{1,0:T(8,128)S(1)}, u32[]{:S(2)}, u32[]{:S(2)}) collective-permute-start(f32[16,640]{1,0:T(8,128)S(1)} %add.67), channel_id=1, source_target_pairs={{0,2},{1,3},{2,0},{3,1},{4,6},{5,7},{6,4},{7,5},{8,10},{9,11},{10,... | collective-permute-start | bytes 122888 | tf_op jit(solution)/shard_map/ppermute | solution.py:35
  28.8 6.0 %collective-permute-start.13 = (f32[16,640]{1,0:T(8,128)S(1)}, f32[16,640]{1,0:T(8,128)S(1)}, u32[]{:S(2)}, u32[]{:S(2)}) collective-permute-start(f32[16,640]{1,0:T(8,128)S(1)} %add_add_fusion.1), channel_id=1, source_target_pairs={{0,24},{1,25},{2,26},{3,27},{4,28},{5,29},{6,30},{7,31},{8,16},{9,... | collective-permute-start | bytes 122888 | tf_op jit(solution)/shard_map/ppermute | solution.py:35
  32.1 4.9 %collective-permute-start.12 = (f32[16,640]{1,0:T(8,128)S(1)}, f32[16,640]{1,0:T(8,128)S(1)}, u32[]{:S(2)}, u32[]{:S(2)}) collective-permute-start(f32[16,640]{1,0:T(8,128)S(1)} %add_add_fusion.1), channel_id=1, source_target_pairs={{0,16},{1,17},{2,18},{3,19},{4,20},{5,21},{6,22},{7,23},{8,24},{9,... | collective-permute-start | bytes 122888 | tf_op jit(solution)/shard_map/ppermute | solution.py:35
  32.1 4.9 %collective-permute-start.11 = (f32[16,640]{1,0:T(8,128)S(1)}, f32[16,640]{1,0:T(8,128)S(1)}, u32[]{:S(2)}, u32[]{:S(2)}) collective-permute-start(f32[16,640]{1,0:T(8,128)S(1)} %add_add_fusion.1), channel_id=1, source_target_pairs={{0,8},{1,9},{2,10},{3,11},{4,12},{5,13},{6,14},{7,15},{8,0},{9,1},... | collective-permute-start | bytes 122888 | tf_op jit(solution)/shard_map/ppermute | solution.py:35
  37.0 1.3 %collective-permute-start.14 = (f32[16,640]{1,0:T(8,128)S(1)}, f32[16,640]{1,0:T(8,128)S(1)}, u32[]{:S(2)}, u32[]{:S(2)}) collective-permute-start(f32[16,640]{1,0:T(8,128)S(1)} %add_add_fusion.held_ref), channel_id=1, source_target_pairs={{0,1},{1,0},{2,3},{3,2},{4,5},{5,4},{6,7},{7,6},{8,9},{9,8},{10,11... | collective-permute-start | bytes 122888 | tf_op jit(solution)/shard_map/ppermute | solution.py:35
  40.2 1.4 %collective-permute-start.15 = (f32[16,512]{1,0:T(8,128)S(1)}, f32[16,512]{1,0:T(8,128)S(1)}, u32[]{:S(2)}, u32[]{:S(2)}) collective-permute-start(f32[16,512]{1,0:T(8,128)S(1)} %get-tuple-element.48), channel_id=1, source_target_pairs={{0,1},{1,0},{2,3},{3,2},{4,5},{5,4},{6,7},{7,6},{8,9},{9,8},{10,11... | collective-permute-start | bytes 98312 | tf_op jit(solution)/shard_map/ppermute | solution.py:35
  41.6 4.9 %collective-permute-start.18 = (f32[16,512]{1,0:T(8,128)S(1)}, f32[16,512]{1,0:T(8,128)S(1)}, u32[]{:S(2)}, u32[]{:S(2)}) collective-permute-start(f32[16,512]{1,0:T(8,128)S(1)} %add.74), channel_id=1, source_target_pairs={{0,6},{1,7},{2,4},{3,5},{4,2},{5,3},{6,0},{7,1},{8,14},{9,15},{10,... | collective-permute-start | bytes 98312 | tf_op jit(solution)/shard_map/ppermute | solution.py:35
  44.1 3.9 %collective-permute-start.17 = (f32[16,512]{1,0:T(8,128)S(1)}, f32[16,512]{1,0:T(8,128)S(1)}, u32[]{:S(2)}, u32[]{:S(2)}) collective-permute-start(f32[16,512]{1,0:T(8,128)S(1)} %add.74), channel_id=1, source_target_pairs={{0,4},{1,5},{2,6},{3,7},{4,0},{5,1},{6,2},{7,3},{8,12},{9,13},{10,... | collective-permute-start | bytes 98312 | tf_op jit(solution)/shard_map/ppermute | solution.py:35
  44.6 3.9 %collective-permute-start.16 = (f32[16,512]{1,0:T(8,128)S(1)}, f32[16,512]{1,0:T(8,128)S(1)}, u32[]{:S(2)}, u32[]{:S(2)}) collective-permute-start(f32[16,512]{1,0:T(8,128)S(1)} %add.74), channel_id=1, source_target_pairs={{0,2},{1,3},{2,0},{3,1},{4,6},{5,7},{6,4},{7,5},{8,10},{9,11},{10,... | collective-permute-start | bytes 98312 | tf_op jit(solution)/shard_map/ppermute | solution.py:35
  48.5 5.8 %collective-permute-start.21 = (f32[16,512]{1,0:T(8,128)S(1)}, f32[16,512]{1,0:T(8,128)S(1)}, u32[]{:S(2)}, u32[]{:S(2)}) collective-permute-start(f32[16,512]{1,0:T(8,128)S(1)} %add_add_fusion.5), channel_id=1, source_target_pairs={{0,24},{1,25},{2,26},{3,27},{4,28},{5,29},{6,30},{7,31},{8,16},{9,... | collective-permute-start | bytes 98312 | tf_op jit(solution)/shard_map/ppermute | solution.py:35
  50.1 4.9 %collective-permute-start.20 = (f32[16,512]{1,0:T(8,128)S(1)}, f32[16,512]{1,0:T(8,128)S(1)}, u32[]{:S(2)}, u32[]{:S(2)}) collective-permute-start(f32[16,512]{1,0:T(8,128)S(1)} %add_add_fusion.5), channel_id=1, source_target_pairs={{0,16},{1,17},{2,18},{3,19},{4,20},{5,21},{6,22},{7,23},{8,24},{9,... | collective-permute-start | bytes 98312 | tf_op jit(solution)/shard_map/ppermute | solution.py:35
  50.7 4.5 %collective-permute-start.19 = (f32[16,512]{1,0:T(8,128)S(1)}, f32[16,512]{1,0:T(8,128)S(1)}, u32[]{:S(2)}, u32[]{:S(2)}) collective-permute-start(f32[16,512]{1,0:T(8,128)S(1)} %add_add_fusion.5), channel_id=1, source_target_pairs={{0,8},{1,9},{2,10},{3,11},{4,12},{5,13},{6,14},{7,15},{8,0},{9,1},... | collective-permute-start | bytes 98312 | tf_op jit(solution)/shard_map/ppermute | solution.py:35
  55.3 1.3 %collective-permute-start.22 = (f32[16,512]{1,0:T(8,128)S(1)}, f32[16,512]{1,0:T(8,128)S(1)}, u32[]{:S(2)}, u32[]{:S(2)}) collective-permute-start(f32[16,512]{1,0:T(8,128)S(1)} %add_add_fusion.4.held_ref), channel_id=1, source_target_pairs={{0,1},{1,0},{2,3},{3,2},{4,5},{5,4},{6,7},{7,6},{8,9},{9,8},{10,11... | collective-permute-start | bytes 98312 | tf_op jit(solution)/shard_map/ppermute | solution.py:35
  58.7 1.4 %collective-permute-start.23 = (f32[16,512]{1,0:T(8,128)S(1)}, f32[16,512]{1,0:T(8,128)S(1)}, u32[]{:S(2)}, u32[]{:S(2)}) collective-permute-start(f32[16,512]{1,0:T(8,128)S(1)} %get-tuple-element.54), channel_id=1, source_target_pairs={{0,1},{1,0},{2,3},{3,2},{4,5},{5,4},{6,7},{7,6},{8,9},{9,8},{10,11... | collective-permute-start | bytes 98312 | tf_op jit(solution)/shard_map/ppermute | solution.py:35
  60.1 4.9 %collective-permute-start.26 = (f32[16,512]{1,0:T(8,128)S(1)}, f32[16,512]{1,0:T(8,128)S(1)}, u32[]{:S(2)}, u32[]{:S(2)}) collective-permute-start(f32[16,512]{1,0:T(8,128)S(1)} %add.81), channel_id=1, source_target_pairs={{0,6},{1,7},{2,4},{3,5},{4,2},{5,3},{6,0},{7,1},{8,14},{9,15},{10,... | collective-permute-start | bytes 98312 | tf_op jit(solution)/shard_map/ppermute | solution.py:35
  61.7 3.9 %collective-permute-start.25 = (f32[16,512]{1,0:T(8,128)S(1)}, f32[16,512]{1,0:T(8,128)S(1)}, u32[]{:S(2)}, u32[]{:S(2)}) collective-permute-start(f32[16,512]{1,0:T(8,128)S(1)} %add.81), channel_id=1, source_target_pairs={{0,4},{1,5},{2,6},{3,7},{4,0},{5,1},{6,2},{7,3},{8,12},{9,13},{10,... | collective-permute-start | bytes 98312 | tf_op jit(solution)/shard_map/ppermute | solution.py:35
  62.2 3.9 %collective-permute-start.24 = (f32[16,512]{1,0:T(8,128)S(1)}, f32[16,512]{1,0:T(8,128)S(1)}, u32[]{:S(2)}, u32[]{:S(2)}) collective-permute-start(f32[16,512]{1,0:T(8,128)S(1)} %add.81), channel_id=1, source_target_pairs={{0,2},{1,3},{2,0},{3,1},{4,6},{5,7},{6,4},{7,5},{8,10},{9,11},{10,... | collective-permute-start | bytes 98312 | tf_op jit(solution)/shard_map/ppermute | solution.py:35
  66.1 6.4 %collective-permute-start.29 = (f32[16,512]{1,0:T(8,128)S(1)}, f32[16,512]{1,0:T(8,128)S(1)}, u32[]{:S(2)}, u32[]{:S(2)}) collective-permute-start(f32[16,512]{1,0:T(8,128)S(1)} %add_add_fusion.3), channel_id=1, source_target_pairs={{0,24},{1,25},{2,26},{3,27},{4,28},{5,29},{6,30},{7,31},{8,16},{9,... | collective-permute-start | bytes 98312 | tf_op jit(solution)/shard_map/ppermute | solution.py:35
  68.5 4.9 %collective-permute-start.28 = (f32[16,512]{1,0:T(8,128)S(1)}, f32[16,512]{1,0:T(8,128)S(1)}, u32[]{:S(2)}, u32[]{:S(2)}) collective-permute-start(f32[16,512]{1,0:T(8,128)S(1)} %add_add_fusion.3), channel_id=1, source_target_pairs={{0,16},{1,17},{2,18},{3,19},{4,20},{5,21},{6,22},{7,23},{8,24},{9,... | collective-permute-start | bytes 98312 | tf_op jit(solution)/shard_map/ppermute | solution.py:35
  69.3 4.3 %collective-permute-start.27 = (f32[16,512]{1,0:T(8,128)S(1)}, f32[16,512]{1,0:T(8,128)S(1)}, u32[]{:S(2)}, u32[]{:S(2)}) collective-permute-start(f32[16,512]{1,0:T(8,128)S(1)} %add_add_fusion.3), channel_id=1, source_target_pairs={{0,8},{1,9},{2,10},{3,11},{4,12},{5,13},{6,14},{7,15},{8,0},{9,1},... | collective-permute-start | bytes 98312 | tf_op jit(solution)/shard_map/ppermute | solution.py:35
  70.9 3.0 %collective-permute-start.31 = (f32[8,2048]{1,0:T(8,128)S(1)}, f32[8,2048]{1,0:T(8,128)S(1)}, u32[]{:S(2)}, u32[]{:S(2)}) collective-permute-start(f32[8,2048]{1,0:T(8,128)S(1)} %get-tuple-element.63), channel_id=1, source_target_pairs={{0,1},{1,0},{2,3},{3,2},{4,5},{5,4},{6,7},{7,6},{8,9},{9,8},{10,11... | collective-permute-start | bytes 196616 | tf_op jit(solution)/shard_map/ppermute | solution.py:35
  71.0 4.5 %collective-permute-start.32 = (f32[8,2048]{1,0:T(8,128)S(1)}, f32[8,2048]{1,0:T(8,128)S(1)}, u32[]{:S(2)}, u32[]{:S(2)}) collective-permute-start(f32[8,2048]{1,0:T(8,128)S(1)} %get-tuple-element.64), channel_id=1, source_target_pairs={{0,2},{1,3},{2,0},{3,1},{4,6},{5,7},{6,4},{7,5},{8,10},{9,11},{10,... | collective-permute-start | bytes 196616 | tf_op jit(solution)/shard_map/ppermute | solution.py:35
  72.5 4.1 %collective-permute-start.33 = (f32[8,2048]{1,0:T(8,128)S(1)}, f32[8,2048]{1,0:T(8,128)S(1)}, u32[]{:S(2)}, u32[]{:S(2)}) collective-permute-start(f32[8,2048]{1,0:T(8,128)S(1)} %get-tuple-element.65), channel_id=1, source_target_pairs={{0,3},{1,2},{2,1},{3,0},{4,7},{5,6},{6,5},{7,4},{8,11},{9,10},{10,... | collective-permute-start | bytes 196616 | tf_op jit(solution)/shard_map/ppermute | solution.py:35
  73.6 3.0 %collective-permute-start.30 = (f32[16,512]{1,0:T(8,128)S(1)}, f32[16,512]{1,0:T(8,128)S(1)}, u32[]{:S(2)}, u32[]{:S(2)}) collective-permute-start(f32[16,512]{1,0:T(8,128)S(1)} %add_add_fusion.2.held_ref), channel_id=1, source_target_pairs={{0,1},{1,0},{2,3},{3,2},{4,5},{5,4},{6,7},{7,6},{8,9},{9,8},{10,11... | collective-permute-start | bytes 98312 | tf_op jit(solution)/shard_map/ppermute | solution.py:35

commit v7 on v6

--- a/solution.py
+++ b/solution.py
@@ -149,18 +149,27 @@
 
 
 def times(vec, khi, klo):
-    both = mm(vec, khi)
-    return both[0:CLASSES] + (both[CLASSES:] + mm(vec[0:CLASSES], klo))
+    one = mm(vec, khi)
+    two = mm(vec[0 : 2 * CLASSES], klo)
+    return one[0:CLASSES] + (one[CLASSES : 2 * CLASSES] + two[0:CLASSES] + (one[2 * CLASSES :] + two[CLASSES:]))
 
 
 def times_back(value, khi, klo):
-    high, low = split2(value)
-    both = mm(jnp.concatenate([high, low], axis=0), khi, NT)
-    return both[0:CLASSES] + (both[CLASSES:] + mm(high, klo, NT))
+    vec = pieces(value)
+    one = mm(vec, khi, NT)
+    two = mm(vec[0 : 2 * CLASSES], klo, NT)
+    return one[0:CLASSES] + (one[CLASSES : 2 * CLASSES] + two[0:CLASSES] + (one[2 * CLASSES :] + two[CLASSES:]))
+
+
+def split3(value):
+    high = value.astype(bf16)
+    rest = value - high.astype(f32)
+    middle = rest.astype(bf16)
+    return high, middle, (rest - middle.astype(f32)).astype(bf16)
 
 
 def pieces(value):
-    return jnp.concatenate(split2(value), axis=0)
+    return jnp.concatenate(split3(value), axis=0)
 
 
 def halves(me_ref, size):
@@ -169,23 +178,22 @@
 
 
 def put_weights(w_ref, spread, tinv):
-    high, low = split2(spread * tinv)
-    w_ref[0:CLASSES, :] = high
-    w_ref[CLASSES:, :] = low
-
-
-def back_rows(w_ref, khi, klo):
-    one = mm(w_ref[...], khi, NT)
-    return one[0:CLASSES] + (one[CLASSES:] + mm(w_ref[0:CLASSES, :], klo, NT))
+    for k, part in enumerate(split3(spread * tinv)):
+        w_ref[k * CLASSES : (k + 1) * CLASSES, :] = part
+
+
+def back_rows(w_ref, khi, klo, dims):
+    one = mm(w_ref[...], khi, dims)
+    two = mm(w_ref[...], klo, dims)
+    out = one[0:CLASSES] + (one[CLASSES : 2 * CLASSES] + two[0:CLASSES] + (one[2 * CLASSES : 3 * CLASSES] + two[CLASSES : 2 * CLASSES]))
+    return out, one[3 * CLASSES :] + two[3 * CLASSES :]
 
 
 def back_degree(w_ref, khi, klo, out_ref):
-    one = mm(w_ref[...], khi, NT)
-    two = mm(w_ref[0 : 2 * CLASSES, :], klo, NT)
-    size = one.shape[1]
-    out_ref[:, 0:size] = one[0:CLASSES] + (one[2 * CLASSES :] + two[0:CLASSES])
-    deg = one[CLASSES : 2 * CLASSES] + two[CLASSES:]
-    deg = deg[0:1] + deg[1:2]
+    out, deg = back_rows(w_ref, khi, klo, NT)
+    size = out.shape[1]
+    deg = deg[0:1] + (deg[1:2] + deg[2:3])
+    out_ref[:, 0:size] = out
     out_ref[:, size:] = jnp.zeros((CLASSES, LANES), f32)
     for k in range(size // LANES):
         out_ref[k : k + 1, size:] = deg[:, k * LANES : (k + 1) * LANES]
@@ -223,12 +231,15 @@
     tinv = tinv_ref[...]
     spread = times(pieces(middle), khi_ref[...], klo_ref[...]) * tinv
     spread_ref[...] = spread
-    high, low = split2(spread * tinv)
+    put_weights(w_ref, spread, tinv)
     row = lax.broadcasted_iota(jnp.int32, (CLASSES, tinv.shape[1]), 0)
-    thigh = tinv.astype(bf16).astype(f32)
-    w_ref[0:CLASSES, :] = high
-    w_ref[CLASSES : 2 * CLASSES, :] = jnp.where(row == 0, thigh, jnp.where(row == 1, tinv - thigh, 0.0)).astype(bf16)
-    w_ref[2 * CLASSES :, :] = low
+    rest = tinv
+    ones = jnp.zeros((CLASSES, tinv.shape[1]), f32)
+    for k in range(3):
+        part = rest.astype(bf16).astype(f32)
+        ones = jnp.where(row == k, part, ones)
+        rest = rest - part
+    w_ref[3 * CLASSES :, :] = ones.astype(bf16)
     _, other = halves(me_ref, khi_ref.shape[0] // 2)
     back_degree(w_ref, khi_ref[other, :], klo_ref[other, :], send_ref)
 
@@ -238,9 +249,14 @@
     back_degree(w_ref, khi_ref[own, :], klo_ref[own, :], mine_ref)
 
 
-def product_own(me_ref, w_ref, khi_ref, klo_ref, mine_ref):
-    own, _ = halves(me_ref, khi_ref.shape[0] // 2)
-    mine_ref[...] = back_rows(w_ref, khi_ref[own, :], klo_ref[own, :])
+def flip_kernel(in_ref, out_ref):
+    for col in range(0, in_ref.shape[1], 256):
+        out_ref[col : col + 256, :] = in_ref[:, col : col + 256].T
+
+
+def product_own(me_ref, w_ref, thi_ref, tlo_ref, mine_ref):
+    own, _ = halves(me_ref, thi_ref.shape[1] // 2)
+    mine_ref[...] = back_rows(w_ref, thi_ref[:, own], tlo_ref[:, own], NN)[0]
 
 
 def residual_part(sums_ref, mid_ref, at, dinv_ref):
@@ -255,14 +271,14 @@
     part_ref[...] = times(pieces(residual_part(held_ref, mid_ref, own, dinv_ref)), khi_ref[own, :], klo_ref[own, :])
 
 
-def second_send(me_ref, got_ref, mid_ref, khi_ref, klo_ref, tinv_ref, part_ref, dinv_own, send_ref, w_ref, dinv_ref, dinv_other):
+def second_send(me_ref, got_ref, mid_ref, khi_ref, klo_ref, thi_ref, tlo_ref, tinv_ref, part_ref, dinv_own, send_ref, w_ref, dinv_ref, dinv_other):
     own, other = halves(me_ref, khi_ref.shape[0] // 2)
     rest = times(pieces(residual_part(got_ref, mid_ref, other, dinv_other)), khi_ref[other, :], klo_ref[other, :])
     dinv_ref[:, own] = dinv_own[...]
     dinv_ref[:, other] = dinv_other[...]
     tinv = tinv_ref[...]
     put_weights(w_ref, (part_ref[...] + rest) * tinv, tinv)
-    send_ref[...] = back_rows(w_ref, khi_ref[other, :], klo_ref[other, :])
+    send_ref[...] = back_rows(w_ref, thi_ref[:, other], tlo_ref[:, other], NN)[0]
 
 
 def label_image(rhs_ref, zhi_ref, zlo_ref, lab_ref):
@@ -281,8 +297,8 @@
     part_ref[...] = times(pieces(image - shift), khi_ref[own, :], klo_ref[own, :])
 
 
-def third_send(lab_scale, graph_scale, me_ref, held_ref, got_ref, rhs_ref, lab_ref, part_ref, spread0_ref, khi_ref, klo_ref, tinv_ref,
-               send_ref, w_ref, spread_ref, direc_ref, mid_ref, first_ref, stats_ref, whole):
+def third_send(lab_scale, graph_scale, me_ref, held_ref, got_ref, rhs_ref, lab_ref, part_ref, spread0_ref, khi_ref, klo_ref,
+               thi_ref, tlo_ref, tinv_ref, send_ref, w_ref, spread_ref, direc_ref, mid_ref, first_ref, stats_ref, whole):
     own, other = halves(me_ref, khi_ref.shape[0] // 2)
     rhs, lab = rhs_ref[...], lab_ref[...]
     whole[:, own] = held_ref[...]
@@ -305,7 +321,7 @@
     tinv = tinv_ref[...]
     spread = (1.0 + beta) * spread0_ref[...] - alpha * ((part_ref[...] + rest) * tinv)
     put_weights(w_ref, spread, tinv)
-    send_ref[...] = back_rows(w_ref, khi_ref[other, :], klo_ref[other, :])
+    send_ref[...] = back_rows(w_ref, thi_ref[:, other], tlo_ref[:, other], NN)[0]
     spread_ref[...] = spread
     stats_ref[0:CLASSES, :] = jnp.broadcast_to(level, (CLASSES, LANES))
     stats_ref[CLASSES : 2 * CLASSES, :] = jnp.broadcast_to(alpha * base, (CLASSES, LANES))
@@ -405,7 +421,7 @@
 
     piece = [near, swap_core(anchors), None, None]
     piece[2] = swap(anchors, 2)
-    piece[3] = swap_core(piece[2])
+    piece[3] = swap(anchors, 3)
 
     held, masks = own, [0]
     bits = list(range(a_bits, n_bits))
@@ -434,19 +450,21 @@
     long_sds = sds((CLASSES, half + LANES), f32)
     docs_sds = sds((CLASSES, docs), f32)
     z_sds = sds((total, labeled), bf16)
-    w_sds = sds((2 * CLASSES, docs), bf16)
+    w_sds = sds((3 * CLASSES, docs), bf16)
     work = dict(flops=4 * total * docs * 64, moved=2 * total * docs)
 
     send, w, rhs, middle, zhi, zlo, spread0 = call(
         functools.partial(first_send, na, labs, slots, CLASSES * lab_scale),
         [SMEM] + [VMEM] * (len(lab_arrays) + 4),
-        [long_sds, sds((3 * CLASSES, docs), bf16), flat_sds, flat_sds, z_sds, z_sds, docs_sds],
+        [long_sds, sds((4 * CLASSES, docs), bf16), flat_sds, flat_sds, z_sds, z_sds, docs_sds],
         [pltpu.VMEM((labeled, feat + LANES), bf16), pltpu.VMEM((labeled, LANES), f32)],
         **work,
     )(me, *lab_arrays, aug, khi, klo, tinv)
     got = swap_core(send)
     mine = call(first_own, [SMEM] + [VMEM] * 3, [long_sds], [], **work)(me, w, khi, klo)[0]
     held = reduce_chips(mine + got, n_bits)
+    thi = call(flip_kernel, [VMEM], [sds((docs, total), bf16)], [])(khi)[0]
+    tlo = call(flip_kernel, [VMEM], [sds((docs, total), bf16)], [])(klo)[0]
     lab = call(label_image, [VMEM] * 3, [flat_sds], [])(rhs, zhi, zlo)[0]
 
     got = swap_core(held)
@@ -454,10 +472,10 @@
         second_own, [SMEM] + [VMEM] * 4, [docs_sds, sds((1, half), f32)], [], **work
     )(me, held, middle, khi, klo)
     send, w, dinv = call(
-        second_send, [SMEM] + [VMEM] * 7, [half_sds, w_sds, sds((1, total), f32)], [pltpu.VMEM((1, half), f32)], **work
-    )(me, got, middle, khi, klo, tinv, part, dinv_own)
+        second_send, [SMEM] + [VMEM] * 9, [half_sds, w_sds, sds((1, total), f32)], [pltpu.VMEM((1, half), f32)], **work
+    )(me, got, middle, khi, klo, thi, tlo, tinv, part, dinv_own)
     got = swap_core(send)
-    mine = call(product_own, [SMEM] + [VMEM] * 3, [half_sds], [], **work)(me, w, khi, klo)[0]
+    mine = call(product_own, [SMEM] + [VMEM] * 3, [half_sds], [], **work)(me, w, thi, tlo)[0]
     held = reduce_chips(mine + got, n_bits)
 
     got = swap_core(held)
@@ -466,13 +484,13 @@
     )(me, held, rhs, lab, khi, klo)[0]
     send, w, spread, direc, middle, first, stats = call(
         functools.partial(third_send, lab_scale, graph_scale),
-        [SMEM] + [VMEM] * 9,
+        [SMEM] + [VMEM] * 11,
         [half_sds, w_sds, docs_sds, flat_sds, flat_sds, flat_sds, sds((2 * CLASSES + 16, LANES), f32)],
         [pltpu.VMEM((CLASSES, total), f32)],
         **work,
-    )(me, held, got, rhs, lab, part, spread0, khi, klo, tinv)
+    )(me, held, got, rhs, lab, part, spread0, khi, klo, thi, tlo, tinv)
     got = swap_core(send)
-    mine = call(product_own, [SMEM] + [VMEM] * 3, [half_sds], [], **work)(me, w, khi, klo)[0]
+    mine = call(product_own, [SMEM] + [VMEM] * 3, [half_sds], [], **work)(me, w, thi, tlo)[0]
     part_rows = 2 * CLASSES // na
     *docs_out, base = call(
         functools.partial(doc_parts, na, lab_scale),

time: 77.6 us -> 78.2 us (level)
    pallas_call x1 -> x3, Pallas kernels: 1.86 us -> 3.87 us  [the longest x1 1.41 us: run(): call(second_send, [SMEM] + [VMEM] * 9, [half_sds, w_sds, sds((1, total),...]
    pallas_call x2, Pallas kernels: 2.47 us -> 1.38 us  [run(): call(product_own, [SMEM] + [VMEM] * 3, [half_sds], [], **work)]
  transfers between devices with their start and end apart: 34 -> 34, of which waited for: 22 -> 22; matrix products, arithmetic and copies ran while one was open for 0% -> 0% of each run, Pallas kernels for 15% -> 17%
where the time goes in v7:
time: 78.2 us; the launch traced here: 78 us
  starting transfers between devices  36.3 us (46%)
  Pallas kernels  20.5 us (26%)
  waiting for transfers between devices  20.2 us (26%)
  between operations  0.8 us (1%)
    ppermute x34, starting transfers between devices, swap(): return lax.ppermute(value, EVERY, [(i, i ^ mask) for i in range(count)])  36.3 us
    ppermute x34, waiting for transfers between devices, swap(): return lax.ppermute(value, EVERY, [(i, i ^ mask) for i in range(count)])  20.2 us
    pallas_call x1, Pallas kernels, run(): call(functools.partial(first_send, na, labs, slots, CLASSES * lab_scale),...  3.7 us
    pallas_call x1, Pallas kernels, run(): call(functools.partial(build_kernel, na), [SMEM] + [VMEM] * 5, [k_sds, k_...  3.45 us
    pallas_call x1, Pallas kernels, run(): pl.pallas_call(functools.partial(label_kernel, na), grid_spec=pltpu.Prefe...  2.06 us
  transfers between devices with their start and end apart: 34, of which 22 were waited for; matrix products, arithmetic and copies ran while one was open for 0% of the time, Pallas kernels for 17%

profile of v7, /device:TPU:0, one launch (start us, length us, event | category | flops | bytes accessed | tf_op | source)
XLA Modules:
  0.0 78.0 jit_solution(4596618733569294420)
XLA Ops:
  0.6 0.6 collective-permute-start.4
  1.2 2.6 %collective-permute-start.6 = (bf16[256,128]{1,0:T(8,128)(2,1)}, bf16[256,128]{1,0:T(8,128)(2,1)S(1)}, u32[]{:S(2)}, u32[]{:S(2)}) collective-permute-start(bf16[256,128]{1,0:T(8,128)(2,1)} %anch_ref.1), channel_id=1, source_target_pairs={{0,3},{1,2},{2,1},{3,0},{4,7},{5,6},{6,5},{7,4},{8,11},{9,10},{10,... | collective-permute-start | bytes 196616 | tf_op jit(solution)/shard_map/ppermute | solution.py:35
  3.8 2.1 %label_rows.1 = (bf16[32,128]{1,0:T(8,128)(2,1)S(1)}, bf16[2048,128]{1,0:T(8,128)(2,1)S(1)}, bf16[256,128]{1,0:T(8,128)(2,1)S(1)}) custom-call(s32[1]{0:T(128)} %bitcast.me_ref, s32[16]{0:T(128)} %idx_ref.1, s32[16]{0:T(128)} %cls_ref.1, bf16[8192,128]{1,0:T(8,128)(2,1)} %feat_ref.1, bf16[256,128]{1,0:T(8,128)(2,1)} %anch_ref.1), custom_call_target="tpu_custom_call" | custom-call | tf_op jit(solution)/shard_map/label_rows/pallas_call | solution.py:402
  5.9 2.1 %collective-permute-start = (bf16[32,128]{1,0:T(8,128)(2,1)S(1)}, bf16[32,128]{1,0:T(8,128)(2,1)S(1)}, u32[]{:S(2)}, u32[]{:S(2)}) collective-permute-start(bf16[32,128]{1,0:T(8,128)(2,1)S(1)} %get-tuple-element.35), channel_id=1, source_target_pairs={{0,4},{1,5},{2,6},{3,7},{4,0},{5,1},{6,2},{7,3},{8,12},{9,13},{10,... | collective-permute-start | bytes 24584 | tf_op jit(solution)/shard_map/ppermute | solution.py:35
  8.0 1.6 %collective-permute-done = bf16[32,128]{1,0:T(8,128)(2,1)S(1)} collective-permute-done((bf16[32,128]{1,0:T(8,128)(2,1)S(1)}, bf16[32,128]{1,0:T(8,128)(2,1)S(1)}, u32[]{:S(2)}, u32[]{:S(2)}) %collective-permute-start) | collective-permute-done | bytes 8224 | tf_op jit(solution)/shard_map/ppermute | solution.py:35
  9.6 4.1 %collective-permute-start.3 = (bf16[64,128]{1,0:T(8,128)(2,1)S(1)}, bf16[64,128]{1,0:T(8,128)(2,1)S(1)}, u32[]{:S(2)}, u32[]{:S(2)}) collective-permute-start(bf16[64,128]{1,0:T(8,128)(2,1)S(1)} %constant_dynamic-update-slice_fusion.refs_0_), channel_id=1, source_target_pairs={{0,24},{1,25},{2,26},{3,27},{4,28},{5,29},{6,30},{7,31},{8,16},{9,... | collective-permute-start | bytes 49160 | tf_op jit(solution)/shard_map/ppermute | solution.py:35
  13.7 0.6 collective-permute-start.1
  14.3 3.5 %shard_map.59 = (bf16[1024,2048]{1,0:T(8,128)(2,1)S(1)}, bf16[1024,2048]{1,0:T(8,128)(2,1)S(1)}, f32[1,2048]{1,0:T(1,128)S(1)}, bf16[1024,256]{1,0:T(8,128)(2,1)S(1)}) custom-call(s32[1]{0:T(128)} %bitcast.me_ref, bf16[256,128]{1,0:T(8,128)(2,1)S(1)} %get-tuple-element.36.a0, bf16[256,128]{1,0:T(8,128)(2,1)S(1)} %collective-permute-done.4.a1, ...), custom_call_target="tpu_custom_call" | custom-call | flops 1073741824 | bytes 8388608 | tf_op jit(solution)/shard_map/pallas_call | solution.py:438
  17.8 0.6 collective-permute-done.2.refs_2_
  18.3 3.7 %shard_map.60 = (f32[16,640]{1,0:T(8,128)S(1)}, bf16[64,2048]{1,0:T(8,128)(2,1)S(1)}, f32[16,1024]{1,0:T(8,128)S(1)}, f32[16,1024]{1,0:T(8,128)S(1)}, bf16[1024,...) custom-call(s32[1]{0:T(128)} %bitcast.me_ref, ...), custom_call_target="tpu_custom_call" | custom-call | flops 536870912 | bytes 4194304 | tf_op jit(solution)/shard_map/pallas_call | solution.py:456
  22.1 1.3 %shard_map.61 = f32[16,640]{1,0:T(8,128)S(1)} custom-call(s32[1]{0:T(128)} %bitcast.me_ref, bf16[64,2048]{1,0:T(8,128)(2,1)S(1)} %get-tuple-element.42.w_ref, bf16[1024,2048]{1,0:T(8,128)(2,1)S(1)} %get-tuple-element.39.refs_5_.khi_ref.in_ref, bf16[1024,2048]{1,0:T(8,128)(2,1)S(1)} %get-tuple-element.40.refs_6_.klo_ref.in_ref), custom_call_target="tpu_custom_call" | custom-call | flops 536870912 | bytes 4194304 | tf_op jit(solution)/shard_map/pallas_call | solution.py:464
  23.5 2.5 %collective-permute-start.10 = (f32[16,640]{1,0:T(8,128)S(1)}, f32[16,640]{1,0:T(8,128)S(1)}, u32[]{:S(2)}, u32[]{:S(2)}) collective-permute-start(f32[16,640]{1,0:T(8,128)S(1)} %add.67), channel_id=1, source_target_pairs={{0,6},{1,7},{2,4},{3,5},{4,2},{5,3},{6,0},{7,1},{8,14},{9,15},{10,... | collective-permute-start | bytes 122888 | tf_op jit(solution)/shard_map/ppermute | solution.py:35
  26.0 0.5 collective-permute-start.9
  26.5 0.5 collective-permute-start.8
  27.1 1.4 %collective-permute-done.10 = f32[16,640]{1,0:T(8,128)S(1)} collective-permute-done((f32[16,640]{1,0:T(8,128)S(1)}, f32[16,640]{1,0:T(8,128)S(1)}, u32[]{:S(2)}, u32[]{:S(2)}) %collective-permute-start.10) | collective-permute-done | bytes 40992 | tf_op jit(solution)/shard_map/ppermute | solution.py:35
  28.5 1.6 %collective-permute-done.9 = f32[16,640]{1,0:T(8,128)S(1)} collective-permute-done((f32[16,640]{1,0:T(8,128)S(1)}, f32[16,640]{1,0:T(8,128)S(1)}, u32[]{:S(2)}, u32[]{:S(2)}) %collective-permute-start.9) | collective-permute-done | bytes 40992 | tf_op jit(solution)/shard_map/ppermute | solution.py:35
  30.0 0.5 collective-permute-done.8
  30.6 3.3 %collective-permute-start.13 = (f32[16,640]{1,0:T(8,128)S(1)}, f32[16,640]{1,0:T(8,128)S(1)}, u32[]{:S(2)}, u32[]{:S(2)}) collective-permute-start(f32[16,640]{1,0:T(8,128)S(1)} %add_add_fusion.1), channel_id=1, source_target_pairs={{0,24},{1,25},{2,26},{3,27},{4,28},{5,29},{6,30},{7,31},{8,16},{9,... | collective-permute-start | bytes 122888 | tf_op jit(solution)/shard_map/ppermute | solution.py:35
  33.9 1.1 %collective-permute-start.11 = (f32[16,640]{1,0:T(8,128)S(1)}, f32[16,640]{1,0:T(8,128)S(1)}, u32[]{:S(2)}, u32[]{:S(2)}) collective-permute-start(f32[16,640]{1,0:T(8,128)S(1)} %add_add_fusion.1), channel_id=1, source_target_pairs={{0,8},{1,9},{2,10},{3,11},{4,12},{5,13},{6,14},{7,15},{8,0},{9,1},... | collective-permute-start | bytes 122888 | tf_op jit(solution)/shard_map/ppermute | solution.py:35
  35.0 1.2 %shard_map.62.thi_ref = bf16[2048,1024]{1,0:T(8,128)(2,1)S(1)} custom-call(bf16[1024,2048]{1,0:T(8,128)(2,1)S(1)} %get-tuple-element.39.refs_5_.khi_ref.in_ref), custom_call_target="tpu_custom_call" | custom-call | flops 1048576 | bytes 262144 | tf_op jit(solution)/shard_map/pallas_call | solution.py:466
  36.3 1.2 %shard_map.63.tlo_ref = bf16[2048,1024]{1,0:T(8,128)(2,1)S(1)} custom-call(bf16[1024,2048]{1,0:T(8,128)(2,1)S(1)} %get-tuple-element.40.refs_6_.klo_ref.in_ref), custom_call_target="tpu_custom_call" | custom-call | flops 1048576 | bytes 262144 | tf_op jit(solution)/shard_map/pallas_call | solution.py:467
  37.5 1.3 %collective-permute-done.12 = f32[16,640]{1,0:T(8,128)S(1)} collective-permute-done((f32[16,640]{1,0:T(8,128)S(1)}, f32[16,640]{1,0:T(8,128)S(1)}, u32[]{:S(2)}, u32[]{:S(2)}) %collective-permute-start.12) | collective-permute-done | bytes 40992 | tf_op jit(solution)/shard_map/ppermute | solution.py:35
  38.9 0.8 shard_map.64
  39.7 0.4 collective-permute-done.14.got_ref
  40.1 1.4 %shard_map.65 = (f32[16,512]{1,0:T(8,128)S(1)}, bf16[48,2048]{1,0:T(8,128)(2,1)S(1)}, f32[1,1024]{1,0:T(1,128)S(1)}) custom-call(s32[1]{0:T(128)} %bitcast.me_ref, f32[16,640]{1,0:T(8,128)S(1)} %collective-permute-done.14.got_ref, f32[16,1024]{1,0:T(8,128)S(1)} %get-tuple-element.44.mid_ref, bf16[1024,2048]{1,0:T(8,128)(2,1)S(1)} %get-tuple-element.39.refs_5_.khi_ref.in_ref, ...), custom_call_target="tpu_custom_call" | custom-call | flops 536870912 | bytes 4194304 | tf_op jit(solution)/shard_map/pallas_call | solution.py:474
  41.5 0.2 collective-permute-start.15
  41.7 0.7 shard_map.66
  42.4 0.3 collective-permute-done.15
  42.8 1.5 %collective-permute-start.18 = (f32[16,512]{1,0:T(8,128)S(1)}, f32[16,512]{1,0:T(8,128)S(1)}, u32[]{:S(2)}, u32[]{:S(2)}) collective-permute-start(f32[16,512]{1,0:T(8,128)S(1)} %add.74), channel_id=1, source_target_pairs={{0,6},{1,7},{2,4},{3,5},{4,2},{5,3},{6,0},{7,1},{8,14},{9,15},{10,... | collective-permute-start | bytes 98312 | tf_op jit(solution)/shard_map/ppermute | solution.py:35
  44.3 0.5 collective-permute-start.17
  44.8 1.5 %collective-permute-start.16 = (f32[16,512]{1,0:T(8,128)S(1)}, f32[16,512]{1,0:T(8,128)S(1)}, u32[]{:S(2)}, u32[]{:S(2)}) collective-permute-start(f32[16,512]{1,0:T(8,128)S(1)} %add.74), channel_id=1, source_target_pairs={{0,2},{1,3},{2,0},{3,1},{4,6},{5,7},{6,4},{7,5},{8,10},{9,11},{10,... | collective-permute-start | bytes 98312 | tf_op jit(solution)/shard_map/ppermute | solution.py:35
  46.3 1.3 %collective-permute-done.18 = f32[16,512]{1,0:T(8,128)S(1)} collective-permute-done((f32[16,512]{1,0:T(8,128)S(1)}, f32[16,512]{1,0:T(8,128)S(1)}, u32[]{:S(2)}, u32[]{:S(2)}) %collective-permute-start.18) | collective-permute-done | bytes 32800 | tf_op jit(solution)/shard_map/ppermute | solution.py:35
  47.6 0.6 collective-permute-done.17
  48.2 0.5 collective-permute-done.16
  48.7 2.1 %collective-permute-start.21 = (f32[16,512]{1,0:T(8,128)S(1)}, f32[16,512]{1,0:T(8,128)S(1)}, u32[]{:S(2)}, u32[]{:S(2)}) collective-permute-start(f32[16,512]{1,0:T(8,128)S(1)} %add_add_fusion.5), channel_id=1, source_target_pairs={{0,24},{1,25},{2,26},{3,27},{4,28},{5,29},{6,30},{7,31},{8,16},{9,... | collective-permute-start | bytes 98312 | tf_op jit(solution)/shard_map/ppermute | solution.py:35
  50.8 0.1 collective-permute-start.20
  50.9 2.3 %collective-permute-start.19 = (f32[16,512]{1,0:T(8,128)S(1)}, f32[16,512]{1,0:T(8,128)S(1)}, u32[]{:S(2)}, u32[]{:S(2)}) collective-permute-start(f32[16,512]{1,0:T(8,128)S(1)} %add_add_fusion.5), channel_id=1, source_target_pairs={{0,8},{1,9},{2,10},{3,11},{4,12},{5,13},{6,14},{7,15},{8,0},{9,1},... | collective-permute-start | bytes 98312 | tf_op jit(solution)/shard_map/ppermute | solution.py:35
  53.2 0.4 shard_map.67.lab_ref
  53.6 1.3 %collective-permute-done.21 = f32[16,512]{1,0:T(8,128)S(1)} collective-permute-done((f32[16,512]{1,0:T(8,128)S(1)}, f32[16,512]{1,0:T(8,128)S(1)}, u32[]{:S(2)}, u32[]{:S(2)}) %collective-permute-start.21) | collective-permute-done | bytes 32800 | tf_op jit(solution)/shard_map/ppermute | solution.py:35
  54.9 1.0 %collective-permute-done.20 = f32[16,512]{1,0:T(8,128)S(1)} collective-permute-done((f32[16,512]{1,0:T(8,128)S(1)}, f32[16,512]{1,0:T(8,128)S(1)}, u32[]{:S(2)}, u32[]{:S(2)}) %collective-permute-start.20) | collective-permute-done | bytes 32800 | tf_op jit(solution)/shard_map/ppermute | solution.py:35
  56.0 0.8 %shard_map.68.part_ref = f32[16,2048]{1,0:T(8,128)S(1)} custom-call(s32[1]{0:T(128)} %bitcast.me_ref, f32[16,512]{1,0:T(8,128)S(1)} %add_add_fusion.4.held_ref, f32[16,1024]{1,0:T(8,128)S(1)} %get-tuple-element.49.rhs_ref, f32[16,1024]{1,0:T(8,128)S(1)} %shard_map.67.lab_ref, bf16[1024,2048]{1,0:T(8,128)(2,1)S(1)} %get-tuple-element.39.refs_5_.khi_ref.in_ref, ...), custom_call_target="tpu_custom_call" | custom-call | flops 536870912 | bytes 4194304 | tf_op jit(solution)/shard_map/pallas_call | solution.py:482
  56.9 0.4 collective-permute-done.22.got_ref
  57.2 1.5 %shard_map.69 = (f32[16,512]{1,0:T(8,128)S(1)}, bf16[48,2048]{1,0:T(8,128)(2,1)S(1)}, f32[16,2048]{1,0:T(8,128)S(1)}, f32[16,1024]{1,0:T(8,128)S(1)}, f32[16,102...) custom-call(s32[1]{0:T(128)} %bitcast.me_ref, f32[16,512]{1,0:T(8,128)S(1)} %add_add_fusion.4.held_ref, ...), custom_call_target="tpu_custom_call" | custom-call | flops 536870912 | bytes 4194304 | tf_op jit(solution)/shard_map/pallas_call | solution.py:485
  58.7 0.3 collective-permute-start.23
  59.0 0.7 shard_map.70
  59.7 0.3 collective-permute-done.23
  60.0 2.5 %collective-permute-start.26 = (f32[16,512]{1,0:T(8,128)S(1)}, f32[16,512]{1,0:T(8,128)S(1)}, u32[]{:S(2)}, u32[]{:S(2)}) collective-permute-start(f32[16,512]{1,0:T(8,128)S(1)} %add.81), channel_id=1, source_target_pairs={{0,6},{1,7},{2,4},{3,5},{4,2},{5,3},{6,0},{7,1},{8,14},{9,15},{10,... | collective-permute-start | bytes 98312 | tf_op jit(solution)/shard_map/ppermute | solution.py:35
  62.5 0.5 collective-permute-start.25
  63.0 0.5 collective-permute-start.24
  63.5 1.3 %collective-permute-done.26 = f32[16,512]{1,0:T(8,128)S(1)} collective-permute-done((f32[16,512]{1,0:T(8,128)S(1)}, f32[16,512]{1,0:T(8,128)S(1)}, u32[]{:S(2)}, u32[]{:S(2)}) %collective-permute-start.26) | collective-permute-done | bytes 32800 | tf_op jit(solution)/shard_map/ppermute | solution.py:35
  64.8 1.6 %collective-permute-done.25 = f32[16,512]{1,0:T(8,128)S(1)} collective-permute-done((f32[16,512]{1,0:T(8,128)S(1)}, f32[16,512]{1,0:T(8,128)S(1)}, u32[]{:S(2)}, u32[]{:S(2)}) %collective-permute-start.25) | collective-permute-done | bytes 32800 | tf_op jit(solution)/shard_map/ppermute | solution.py:35
  66.4 0.5 collective-permute-done.24
  66.9 1.9 %collective-permute-start.29 = (f32[16,512]{1,0:T(8,128)S(1)}, f32[16,512]{1,0:T(8,128)S(1)}, u32[]{:S(2)}, u32[]{:S(2)}) collective-permute-start(f32[16,512]{1,0:T(8,128)S(1)} %add_add_fusion.3), channel_id=1, source_target_pairs={{0,24},{1,25},{2,26},{3,27},{4,28},{5,29},{6,30},{7,31},{8,16},{9,... | collective-permute-start | bytes 98312 | tf_op jit(solution)/shard_map/ppermute | solution.py:35
  68.8 0.8 %collective-permute-start.28 = (f32[16,512]{1,0:T(8,128)S(1)}, f32[16,512]{1,0:T(8,128)S(1)}, u32[]{:S(2)}, u32[]{:S(2)}) collective-permute-start(f32[16,512]{1,0:T(8,128)S(1)} %add_add_fusion.3), channel_id=1, source_target_pairs={{0,16},{1,17},{2,18},{3,19},{4,20},{5,21},{6,22},{7,23},{8,24},{9,... | collective-permute-start | bytes 98312 | tf_op jit(solution)/shard_map/ppermute | solution.py:35
  69.6 1.8 %collective-permute-start.27 = (f32[16,512]{1,0:T(8,128)S(1)}, f32[16,512]{1,0:T(8,128)S(1)}, u32[]{:S(2)}, u32[]{:S(2)}) collective-permute-start(f32[16,512]{1,0:T(8,128)S(1)} %add_add_fusion.3), channel_id=1, source_target_pairs={{0,8},{1,9},{2,10},{3,11},{4,12},{5,13},{6,14},{7,15},{8,0},{9,1},... | collective-permute-start | bytes 98312 | tf_op jit(solution)/shard_map/ppermute | solution.py:35
  71.4 0.3 shard_map.71
  71.8 0.6 collective-permute-start.32
  72.4 0.3 collective-permute-done.29
  72.7 0.9 %collective-permute-start.33 = (f32[8,2048]{1,0:T(8,128)S(1)}, f32[8,2048]{1,0:T(8,128)S(1)}, u32[]{:S(2)}, u32[]{:S(2)}) collective-permute-start(f32[8,2048]{1,0:T(8,128)S(1)} %get-tuple-element.65), channel_id=1, source_target_pairs={{0,3},{1,2},{2,1},{3,0},{4,7},{5,6},{6,5},{7,4},{8,11},{9,10},{10,... | collective-permute-start | bytes 196616 | tf_op jit(solution)/shard_map/ppermute | solution.py:35
  73.6 0.2 collective-permute-done.28
  73.9 0.2 collective-permute-start.30
  74.1 2.7 %collective-permute-done.32.refs_2_ = f32[8,2048]{1,0:T(8,128)S(1)} collective-permute-done((f32[8,2048]{1,0:T(8,128)S(1)}, f32[8,2048]{1,0:T(8,128)S(1)}, u32[]{:S(2)}, u32[]{:S(2)}) %collective-permute-start.32) | collective-permute-done | bytes 65568 | tf_op jit(solution)/shard_map/ppermute | solution.py:35
  76.8 0.3 collective-permute-done.33.refs_3_
  77.1 0.8 %shard_map.72 = (f32[16,256]{1,0:T(8,128)}, f32[4,8192]{1,0:T(4,128)}) custom-call(s32[1]{0:T(128)} %bitcast.me_ref, f32[16,512]{1,0:T(8,128)S(1)} %add_add_fusion.2.held_ref, f32[16,512]{1,0:T(8,128)S(1)} %collective-permute-done.30.got_ref, f32[16,1024]{1,0:T(8,128)S(1)} %get-tuple-element.55.direc_ref, f32[16,1024]{1,0:T(8,128)S(1)} %get-tuple-element.56.mid_ref, ...), custom_call_target="tpu_custom_call" | custom-call | flops 1048576 | bytes 262144 | tf_op jit(solution)/shard_map/pallas_call | solution.py:507
  (30 shorter events, 0.5 us)
Async XLA Ops:
  0.6 13.1 %collective-permute-start.4 = (bf16[256,128]{1,0:T(8,128)(2,1)}, bf16[256,128]{1,0:T(8,128)(2,1)S(1)}, u32[]{:S(2)}, u32[]{:S(2)}) collective-permute-start(bf16[256,128]{1,0:T(8,128)(2,1)} %anch_ref.1), channel_id=1, source_target_pairs={{0,1},{1,0},{2,3},{3,2},{4,5},{5,4},{6,7},{7,6},{8,9},{9,8},{10,11... | collective-permute-start | bytes 196616 | tf_op jit(solution)/shard_map/ppermute | solution.py:35
  1.2 13.1 %collective-permute-start.6 = (bf16[256,128]{1,0:T(8,128)(2,1)}, bf16[256,128]{1,0:T(8,128)(2,1)S(1)}, u32[]{:S(2)}, u32[]{:S(2)}) collective-permute-start(bf16[256,128]{1,0:T(8,128)(2,1)} %anch_ref.1), channel_id=1, source_target_pairs={{0,3},{1,2},{2,1},{3,0},{4,7},{5,6},{6,5},{7,4},{8,11},{9,10},{10,... | collective-permute-start | bytes 196616 | tf_op jit(solution)/shard_map/ppermute | solution.py:35
  3.8 10.5 %collective-permute-start.5 = (bf16[256,128]{1,0:T(8,128)(2,1)}, bf16[256,128]{1,0:T(8,128)(2,1)S(1)}, u32[]{:S(2)}, u32[]{:S(2)}) collective-permute-start(bf16[256,128]{1,0:T(8,128)(2,1)} %anch_ref.1), channel_id=1, source_target_pairs={{0,2},{1,3},{2,0},{3,1},{4,6},{5,7},{6,4},{7,5},{8,10},{9,11},{10,... | collective-permute-start | bytes 196616 | tf_op jit(solution)/shard_map/ppermute | solution.py:35
  5.9 3.7 %collective-permute-start = (bf16[32,128]{1,0:T(8,128)(2,1)S(1)}, bf16[32,128]{1,0:T(8,128)(2,1)S(1)}, u32[]{:S(2)}, u32[]{:S(2)}) collective-permute-start(bf16[32,128]{1,0:T(8,128)(2,1)S(1)} %get-tuple-element.35), channel_id=1, source_target_pairs={{0,4},{1,5},{2,6},{3,7},{4,0},{5,1},{6,2},{7,3},{8,12},{9,13},{10,... | collective-permute-start | bytes 24584 | tf_op jit(solution)/shard_map/ppermute | solution.py:35
  9.6 8.1 %collective-permute-start.3 = (bf16[64,128]{1,0:T(8,128)(2,1)S(1)}, bf16[64,128]{1,0:T(8,128)(2,1)S(1)}, u32[]{:S(2)}, u32[]{:S(2)}) collective-permute-start(bf16[64,128]{1,0:T(8,128)(2,1)S(1)} %constant_dynamic-update-slice_fusion.refs_0_), channel_id=1, source_target_pairs={{0,24},{1,25},{2,26},{3,27},{4,28},{5,29},{6,30},{7,31},{8,16},{9,... | collective-permute-start | bytes 49160 | tf_op jit(solution)/shard_map/ppermute | solution.py:35
  13.7 4.6 %collective-permute-start.2 = (bf16[64,128]{1,0:T(8,128)(2,1)S(1)}, bf16[64,128]{1,0:T(8,128)(2,1)S(1)}, u32[]{:S(2)}, u32[]{:S(2)}) collective-permute-start(bf16[64,128]{1,0:T(8,128)(2,1)S(1)} %constant_dynamic-update-slice_fusion.refs_0_), channel_id=1, source_target_pairs={{0,16},{1,17},{2,18},{3,19},{4,20},{5,21},{6,22},{7,23},{8,24},{9,... | collective-permute-start | bytes 49160 | tf_op jit(solution)/shard_map/ppermute | solution.py:35
  13.7 4.6 %collective-permute-start.1 = (bf16[64,128]{1,0:T(8,128)(2,1)S(1)}, bf16[64,128]{1,0:T(8,128)(2,1)S(1)}, u32[]{:S(2)}, u32[]{:S(2)}) collective-permute-start(bf16[64,128]{1,0:T(8,128)(2,1)S(1)} %constant_dynamic-update-slice_fusion.refs_0_), channel_id=1, source_target_pairs={{0,8},{1,9},{2,10},{3,11},{4,12},{5,13},{6,14},{7,15},{8,0},{9,1},... | collective-permute-start | bytes 49160 | tf_op jit(solution)/shard_map/ppermute | solution.py:35
  22.1 1.4 %collective-permute-start.7 = (f32[16,640]{1,0:T(8,128)S(1)}, f32[16,640]{1,0:T(8,128)S(1)}, u32[]{:S(2)}, u32[]{:S(2)}) collective-permute-start(f32[16,640]{1,0:T(8,128)S(1)} %get-tuple-element.43), channel_id=1, source_target_pairs={{0,1},{1,0},{2,3},{3,2},{4,5},{5,4},{6,7},{7,6},{8,9},{9,8},{10,11... | collective-permute-start | bytes 122888 | tf_op jit(solution)/shard_map/ppermute | solution.py:35
  23.5 5.0 %collective-permute-start.10 = (f32[16,640]{1,0:T(8,128)S(1)}, f32[16,640]{1,0:T(8,128)S(1)}, u32[]{:S(2)}, u32[]{:S(2)}) collective-permute-start(f32[16,640]{1,0:T(8,128)S(1)} %add.67), channel_id=1, source_target_pairs={{0,6},{1,7},{2,4},{3,5},{4,2},{5,3},{6,0},{7,1},{8,14},{9,15},{10,... | collective-permute-start | bytes 122888 | tf_op jit(solution)/shard_map/ppermute | solution.py:35
  26.0 4.0 %collective-permute-start.9 = (f32[16,640]{1,0:T(8,128)S(1)}, f32[16,640]{1,0:T(8,128)S(1)}, u32[]{:S(2)}, u32[]{:S(2)}) collective-permute-start(f32[16,640]{1,0:T(8,128)S(1)} %add.67), channel_id=1, source_target_pairs={{0,4},{1,5},{2,6},{3,7},{4,0},{5,1},{6,2},{7,3},{8,12},{9,13},{10,... | collective-permute-start | bytes 122888 | tf_op jit(solution)/shard_map/ppermute | solution.py:35
  26.5 4.0 %collective-permute-start.8 = (f32[16,640]{1,0:T(8,128)S(1)}, f32[16,640]{1,0:T(8,128)S(1)}, u32[]{:S(2)}, u32[]{:S(2)}) collective-permute-start(f32[16,640]{1,0:T(8,128)S(1)} %add.67), channel_id=1, source_target_pairs={{0,2},{1,3},{2,0},{3,1},{4,6},{5,7},{6,4},{7,5},{8,10},{9,11},{10,... | collective-permute-start | bytes 122888 | tf_op jit(solution)/shard_map/ppermute | solution.py:35
  30.6 6.9 %collective-permute-start.13 = (f32[16,640]{1,0:T(8,128)S(1)}, f32[16,640]{1,0:T(8,128)S(1)}, u32[]{:S(2)}, u32[]{:S(2)}) collective-permute-start(f32[16,640]{1,0:T(8,128)S(1)} %add_add_fusion.1), channel_id=1, source_target_pairs={{0,24},{1,25},{2,26},{3,27},{4,28},{5,29},{6,30},{7,31},{8,16},{9,... | collective-permute-start | bytes 122888 | tf_op jit(solution)/shard_map/ppermute | solution.py:35
  33.9 4.9 %collective-permute-start.12 = (f32[16,640]{1,0:T(8,128)S(1)}, f32[16,640]{1,0:T(8,128)S(1)}, u32[]{:S(2)}, u32[]{:S(2)}) collective-permute-start(f32[16,640]{1,0:T(8,128)S(1)} %add_add_fusion.1), channel_id=1, source_target_pairs={{0,16},{1,17},{2,18},{3,19},{4,20},{5,21},{6,22},{7,23},{8,24},{9,... | collective-permute-start | bytes 122888 | tf_op jit(solution)/shard_map/ppermute | solution.py:35
  33.9 4.9 %collective-permute-start.11 = (f32[16,640]{1,0:T(8,128)S(1)}, f32[16,640]{1,0:T(8,128)S(1)}, u32[]{:S(2)}, u32[]{:S(2)}) collective-permute-start(f32[16,640]{1,0:T(8,128)S(1)} %add_add_fusion.1), channel_id=1, source_target_pairs={{0,8},{1,9},{2,10},{3,11},{4,12},{5,13},{6,14},{7,15},{8,0},{9,1},... | collective-permute-start | bytes 122888 | tf_op jit(solution)/shard_map/ppermute | solution.py:35
  38.8 1.3 %collective-permute-start.14 = (f32[16,640]{1,0:T(8,128)S(1)}, f32[16,640]{1,0:T(8,128)S(1)}, u32[]{:S(2)}, u32[]{:S(2)}) collective-permute-start(f32[16,640]{1,0:T(8,128)S(1)} %add_add_fusion.held_ref), channel_id=1, source_target_pairs={{0,1},{1,0},{2,3},{3,2},{4,5},{5,4},{6,7},{7,6},{8,9},{9,8},{10,11... | collective-permute-start | bytes 122888 | tf_op jit(solution)/shard_map/ppermute | solution.py:35
  41.5 1.3 %collective-permute-start.15 = (f32[16,512]{1,0:T(8,128)S(1)}, f32[16,512]{1,0:T(8,128)S(1)}, u32[]{:S(2)}, u32[]{:S(2)}) collective-permute-start(f32[16,512]{1,0:T(8,128)S(1)} %get-tuple-element.48), channel_id=1, source_target_pairs={{0,1},{1,0},{2,3},{3,2},{4,5},{5,4},{6,7},{7,6},{8,9},{9,8},{10,11... | collective-permute-start | bytes 98312 | tf_op jit(solution)/shard_map/ppermute | solution.py:35
  42.8 4.8 %collective-permute-start.18 = (f32[16,512]{1,0:T(8,128)S(1)}, f32[16,512]{1,0:T(8,128)S(1)}, u32[]{:S(2)}, u32[]{:S(2)}) collective-permute-start(f32[16,512]{1,0:T(8,128)S(1)} %add.74), channel_id=1, source_target_pairs={{0,6},{1,7},{2,4},{3,5},{4,2},{5,3},{6,0},{7,1},{8,14},{9,15},{10,... | collective-permute-start | bytes 98312 | tf_op jit(solution)/shard_map/ppermute | solution.py:35
  44.3 3.9 %collective-permute-start.17 = (f32[16,512]{1,0:T(8,128)S(1)}, f32[16,512]{1,0:T(8,128)S(1)}, u32[]{:S(2)}, u32[]{:S(2)}) collective-permute-start(f32[16,512]{1,0:T(8,128)S(1)} %add.74), channel_id=1, source_target_pairs={{0,4},{1,5},{2,6},{3,7},{4,0},{5,1},{6,2},{7,3},{8,12},{9,13},{10,... | collective-permute-start | bytes 98312 | tf_op jit(solution)/shard_map/ppermute | solution.py:35
  44.8 3.9 %collective-permute-start.16 = (f32[16,512]{1,0:T(8,128)S(1)}, f32[16,512]{1,0:T(8,128)S(1)}, u32[]{:S(2)}, u32[]{:S(2)}) collective-permute-start(f32[16,512]{1,0:T(8,128)S(1)} %add.74), channel_id=1, source_target_pairs={{0,2},{1,3},{2,0},{3,1},{4,6},{5,7},{6,4},{7,5},{8,10},{9,11},{10,... | collective-permute-start | bytes 98312 | tf_op jit(solution)/shard_map/ppermute | solution.py:35
  48.7 6.2 %collective-permute-start.21 = (f32[16,512]{1,0:T(8,128)S(1)}, f32[16,512]{1,0:T(8,128)S(1)}, u32[]{:S(2)}, u32[]{:S(2)}) collective-permute-start(f32[16,512]{1,0:T(8,128)S(1)} %add_add_fusion.5), channel_id=1, source_target_pairs={{0,24},{1,25},{2,26},{3,27},{4,28},{5,29},{6,30},{7,31},{8,16},{9,... | collective-permute-start | bytes 98312 | tf_op jit(solution)/shard_map/ppermute | solution.py:35
  50.8 5.2 %collective-permute-start.20 = (f32[16,512]{1,0:T(8,128)S(1)}, f32[16,512]{1,0:T(8,128)S(1)}, u32[]{:S(2)}, u32[]{:S(2)}) collective-permute-start(f32[16,512]{1,0:T(8,128)S(1)} %add_add_fusion.5), channel_id=1, source_target_pairs={{0,16},{1,17},{2,18},{3,19},{4,20},{5,21},{6,22},{7,23},{8,24},{9,... | collective-permute-start | bytes 98312 | tf_op jit(solution)/shard_map/ppermute | solution.py:35
  50.9 5.0 %collective-permute-start.19 = (f32[16,512]{1,0:T(8,128)S(1)}, f32[16,512]{1,0:T(8,128)S(1)}, u32[]{:S(2)}, u32[]{:S(2)}) collective-permute-start(f32[16,512]{1,0:T(8,128)S(1)} %add_add_fusion.5), channel_id=1, source_target_pairs={{0,8},{1,9},{2,10},{3,11},{4,12},{5,13},{6,14},{7,15},{8,0},{9,1},... | collective-permute-start | bytes 98312 | tf_op jit(solution)/shard_map/ppermute | solution.py:35
  55.9 1.3 %collective-permute-start.22 = (f32[16,512]{1,0:T(8,128)S(1)}, f32[16,512]{1,0:T(8,128)S(1)}, u32[]{:S(2)}, u32[]{:S(2)}) collective-permute-start(f32[16,512]{1,0:T(8,128)S(1)} %add_add_fusion.4.held_ref), channel_id=1, source_target_pairs={{0,1},{1,0},{2,3},{3,2},{4,5},{5,4},{6,7},{7,6},{8,9},{9,8},{10,11... | collective-permute-start | bytes 98312 | tf_op jit(solution)/shard_map/ppermute | solution.py:35
  58.7 1.3 %collective-permute-start.23 = (f32[16,512]{1,0:T(8,128)S(1)}, f32[16,512]{1,0:T(8,128)S(1)}, u32[]{:S(2)}, u32[]{:S(2)}) collective-permute-start(f32[16,512]{1,0:T(8,128)S(1)} %get-tuple-element.54), channel_id=1, source_target_pairs={{0,1},{1,0},{2,3},{3,2},{4,5},{5,4},{6,7},{7,6},{8,9},{9,8},{10,11... | collective-permute-start | bytes 98312 | tf_op jit(solution)/shard_map/ppermute | solution.py:35
  60.0 4.8 %collective-permute-start.26 = (f32[16,512]{1,0:T(8,128)S(1)}, f32[16,512]{1,0:T(8,128)S(1)}, u32[]{:S(2)}, u32[]{:S(2)}) collective-permute-start(f32[16,512]{1,0:T(8,128)S(1)} %add.81), channel_id=1, source_target_pairs={{0,6},{1,7},{2,4},{3,5},{4,2},{5,3},{6,0},{7,1},{8,14},{9,15},{10,... | collective-permute-start | bytes 98312 | tf_op jit(solution)/shard_map/ppermute | solution.py:35
  62.5 3.9 %collective-permute-start.25 = (f32[16,512]{1,0:T(8,128)S(1)}, f32[16,512]{1,0:T(8,128)S(1)}, u32[]{:S(2)}, u32[]{:S(2)}) collective-permute-start(f32[16,512]{1,0:T(8,128)S(1)} %add.81), channel_id=1, source_target_pairs={{0,4},{1,5},{2,6},{3,7},{4,0},{5,1},{6,2},{7,3},{8,12},{9,13},{10,... | collective-permute-start | bytes 98312 | tf_op jit(solution)/shard_map/ppermute | solution.py:35
  63.0 3.9 %collective-permute-start.24 = (f32[16,512]{1,0:T(8,128)S(1)}, f32[16,512]{1,0:T(8,128)S(1)}, u32[]{:S(2)}, u32[]{:S(2)}) collective-permute-start(f32[16,512]{1,0:T(8,128)S(1)} %add.81), channel_id=1, source_target_pairs={{0,2},{1,3},{2,0},{3,1},{4,6},{5,7},{6,4},{7,5},{8,10},{9,11},{10,... | collective-permute-start | bytes 98312 | tf_op jit(solution)/shard_map/ppermute | solution.py:35
  66.9 5.8 %collective-permute-start.29 = (f32[16,512]{1,0:T(8,128)S(1)}, f32[16,512]{1,0:T(8,128)S(1)}, u32[]{:S(2)}, u32[]{:S(2)}) collective-permute-start(f32[16,512]{1,0:T(8,128)S(1)} %add_add_fusion.3), channel_id=1, source_target_pairs={{0,24},{1,25},{2,26},{3,27},{4,28},{5,29},{6,30},{7,31},{8,16},{9,... | collective-permute-start | bytes 98312 | tf_op jit(solution)/shard_map/ppermute | solution.py:35
  68.8 5.0 %collective-permute-start.28 = (f32[16,512]{1,0:T(8,128)S(1)}, f32[16,512]{1,0:T(8,128)S(1)}, u32[]{:S(2)}, u32[]{:S(2)}) collective-permute-start(f32[16,512]{1,0:T(8,128)S(1)} %add_add_fusion.3), channel_id=1, source_target_pairs={{0,16},{1,17},{2,18},{3,19},{4,20},{5,21},{6,22},{7,23},{8,24},{9,... | collective-permute-start | bytes 98312 | tf_op jit(solution)/shard_map/ppermute | solution.py:35
  69.6 4.3 %collective-permute-start.27 = (f32[16,512]{1,0:T(8,128)S(1)}, f32[16,512]{1,0:T(8,128)S(1)}, u32[]{:S(2)}, u32[]{:S(2)}) collective-permute-start(f32[16,512]{1,0:T(8,128)S(1)} %add_add_fusion.3), channel_id=1, source_target_pairs={{0,8},{1,9},{2,10},{3,11},{4,12},{5,13},{6,14},{7,15},{8,0},{9,1},... | collective-permute-start | bytes 98312 | tf_op jit(solution)/shard_map/ppermute | solution.py:35
  71.7 2.4 %collective-permute-start.31 = (f32[8,2048]{1,0:T(8,128)S(1)}, f32[8,2048]{1,0:T(8,128)S(1)}, u32[]{:S(2)}, u32[]{:S(2)}) collective-permute-start(f32[8,2048]{1,0:T(8,128)S(1)} %get-tuple-element.63), channel_id=1, source_target_pairs={{0,1},{1,0},{2,3},{3,2},{4,5},{5,4},{6,7},{7,6},{8,9},{9,8},{10,11... | collective-permute-start | bytes 196616 | tf_op jit(solution)/shard_map/ppermute | solution.py:35
  71.8 5.0 %collective-permute-start.32 = (f32[8,2048]{1,0:T(8,128)S(1)}, f32[8,2048]{1,0:T(8,128)S(1)}, u32[]{:S(2)}, u32[]{:S(2)}) collective-permute-start(f32[8,2048]{1,0:T(8,128)S(1)} %get-tuple-element.64), channel_id=1, source_target_pairs={{0,2},{1,3},{2,0},{3,1},{4,6},{5,7},{6,4},{7,5},{8,10},{9,11},{10,... | collective-permute-start | bytes 196616 | tf_op jit(solution)/shard_map/ppermute | solution.py:35
  72.7 4.4 %collective-permute-start.33 = (f32[8,2048]{1,0:T(8,128)S(1)}, f32[8,2048]{1,0:T(8,128)S(1)}, u32[]{:S(2)}, u32[]{:S(2)}) collective-permute-start(f32[8,2048]{1,0:T(8,128)S(1)} %get-tuple-element.65), channel_id=1, source_target_pairs={{0,3},{1,2},{2,1},{3,0},{4,7},{5,6},{6,5},{7,4},{8,11},{9,10},{10,... | collective-permute-start | bytes 196616 | tf_op jit(solution)/shard_map/ppermute | solution.py:35
  73.9 3.3 %collective-permute-start.30 = (f32[16,512]{1,0:T(8,128)S(1)}, f32[16,512]{1,0:T(8,128)S(1)}, u32[]{:S(2)}, u32[]{:S(2)}) collective-permute-start(f32[16,512]{1,0:T(8,128)S(1)} %add_add_fusion.2.held_ref), channel_id=1, source_target_pairs={{0,1},{1,0},{2,3},{3,2},{4,5},{5,4},{6,7},{7,6},{8,9},{9,8},{10,11... | collective-permute-start | bytes 98312 | tf_op jit(solution)/shard_map/ppermute | solution.py:35

commit v8 on v7

--- a/solution.py
+++ b/solution.py
@@ -124,7 +124,7 @@
     points.wait()
 
 
-def build_kernel(na, me_ref, a0, a1, a2, a3, x_ref, khi_ref, klo_ref, tinv_ref, aug_ref):
+def build_kernel(na, me_ref, a0, a1, a2, a3, x_ref, khi_ref, klo_ref, aug_ref):
     docs, feat = x_ref.shape
     quarter = a0.shape[0]
     scale = 1.0 / (feat * width_h)
@@ -135,23 +135,29 @@
         aug_ref[at, 0:feat] = (value * (-2.0 * scale)).astype(bf16)
         aug_ref[at, feat:] = aug_columns(row_sizes(value) * scale + 1.0, None, quarter)
     tile = min(256, docs)
+    row = lax.broadcasted_iota(jnp.int32, (16, tile), 0)
+    rest = jnp.zeros((aug_ref.shape[1] - feat - 16, tile), bf16)
     for col in range(0, docs, tile):
-        raw = x_ref[col : col + tile, :]
-        right = jnp.concatenate([raw, aug_columns(None, row_sizes(raw.astype(f32)) * scale, tile)], axis=1)
-        total = jnp.zeros((8, tile), f32)
+        turned = x_ref[col : col + tile, :].T
+        wide = turned.astype(f32)
+        size = jnp.sum(wide * wide, axis=0, keepdims=True) * scale
+        extra = jnp.where(row < 3, 1.0, 0.0)
+        for k, part in enumerate(split3(size)):
+            extra = jnp.where(row == 3 + k, part.astype(f32), extra)
+        right = jnp.concatenate([turned, extra.astype(bf16), rest], axis=0)
         for at in range(0, aug_ref.shape[0], 256):
-            kern = eighth(mm(aug_ref[at : at + 256, :], right, NT))
+            kern = eighth(mm(aug_ref[at : at + 256, :], right))
             high, low = split2(kern)
             khi_ref[at : at + 256, col : col + tile] = high
             klo_ref[at : at + 256, col : col + tile] = low
-            total = total + jnp.sum(kern.reshape(32, 8, tile), axis=0)
-        tinv_ref[:, col : col + tile] = 1.0 / jnp.sum(total, axis=0, keepdims=True)
 
 
 def times(vec, khi, klo):
+    more = vec.shape[0] > 3 * CLASSES
     one = mm(vec, khi)
-    two = mm(vec[0 : 2 * CLASSES], klo)
-    return one[0:CLASSES] + (one[CLASSES : 2 * CLASSES] + two[0:CLASSES] + (one[2 * CLASSES :] + two[CLASSES:]))
+    two = mm(vec if more else vec[0 : 2 * CLASSES], klo)
+    out = one[0:CLASSES] + (one[CLASSES : 2 * CLASSES] + two[0:CLASSES] + (one[2 * CLASSES : 3 * CLASSES] + two[CLASSES : 2 * CLASSES]))
+    return (out, one[3 * CLASSES :] + two[3 * CLASSES :]) if more else out
 
 
 def times_back(value, khi, klo):
@@ -184,9 +190,10 @@
 
 def back_rows(w_ref, khi, klo, dims):
     one = mm(w_ref[...], khi, dims)
-    two = mm(w_ref[...], klo, dims)
+    rows = w_ref.shape[0]
+    two = mm(w_ref[0 : 2 * CLASSES, :] if rows == 3 * CLASSES else w_ref[...], klo, dims)
     out = one[0:CLASSES] + (one[CLASSES : 2 * CLASSES] + two[0:CLASSES] + (one[2 * CLASSES : 3 * CLASSES] + two[CLASSES : 2 * CLASSES]))
-    return out, one[3 * CLASSES :] + two[3 * CLASSES :]
+    return out, one[3 * CLASSES :] + two[3 * CLASSES :] if rows > 3 * CLASSES else None
 
 
 def back_degree(w_ref, khi, klo, out_ref):
@@ -209,7 +216,7 @@
 
 def first_send(na, labs, slots, gain, me_ref, *refs):
     lab_refs = refs[: len(slots)]
-    (aug_ref, khi_ref, klo_ref, tinv_ref, send_ref, w_ref, rhs_ref, mid_ref, zhi_ref, zlo_ref, spread_ref,
+    (aug_ref, khi_ref, klo_ref, send_ref, w_ref, rhs_ref, mid_ref, zhi_ref, zlo_ref, spread_ref, tinv_ref,
      laug, hot) = refs[len(slots) :]
     feat = laug.shape[1] - LANES
     docs = me_ref[0] // na
@@ -228,8 +235,11 @@
     rhs_ref[...] = rhs
     middle = rhs - mean_of(rhs)
     mid_ref[...] = middle
-    tinv = tinv_ref[...]
-    spread = times(pieces(middle), khi_ref[...], klo_ref[...]) * tinv
+    vec = jnp.concatenate([*split3(middle), jnp.ones(middle.shape, bf16)], axis=0)
+    spread, sums = times(vec, khi_ref[...], klo_ref[...])
+    tinv = 1.0 / sums[0:1]
+    tinv_ref[...] = tinv
+    spread = spread * tinv
     spread_ref[...] = spread
     put_weights(w_ref, spread, tinv)
     row = lax.broadcasted_iota(jnp.int32, (CLASSES, tinv.shape[1]), 0)
@@ -435,10 +445,10 @@
     slots = [[m >> a_bits for m in masks]] + [[(m ^ mask) >> a_bits for m in masks] for mask in stages[-1]]
 
     k_sds = sds((total, docs), bf16)
-    khi, klo, tinv, aug = call(
+    khi, klo, aug = call(
         functools.partial(build_kernel, na),
         [SMEM] + [VMEM] * 5,
-        [k_sds, k_sds, sds((1, docs), f32), sds((total, feat + LANES), bf16)],
+        [k_sds, k_sds, sds((total, feat + LANES), bf16)],
         [],
         flops=2 * total * docs * 256,
         moved=4 * total * docs,
@@ -453,13 +463,13 @@
     w_sds = sds((3 * CLASSES, docs), bf16)
     work = dict(flops=4 * total * docs * 64, moved=2 * total * docs)
 
-    send, w, rhs, middle, zhi, zlo, spread0 = call(
+    send, w, rhs, middle, zhi, zlo, spread0, tinv = call(
         functools.partial(first_send, na, labs, slots, CLASSES * lab_scale),
-        [SMEM] + [VMEM] * (len(lab_arrays) + 4),
-        [long_sds, sds((4 * CLASSES, docs), bf16), flat_sds, flat_sds, z_sds, z_sds, docs_sds],
+        [SMEM] + [VMEM] * (len(lab_arrays) + 3),
+        [long_sds, sds((4 * CLASSES, docs), bf16), flat_sds, flat_sds, z_sds, z_sds, docs_sds, sds((1, docs), f32)],
         [pltpu.VMEM((labeled, feat + LANES), bf16), pltpu.VMEM((labeled, LANES), f32)],
         **work,
-    )(me, *lab_arrays, aug, khi, klo, tinv)
+    )(me, *lab_arrays, aug, khi, klo)
     got = swap_core(send)
     mine = call(first_own, [SMEM] + [VMEM] * 3, [long_sds], [], **work)(me, w, khi, klo)[0]
     held = reduce_chips(mine + got, n_bits)

time: 78.2 us -> 77.6 us (level)
  no operation moved by 1% of the time
where the time goes in v8:
time: 77.6 us; the launch traced here: 77.4 us
  starting transfers between devices  36.2 us (47%)
  Pallas kernels  20.4 us (26%)
  waiting for transfers between devices  19.9 us (26%)
  between operations  0.8 us (1%)
    ppermute x34, starting transfers between devices, swap(): return lax.ppermute(value, EVERY, [(i, i ^ mask) for i in range(count)])  36.2 us
    ppermute x34, waiting for transfers between devices, swap(): return lax.ppermute(value, EVERY, [(i, i ^ mask) for i in range(count)])  19.9 us
    pallas_call x1, Pallas kernels, run(): call(functools.partial(first_send, na, labs, slots, CLASSES * lab_scale),...  3.74 us
    pallas_call x1, Pallas kernels, run(): call(functools.partial(build_kernel, na), [SMEM] + [VMEM] * 5, [k_sds, k_...  2.87 us
    pallas_call x1, Pallas kernels, run(): pl.pallas_call(functools.partial(label_kernel, na), grid_spec=pltpu.Prefe...  2.06 us
    pallas_call x1, Pallas kernels, run(): call(functools.partial(third_send, lab_scale, graph_scale), [SMEM] + [VME...  1.55 us
  transfers between devices with their start and end apart: 34, of which 22 were waited for; matrix products, arithmetic and copies ran while one was open for 0% of the time, Pallas kernels for 17%

profile of v8, /device:TPU:0, one launch (start us, length us, event | category | flops | bytes accessed | tf_op | source)
XLA Modules:
  0.0 77.4 jit_solution(12784684096913312844)
XLA Ops:
  0.6 0.6 collective-permute-start.4
  1.2 2.6 %collective-permute-start.6 = (bf16[256,128]{1,0:T(8,128)(2,1)}, bf16[256,128]{1,0:T(8,128)(2,1)S(1)}, u32[]{:S(2)}, u32[]{:S(2)}) collective-permute-start(bf16[256,128]{1,0:T(8,128)(2,1)} %anch_ref.1), channel_id=1, source_target_pairs={{0,3},{1,2},{2,1},{3,0},{4,7},{5,6},{6,5},{7,4},{8,11},{9,10},{10,... | collective-permute-start | bytes 196616 | tf_op jit(solution)/shard_map/ppermute | solution.py:35
  3.8 2.1 %label_rows.1 = (bf16[32,128]{1,0:T(8,128)(2,1)S(1)}, bf16[2048,128]{1,0:T(8,128)(2,1)S(1)}, bf16[256,128]{1,0:T(8,128)(2,1)S(1)}) custom-call(s32[1]{0:T(128)} %bitcast.me_ref, s32[16]{0:T(128)} %idx_ref.1, s32[16]{0:T(128)} %cls_ref.1, bf16[8192,128]{1,0:T(8,128)(2,1)} %feat_ref.1, bf16[256,128]{1,0:T(8,128)(2,1)} %anch_ref.1), custom_call_target="tpu_custom_call" | custom-call | tf_op jit(solution)/shard_map/label_rows/pallas_call | solution.py:412
  5.9 2.1 %collective-permute-start = (bf16[32,128]{1,0:T(8,128)(2,1)S(1)}, bf16[32,128]{1,0:T(8,128)(2,1)S(1)}, u32[]{:S(2)}, u32[]{:S(2)}) collective-permute-start(bf16[32,128]{1,0:T(8,128)(2,1)S(1)} %get-tuple-element.35), channel_id=1, source_target_pairs={{0,4},{1,5},{2,6},{3,7},{4,0},{5,1},{6,2},{7,3},{8,12},{9,13},{10,... | collective-permute-start | bytes 24584 | tf_op jit(solution)/shard_map/ppermute | solution.py:35
  8.0 1.6 %collective-permute-done = bf16[32,128]{1,0:T(8,128)(2,1)S(1)} collective-permute-done((bf16[32,128]{1,0:T(8,128)(2,1)S(1)}, bf16[32,128]{1,0:T(8,128)(2,1)S(1)}, u32[]{:S(2)}, u32[]{:S(2)}) %collective-permute-start) | collective-permute-done | bytes 8224 | tf_op jit(solution)/shard_map/ppermute | solution.py:35
  9.6 4.1 %collective-permute-start.3 = (bf16[64,128]{1,0:T(8,128)(2,1)S(1)}, bf16[64,128]{1,0:T(8,128)(2,1)S(1)}, u32[]{:S(2)}, u32[]{:S(2)}) collective-permute-start(bf16[64,128]{1,0:T(8,128)(2,1)S(1)} %constant_dynamic-update-slice_fusion.refs_0_), channel_id=1, source_target_pairs={{0,24},{1,25},{2,26},{3,27},{4,28},{5,29},{6,30},{7,31},{8,16},{9,... | collective-permute-start | bytes 49160 | tf_op jit(solution)/shard_map/ppermute | solution.py:35
  13.7 0.6 collective-permute-start.1
  14.3 2.9 %shard_map.59 = (bf16[1024,2048]{1,0:T(8,128)(2,1)S(1)}, bf16[1024,2048]{1,0:T(8,128)(2,1)S(1)}, bf16[1024,256]{1,0:T(8,128)(2,1)S(1)}) custom-call(s32[1]{0:T(128)} %bitcast.me_ref, bf16[256,128]{1,0:T(8,128)(2,1)S(1)} %get-tuple-element.36.a0, bf16[256,128]{1,0:T(8,128)(2,1)S(1)} %collective-permute-done.4.a1, ...), custom_call_target="tpu_custom_call" | custom-call | flops 1073741824 | bytes 8388608 | tf_op jit(solution)/shard_map/pallas_call | solution.py:448
  17.2 1.2 %collective-permute-done.2.refs_2_ = bf16[64,128]{1,0:T(8,128)(2,1)S(1)} collective-permute-done((bf16[64,128]{1,0:T(8,128)(2,1)S(1)}, bf16[64,128]{1,0:T(8,128)(2,1)S(1)}, u32[]{:S(2)}, u32[]{:S(2)}) %collective-permute-start.2) | collective-permute-done | bytes 16416 | tf_op jit(solution)/shard_map/ppermute | solution.py:35
  18.3 3.7 %shard_map.60 = (f32[16,640]{1,0:T(8,128)S(1)}, bf16[64,2048]{1,0:T(8,128)(2,1)S(1)}, f32[16,1024]{1,0:T(8,128)S(1)}, f32[16,1024]{1,0:T(8,128)S(1)}, bf16[1024,...) custom-call(s32[1]{0:T(128)} %bitcast.me_ref, ...), custom_call_target="tpu_custom_call" | custom-call | flops 536870912 | bytes 4194304 | tf_op jit(solution)/shard_map/pallas_call | solution.py:466
  22.2 1.3 %shard_map.61 = f32[16,640]{1,0:T(8,128)S(1)} custom-call(s32[1]{0:T(128)} %bitcast.me_ref, bf16[64,2048]{1,0:T(8,128)(2,1)S(1)} %get-tuple-element.41.w_ref, bf16[1024,2048]{1,0:T(8,128)(2,1)S(1)} %get-tuple-element.39.refs_5_.khi_ref.in_ref, bf16[1024,2048]{1,0:T(8,128)(2,1)S(1)} %get-tuple-element.40.refs_6_.klo_ref.in_ref), custom_call_target="tpu_custom_call" | custom-call | flops 536870912 | bytes 4194304 | tf_op jit(solution)/shard_map/pallas_call | solution.py:474
  23.5 2.5 %collective-permute-start.10 = (f32[16,640]{1,0:T(8,128)S(1)}, f32[16,640]{1,0:T(8,128)S(1)}, u32[]{:S(2)}, u32[]{:S(2)}) collective-permute-start(f32[16,640]{1,0:T(8,128)S(1)} %add.67), channel_id=1, source_target_pairs={{0,6},{1,7},{2,4},{3,5},{4,2},{5,3},{6,0},{7,1},{8,14},{9,15},{10,... | collective-permute-start | bytes 122888 | tf_op jit(solution)/shard_map/ppermute | solution.py:35
  26.1 0.5 collective-permute-start.9
  26.6 0.5 collective-permute-start.8
  27.1 1.4 %collective-permute-done.10 = f32[16,640]{1,0:T(8,128)S(1)} collective-permute-done((f32[16,640]{1,0:T(8,128)S(1)}, f32[16,640]{1,0:T(8,128)S(1)}, u32[]{:S(2)}, u32[]{:S(2)}) %collective-permute-start.10) | collective-permute-done | bytes 40992 | tf_op jit(solution)/shard_map/ppermute | solution.py:35
  28.5 1.5 %collective-permute-done.9 = f32[16,640]{1,0:T(8,128)S(1)} collective-permute-done((f32[16,640]{1,0:T(8,128)S(1)}, f32[16,640]{1,0:T(8,128)S(1)}, u32[]{:S(2)}, u32[]{:S(2)}) %collective-permute-start.9) | collective-permute-done | bytes 40992 | tf_op jit(solution)/shard_map/ppermute | solution.py:35
  30.1 0.5 collective-permute-done.8
  30.6 2.7 %collective-permute-start.13 = (f32[16,640]{1,0:T(8,128)S(1)}, f32[16,640]{1,0:T(8,128)S(1)}, u32[]{:S(2)}, u32[]{:S(2)}) collective-permute-start(f32[16,640]{1,0:T(8,128)S(1)} %add_add_fusion.1), channel_id=1, source_target_pairs={{0,24},{1,25},{2,26},{3,27},{4,28},{5,29},{6,30},{7,31},{8,16},{9,... | collective-permute-start | bytes 122888 | tf_op jit(solution)/shard_map/ppermute | solution.py:35
  33.3 1.7 %collective-permute-start.11 = (f32[16,640]{1,0:T(8,128)S(1)}, f32[16,640]{1,0:T(8,128)S(1)}, u32[]{:S(2)}, u32[]{:S(2)}) collective-permute-start(f32[16,640]{1,0:T(8,128)S(1)} %add_add_fusion.1), channel_id=1, source_target_pairs={{0,8},{1,9},{2,10},{3,11},{4,12},{5,13},{6,14},{7,15},{8,0},{9,1},... | collective-permute-start | bytes 122888 | tf_op jit(solution)/shard_map/ppermute | solution.py:35
  35.0 1.2 %shard_map.62.thi_ref = bf16[2048,1024]{1,0:T(8,128)(2,1)S(1)} custom-call(bf16[1024,2048]{1,0:T(8,128)(2,1)S(1)} %get-tuple-element.39.refs_5_.khi_ref.in_ref), custom_call_target="tpu_custom_call" | custom-call | flops 1048576 | bytes 262144 | tf_op jit(solution)/shard_map/pallas_call | solution.py:476
  36.3 1.2 %shard_map.63.tlo_ref = bf16[2048,1024]{1,0:T(8,128)(2,1)S(1)} custom-call(bf16[1024,2048]{1,0:T(8,128)(2,1)S(1)} %get-tuple-element.40.refs_6_.klo_ref.in_ref), custom_call_target="tpu_custom_call" | custom-call | flops 1048576 | bytes 262144 | tf_op jit(solution)/shard_map/pallas_call | solution.py:477
  37.5 0.7 collective-permute-done.12
  38.3 0.8 %shard_map.64 = (f32[16,2048]{1,0:T(8,128)S(1)}, f32[1,512]{1,0:T(1,128)S(1)}) custom-call(s32[1]{0:T(128)} %bitcast.me_ref, f32[16,640]{1,0:T(8,128)S(1)} %add_add_fusion.held_ref, f32[16,1024]{1,0:T(8,128)S(1)} %get-tuple-element.43.mid_ref, bf16[1024,2048]{1,0:T(8,128)(2,1)S(1)} %get-tuple-element.39.refs_5_.khi_ref.in_ref, ...), custom_call_target="tpu_custom_call" | custom-call | flops 536870912 | bytes 4194304 | tf_op jit(solution)/shard_map/pallas_call | solution.py:481
  39.1 0.4 collective-permute-done.14.got_ref
  39.5 1.5 %shard_map.65 = (f32[16,512]{1,0:T(8,128)S(1)}, bf16[48,2048]{1,0:T(8,128)(2,1)S(1)}, f32[1,1024]{1,0:T(1,128)S(1)}) custom-call(s32[1]{0:T(128)} %bitcast.me_ref, f32[16,640]{1,0:T(8,128)S(1)} %collective-permute-done.14.got_ref, f32[16,1024]{1,0:T(8,128)S(1)} %get-tuple-element.43.mid_ref, bf16[1024,2048]{1,0:T(8,128)(2,1)S(1)} %get-tuple-element.39.refs_5_.khi_ref.in_ref, ...), custom_call_target="tpu_custom_call" | custom-call | flops 536870912 | bytes 4194304 | tf_op jit(solution)/shard_map/pallas_call | solution.py:484
  41.0 0.2 collective-permute-start.15
  41.1 0.8 shard_map.66
  41.9 0.3 collective-permute-done.15
  42.2 1.5 %collective-permute-start.18 = (f32[16,512]{1,0:T(8,128)S(1)}, f32[16,512]{1,0:T(8,128)S(1)}, u32[]{:S(2)}, u32[]{:S(2)}) collective-permute-start(f32[16,512]{1,0:T(8,128)S(1)} %add.74), channel_id=1, source_target_pairs={{0,6},{1,7},{2,4},{3,5},{4,2},{5,3},{6,0},{7,1},{8,14},{9,15},{10,... | collective-permute-start | bytes 98312 | tf_op jit(solution)/shard_map/ppermute | solution.py:35
  43.7 0.5 collective-permute-start.17
  44.2 1.5 %collective-permute-start.16 = (f32[16,512]{1,0:T(8,128)S(1)}, f32[16,512]{1,0:T(8,128)S(1)}, u32[]{:S(2)}, u32[]{:S(2)}) collective-permute-start(f32[16,512]{1,0:T(8,128)S(1)} %add.74), channel_id=1, source_target_pairs={{0,2},{1,3},{2,0},{3,1},{4,6},{5,7},{6,4},{7,5},{8,10},{9,11},{10,... | collective-permute-start | bytes 98312 | tf_op jit(solution)/shard_map/ppermute | solution.py:35
  45.7 1.3 %collective-permute-done.18 = f32[16,512]{1,0:T(8,128)S(1)} collective-permute-done((f32[16,512]{1,0:T(8,128)S(1)}, f32[16,512]{1,0:T(8,128)S(1)}, u32[]{:S(2)}, u32[]{:S(2)}) %collective-permute-start.18) | collective-permute-done | bytes 32800 | tf_op jit(solution)/shard_map/ppermute | solution.py:35
  47.0 0.6 collective-permute-done.17
  47.6 0.5 collective-permute-done.16
  48.2 2.1 %collective-permute-start.21 = (f32[16,512]{1,0:T(8,128)S(1)}, f32[16,512]{1,0:T(8,128)S(1)}, u32[]{:S(2)}, u32[]{:S(2)}) collective-permute-start(f32[16,512]{1,0:T(8,128)S(1)} %add_add_fusion.5), channel_id=1, source_target_pairs={{0,24},{1,25},{2,26},{3,27},{4,28},{5,29},{6,30},{7,31},{8,16},{9,... | collective-permute-start | bytes 98312 | tf_op jit(solution)/shard_map/ppermute | solution.py:35
  50.2 0.3 collective-permute-start.20
  50.5 2.1 %collective-permute-start.19 = (f32[16,512]{1,0:T(8,128)S(1)}, f32[16,512]{1,0:T(8,128)S(1)}, u32[]{:S(2)}, u32[]{:S(2)}) collective-permute-start(f32[16,512]{1,0:T(8,128)S(1)} %add_add_fusion.5), channel_id=1, source_target_pairs={{0,8},{1,9},{2,10},{3,11},{4,12},{5,13},{6,14},{7,15},{8,0},{9,1},... | collective-permute-start | bytes 98312 | tf_op jit(solution)/shard_map/ppermute | solution.py:35
  52.6 0.6 shard_map.67.lab_ref
  53.2 0.9 %collective-permute-done.21 = f32[16,512]{1,0:T(8,128)S(1)} collective-permute-done((f32[16,512]{1,0:T(8,128)S(1)}, f32[16,512]{1,0:T(8,128)S(1)}, u32[]{:S(2)}, u32[]{:S(2)}) %collective-permute-start.21) | collective-permute-done | bytes 32800 | tf_op jit(solution)/shard_map/ppermute | solution.py:35
  54.1 1.3 %collective-permute-done.20 = f32[16,512]{1,0:T(8,128)S(1)} collective-permute-done((f32[16,512]{1,0:T(8,128)S(1)}, f32[16,512]{1,0:T(8,128)S(1)}, u32[]{:S(2)}, u32[]{:S(2)}) %collective-permute-start.20) | collective-permute-done | bytes 32800 | tf_op jit(solution)/shard_map/ppermute | solution.py:35
  55.5 0.8 %shard_map.68.part_ref = f32[16,2048]{1,0:T(8,128)S(1)} custom-call(s32[1]{0:T(128)} %bitcast.me_ref, f32[16,512]{1,0:T(8,128)S(1)} %add_add_fusion.4.held_ref, f32[16,1024]{1,0:T(8,128)S(1)} %get-tuple-element.49.rhs_ref, f32[16,1024]{1,0:T(8,128)S(1)} %shard_map.67.lab_ref, bf16[1024,2048]{1,0:T(8,128)(2,1)S(1)} %get-tuple-element.39.refs_5_.khi_ref.in_ref, ...), custom_call_target="tpu_custom_call" | custom-call | flops 536870912 | bytes 4194304 | tf_op jit(solution)/shard_map/pallas_call | solution.py:492
  56.3 0.4 collective-permute-done.22.got_ref
  56.7 1.6 %shard_map.69 = (f32[16,512]{1,0:T(8,128)S(1)}, bf16[48,2048]{1,0:T(8,128)(2,1)S(1)}, f32[16,2048]{1,0:T(8,128)S(1)}, f32[16,1024]{1,0:T(8,128)S(1)}, f32[16,102...) custom-call(s32[1]{0:T(128)} %bitcast.me_ref, f32[16,512]{1,0:T(8,128)S(1)} %add_add_fusion.4.held_ref, ...), custom_call_target="tpu_custom_call" | custom-call | flops 536870912 | bytes 4194304 | tf_op jit(solution)/shard_map/pallas_call | solution.py:495
  58.2 0.2 collective-permute-start.23
  58.4 0.8 shard_map.70
  59.2 0.3 collective-permute-done.23
  59.4 2.4 %collective-permute-start.26 = (f32[16,512]{1,0:T(8,128)S(1)}, f32[16,512]{1,0:T(8,128)S(1)}, u32[]{:S(2)}, u32[]{:S(2)}) collective-permute-start(f32[16,512]{1,0:T(8,128)S(1)} %add.81), channel_id=1, source_target_pairs={{0,6},{1,7},{2,4},{3,5},{4,2},{5,3},{6,0},{7,1},{8,14},{9,15},{10,... | collective-permute-start | bytes 98312 | tf_op jit(solution)/shard_map/ppermute | solution.py:35
  61.9 0.5 collective-permute-start.25
  62.4 0.5 collective-permute-start.24
  62.9 1.3 %collective-permute-done.26 = f32[16,512]{1,0:T(8,128)S(1)} collective-permute-done((f32[16,512]{1,0:T(8,128)S(1)}, f32[16,512]{1,0:T(8,128)S(1)}, u32[]{:S(2)}, u32[]{:S(2)}) %collective-permute-start.26) | collective-permute-done | bytes 32800 | tf_op jit(solution)/shard_map/ppermute | solution.py:35
  64.3 1.5 %collective-permute-done.25 = f32[16,512]{1,0:T(8,128)S(1)} collective-permute-done((f32[16,512]{1,0:T(8,128)S(1)}, f32[16,512]{1,0:T(8,128)S(1)}, u32[]{:S(2)}, u32[]{:S(2)}) %collective-permute-start.25) | collective-permute-done | bytes 32800 | tf_op jit(solution)/shard_map/ppermute | solution.py:35
  65.8 0.5 collective-permute-done.24
  66.3 1.9 %collective-permute-start.29 = (f32[16,512]{1,0:T(8,128)S(1)}, f32[16,512]{1,0:T(8,128)S(1)}, u32[]{:S(2)}, u32[]{:S(2)}) collective-permute-start(f32[16,512]{1,0:T(8,128)S(1)} %add_add_fusion.3), channel_id=1, source_target_pairs={{0,24},{1,25},{2,26},{3,27},{4,28},{5,29},{6,30},{7,31},{8,16},{9,... | collective-permute-start | bytes 98312 | tf_op jit(solution)/shard_map/ppermute | solution.py:35
  68.2 0.8 %collective-permute-start.28 = (f32[16,512]{1,0:T(8,128)S(1)}, f32[16,512]{1,0:T(8,128)S(1)}, u32[]{:S(2)}, u32[]{:S(2)}) collective-permute-start(f32[16,512]{1,0:T(8,128)S(1)} %add_add_fusion.3), channel_id=1, source_target_pairs={{0,16},{1,17},{2,18},{3,19},{4,20},{5,21},{6,22},{7,23},{8,24},{9,... | collective-permute-start | bytes 98312 | tf_op jit(solution)/shard_map/ppermute | solution.py:35
  69.0 1.8 %collective-permute-start.27 = (f32[16,512]{1,0:T(8,128)S(1)}, f32[16,512]{1,0:T(8,128)S(1)}, u32[]{:S(2)}, u32[]{:S(2)}) collective-permute-start(f32[16,512]{1,0:T(8,128)S(1)} %add_add_fusion.3), channel_id=1, source_target_pairs={{0,8},{1,9},{2,10},{3,11},{4,12},{5,13},{6,14},{7,15},{8,0},{9,1},... | collective-permute-start | bytes 98312 | tf_op jit(solution)/shard_map/ppermute | solution.py:35
  70.8 0.3 shard_map.71
  71.2 0.6 collective-permute-start.32
  71.8 0.3 collective-permute-done.29
  72.1 0.9 %collective-permute-start.33 = (f32[8,2048]{1,0:T(8,128)S(1)}, f32[8,2048]{1,0:T(8,128)S(1)}, u32[]{:S(2)}, u32[]{:S(2)}) collective-permute-start(f32[8,2048]{1,0:T(8,128)S(1)} %get-tuple-element.65), channel_id=1, source_target_pairs={{0,3},{1,2},{2,1},{3,0},{4,7},{5,6},{6,5},{7,4},{8,11},{9,10},{10,... | collective-permute-start | bytes 196616 | tf_op jit(solution)/shard_map/ppermute | solution.py:35
  73.0 0.2 collective-permute-done.28
  73.3 0.2 collective-permute-start.30
  73.5 2.7 %collective-permute-done.32.refs_2_ = f32[8,2048]{1,0:T(8,128)S(1)} collective-permute-done((f32[8,2048]{1,0:T(8,128)S(1)}, f32[8,2048]{1,0:T(8,128)S(1)}, u32[]{:S(2)}, u32[]{:S(2)}) %collective-permute-start.32) | collective-permute-done | bytes 65568 | tf_op jit(solution)/shard_map/ppermute | solution.py:35
  76.2 0.3 collective-permute-done.33.refs_3_
  76.5 0.8 %shard_map.72 = (f32[16,256]{1,0:T(8,128)}, f32[4,8192]{1,0:T(4,128)}) custom-call(s32[1]{0:T(128)} %bitcast.me_ref, f32[16,512]{1,0:T(8,128)S(1)} %add_add_fusion.2.held_ref, f32[16,512]{1,0:T(8,128)S(1)} %collective-permute-done.30.got_ref, f32[16,1024]{1,0:T(8,128)S(1)} %get-tuple-element.55.direc_ref, f32[16,1024]{1,0:T(8,128)S(1)} %get-tuple-element.56.mid_ref, ...), custom_call_target="tpu_custom_call" | custom-call | flops 1048576 | bytes 262144 | tf_op jit(solution)/shard_map/pallas_call | solution.py:517
  (30 shorter events, 0.5 us)
Async XLA Ops:
  0.6 13.1 %collective-permute-start.4 = (bf16[256,128]{1,0:T(8,128)(2,1)}, bf16[256,128]{1,0:T(8,128)(2,1)S(1)}, u32[]{:S(2)}, u32[]{:S(2)}) collective-permute-start(bf16[256,128]{1,0:T(8,128)(2,1)} %anch_ref.1), channel_id=1, source_target_pairs={{0,1},{1,0},{2,3},{3,2},{4,5},{5,4},{6,7},{7,6},{8,9},{9,8},{10,11... | collective-permute-start | bytes 196616 | tf_op jit(solution)/shard_map/ppermute | solution.py:35
  1.2 13.1 %collective-permute-start.6 = (bf16[256,128]{1,0:T(8,128)(2,1)}, bf16[256,128]{1,0:T(8,128)(2,1)S(1)}, u32[]{:S(2)}, u32[]{:S(2)}) collective-permute-start(bf16[256,128]{1,0:T(8,128)(2,1)} %anch_ref.1), channel_id=1, source_target_pairs={{0,3},{1,2},{2,1},{3,0},{4,7},{5,6},{6,5},{7,4},{8,11},{9,10},{10,... | collective-permute-start | bytes 196616 | tf_op jit(solution)/shard_map/ppermute | solution.py:35
  3.8 10.5 %collective-permute-start.5 = (bf16[256,128]{1,0:T(8,128)(2,1)}, bf16[256,128]{1,0:T(8,128)(2,1)S(1)}, u32[]{:S(2)}, u32[]{:S(2)}) collective-permute-start(bf16[256,128]{1,0:T(8,128)(2,1)} %anch_ref.1), channel_id=1, source_target_pairs={{0,2},{1,3},{2,0},{3,1},{4,6},{5,7},{6,4},{7,5},{8,10},{9,11},{10,... | collective-permute-start | bytes 196616 | tf_op jit(solution)/shard_map/ppermute | solution.py:35
  5.9 3.7 %collective-permute-start = (bf16[32,128]{1,0:T(8,128)(2,1)S(1)}, bf16[32,128]{1,0:T(8,128)(2,1)S(1)}, u32[]{:S(2)}, u32[]{:S(2)}) collective-permute-start(bf16[32,128]{1,0:T(8,128)(2,1)S(1)} %get-tuple-element.35), channel_id=1, source_target_pairs={{0,4},{1,5},{2,6},{3,7},{4,0},{5,1},{6,2},{7,3},{8,12},{9,13},{10,... | collective-permute-start | bytes 24584 | tf_op jit(solution)/shard_map/ppermute | solution.py:35
  9.6 7.6 %collective-permute-start.3 = (bf16[64,128]{1,0:T(8,128)(2,1)S(1)}, bf16[64,128]{1,0:T(8,128)(2,1)S(1)}, u32[]{:S(2)}, u32[]{:S(2)}) collective-permute-start(bf16[64,128]{1,0:T(8,128)(2,1)S(1)} %constant_dynamic-update-slice_fusion.refs_0_), channel_id=1, source_target_pairs={{0,24},{1,25},{2,26},{3,27},{4,28},{5,29},{6,30},{7,31},{8,16},{9,... | collective-permute-start | bytes 49160 | tf_op jit(solution)/shard_map/ppermute | solution.py:35
  13.7 4.6 %collective-permute-start.2 = (bf16[64,128]{1,0:T(8,128)(2,1)S(1)}, bf16[64,128]{1,0:T(8,128)(2,1)S(1)}, u32[]{:S(2)}, u32[]{:S(2)}) collective-permute-start(bf16[64,128]{1,0:T(8,128)(2,1)S(1)} %constant_dynamic-update-slice_fusion.refs_0_), channel_id=1, source_target_pairs={{0,16},{1,17},{2,18},{3,19},{4,20},{5,21},{6,22},{7,23},{8,24},{9,... | collective-permute-start | bytes 49160 | tf_op jit(solution)/shard_map/ppermute | solution.py:35
  13.7 4.6 %collective-permute-start.1 = (bf16[64,128]{1,0:T(8,128)(2,1)S(1)}, bf16[64,128]{1,0:T(8,128)(2,1)S(1)}, u32[]{:S(2)}, u32[]{:S(2)}) collective-permute-start(bf16[64,128]{1,0:T(8,128)(2,1)S(1)} %constant_dynamic-update-slice_fusion.refs_0_), channel_id=1, source_target_pairs={{0,8},{1,9},{2,10},{3,11},{4,12},{5,13},{6,14},{7,15},{8,0},{9,1},... | collective-permute-start | bytes 49160 | tf_op jit(solution)/shard_map/ppermute | solution.py:35
  22.1 1.4 %collective-permute-start.7 = (f32[16,640]{1,0:T(8,128)S(1)}, f32[16,640]{1,0:T(8,128)S(1)}, u32[]{:S(2)}, u32[]{:S(2)}) collective-permute-start(f32[16,640]{1,0:T(8,128)S(1)} %get-tuple-element.42), channel_id=1, source_target_pairs={{0,1},{1,0},{2,3},{3,2},{4,5},{5,4},{6,7},{7,6},{8,9},{9,8},{10,11... | collective-permute-start | bytes 122888 | tf_op jit(solution)/shard_map/ppermute | solution.py:35
  23.5 5.0 %collective-permute-start.10 = (f32[16,640]{1,0:T(8,128)S(1)}, f32[16,640]{1,0:T(8,128)S(1)}, u32[]{:S(2)}, u32[]{:S(2)}) collective-permute-start(f32[16,640]{1,0:T(8,128)S(1)} %add.67), channel_id=1, source_target_pairs={{0,6},{1,7},{2,4},{3,5},{4,2},{5,3},{6,0},{7,1},{8,14},{9,15},{10,... | collective-permute-start | bytes 122888 | tf_op jit(solution)/shard_map/ppermute | solution.py:35
  26.1 4.0 %collective-permute-start.9 = (f32[16,640]{1,0:T(8,128)S(1)}, f32[16,640]{1,0:T(8,128)S(1)}, u32[]{:S(2)}, u32[]{:S(2)}) collective-permute-start(f32[16,640]{1,0:T(8,128)S(1)} %add.67), channel_id=1, source_target_pairs={{0,4},{1,5},{2,6},{3,7},{4,0},{5,1},{6,2},{7,3},{8,12},{9,13},{10,... | collective-permute-start | bytes 122888 | tf_op jit(solution)/shard_map/ppermute | solution.py:35
  26.6 4.0 %collective-permute-start.8 = (f32[16,640]{1,0:T(8,128)S(1)}, f32[16,640]{1,0:T(8,128)S(1)}, u32[]{:S(2)}, u32[]{:S(2)}) collective-permute-start(f32[16,640]{1,0:T(8,128)S(1)} %add.67), channel_id=1, source_target_pairs={{0,2},{1,3},{2,0},{3,1},{4,6},{5,7},{6,4},{7,5},{8,10},{9,11},{10,... | collective-permute-start | bytes 122888 | tf_op jit(solution)/shard_map/ppermute | solution.py:35
  30.6 6.9 %collective-permute-start.13 = (f32[16,640]{1,0:T(8,128)S(1)}, f32[16,640]{1,0:T(8,128)S(1)}, u32[]{:S(2)}, u32[]{:S(2)}) collective-permute-start(f32[16,640]{1,0:T(8,128)S(1)} %add_add_fusion.1), channel_id=1, source_target_pairs={{0,24},{1,25},{2,26},{3,27},{4,28},{5,29},{6,30},{7,31},{8,16},{9,... | collective-permute-start | bytes 122888 | tf_op jit(solution)/shard_map/ppermute | solution.py:35
  33.3 4.9 %collective-permute-start.12 = (f32[16,640]{1,0:T(8,128)S(1)}, f32[16,640]{1,0:T(8,128)S(1)}, u32[]{:S(2)}, u32[]{:S(2)}) collective-permute-start(f32[16,640]{1,0:T(8,128)S(1)} %add_add_fusion.1), channel_id=1, source_target_pairs={{0,16},{1,17},{2,18},{3,19},{4,20},{5,21},{6,22},{7,23},{8,24},{9,... | collective-permute-start | bytes 122888 | tf_op jit(solution)/shard_map/ppermute | solution.py:35
  33.3 4.9 %collective-permute-start.11 = (f32[16,640]{1,0:T(8,128)S(1)}, f32[16,640]{1,0:T(8,128)S(1)}, u32[]{:S(2)}, u32[]{:S(2)}) collective-permute-start(f32[16,640]{1,0:T(8,128)S(1)} %add_add_fusion.1), channel_id=1, source_target_pairs={{0,8},{1,9},{2,10},{3,11},{4,12},{5,13},{6,14},{7,15},{8,0},{9,1},... | collective-permute-start | bytes 122888 | tf_op jit(solution)/shard_map/ppermute | solution.py:35
  38.2 1.3 %collective-permute-start.14 = (f32[16,640]{1,0:T(8,128)S(1)}, f32[16,640]{1,0:T(8,128)S(1)}, u32[]{:S(2)}, u32[]{:S(2)}) collective-permute-start(f32[16,640]{1,0:T(8,128)S(1)} %add_add_fusion.held_ref), channel_id=1, source_target_pairs={{0,1},{1,0},{2,3},{3,2},{4,5},{5,4},{6,7},{7,6},{8,9},{9,8},{10,11... | collective-permute-start | bytes 122888 | tf_op jit(solution)/shard_map/ppermute | solution.py:35
  41.0 1.2 %collective-permute-start.15 = (f32[16,512]{1,0:T(8,128)S(1)}, f32[16,512]{1,0:T(8,128)S(1)}, u32[]{:S(2)}, u32[]{:S(2)}) collective-permute-start(f32[16,512]{1,0:T(8,128)S(1)} %get-tuple-element.48), channel_id=1, source_target_pairs={{0,1},{1,0},{2,3},{3,2},{4,5},{5,4},{6,7},{7,6},{8,9},{9,8},{10,11... | collective-permute-start | bytes 98312 | tf_op jit(solution)/shard_map/ppermute | solution.py:35
  42.2 4.8 %collective-permute-start.18 = (f32[16,512]{1,0:T(8,128)S(1)}, f32[16,512]{1,0:T(8,128)S(1)}, u32[]{:S(2)}, u32[]{:S(2)}) collective-permute-start(f32[16,512]{1,0:T(8,128)S(1)} %add.74), channel_id=1, source_target_pairs={{0,6},{1,7},{2,4},{3,5},{4,2},{5,3},{6,0},{7,1},{8,14},{9,15},{10,... | collective-permute-start | bytes 98312 | tf_op jit(solution)/shard_map/ppermute | solution.py:35
  43.7 3.9 %collective-permute-start.17 = (f32[16,512]{1,0:T(8,128)S(1)}, f32[16,512]{1,0:T(8,128)S(1)}, u32[]{:S(2)}, u32[]{:S(2)}) collective-permute-start(f32[16,512]{1,0:T(8,128)S(1)} %add.74), channel_id=1, source_target_pairs={{0,4},{1,5},{2,6},{3,7},{4,0},{5,1},{6,2},{7,3},{8,12},{9,13},{10,... | collective-permute-start | bytes 98312 | tf_op jit(solution)/shard_map/ppermute | solution.py:35
  44.2 3.9 %collective-permute-start.16 = (f32[16,512]{1,0:T(8,128)S(1)}, f32[16,512]{1,0:T(8,128)S(1)}, u32[]{:S(2)}, u32[]{:S(2)}) collective-permute-start(f32[16,512]{1,0:T(8,128)S(1)} %add.74), channel_id=1, source_target_pairs={{0,2},{1,3},{2,0},{3,1},{4,6},{5,7},{6,4},{7,5},{8,10},{9,11},{10,... | collective-permute-start | bytes 98312 | tf_op jit(solution)/shard_map/ppermute | solution.py:35
  48.2 6.0 %collective-permute-start.21 = (f32[16,512]{1,0:T(8,128)S(1)}, f32[16,512]{1,0:T(8,128)S(1)}, u32[]{:S(2)}, u32[]{:S(2)}) collective-permute-start(f32[16,512]{1,0:T(8,128)S(1)} %add_add_fusion.5), channel_id=1, source_target_pairs={{0,24},{1,25},{2,26},{3,27},{4,28},{5,29},{6,30},{7,31},{8,16},{9,... | collective-permute-start | bytes 98312 | tf_op jit(solution)/shard_map/ppermute | solution.py:35
  50.2 5.2 %collective-permute-start.20 = (f32[16,512]{1,0:T(8,128)S(1)}, f32[16,512]{1,0:T(8,128)S(1)}, u32[]{:S(2)}, u32[]{:S(2)}) collective-permute-start(f32[16,512]{1,0:T(8,128)S(1)} %add_add_fusion.5), channel_id=1, source_target_pairs={{0,16},{1,17},{2,18},{3,19},{4,20},{5,21},{6,22},{7,23},{8,24},{9,... | collective-permute-start | bytes 98312 | tf_op jit(solution)/shard_map/ppermute | solution.py:35
  50.5 4.9 %collective-permute-start.19 = (f32[16,512]{1,0:T(8,128)S(1)}, f32[16,512]{1,0:T(8,128)S(1)}, u32[]{:S(2)}, u32[]{:S(2)}) collective-permute-start(f32[16,512]{1,0:T(8,128)S(1)} %add_add_fusion.5), channel_id=1, source_target_pairs={{0,8},{1,9},{2,10},{3,11},{4,12},{5,13},{6,14},{7,15},{8,0},{9,1},... | collective-permute-start | bytes 98312 | tf_op jit(solution)/shard_map/ppermute | solution.py:35
  55.4 1.3 %collective-permute-start.22 = (f32[16,512]{1,0:T(8,128)S(1)}, f32[16,512]{1,0:T(8,128)S(1)}, u32[]{:S(2)}, u32[]{:S(2)}) collective-permute-start(f32[16,512]{1,0:T(8,128)S(1)} %add_add_fusion.4.held_ref), channel_id=1, source_target_pairs={{0,1},{1,0},{2,3},{3,2},{4,5},{5,4},{6,7},{7,6},{8,9},{9,8},{10,11... | collective-permute-start | bytes 98312 | tf_op jit(solution)/shard_map/ppermute | solution.py:35
  58.2 1.2 %collective-permute-start.23 = (f32[16,512]{1,0:T(8,128)S(1)}, f32[16,512]{1,0:T(8,128)S(1)}, u32[]{:S(2)}, u32[]{:S(2)}) collective-permute-start(f32[16,512]{1,0:T(8,128)S(1)} %get-tuple-element.54), channel_id=1, source_target_pairs={{0,1},{1,0},{2,3},{3,2},{4,5},{5,4},{6,7},{7,6},{8,9},{9,8},{10,11... | collective-permute-start | bytes 98312 | tf_op jit(solution)/shard_map/ppermute | solution.py:35
  59.4 4.8 %collective-permute-start.26 = (f32[16,512]{1,0:T(8,128)S(1)}, f32[16,512]{1,0:T(8,128)S(1)}, u32[]{:S(2)}, u32[]{:S(2)}) collective-permute-start(f32[16,512]{1,0:T(8,128)S(1)} %add.81), channel_id=1, source_target_pairs={{0,6},{1,7},{2,4},{3,5},{4,2},{5,3},{6,0},{7,1},{8,14},{9,15},{10,... | collective-permute-start | bytes 98312 | tf_op jit(solution)/shard_map/ppermute | solution.py:35
  61.9 3.9 %collective-permute-start.25 = (f32[16,512]{1,0:T(8,128)S(1)}, f32[16,512]{1,0:T(8,128)S(1)}, u32[]{:S(2)}, u32[]{:S(2)}) collective-permute-start(f32[16,512]{1,0:T(8,128)S(1)} %add.81), channel_id=1, source_target_pairs={{0,4},{1,5},{2,6},{3,7},{4,0},{5,1},{6,2},{7,3},{8,12},{9,13},{10,... | collective-permute-start | bytes 98312 | tf_op jit(solution)/shard_map/ppermute | solution.py:35
  62.4 3.9 %collective-permute-start.24 = (f32[16,512]{1,0:T(8,128)S(1)}, f32[16,512]{1,0:T(8,128)S(1)}, u32[]{:S(2)}, u32[]{:S(2)}) collective-permute-start(f32[16,512]{1,0:T(8,128)S(1)} %add.81), channel_id=1, source_target_pairs={{0,2},{1,3},{2,0},{3,1},{4,6},{5,7},{6,4},{7,5},{8,10},{9,11},{10,... | collective-permute-start | bytes 98312 | tf_op jit(solution)/shard_map/ppermute | solution.py:35
  66.3 5.8 %collective-permute-start.29 = (f32[16,512]{1,0:T(8,128)S(1)}, f32[16,512]{1,0:T(8,128)S(1)}, u32[]{:S(2)}, u32[]{:S(2)}) collective-permute-start(f32[16,512]{1,0:T(8,128)S(1)} %add_add_fusion.3), channel_id=1, source_target_pairs={{0,24},{1,25},{2,26},{3,27},{4,28},{5,29},{6,30},{7,31},{8,16},{9,... | collective-permute-start | bytes 98312 | tf_op jit(solution)/shard_map/ppermute | solution.py:35
  68.2 5.0 %collective-permute-start.28 = (f32[16,512]{1,0:T(8,128)S(1)}, f32[16,512]{1,0:T(8,128)S(1)}, u32[]{:S(2)}, u32[]{:S(2)}) collective-permute-start(f32[16,512]{1,0:T(8,128)S(1)} %add_add_fusion.3), channel_id=1, source_target_pairs={{0,16},{1,17},{2,18},{3,19},{4,20},{5,21},{6,22},{7,23},{8,24},{9,... | collective-permute-start | bytes 98312 | tf_op jit(solution)/shard_map/ppermute | solution.py:35
  69.0 4.3 %collective-permute-start.27 = (f32[16,512]{1,0:T(8,128)S(1)}, f32[16,512]{1,0:T(8,128)S(1)}, u32[]{:S(2)}, u32[]{:S(2)}) collective-permute-start(f32[16,512]{1,0:T(8,128)S(1)} %add_add_fusion.3), channel_id=1, source_target_pairs={{0,8},{1,9},{2,10},{3,11},{4,12},{5,13},{6,14},{7,15},{8,0},{9,1},... | collective-permute-start | bytes 98312 | tf_op jit(solution)/shard_map/ppermute | solution.py:35
  71.1 2.4 %collective-permute-start.31 = (f32[8,2048]{1,0:T(8,128)S(1)}, f32[8,2048]{1,0:T(8,128)S(1)}, u32[]{:S(2)}, u32[]{:S(2)}) collective-permute-start(f32[8,2048]{1,0:T(8,128)S(1)} %get-tuple-element.63), channel_id=1, source_target_pairs={{0,1},{1,0},{2,3},{3,2},{4,5},{5,4},{6,7},{7,6},{8,9},{9,8},{10,11... | collective-permute-start | bytes 196616 | tf_op jit(solution)/shard_map/ppermute | solution.py:35
  71.2 5.0 %collective-permute-start.32 = (f32[8,2048]{1,0:T(8,128)S(1)}, f32[8,2048]{1,0:T(8,128)S(1)}, u32[]{:S(2)}, u32[]{:S(2)}) collective-permute-start(f32[8,2048]{1,0:T(8,128)S(1)} %get-tuple-element.64), channel_id=1, source_target_pairs={{0,2},{1,3},{2,0},{3,1},{4,6},{5,7},{6,4},{7,5},{8,10},{9,11},{10,... | collective-permute-start | bytes 196616 | tf_op jit(solution)/shard_map/ppermute | solution.py:35
  72.1 4.4 %collective-permute-start.33 = (f32[8,2048]{1,0:T(8,128)S(1)}, f32[8,2048]{1,0:T(8,128)S(1)}, u32[]{:S(2)}, u32[]{:S(2)}) collective-permute-start(f32[8,2048]{1,0:T(8,128)S(1)} %get-tuple-element.65), channel_id=1, source_target_pairs={{0,3},{1,2},{2,1},{3,0},{4,7},{5,6},{6,5},{7,4},{8,11},{9,10},{10,... | collective-permute-start | bytes 196616 | tf_op jit(solution)/shard_map/ppermute | solution.py:35
  73.3 3.3 %collective-permute-start.30 = (f32[16,512]{1,0:T(8,128)S(1)}, f32[16,512]{1,0:T(8,128)S(1)}, u32[]{:S(2)}, u32[]{:S(2)}) collective-permute-start(f32[16,512]{1,0:T(8,128)S(1)} %add_add_fusion.2.held_ref), channel_id=1, source_target_pairs={{0,1},{1,0},{2,3},{3,2},{4,5},{5,4},{6,7},{7,6},{8,9},{9,8},{10,11... | collective-permute-start | bytes 98312 | tf_op jit(solution)/shard_map/ppermute | solution.py:35

commit v9 on v8

--- a/solution.py
+++ b/solution.py
@@ -70,23 +70,14 @@
     return swap(value, 1)
 
 
-def aug_columns(first, second, rows):
-    lane = lax.broadcasted_iota(jnp.int32, (rows, LANES), 1)
-    out = jnp.zeros((rows, LANES), f32)
-    for base, column in ((0, first), (3, second)):
-        if column is None:
-            out = jnp.where((lane >= base) & (lane < base + 3), 1.0, out)
-        else:
-            rest = column
-            for piece in range(3):
-                part = rest.astype(bf16).astype(f32)
-                out = jnp.where(lane == base + piece, part, out)
-                rest = rest - part
-    return out.astype(bf16)
-
-
-def row_sizes(value):
-    return jnp.sum(value * value, axis=1, keepdims=True)
+def side_rows(turned, scale, shift, first, size):
+    wide = turned.astype(f32)
+    norms = jnp.sum(wide * wide, axis=0, keepdims=True) * scale + shift
+    row = lax.broadcasted_iota(jnp.int32, (16, turned.shape[1]), 0)
+    out = jnp.where(row < 6, 1.0, 0.0)
+    for k, part in enumerate(split3(norms)):
+        out = jnp.where(row == first + k, part.astype(f32), out)
+    return jnp.concatenate([out.astype(bf16), jnp.zeros((size - 16, turned.shape[1]), bf16)], axis=0)
 
 
 def eighth(value):
@@ -115,8 +106,9 @@
     lane = lax.broadcasted_iota(jnp.int32, (1, LANES), 1)
     for k in range(count):
         picked[count + k : count + k + 1, :] = jnp.where(lane == cls_ref[k], 1.0, 0.0)
+    for copy in copies:
+        copy.wait()
     for k in range(count):
-        copies[k].wait()
         chosen = jnp.where(sub == ((idx_ref[k] - base) & 15), rows[k].astype(f32), 0.0)
         picked[k : k + 1, :] = jnp.sum(chosen, axis=0, keepdims=True)
     out_ref[...] = picked[...].astype(bf16)
@@ -131,20 +123,12 @@
     me = me_ref[0] % na
     for mask, piece in enumerate((a0, a1, a2, a3)):
         at = pl.ds(pl.multiple_of((me ^ mask) * quarter, quarter), quarter)
-        value = piece[...].astype(f32)
-        aug_ref[at, 0:feat] = (value * (-2.0 * scale)).astype(bf16)
-        aug_ref[at, feat:] = aug_columns(row_sizes(value) * scale + 1.0, None, quarter)
+        aug_ref[at, 0:feat] = (piece[...].astype(f32) * (-2.0 * scale)).astype(bf16)
+        aug_ref[at, feat:] = side_rows(piece[...].T, scale, 1.0, 0, LANES).T
     tile = min(256, docs)
-    row = lax.broadcasted_iota(jnp.int32, (16, tile), 0)
-    rest = jnp.zeros((aug_ref.shape[1] - feat - 16, tile), bf16)
     for col in range(0, docs, tile):
         turned = x_ref[col : col + tile, :].T
-        wide = turned.astype(f32)
-        size = jnp.sum(wide * wide, axis=0, keepdims=True) * scale
-        extra = jnp.where(row < 3, 1.0, 0.0)
-        for k, part in enumerate(split3(size)):
-            extra = jnp.where(row == 3 + k, part.astype(f32), extra)
-        right = jnp.concatenate([turned, extra.astype(bf16), rest], axis=0)
+        right = jnp.concatenate([turned, side_rows(turned, scale, 0.0, 3, LANES)], axis=0)
         for at in range(0, aug_ref.shape[0], 256):
             kern = eighth(mm(aug_ref[at : at + 256, :], right))
             high, low = split2(kern)
@@ -218,16 +202,16 @@
     lab_refs = refs[: len(slots)]
     (aug_ref, khi_ref, klo_ref, send_ref, w_ref, rhs_ref, mid_ref, zhi_ref, zlo_ref, spread_ref, tinv_ref,
      laug, hot) = refs[len(slots) :]
-    feat = laug.shape[1] - LANES
+    feat = laug.shape[1]
     docs = me_ref[0] // na
     for masks, ref in zip(slots, lab_refs):
         for k, mask in enumerate(masks):
             at = pl.ds(pl.multiple_of((docs ^ mask) * labs, labs), labs)
-            laug[at, 0:feat] = ref[2 * labs * k : 2 * labs * k + labs, :]
+            laug[at, :] = ref[2 * labs * k : 2 * labs * k + labs, :]
             hot[at, :] = ref[2 * labs * k + labs : 2 * labs * (k + 1), :].astype(f32)
-    size = row_sizes(laug[:, 0:feat].astype(f32)) * (1.0 / (feat * width_h))
-    laug[:, feat:] = aug_columns(None, size, laug.shape[0])
-    kern = eighth(mm(aug_ref[...], laug[...], NT))
+    turned = laug[...].T
+    right = jnp.concatenate([turned, side_rows(turned, 1.0 / (feat * width_h), 0.0, 3, LANES)], axis=0)
+    kern = eighth(mm(aug_ref[...], right))
     zhi, zlo = split2(kern / jnp.sum(kern, axis=0, keepdims=True))
     zhi_ref[...], zlo_ref[...] = zhi, zlo
     onehot = hot[...].T[0:CLASSES, :].astype(bf16)
@@ -467,7 +451,7 @@
         functools.partial(first_send, na, labs, slots, CLASSES * lab_scale),
         [SMEM] + [VMEM] * (len(lab_arrays) + 3),
         [long_sds, sds((4 * CLASSES, docs), bf16), flat_sds, flat_sds, z_sds, z_sds, docs_sds, sds((1, docs), f32)],
-        [pltpu.VMEM((labeled, feat + LANES), bf16), pltpu.VMEM((labeled, LANES), f32)],
+        [pltpu.VMEM((labeled, feat), bf16), pltpu.VMEM((labeled, LANES), f32)],
         **work,
     )(me, *lab_arrays, aug, khi, klo)
     got = swap_core(send)

time: 77.6 us -> 77.7 us (level)
  transfers between devices with their start and end apart: 34 -> 34, of which waited for: 22 -> 22; matrix products, arithmetic and copies ran while one was open for 0% -> 0% of each run, Pallas kernels for 17% -> 16%
where the time goes in v9:
time: 77.7 us; the launch traced here: 77.5 us
  starting transfers between devices  36.4 us (47%)
  Pallas kernels  20.1 us (26%)
  waiting for transfers between devices  20.1 us (26%)
  between operations  0.8 us (1%)
    ppermute x34, starting transfers between devices, swap(): return lax.ppermute(value, EVERY, [(i, i ^ mask) for i in range(count)])  36.4 us
    ppermute x34, waiting for transfers between devices, swap(): return lax.ppermute(value, EVERY, [(i, i ^ mask) for i in range(count)])  20.1 us
    pallas_call x1, Pallas kernels, run(): call(functools.partial(first_send, na, labs, slots, CLASSES * lab_scale),...  3.68 us
    pallas_call x1, Pallas kernels, run(): call(functools.partial(build_kernel, na), [SMEM] + [VMEM] * 5, [k_sds, k_...  2.8 us
    pallas_call x1, Pallas kernels, run(): pl.pallas_call(functools.partial(label_kernel, na), grid_spec=pltpu.Prefe...  2.06 us
  transfers between devices with their start and end apart: 34, of which 22 were waited for; matrix products, arithmetic and copies ran while one was open for 0% of the time, Pallas kernels for 16%

profile of v9, /device:TPU:0, one launch (start us, length us, event | category | flops | bytes accessed | tf_op | source)
XLA Modules:
  0.0 77.5 jit_solution(17504538225073488489)
XLA Ops:
  0.6 0.6 collective-permute-start.4
  1.2 2.6 %collective-permute-start.6 = (bf16[256,128]{1,0:T(8,128)(2,1)}, bf16[256,128]{1,0:T(8,128)(2,1)S(1)}, u32[]{:S(2)}, u32[]{:S(2)}) collective-permute-start(bf16[256,128]{1,0:T(8,128)(2,1)} %anch_ref.1), channel_id=1, source_target_pairs={{0,3},{1,2},{2,1},{3,0},{4,7},{5,6},{6,5},{7,4},{8,11},{9,10},{10,... | collective-permute-start | bytes 196616 | tf_op jit(solution)/shard_map/ppermute | solution.py:35
  3.8 2.1 %label_rows.1 = (bf16[32,128]{1,0:T(8,128)(2,1)S(1)}, bf16[2048,128]{1,0:T(8,128)(2,1)S(1)}, bf16[256,128]{1,0:T(8,128)(2,1)S(1)}) custom-call(s32[1]{0:T(128)} %bitcast.me_ref, s32[16]{0:T(128)} %idx_ref.1, s32[16]{0:T(128)} %cls_ref.1, bf16[8192,128]{1,0:T(8,128)(2,1)} %feat_ref.1, bf16[256,128]{1,0:T(8,128)(2,1)} %anch_ref.1), custom_call_target="tpu_custom_call" | custom-call | tf_op jit(solution)/shard_map/label_rows/pallas_call | solution.py:396
  5.9 2.1 %collective-permute-start = (bf16[32,128]{1,0:T(8,128)(2,1)S(1)}, bf16[32,128]{1,0:T(8,128)(2,1)S(1)}, u32[]{:S(2)}, u32[]{:S(2)}) collective-permute-start(bf16[32,128]{1,0:T(8,128)(2,1)S(1)} %get-tuple-element.35), channel_id=1, source_target_pairs={{0,4},{1,5},{2,6},{3,7},{4,0},{5,1},{6,2},{7,3},{8,12},{9,13},{10,... | collective-permute-start | bytes 24584 | tf_op jit(solution)/shard_map/ppermute | solution.py:35
  8.0 1.6 %collective-permute-done = bf16[32,128]{1,0:T(8,128)(2,1)S(1)} collective-permute-done((bf16[32,128]{1,0:T(8,128)(2,1)S(1)}, bf16[32,128]{1,0:T(8,128)(2,1)S(1)}, u32[]{:S(2)}, u32[]{:S(2)}) %collective-permute-start) | collective-permute-done | bytes 8224 | tf_op jit(solution)/shard_map/ppermute | solution.py:35
  9.6 4.1 %collective-permute-start.3 = (bf16[64,128]{1,0:T(8,128)(2,1)S(1)}, bf16[64,128]{1,0:T(8,128)(2,1)S(1)}, u32[]{:S(2)}, u32[]{:S(2)}) collective-permute-start(bf16[64,128]{1,0:T(8,128)(2,1)S(1)} %constant_dynamic-update-slice_fusion.refs_0_), channel_id=1, source_target_pairs={{0,24},{1,25},{2,26},{3,27},{4,28},{5,29},{6,30},{7,31},{8,16},{9,... | collective-permute-start | bytes 49160 | tf_op jit(solution)/shard_map/ppermute | solution.py:35
  13.7 0.6 collective-permute-start.1
  14.3 2.8 %shard_map.59 = (bf16[1024,2048]{1,0:T(8,128)(2,1)S(1)}, bf16[1024,2048]{1,0:T(8,128)(2,1)S(1)}, bf16[1024,256]{1,0:T(8,128)(2,1)S(1)}) custom-call(s32[1]{0:T(128)} %bitcast.me_ref, bf16[256,128]{1,0:T(8,128)(2,1)S(1)} %get-tuple-element.36.a0, bf16[256,128]{1,0:T(8,128)(2,1)S(1)} %collective-permute-done.4.a1, ...), custom_call_target="tpu_custom_call" | custom-call | flops 1073741824 | bytes 8388608 | tf_op jit(solution)/shard_map/pallas_call | solution.py:432
  17.1 1.2 %collective-permute-done.2.refs_2_ = bf16[64,128]{1,0:T(8,128)(2,1)S(1)} collective-permute-done((bf16[64,128]{1,0:T(8,128)(2,1)S(1)}, bf16[64,128]{1,0:T(8,128)(2,1)S(1)}, u32[]{:S(2)}, u32[]{:S(2)}) %collective-permute-start.2) | collective-permute-done | bytes 16416 | tf_op jit(solution)/shard_map/ppermute | solution.py:35
  18.3 3.7 %shard_map.60 = (f32[16,640]{1,0:T(8,128)S(1)}, bf16[64,2048]{1,0:T(8,128)(2,1)S(1)}, f32[16,1024]{1,0:T(8,128)S(1)}, f32[16,1024]{1,0:T(8,128)S(1)}, bf16[1024,...) custom-call(s32[1]{0:T(128)} %bitcast.me_ref, ...), custom_call_target="tpu_custom_call" | custom-call | flops 536870912 | bytes 4194304 | tf_op jit(solution)/shard_map/pallas_call | solution.py:450
  22.1 1.3 %shard_map.61 = f32[16,640]{1,0:T(8,128)S(1)} custom-call(s32[1]{0:T(128)} %bitcast.me_ref, bf16[64,2048]{1,0:T(8,128)(2,1)S(1)} %get-tuple-element.41.w_ref, bf16[1024,2048]{1,0:T(8,128)(2,1)S(1)} %get-tuple-element.39.refs_5_.khi_ref.in_ref, bf16[1024,2048]{1,0:T(8,128)(2,1)S(1)} %get-tuple-element.40.refs_6_.klo_ref.in_ref), custom_call_target="tpu_custom_call" | custom-call | flops 536870912 | bytes 4194304 | tf_op jit(solution)/shard_map/pallas_call | solution.py:458
  23.5 2.5 %collective-permute-start.10 = (f32[16,640]{1,0:T(8,128)S(1)}, f32[16,640]{1,0:T(8,128)S(1)}, u32[]{:S(2)}, u32[]{:S(2)}) collective-permute-start(f32[16,640]{1,0:T(8,128)S(1)} %add.67), channel_id=1, source_target_pairs={{0,6},{1,7},{2,4},{3,5},{4,2},{5,3},{6,0},{7,1},{8,14},{9,15},{10,... | collective-permute-start | bytes 122888 | tf_op jit(solution)/shard_map/ppermute | solution.py:35
  26.0 0.5 collective-permute-start.9
  26.5 0.5 collective-permute-start.8
  27.0 1.4 %collective-permute-done.10 = f32[16,640]{1,0:T(8,128)S(1)} collective-permute-done((f32[16,640]{1,0:T(8,128)S(1)}, f32[16,640]{1,0:T(8,128)S(1)}, u32[]{:S(2)}, u32[]{:S(2)}) %collective-permute-start.10) | collective-permute-done | bytes 40992 | tf_op jit(solution)/shard_map/ppermute | solution.py:35
  28.5 1.5 %collective-permute-done.9 = f32[16,640]{1,0:T(8,128)S(1)} collective-permute-done((f32[16,640]{1,0:T(8,128)S(1)}, f32[16,640]{1,0:T(8,128)S(1)}, u32[]{:S(2)}, u32[]{:S(2)}) %collective-permute-start.9) | collective-permute-done | bytes 40992 | tf_op jit(solution)/shard_map/ppermute | solution.py:35
  30.0 0.5 collective-permute-done.8
  30.5 2.7 %collective-permute-start.13 = (f32[16,640]{1,0:T(8,128)S(1)}, f32[16,640]{1,0:T(8,128)S(1)}, u32[]{:S(2)}, u32[]{:S(2)}) collective-permute-start(f32[16,640]{1,0:T(8,128)S(1)} %add_add_fusion.1), channel_id=1, source_target_pairs={{0,24},{1,25},{2,26},{3,27},{4,28},{5,29},{6,30},{7,31},{8,16},{9,... | collective-permute-start | bytes 122888 | tf_op jit(solution)/shard_map/ppermute | solution.py:35
  33.2 1.8 %collective-permute-start.11 = (f32[16,640]{1,0:T(8,128)S(1)}, f32[16,640]{1,0:T(8,128)S(1)}, u32[]{:S(2)}, u32[]{:S(2)}) collective-permute-start(f32[16,640]{1,0:T(8,128)S(1)} %add_add_fusion.1), channel_id=1, source_target_pairs={{0,8},{1,9},{2,10},{3,11},{4,12},{5,13},{6,14},{7,15},{8,0},{9,1},... | collective-permute-start | bytes 122888 | tf_op jit(solution)/shard_map/ppermute | solution.py:35
  35.0 1.2 %shard_map.62.thi_ref = bf16[2048,1024]{1,0:T(8,128)(2,1)S(1)} custom-call(bf16[1024,2048]{1,0:T(8,128)(2,1)S(1)} %get-tuple-element.39.refs_5_.khi_ref.in_ref), custom_call_target="tpu_custom_call" | custom-call | flops 1048576 | bytes 262144 | tf_op jit(solution)/shard_map/pallas_call | solution.py:460
  36.2 1.2 %shard_map.63.tlo_ref = bf16[2048,1024]{1,0:T(8,128)(2,1)S(1)} custom-call(bf16[1024,2048]{1,0:T(8,128)(2,1)S(1)} %get-tuple-element.40.refs_6_.klo_ref.in_ref), custom_call_target="tpu_custom_call" | custom-call | flops 1048576 | bytes 262144 | tf_op jit(solution)/shard_map/pallas_call | solution.py:461
  37.5 0.6 collective-permute-done.12
  38.2 0.8 %shard_map.64 = (f32[16,2048]{1,0:T(8,128)S(1)}, f32[1,512]{1,0:T(1,128)S(1)}) custom-call(s32[1]{0:T(128)} %bitcast.me_ref, f32[16,640]{1,0:T(8,128)S(1)} %add_add_fusion.held_ref, f32[16,1024]{1,0:T(8,128)S(1)} %get-tuple-element.43.mid_ref, bf16[1024,2048]{1,0:T(8,128)(2,1)S(1)} %get-tuple-element.39.refs_5_.khi_ref.in_ref, ...), custom_call_target="tpu_custom_call" | custom-call | flops 536870912 | bytes 4194304 | tf_op jit(solution)/shard_map/pallas_call | solution.py:465
  39.0 0.4 collective-permute-done.14.got_ref
  39.4 1.5 %shard_map.65 = (f32[16,512]{1,0:T(8,128)S(1)}, bf16[48,2048]{1,0:T(8,128)(2,1)S(1)}, f32[1,1024]{1,0:T(1,128)S(1)}) custom-call(s32[1]{0:T(128)} %bitcast.me_ref, f32[16,640]{1,0:T(8,128)S(1)} %collective-permute-done.14.got_ref, f32[16,1024]{1,0:T(8,128)S(1)} %get-tuple-element.43.mid_ref, bf16[1024,2048]{1,0:T(8,128)(2,1)S(1)} %get-tuple-element.39.refs_5_.khi_ref.in_ref, ...), custom_call_target="tpu_custom_call" | custom-call | flops 536870912 | bytes 4194304 | tf_op jit(solution)/shard_map/pallas_call | solution.py:468
  41.0 0.8 shard_map.66
  41.8 0.3 collective-permute-done.15
  42.1 1.5 %collective-permute-start.18 = (f32[16,512]{1,0:T(8,128)S(1)}, f32[16,512]{1,0:T(8,128)S(1)}, u32[]{:S(2)}, u32[]{:S(2)}) collective-permute-start(f32[16,512]{1,0:T(8,128)S(1)} %add.74), channel_id=1, source_target_pairs={{0,6},{1,7},{2,4},{3,5},{4,2},{5,3},{6,0},{7,1},{8,14},{9,15},{10,... | collective-permute-start | bytes 98312 | tf_op jit(solution)/shard_map/ppermute | solution.py:35
  43.6 0.5 collective-permute-start.17
  44.1 1.5 %collective-permute-start.16 = (f32[16,512]{1,0:T(8,128)S(1)}, f32[16,512]{1,0:T(8,128)S(1)}, u32[]{:S(2)}, u32[]{:S(2)}) collective-permute-start(f32[16,512]{1,0:T(8,128)S(1)} %add.74), channel_id=1, source_target_pairs={{0,2},{1,3},{2,0},{3,1},{4,6},{5,7},{6,4},{7,5},{8,10},{9,11},{10,... | collective-permute-start | bytes 98312 | tf_op jit(solution)/shard_map/ppermute | solution.py:35
  45.6 1.3 %collective-permute-done.18 = f32[16,512]{1,0:T(8,128)S(1)} collective-permute-done((f32[16,512]{1,0:T(8,128)S(1)}, f32[16,512]{1,0:T(8,128)S(1)}, u32[]{:S(2)}, u32[]{:S(2)}) %collective-permute-start.18) | collective-permute-done | bytes 32800 | tf_op jit(solution)/shard_map/ppermute | solution.py:35
  46.9 0.6 collective-permute-done.17
  47.5 0.5 collective-permute-done.16
  48.1 2.1 %collective-permute-start.21 = (f32[16,512]{1,0:T(8,128)S(1)}, f32[16,512]{1,0:T(8,128)S(1)}, u32[]{:S(2)}, u32[]{:S(2)}) collective-permute-start(f32[16,512]{1,0:T(8,128)S(1)} %add_add_fusion.5), channel_id=1, source_target_pairs={{0,24},{1,25},{2,26},{3,27},{4,28},{5,29},{6,30},{7,31},{8,16},{9,... | collective-permute-start | bytes 98312 | tf_op jit(solution)/shard_map/ppermute | solution.py:35
  50.1 0.3 collective-permute-start.20
  50.4 2.1 %collective-permute-start.19 = (f32[16,512]{1,0:T(8,128)S(1)}, f32[16,512]{1,0:T(8,128)S(1)}, u32[]{:S(2)}, u32[]{:S(2)}) collective-permute-start(f32[16,512]{1,0:T(8,128)S(1)} %add_add_fusion.5), channel_id=1, source_target_pairs={{0,8},{1,9},{2,10},{3,11},{4,12},{5,13},{6,14},{7,15},{8,0},{9,1},... | collective-permute-start | bytes 98312 | tf_op jit(solution)/shard_map/ppermute | solution.py:35
  52.5 0.4 shard_map.67.lab_ref
  52.9 1.1 %collective-permute-done.21 = f32[16,512]{1,0:T(8,128)S(1)} collective-permute-done((f32[16,512]{1,0:T(8,128)S(1)}, f32[16,512]{1,0:T(8,128)S(1)}, u32[]{:S(2)}, u32[]{:S(2)}) %collective-permute-start.21) | collective-permute-done | bytes 32800 | tf_op jit(solution)/shard_map/ppermute | solution.py:35
  54.1 1.2 %collective-permute-done.20 = f32[16,512]{1,0:T(8,128)S(1)} collective-permute-done((f32[16,512]{1,0:T(8,128)S(1)}, f32[16,512]{1,0:T(8,128)S(1)}, u32[]{:S(2)}, u32[]{:S(2)}) %collective-permute-start.20) | collective-permute-done | bytes 32800 | tf_op jit(solution)/shard_map/ppermute | solution.py:35
  55.3 0.3 collective-permute-start.22
  55.6 0.8 %shard_map.68.part_ref = f32[16,2048]{1,0:T(8,128)S(1)} custom-call(s32[1]{0:T(128)} %bitcast.me_ref, f32[16,512]{1,0:T(8,128)S(1)} %add_add_fusion.4.held_ref, f32[16,1024]{1,0:T(8,128)S(1)} %get-tuple-element.49.rhs_ref, f32[16,1024]{1,0:T(8,128)S(1)} %shard_map.67.lab_ref, bf16[1024,2048]{1,0:T(8,128)(2,1)S(1)} %get-tuple-element.39.refs_5_.khi_ref.in_ref, ...), custom_call_target="tpu_custom_call" | custom-call | flops 536870912 | bytes 4194304 | tf_op jit(solution)/shard_map/pallas_call | solution.py:476
  56.4 0.4 collective-permute-done.22.got_ref
  56.8 1.6 %shard_map.69 = (f32[16,512]{1,0:T(8,128)S(1)}, bf16[48,2048]{1,0:T(8,128)(2,1)S(1)}, f32[16,2048]{1,0:T(8,128)S(1)}, f32[16,1024]{1,0:T(8,128)S(1)}, f32[16,102...) custom-call(s32[1]{0:T(128)} %bitcast.me_ref, f32[16,512]{1,0:T(8,128)S(1)} %add_add_fusion.4.held_ref, ...), custom_call_target="tpu_custom_call" | custom-call | flops 536870912 | bytes 4194304 | tf_op jit(solution)/shard_map/pallas_call | solution.py:479
  58.3 0.2 collective-permute-start.23
  58.5 0.8 shard_map.70
  59.2 0.3 collective-permute-done.23
  59.5 2.4 %collective-permute-start.26 = (f32[16,512]{1,0:T(8,128)S(1)}, f32[16,512]{1,0:T(8,128)S(1)}, u32[]{:S(2)}, u32[]{:S(2)}) collective-permute-start(f32[16,512]{1,0:T(8,128)S(1)} %add.81), channel_id=1, source_target_pairs={{0,6},{1,7},{2,4},{3,5},{4,2},{5,3},{6,0},{7,1},{8,14},{9,15},{10,... | collective-permute-start | bytes 98312 | tf_op jit(solution)/shard_map/ppermute | solution.py:35
  62.0 0.5 collective-permute-start.25
  62.5 0.6 collective-permute-start.24
  63.0 1.3 %collective-permute-done.26 = f32[16,512]{1,0:T(8,128)S(1)} collective-permute-done((f32[16,512]{1,0:T(8,128)S(1)}, f32[16,512]{1,0:T(8,128)S(1)}, u32[]{:S(2)}, u32[]{:S(2)}) %collective-permute-start.26) | collective-permute-done | bytes 32800 | tf_op jit(solution)/shard_map/ppermute | solution.py:35
  64.3 1.5 %collective-permute-done.25 = f32[16,512]{1,0:T(8,128)S(1)} collective-permute-done((f32[16,512]{1,0:T(8,128)S(1)}, f32[16,512]{1,0:T(8,128)S(1)}, u32[]{:S(2)}, u32[]{:S(2)}) %collective-permute-start.25) | collective-permute-done | bytes 32800 | tf_op jit(solution)/shard_map/ppermute | solution.py:35
  65.9 0.5 collective-permute-done.24
  66.4 1.9 %collective-permute-start.29 = (f32[16,512]{1,0:T(8,128)S(1)}, f32[16,512]{1,0:T(8,128)S(1)}, u32[]{:S(2)}, u32[]{:S(2)}) collective-permute-start(f32[16,512]{1,0:T(8,128)S(1)} %add_add_fusion.3), channel_id=1, source_target_pairs={{0,24},{1,25},{2,26},{3,27},{4,28},{5,29},{6,30},{7,31},{8,16},{9,... | collective-permute-start | bytes 98312 | tf_op jit(solution)/shard_map/ppermute | solution.py:35
  68.3 0.8 collective-permute-start.28
  69.1 1.8 %collective-permute-start.27 = (f32[16,512]{1,0:T(8,128)S(1)}, f32[16,512]{1,0:T(8,128)S(1)}, u32[]{:S(2)}, u32[]{:S(2)}) collective-permute-start(f32[16,512]{1,0:T(8,128)S(1)} %add_add_fusion.3), channel_id=1, source_target_pairs={{0,8},{1,9},{2,10},{3,11},{4,12},{5,13},{6,14},{7,15},{8,0},{9,1},... | collective-permute-start | bytes 98312 | tf_op jit(solution)/shard_map/ppermute | solution.py:35
  70.8 0.3 shard_map.71
  71.3 0.6 collective-permute-start.32
  71.9 0.3 collective-permute-done.29
  72.2 0.9 %collective-permute-start.33 = (f32[8,2048]{1,0:T(8,128)S(1)}, f32[8,2048]{1,0:T(8,128)S(1)}, u32[]{:S(2)}, u32[]{:S(2)}) collective-permute-start(f32[8,2048]{1,0:T(8,128)S(1)} %get-tuple-element.65), channel_id=1, source_target_pairs={{0,3},{1,2},{2,1},{3,0},{4,7},{5,6},{6,5},{7,4},{8,11},{9,10},{10,... | collective-permute-start | bytes 196616 | tf_op jit(solution)/shard_map/ppermute | solution.py:35
  73.1 0.2 collective-permute-done.28
  73.3 0.2 collective-permute-start.30
  73.6 2.7 %collective-permute-done.32.refs_2_ = f32[8,2048]{1,0:T(8,128)S(1)} collective-permute-done((f32[8,2048]{1,0:T(8,128)S(1)}, f32[8,2048]{1,0:T(8,128)S(1)}, u32[]{:S(2)}, u32[]{:S(2)}) %collective-permute-start.32) | collective-permute-done | bytes 65568 | tf_op jit(solution)/shard_map/ppermute | solution.py:35
  76.3 0.3 collective-permute-done.33.refs_3_
  76.6 0.8 %shard_map.72 = (f32[16,256]{1,0:T(8,128)}, f32[4,8192]{1,0:T(4,128)}) custom-call(s32[1]{0:T(128)} %bitcast.me_ref, f32[16,512]{1,0:T(8,128)S(1)} %add_add_fusion.2.held_ref, f32[16,512]{1,0:T(8,128)S(1)} %collective-permute-done.30.got_ref, f32[16,1024]{1,0:T(8,128)S(1)} %get-tuple-element.55.direc_ref, f32[16,1024]{1,0:T(8,128)S(1)} %get-tuple-element.56.mid_ref, ...), custom_call_target="tpu_custom_call" | custom-call | flops 1048576 | bytes 262144 | tf_op jit(solution)/shard_map/pallas_call | solution.py:501
  (30 shorter events, 0.6 us)
Async XLA Ops:
  0.6 13.1 %collective-permute-start.4 = (bf16[256,128]{1,0:T(8,128)(2,1)}, bf16[256,128]{1,0:T(8,128)(2,1)S(1)}, u32[]{:S(2)}, u32[]{:S(2)}) collective-permute-start(bf16[256,128]{1,0:T(8,128)(2,1)} %anch_ref.1), channel_id=1, source_target_pairs={{0,1},{1,0},{2,3},{3,2},{4,5},{5,4},{6,7},{7,6},{8,9},{9,8},{10,11... | collective-permute-start | bytes 196616 | tf_op jit(solution)/shard_map/ppermute | solution.py:35
  1.2 13.1 %collective-permute-start.6 = (bf16[256,128]{1,0:T(8,128)(2,1)}, bf16[256,128]{1,0:T(8,128)(2,1)S(1)}, u32[]{:S(2)}, u32[]{:S(2)}) collective-permute-start(bf16[256,128]{1,0:T(8,128)(2,1)} %anch_ref.1), channel_id=1, source_target_pairs={{0,3},{1,2},{2,1},{3,0},{4,7},{5,6},{6,5},{7,4},{8,11},{9,10},{10,... | collective-permute-start | bytes 196616 | tf_op jit(solution)/shard_map/ppermute | solution.py:35
  3.8 10.5 %collective-permute-start.5 = (bf16[256,128]{1,0:T(8,128)(2,1)}, bf16[256,128]{1,0:T(8,128)(2,1)S(1)}, u32[]{:S(2)}, u32[]{:S(2)}) collective-permute-start(bf16[256,128]{1,0:T(8,128)(2,1)} %anch_ref.1), channel_id=1, source_target_pairs={{0,2},{1,3},{2,0},{3,1},{4,6},{5,7},{6,4},{7,5},{8,10},{9,11},{10,... | collective-permute-start | bytes 196616 | tf_op jit(solution)/shard_map/ppermute | solution.py:35
  5.9 3.7 %collective-permute-start = (bf16[32,128]{1,0:T(8,128)(2,1)S(1)}, bf16[32,128]{1,0:T(8,128)(2,1)S(1)}, u32[]{:S(2)}, u32[]{:S(2)}) collective-permute-start(bf16[32,128]{1,0:T(8,128)(2,1)S(1)} %get-tuple-element.35), channel_id=1, source_target_pairs={{0,4},{1,5},{2,6},{3,7},{4,0},{5,1},{6,2},{7,3},{8,12},{9,13},{10,... | collective-permute-start | bytes 24584 | tf_op jit(solution)/shard_map/ppermute | solution.py:35
  9.6 7.5 %collective-permute-start.3 = (bf16[64,128]{1,0:T(8,128)(2,1)S(1)}, bf16[64,128]{1,0:T(8,128)(2,1)S(1)}, u32[]{:S(2)}, u32[]{:S(2)}) collective-permute-start(bf16[64,128]{1,0:T(8,128)(2,1)S(1)} %constant_dynamic-update-slice_fusion.refs_0_), channel_id=1, source_target_pairs={{0,24},{1,25},{2,26},{3,27},{4,28},{5,29},{6,30},{7,31},{8,16},{9,... | collective-permute-start | bytes 49160 | tf_op jit(solution)/shard_map/ppermute | solution.py:35
  13.7 4.6 %collective-permute-start.2 = (bf16[64,128]{1,0:T(8,128)(2,1)S(1)}, bf16[64,128]{1,0:T(8,128)(2,1)S(1)}, u32[]{:S(2)}, u32[]{:S(2)}) collective-permute-start(bf16[64,128]{1,0:T(8,128)(2,1)S(1)} %constant_dynamic-update-slice_fusion.refs_0_), channel_id=1, source_target_pairs={{0,16},{1,17},{2,18},{3,19},{4,20},{5,21},{6,22},{7,23},{8,24},{9,... | collective-permute-start | bytes 49160 | tf_op jit(solution)/shard_map/ppermute | solution.py:35
  13.7 4.6 %collective-permute-start.1 = (bf16[64,128]{1,0:T(8,128)(2,1)S(1)}, bf16[64,128]{1,0:T(8,128)(2,1)S(1)}, u32[]{:S(2)}, u32[]{:S(2)}) collective-permute-start(bf16[64,128]{1,0:T(8,128)(2,1)S(1)} %constant_dynamic-update-slice_fusion.refs_0_), channel_id=1, source_target_pairs={{0,8},{1,9},{2,10},{3,11},{4,12},{5,13},{6,14},{7,15},{8,0},{9,1},... | collective-permute-start | bytes 49160 | tf_op jit(solution)/shard_map/ppermute | solution.py:35
  22.0 1.4 %collective-permute-start.7 = (f32[16,640]{1,0:T(8,128)S(1)}, f32[16,640]{1,0:T(8,128)S(1)}, u32[]{:S(2)}, u32[]{:S(2)}) collective-permute-start(f32[16,640]{1,0:T(8,128)S(1)} %get-tuple-element.42), channel_id=1, source_target_pairs={{0,1},{1,0},{2,3},{3,2},{4,5},{5,4},{6,7},{7,6},{8,9},{9,8},{10,11... | collective-permute-start | bytes 122888 | tf_op jit(solution)/shard_map/ppermute | solution.py:35
  23.5 5.0 %collective-permute-start.10 = (f32[16,640]{1,0:T(8,128)S(1)}, f32[16,640]{1,0:T(8,128)S(1)}, u32[]{:S(2)}, u32[]{:S(2)}) collective-permute-start(f32[16,640]{1,0:T(8,128)S(1)} %add.67), channel_id=1, source_target_pairs={{0,6},{1,7},{2,4},{3,5},{4,2},{5,3},{6,0},{7,1},{8,14},{9,15},{10,... | collective-permute-start | bytes 122888 | tf_op jit(solution)/shard_map/ppermute | solution.py:35
  26.0 4.0 %collective-permute-start.9 = (f32[16,640]{1,0:T(8,128)S(1)}, f32[16,640]{1,0:T(8,128)S(1)}, u32[]{:S(2)}, u32[]{:S(2)}) collective-permute-start(f32[16,640]{1,0:T(8,128)S(1)} %add.67), channel_id=1, source_target_pairs={{0,4},{1,5},{2,6},{3,7},{4,0},{5,1},{6,2},{7,3},{8,12},{9,13},{10,... | collective-permute-start | bytes 122888 | tf_op jit(solution)/shard_map/ppermute | solution.py:35
  26.5 4.0 %collective-permute-start.8 = (f32[16,640]{1,0:T(8,128)S(1)}, f32[16,640]{1,0:T(8,128)S(1)}, u32[]{:S(2)}, u32[]{:S(2)}) collective-permute-start(f32[16,640]{1,0:T(8,128)S(1)} %add.67), channel_id=1, source_target_pairs={{0,2},{1,3},{2,0},{3,1},{4,6},{5,7},{6,4},{7,5},{8,10},{9,11},{10,... | collective-permute-start | bytes 122888 | tf_op jit(solution)/shard_map/ppermute | solution.py:35
  30.5 6.9 %collective-permute-start.13 = (f32[16,640]{1,0:T(8,128)S(1)}, f32[16,640]{1,0:T(8,128)S(1)}, u32[]{:S(2)}, u32[]{:S(2)}) collective-permute-start(f32[16,640]{1,0:T(8,128)S(1)} %add_add_fusion.1), channel_id=1, source_target_pairs={{0,24},{1,25},{2,26},{3,27},{4,28},{5,29},{6,30},{7,31},{8,16},{9,... | collective-permute-start | bytes 122888 | tf_op jit(solution)/shard_map/ppermute | solution.py:35
  33.2 4.9 %collective-permute-start.12 = (f32[16,640]{1,0:T(8,128)S(1)}, f32[16,640]{1,0:T(8,128)S(1)}, u32[]{:S(2)}, u32[]{:S(2)}) collective-permute-start(f32[16,640]{1,0:T(8,128)S(1)} %add_add_fusion.1), channel_id=1, source_target_pairs={{0,16},{1,17},{2,18},{3,19},{4,20},{5,21},{6,22},{7,23},{8,24},{9,... | collective-permute-start | bytes 122888 | tf_op jit(solution)/shard_map/ppermute | solution.py:35
  33.2 4.9 %collective-permute-start.11 = (f32[16,640]{1,0:T(8,128)S(1)}, f32[16,640]{1,0:T(8,128)S(1)}, u32[]{:S(2)}, u32[]{:S(2)}) collective-permute-start(f32[16,640]{1,0:T(8,128)S(1)} %add_add_fusion.1), channel_id=1, source_target_pairs={{0,8},{1,9},{2,10},{3,11},{4,12},{5,13},{6,14},{7,15},{8,0},{9,1},... | collective-permute-start | bytes 122888 | tf_op jit(solution)/shard_map/ppermute | solution.py:35
  38.1 1.3 %collective-permute-start.14 = (f32[16,640]{1,0:T(8,128)S(1)}, f32[16,640]{1,0:T(8,128)S(1)}, u32[]{:S(2)}, u32[]{:S(2)}) collective-permute-start(f32[16,640]{1,0:T(8,128)S(1)} %add_add_fusion.held_ref), channel_id=1, source_target_pairs={{0,1},{1,0},{2,3},{3,2},{4,5},{5,4},{6,7},{7,6},{8,9},{9,8},{10,11... | collective-permute-start | bytes 122888 | tf_op jit(solution)/shard_map/ppermute | solution.py:35
  40.9 1.2 %collective-permute-start.15 = (f32[16,512]{1,0:T(8,128)S(1)}, f32[16,512]{1,0:T(8,128)S(1)}, u32[]{:S(2)}, u32[]{:S(2)}) collective-permute-start(f32[16,512]{1,0:T(8,128)S(1)} %get-tuple-element.48), channel_id=1, source_target_pairs={{0,1},{1,0},{2,3},{3,2},{4,5},{5,4},{6,7},{7,6},{8,9},{9,8},{10,11... | collective-permute-start | bytes 98312 | tf_op jit(solution)/shard_map/ppermute | solution.py:35
  42.1 4.8 %collective-permute-start.18 = (f32[16,512]{1,0:T(8,128)S(1)}, f32[16,512]{1,0:T(8,128)S(1)}, u32[]{:S(2)}, u32[]{:S(2)}) collective-permute-start(f32[16,512]{1,0:T(8,128)S(1)} %add.74), channel_id=1, source_target_pairs={{0,6},{1,7},{2,4},{3,5},{4,2},{5,3},{6,0},{7,1},{8,14},{9,15},{10,... | collective-permute-start | bytes 98312 | tf_op jit(solution)/shard_map/ppermute | solution.py:35
  43.6 3.9 %collective-permute-start.17 = (f32[16,512]{1,0:T(8,128)S(1)}, f32[16,512]{1,0:T(8,128)S(1)}, u32[]{:S(2)}, u32[]{:S(2)}) collective-permute-start(f32[16,512]{1,0:T(8,128)S(1)} %add.74), channel_id=1, source_target_pairs={{0,4},{1,5},{2,6},{3,7},{4,0},{5,1},{6,2},{7,3},{8,12},{9,13},{10,... | collective-permute-start | bytes 98312 | tf_op jit(solution)/shard_map/ppermute | solution.py:35
  44.1 3.9 %collective-permute-start.16 = (f32[16,512]{1,0:T(8,128)S(1)}, f32[16,512]{1,0:T(8,128)S(1)}, u32[]{:S(2)}, u32[]{:S(2)}) collective-permute-start(f32[16,512]{1,0:T(8,128)S(1)} %add.74), channel_id=1, source_target_pairs={{0,2},{1,3},{2,0},{3,1},{4,6},{5,7},{6,4},{7,5},{8,10},{9,11},{10,... | collective-permute-start | bytes 98312 | tf_op jit(solution)/shard_map/ppermute | solution.py:35
  48.1 6.0 %collective-permute-start.21 = (f32[16,512]{1,0:T(8,128)S(1)}, f32[16,512]{1,0:T(8,128)S(1)}, u32[]{:S(2)}, u32[]{:S(2)}) collective-permute-start(f32[16,512]{1,0:T(8,128)S(1)} %add_add_fusion.5), channel_id=1, source_target_pairs={{0,24},{1,25},{2,26},{3,27},{4,28},{5,29},{6,30},{7,31},{8,16},{9,... | collective-permute-start | bytes 98312 | tf_op jit(solution)/shard_map/ppermute | solution.py:35
  50.1 5.1 %collective-permute-start.20 = (f32[16,512]{1,0:T(8,128)S(1)}, f32[16,512]{1,0:T(8,128)S(1)}, u32[]{:S(2)}, u32[]{:S(2)}) collective-permute-start(f32[16,512]{1,0:T(8,128)S(1)} %add_add_fusion.5), channel_id=1, source_target_pairs={{0,16},{1,17},{2,18},{3,19},{4,20},{5,21},{6,22},{7,23},{8,24},{9,... | collective-permute-start | bytes 98312 | tf_op jit(solution)/shard_map/ppermute | solution.py:35
  50.4 4.9 %collective-permute-start.19 = (f32[16,512]{1,0:T(8,128)S(1)}, f32[16,512]{1,0:T(8,128)S(1)}, u32[]{:S(2)}, u32[]{:S(2)}) collective-permute-start(f32[16,512]{1,0:T(8,128)S(1)} %add_add_fusion.5), channel_id=1, source_target_pairs={{0,8},{1,9},{2,10},{3,11},{4,12},{5,13},{6,14},{7,15},{8,0},{9,1},... | collective-permute-start | bytes 98312 | tf_op jit(solution)/shard_map/ppermute | solution.py:35
  55.3 1.5 %collective-permute-start.22 = (f32[16,512]{1,0:T(8,128)S(1)}, f32[16,512]{1,0:T(8,128)S(1)}, u32[]{:S(2)}, u32[]{:S(2)}) collective-permute-start(f32[16,512]{1,0:T(8,128)S(1)} %add_add_fusion.4.held_ref), channel_id=1, source_target_pairs={{0,1},{1,0},{2,3},{3,2},{4,5},{5,4},{6,7},{7,6},{8,9},{9,8},{10,11... | collective-permute-start | bytes 98312 | tf_op jit(solution)/shard_map/ppermute | solution.py:35
  58.3 1.2 %collective-permute-start.23 = (f32[16,512]{1,0:T(8,128)S(1)}, f32[16,512]{1,0:T(8,128)S(1)}, u32[]{:S(2)}, u32[]{:S(2)}) collective-permute-start(f32[16,512]{1,0:T(8,128)S(1)} %get-tuple-element.54), channel_id=1, source_target_pairs={{0,1},{1,0},{2,3},{3,2},{4,5},{5,4},{6,7},{7,6},{8,9},{9,8},{10,11... | collective-permute-start | bytes 98312 | tf_op jit(solution)/shard_map/ppermute | solution.py:35
  59.5 4.8 %collective-permute-start.26 = (f32[16,512]{1,0:T(8,128)S(1)}, f32[16,512]{1,0:T(8,128)S(1)}, u32[]{:S(2)}, u32[]{:S(2)}) collective-permute-start(f32[16,512]{1,0:T(8,128)S(1)} %add.81), channel_id=1, source_target_pairs={{0,6},{1,7},{2,4},{3,5},{4,2},{5,3},{6,0},{7,1},{8,14},{9,15},{10,... | collective-permute-start | bytes 98312 | tf_op jit(solution)/shard_map/ppermute | solution.py:35
  62.0 3.9 %collective-permute-start.25 = (f32[16,512]{1,0:T(8,128)S(1)}, f32[16,512]{1,0:T(8,128)S(1)}, u32[]{:S(2)}, u32[]{:S(2)}) collective-permute-start(f32[16,512]{1,0:T(8,128)S(1)} %add.81), channel_id=1, source_target_pairs={{0,4},{1,5},{2,6},{3,7},{4,0},{5,1},{6,2},{7,3},{8,12},{9,13},{10,... | collective-permute-start | bytes 98312 | tf_op jit(solution)/shard_map/ppermute | solution.py:35
  62.5 3.9 %collective-permute-start.24 = (f32[16,512]{1,0:T(8,128)S(1)}, f32[16,512]{1,0:T(8,128)S(1)}, u32[]{:S(2)}, u32[]{:S(2)}) collective-permute-start(f32[16,512]{1,0:T(8,128)S(1)} %add.81), channel_id=1, source_target_pairs={{0,2},{1,3},{2,0},{3,1},{4,6},{5,7},{6,4},{7,5},{8,10},{9,11},{10,... | collective-permute-start | bytes 98312 | tf_op jit(solution)/shard_map/ppermute | solution.py:35
  66.4 5.8 %collective-permute-start.29 = (f32[16,512]{1,0:T(8,128)S(1)}, f32[16,512]{1,0:T(8,128)S(1)}, u32[]{:S(2)}, u32[]{:S(2)}) collective-permute-start(f32[16,512]{1,0:T(8,128)S(1)} %add_add_fusion.3), channel_id=1, source_target_pairs={{0,24},{1,25},{2,26},{3,27},{4,28},{5,29},{6,30},{7,31},{8,16},{9,... | collective-permute-start | bytes 98312 | tf_op jit(solution)/shard_map/ppermute | solution.py:35
  68.3 5.0 %collective-permute-start.28 = (f32[16,512]{1,0:T(8,128)S(1)}, f32[16,512]{1,0:T(8,128)S(1)}, u32[]{:S(2)}, u32[]{:S(2)}) collective-permute-start(f32[16,512]{1,0:T(8,128)S(1)} %add_add_fusion.3), channel_id=1, source_target_pairs={{0,16},{1,17},{2,18},{3,19},{4,20},{5,21},{6,22},{7,23},{8,24},{9,... | collective-permute-start | bytes 98312 | tf_op jit(solution)/shard_map/ppermute | solution.py:35
  69.1 4.3 %collective-permute-start.27 = (f32[16,512]{1,0:T(8,128)S(1)}, f32[16,512]{1,0:T(8,128)S(1)}, u32[]{:S(2)}, u32[]{:S(2)}) collective-permute-start(f32[16,512]{1,0:T(8,128)S(1)} %add_add_fusion.3), channel_id=1, source_target_pairs={{0,8},{1,9},{2,10},{3,11},{4,12},{5,13},{6,14},{7,15},{8,0},{9,1},... | collective-permute-start | bytes 98312 | tf_op jit(solution)/shard_map/ppermute | solution.py:35
  71.2 2.4 %collective-permute-start.31 = (f32[8,2048]{1,0:T(8,128)S(1)}, f32[8,2048]{1,0:T(8,128)S(1)}, u32[]{:S(2)}, u32[]{:S(2)}) collective-permute-start(f32[8,2048]{1,0:T(8,128)S(1)} %get-tuple-element.63), channel_id=1, source_target_pairs={{0,1},{1,0},{2,3},{3,2},{4,5},{5,4},{6,7},{7,6},{8,9},{9,8},{10,11... | collective-permute-start | bytes 196616 | tf_op jit(solution)/shard_map/ppermute | solution.py:35
  71.3 5.0 %collective-permute-start.32 = (f32[8,2048]{1,0:T(8,128)S(1)}, f32[8,2048]{1,0:T(8,128)S(1)}, u32[]{:S(2)}, u32[]{:S(2)}) collective-permute-start(f32[8,2048]{1,0:T(8,128)S(1)} %get-tuple-element.64), channel_id=1, source_target_pairs={{0,2},{1,3},{2,0},{3,1},{4,6},{5,7},{6,4},{7,5},{8,10},{9,11},{10,... | collective-permute-start | bytes 196616 | tf_op jit(solution)/shard_map/ppermute | solution.py:35
  72.2 4.4 %collective-permute-start.33 = (f32[8,2048]{1,0:T(8,128)S(1)}, f32[8,2048]{1,0:T(8,128)S(1)}, u32[]{:S(2)}, u32[]{:S(2)}) collective-permute-start(f32[8,2048]{1,0:T(8,128)S(1)} %get-tuple-element.65), channel_id=1, source_target_pairs={{0,3},{1,2},{2,1},{3,0},{4,7},{5,6},{6,5},{7,4},{8,11},{9,10},{10,... | collective-permute-start | bytes 196616 | tf_op jit(solution)/shard_map/ppermute | solution.py:35
  73.3 3.3 %collective-permute-start.30 = (f32[16,512]{1,0:T(8,128)S(1)}, f32[16,512]{1,0:T(8,128)S(1)}, u32[]{:S(2)}, u32[]{:S(2)}) collective-permute-start(f32[16,512]{1,0:T(8,128)S(1)} %add_add_fusion.2.held_ref), channel_id=1, source_target_pairs={{0,1},{1,0},{2,3},{3,2},{4,5},{5,4},{6,7},{7,6},{8,9},{9,8},{10,11... | collective-permute-start | bytes 98312 | tf_op jit(solution)/shard_map/ppermute | solution.py:35
